TPU v7x, 256 devices: a whole 4x4x8 slice. The times are simulated.
256 devices in a mesh: dp: 4 (over y), tensor: 16 (over z, core), owner: 4 (over x).
Axes of the slice: x: 4, y: 4, z: 8, core: 2. Of those that a mesh axis runs over, the one named last changes fastest.
Arguments:
- queries: bfloat16 [512, 8192], P(('dp', 'tensor'), 'owner'), may hold values from -360 to 360
- cached_key_rows: bfloat16 [512, 512, 8, 128], P(('dp', 'tensor'), None, 'owner'), may hold values from -6 to 6
- cached_value_rows: bfloat16 [512, 512, 8, 128], P(('dp', 'tensor'), None, 'owner'), may hold values from -6 to 6
- newest_key: bfloat16 [512, 8, 128], P(('dp', 'tensor'), 'owner'), may hold values from -6 to 6
- newest_value: bfloat16 [512, 8, 128], P(('dp', 'tensor'), 'owner'), may hold values from -6 to 6
- output_weight: bfloat16 [8, 1024, 8192], P('owner', 'tensor'), may hold values from -0.75 to 0.75
- adapter_down_weight: bfloat16 [128, 8, 1024, 64], P('owner', None, 'tensor'), may hold values from -0.5 to 0.5
- adapter_up_weight: bfloat16 [128, 64, 8192], P('owner', None, 'tensor'), may hold values from -0.75 to 0.75
- adapter_store_row: int32 [128], replicated, may hold values from 0 to 127, each once
- adapters_by_group: int32 [4, 16], P('dp'), may hold values from 0 to 127, as said below
- adapter_per_row: int32 [512], P('dp'), may hold values from 0 to 127, as said below
Outputs:
- output: bfloat16 [512, 8192], P('dp', ('tensor', 'owner'))
Inputs may be any that keep to these rules, and one draw needn't show every extreme that they name: `adapter_per_row`: the rows g * 128 to (g + 1) * 128 - 1 form dp group g; each row's adapter is one of its group's listed adapters, and each listed one is used by some row of the group. `adapters_by_group`: the 16 adapters of a group are distinct.
All inputs are finite; a program needn't handle non-finite values.
Results may differ from a plain program's by a relative error of at most 0.015.
Values may be sent and summed in bfloat16 or wider, within the bound.
No kernel may reach another device: no remote copies, remote signals or barrier semaphores. Data moves between devices by JAX's collectives and lax.ppermute only.
A program may use at most 128 MiB of HBM per device.

v0:
```python
import jax
import jax.numpy as jnp
from jax import lax
from jax.sharding import PartitionSpec as P

ADAPTER_SCALE = 2.0


def shards(
    queries,
    cached_key_rows,
    cached_value_rows,
    newest_key,
    newest_value,
    output_weight,
    adapter_down_weight,
    adapter_up_weight,
    adapter_store_row,
    adapters_by_group,
    adapter_per_row,
):
    owner_index = lax.axis_index("owner")
    row_count = queries.shape[0]
    local_heads = newest_key.shape[1]
    head_width = newest_key.shape[2]
    group_width = queries.shape[1] // local_heads
    query_heads = queries.reshape(row_count, local_heads, group_width // head_width, head_width)
    inverse_root = head_width ** (-0.5)
    scores = (
        jnp.einsum(
            "rkgh,rckh->rkgc", query_heads, cached_key_rows, preferred_element_type=jnp.float32
        )
        * inverse_root
    )
    fresh_score = (
        jnp.einsum("rkgh,rkh->rkg", query_heads, newest_key, preferred_element_type=jnp.float32)
        * inverse_root
    )
    overall = jnp.maximum(jnp.max(scores, axis=-1), fresh_score)
    weights_exp = jnp.exp(scores - overall[..., None])
    fresh_weight = jnp.exp(fresh_score - overall)
    denominator = jnp.sum(weights_exp, axis=-1) + fresh_weight
    mixed = jnp.einsum(
        "rkgc,rckh->rkgh", weights_exp, cached_value_rows, preferred_element_type=jnp.float32
    )
    mixed = mixed + fresh_weight[..., None] * newest_value.astype(jnp.float32)[:, :, None, :]
    mixed = (
        (mixed / denominator[..., None])
        .astype(jnp.bfloat16)
        .reshape(row_count, local_heads, group_width)
    )
    attention = lax.all_to_all(mixed, "tensor", split_axis=2, concat_axis=0, tiled=True)
    slot_ids = adapters_by_group[0]
    adapter_total = adapter_store_row.shape[0]
    matches = slot_ids[:, None] == jnp.arange(adapter_total, dtype=jnp.int32)[None, :]
    slot_home = jnp.sum(jnp.where(matches, adapter_store_row[None, :], 0), axis=1)
    store_count = adapter_down_weight.shape[0]
    slot_match = (adapter_per_row[:, None] == slot_ids[None, :]).astype(jnp.float32)
    position = slot_home - owner_index * store_count
    is_present = (position >= 0) & (position < store_count)
    clamped_index = jnp.clip(position, 0, store_count - 1)
    down_projected = jnp.where(
        is_present[:, None, None, None], adapter_down_weight[clamped_index], 0
    )
    up_projected = jnp.where(is_present[:, None, None], adapter_up_weight[clamped_index], 0)
    down_total, up_total = (
        lax.psum_scatter(down_projected, "owner", scatter_dimension=1, tiled=True).astype(
            jnp.float32
        ),
        lax.psum_scatter(up_projected, "owner", scatter_dimension=2, tiled=True).astype(
            jnp.float32
        ),
    )
    slot_down = down_total.astype(jnp.bfloat16)
    slot_up = up_total.astype(jnp.bfloat16)
    rank_slots = jnp.einsum(
        "rkf,skfn->rsn", attention, slot_down, preferred_element_type=jnp.float32
    )
    rank_part = jnp.sum(slot_match[:, :, None] * rank_slots, axis=1)
    rank_code = lax.psum(rank_part, ("tensor", "owner")).astype(jnp.bfloat16)
    update_slots = jnp.einsum("rn,snc->rsc", rank_code, slot_up, preferred_element_type=jnp.float32)
    adapter_delta = jnp.sum(slot_match[:, :, None] * update_slots, axis=1)
    partial_sum = jnp.einsum(
        "rkf,kfd->rd", attention, output_weight, preferred_element_type=jnp.float32
    )
    base_output = lax.psum_scatter(
        partial_sum, ("tensor", "owner"), scatter_dimension=1, tiled=True
    )
    return (base_output + ADAPTER_SCALE * adapter_delta).astype(jnp.bfloat16)


def solution(mesh):
    return jax.shard_map(
        shards,
        mesh=mesh,
        in_specs=(
            P(("dp", "tensor"), "owner"),
            P(("dp", "tensor"), None, "owner", None),
            P(("dp", "tensor"), None, "owner", None),
            P(("dp", "tensor"), "owner", None),
            P(("dp", "tensor"), "owner", None),
            P("owner", "tensor", None),
            P("owner", None, "tensor", None),
            P("owner", None, "tensor"),
            P(),
            P("dp", None),
            P("dp"),
        ),
        out_specs=P("dp", ("tensor", "owner")),
        check_vma=False,
    )
```

profile of v0, /device:TPU:24, one launch (start us, length us, event | category | flops | bytes accessed | tf_op | source)
XLA Modules:
  0.0 342.6 jit_solution(8786427746575031881)
XLA Ops:
  6.5 1.0 select_reduce_fusion
  7.6 4.3 %gather_fusion = bf16[16,8,64,64]{3,2,1,0:T(8,128)(2,1)} fusion(bf16[32,8,64,64]{3,2,1,0:T(8,128)(2,1)} %param.17, s32[1024]{0:T(1024)S(1)} %pad_clamp_fusion), kind=kCustom, calls=%fused_computation | custom fusion | bytes 2097216 | tf_op jit(solution)/shard_map/gather | solution.py:63
  11.9 3.1 broadcast_select_fusion
  15.1 3.2 gather_fusion.1
  18.3 1.4 broadcast_select_fusion.1
  19.7 2.9 copy.60
  22.6 4.2 %reshape.104 = bf16[512,1024]{1,0:T(8,128)(2,1)} reshape(bf16[512,16,64]{2,1,0:T(8,128)(2,1)} %bitcast.44) | data formatting | bytes 2097152
  27.0 2.5 fusion.34
  29.5 0.2 fusion.21
  29.8 0.5 fusion.16
  30.2 0.3 copy.54
  30.5 0.5 reshape.107
  31.1 16.2 %all_to_all.18 = bf16[16,2,512]{2,1,0:T(2,128)(2,1)S(1)} all-to-all(bf16[16,2,512]{2,1,0:T(2,128)(2,1)S(1)} %reshape.107), channel_id=1, replica_groups=mesh['dp'=4,'tensor'=16,'owner'=4] {'tensor'}, dimensions={0} | all-to-all | bytes 65536 | tf_op jit(solution)/shard_map/all_to_all | solution.py:52
  47.3 0.6 reshape.108
  47.9 0.4 copy.56
  48.3 2.7 convolution_bitcast_fusion
  51.0 0.6 copy-done.7
  51.7 0.6 dynamic-slice
  53.0 28.8 %all-reduce.3.cloned.1.call-done = bf16[16,8,64,64]{3,2,1,0:T(8,128)(2,1)} async-done(((bf16[16,8,64,64]{3,2,1,0:T(8,128)(2,1)}), bf16[16,8,64,64]{3,2,1,0:T(8,128)(2,1)}) %all-reduce.3.cloned.1.call-update) | async-done | bytes 1048592
  81.7 1.4 fusion.6
  83.1 249.6 %psum.7 = bf16[128,64]{0,1:T(8,128)(2,1)S(1)} all-reduce(f32[128,64]{0,1:T(8,128)S(1)} %fusion.6), channel_id=1, replica_groups=mesh['dp'=4,'tensor'=16,'owner'=4] {'tensor','owner'}, use_global_device_ids=true, to_apply=%region_6.7 | all-reduce | flops 8192 | bytes 49152 | tf_op jit(solution)/shard_map/psum | solution.py:80
  332.8 1.3 reshape.105
  334.1 0.4 fusion.4
  334.6 1.5 add_convert_fusion
  (31 shorter events, 0.5 us)
Async XLA Ops:
  6.5 41.8 %copy-start = (bf16[2,64,8192]{2,1,0:T(8,128)(2,1)S(1)}, bf16[2,64,8192]{2,1,0:T(8,128)(2,1)}, u32[]{:S(2)}) copy-start(bf16[2,64,8192]{2,1,0:T(8,128)(2,1)} %param.16) | copy-start | bytes 6291460
  6.5 75.2 %all-reduce.3.cloned.1.call-start = ((), (), s32[]{:S(2)}) async-start(), calls=%async_computation.5 | async-start | bytes 4194304
  15.1 317.7 %reduce-scatter.8.cloned.1.call-start = ((), (), s32[]{:S(2)}) async-start(), calls=%async_computation.4 | async-start | bytes 1310720
  22.6 4.2 %copy-start.2 = (bf16[8,2,128]{2,1,0:T(2,128)(2,1)S(1)}, bf16[8,2,128]{2,1,0:T(2,128)(2,1)}, u32[]{:S(2)}) copy-start(bf16[8,2,128]{2,1,0:T(2,128)(2,1)} %param.15) | copy-start | bytes 12292
  22.6 4.3 %copy-start.1 = (bf16[8,2048]{1,0:T(8,128)(2,1)S(1)}, bf16[8,2048]{1,0:T(8,128)(2,1)}, u32[]{:S(2)}) copy-start(bf16[8,2048]{1,0:T(8,128)(2,1)} %param.11) | copy-start | bytes 98308
  22.6 4.3 %copy-start.6 = (bf16[8,2,128]{2,1,0:T(2,128)(2,1)S(1)}, bf16[8,2,128]{2,1,0:T(2,128)(2,1)}, u32[]{:S(2)}) copy-start(bf16[8,2,128]{2,1,0:T(2,128)(2,1)} %param.14) | copy-start | bytes 12292
  26.8 307.8 %reduce-scatter.6.cloned.1.call-start = ((), (), s32[]{:S(2)}) async-start(), calls=%async_computation.3 | async-start | bytes 4259840 | tf_op jit(solution)/shard_map/reduce_scatter | solution.py:86
  26.9 2.9 copy-start.5
  51.0 0.7 copy-start.7
  51.0 1.9 copy-start.3
  51.0 1.9 copy-start.4
Sparse Core Ops, SparseCore 0:
  15.2 66.4 all-reduce.2
  84.5 25.9 reduce-scatter.7
  114.6 143.6 reduce-scatter.5
where the time goes:
time: 343 us
  blocking collectives  266 us (78%)
  waiting for transfers between devices  28.8 us (8%)
  local copies, waits for them, and re-layouts  19 us (6%)
  between operations  13.9 us (4%)
  matrix products  7.57 us (2%)
  other arithmetic  7.3 us (2%)
    psum x1, blocking collectives, shards(): rank_code = lax.psum(rank_part, ('tensor', 'owner')).astype(jnp.bfloat16)  250 us
    unnamed x5, waiting for transfers between devices  28.8 us
    all_to_all x1, blocking collectives, shards(): lax.all_to_all(mixed, 'tensor', split_axis=2, concat_axis=0, tiled=True)  16.2 us
    unnamed x22, local copies, waits for them, and re-layouts  10.8 us
  transfers between devices with their start and end apart: 3, of which 1 were waited for; matrix products, arithmetic and copies ran while one was open for 7% of the time, Pallas kernels for 0%

commit v1 on v0

v1 whole, which is shorter than its diff:
```python
import jax
import jax.numpy as jnp
from jax import lax
from jax.experimental import pallas as pl
from jax.experimental.pallas import tpu as pltpu
from jax.sharding import PartitionSpec as P

ADAPTER_SCALE = 2.0
BF16 = jnp.bfloat16
F32 = jnp.float32

VMEM = pl.BlockSpec(memory_space=pltpu.VMEM)
SMEM = pl.BlockSpec(memory_space=pltpu.SMEM)
ANY = pl.BlockSpec(memory_space=pl.ANY)


def slot_position(slot, group_ref, store_ref, stored):
    spot = store_ref[group_ref[0, slot]] - lax.axis_index("owner") * stored
    here = jnp.logical_and(spot >= 0, spot < stored)
    return jnp.clip(spot, 0, stored - 1), here


def row_adapters(rows_ref, width):
    rows = rows_ref.shape[1]
    return jnp.transpose(jnp.broadcast_to(rows_ref[...], (rows, rows)))[:, :width]


def project_kernel(
    group_ref, store_ref, rows_ref, att_ref, w_ref, down_ref, keep_ref, send_ref, dbuf, acc, sems
):
    slots = dbuf.shape[0]
    stored = down_ref.shape[0]
    copies = []
    for s in range(slots):
        spot, _ = slot_position(s, group_ref, store_ref, stored)
        copy = pltpu.make_async_copy(down_ref.at[spot], dbuf.at[s], sems.at[s])
        copy.start()
        copies.append(copy)
    owners, rows, feats = att_ref.shape
    att = jnp.concatenate([att_ref[o] for o in range(owners)], axis=1)
    weight = w_ref[...].reshape(owners * feats, w_ref.shape[2])
    first = lax.rem(lax.axis_index("tensor"), 2) == 0
    planes = w_ref.shape[2] // 256
    for z in range(planes):
        part = jnp.dot(att, weight[:, 256 * z : 256 * z + 256], preferred_element_type=F32)
        even, odd = part[:, :128], part[:, 128:]
        keep_ref[z * rows : (z + 1) * rows, :] = jnp.where(first, even, odd)
        send_ref[z * rows : (z + 1) * rows, :] = jnp.where(first, odd, even).astype(BF16)
    rank = dbuf.shape[-1]
    ids = row_adapters(rows_ref, rank)
    acc[...] = jnp.zeros_like(acc)
    for s in range(slots):
        copies[s].wait()
        _, here = slot_position(s, group_ref, store_ref, stored)

        @pl.when(here)
        def _(s=s):
            table = dbuf[s].reshape(owners * feats, rank)
            code = jnp.dot(att, table, preferred_element_type=F32)
            acc[...] += jnp.where(ids == group_ref[0, s], code, 0.0)

    half = rows // 2
    code = jnp.concatenate([acc[:half, :], acc[half:, :]], axis=1)
    keep_ref[planes * rows :, :] = code
    send_ref[planes * rows :, :] = code.astype(BF16)


def pair_kernel(keep_ref, got_ref, out_ref):
    planes, total, _ = out_ref.shape
    rows = (keep_ref.shape[0] - total) // (planes - 1)
    code = (keep_ref[planes * rows :, :] + got_ref[planes * rows :, :].astype(F32)).astype(BF16)
    for z in range(planes):
        span = pl.ds(z * rows, rows)
        out_ref[z, :rows, :] = (keep_ref[span, :] + got_ref[span, :].astype(F32)).astype(BF16)
        out_ref[z, rows:, :] = code


def update_kernel(
    group_ref, store_ref, rows_ref, parts_ref, up_ref, base_ref, send_ref, ubuf, acc, sems
):
    slots = ubuf.shape[0]
    stored = up_ref.shape[0]
    copies = []
    for s in range(slots):
        spot, _ = slot_position(s, group_ref, store_ref, stored)
        copy = pltpu.make_async_copy(up_ref.at[spot], ubuf.at[s], sems.at[s])
        copy.start()
        copies.append(copy)
    total = parts_ref[0].astype(F32)
    for z in range(1, parts_ref.shape[0]):
        total = total + parts_ref[z].astype(F32)
    rows = base_ref.shape[0]
    base_ref[...] = total[:rows]
    rank = ubuf.shape[1]
    packed = total[rows:]
    code = jnp.concatenate([packed[:, :rank], packed[:, rank:]], axis=0).astype(BF16)
    ids = row_adapters(rows_ref, rank)
    acc[...] = jnp.zeros_like(acc)
    for s in range(slots):
        copies[s].wait()
        _, here = slot_position(s, group_ref, store_ref, stored)

        @pl.when(here)
        def _(s=s):
            chosen = jnp.where(ids == group_ref[0, s], code.astype(F32), 0.0).astype(BF16)
            acc[...] += jnp.dot(chosen, ubuf[s], preferred_element_type=F32)

    width = send_ref.shape[2]
    for o in range(send_ref.shape[0]):
        send_ref[o] = acc[:, o * width : (o + 1) * width].astype(BF16)


def final_kernel(base_ref, got_ref, out_ref):
    update = got_ref[0].astype(F32)
    for o in range(1, got_ref.shape[0]):
        update = update + got_ref[o].astype(F32)
    out_ref[...] = (base_ref[...] + ADAPTER_SCALE * update).astype(BF16)


def attend(queries, cached_key_rows, cached_value_rows, newest_key, newest_value):
    row_count = queries.shape[0]
    local_heads = newest_key.shape[1]
    head_width = newest_key.shape[2]
    group_width = queries.shape[1] // local_heads
    query_heads = queries.reshape(row_count, local_heads, group_width // head_width, head_width)
    inverse_root = head_width ** (-0.5)
    scores = (
        jnp.einsum(
            "rkgh,rckh->rkgc", query_heads, cached_key_rows, preferred_element_type=jnp.float32
        )
        * inverse_root
    )
    fresh_score = (
        jnp.einsum("rkgh,rkh->rkg", query_heads, newest_key, preferred_element_type=jnp.float32)
        * inverse_root
    )
    overall = jnp.maximum(jnp.max(scores, axis=-1), fresh_score)
    weights_exp = jnp.exp(scores - overall[..., None])
    fresh_weight = jnp.exp(fresh_score - overall)
    denominator = jnp.sum(weights_exp, axis=-1) + fresh_weight
    mixed = jnp.einsum(
        "rkgc,rckh->rkgh", weights_exp, cached_value_rows, preferred_element_type=jnp.float32
    )
    mixed = mixed + fresh_weight[..., None] * newest_value.astype(jnp.float32)[:, :, None, :]
    return (mixed / denominator[..., None]).astype(jnp.bfloat16)


def shards(
    queries,
    cached_key_rows,
    cached_value_rows,
    newest_key,
    newest_value,
    output_weight,
    adapter_down_weight,
    adapter_up_weight,
    adapter_store_row,
    adapters_by_group,
    adapter_per_row,
):
    owners = lax.axis_size("owner")
    tensors = lax.axis_size("tensor")
    planes = tensors // 2
    slots = adapters_by_group.shape[1]
    row_count, local_heads, head_width = newest_key.shape
    rows = adapter_per_row.shape[0]
    feats = local_heads * output_weight.shape[1]
    columns = output_weight.shape[2]
    block = columns // (tensors * owners)
    rank = adapter_down_weight.shape[-1]
    row_ids = adapter_per_row.reshape(1, rows)

    weight = output_weight.reshape(feats, tensors, owners, block).transpose(2, 0, 1, 3)
    weight = weight.reshape(owners, feats, tensors * block)
    weight = lax.all_to_all(weight, "owner", split_axis=0, concat_axis=0, tiled=True)

    mixed = attend(queries, cached_key_rows, cached_value_rows, newest_key, newest_value)
    part = output_weight.shape[1]
    outgoing = mixed.reshape(row_count, local_heads, tensors, part).transpose(2, 0, 1, 3)
    outgoing = outgoing.reshape(1, tensors, row_count, feats)
    outgoing = jnp.broadcast_to(outgoing, (owners, tensors, row_count, feats))
    outgoing = outgoing.reshape(owners * tensors, row_count, feats)
    attention = lax.all_to_all(
        outgoing, ("owner", "tensor"), split_axis=0, concat_axis=0, tiled=True
    )
    attention = attention.reshape(owners, rows, feats)

    tall = planes * rows + rows // 2
    keep, send = pl.pallas_call(
        project_kernel,
        name="project",
        out_shape=(
            jax.ShapeDtypeStruct((tall, block), F32),
            jax.ShapeDtypeStruct((tall, block), BF16),
        ),
        in_specs=[SMEM, SMEM, VMEM, VMEM, VMEM, ANY],
        out_specs=(VMEM, VMEM),
        scratch_shapes=[
            pltpu.VMEM((slots,) + adapter_down_weight.shape[1:], BF16),
            pltpu.VMEM((rows, rank), F32),
            pltpu.SemaphoreType.DMA((slots,)),
        ],
    )(adapters_by_group, adapter_store_row, row_ids, attention, weight, adapter_down_weight)
    got = lax.ppermute(send, "tensor", [(t, t ^ 1) for t in range(tensors)])
    pieces = pl.pallas_call(
        pair_kernel,
        name="pair",
        out_shape=jax.ShapeDtypeStruct((planes, rows + rows // 2, block), BF16),
        in_specs=[VMEM, VMEM],
        out_specs=VMEM,
    )(keep, got)
    groups = [[2 * z + c for z in range(planes)] for c in range(2)]
    parts = lax.all_to_all(
        pieces, "tensor", split_axis=0, concat_axis=0, tiled=True, axis_index_groups=groups
    )
    base, update = pl.pallas_call(
        update_kernel,
        name="update",
        out_shape=(
            jax.ShapeDtypeStruct((rows, block), F32),
            jax.ShapeDtypeStruct((owners, rows, block), BF16),
        ),
        in_specs=[SMEM, SMEM, VMEM, VMEM, ANY],
        out_specs=(VMEM, VMEM),
        scratch_shapes=[
            pltpu.VMEM((slots,) + adapter_up_weight.shape[1:], BF16),
            pltpu.VMEM((rows, owners * block), F32),
            pltpu.SemaphoreType.DMA((slots,)),
        ],
    )(adapters_by_group, adapter_store_row, row_ids, parts, adapter_up_weight)
    update = lax.all_to_all(update, "owner", split_axis=0, concat_axis=0, tiled=True)
    return pl.pallas_call(
        final_kernel,
        name="final",
        out_shape=jax.ShapeDtypeStruct((rows, block), BF16),
        in_specs=[VMEM, VMEM],
        out_specs=VMEM,
    )(base, update)


def solution(mesh):
    return jax.shard_map(
        shards,
        mesh=mesh,
        in_specs=(
            P(("dp", "tensor"), "owner"),
            P(("dp", "tensor"), None, "owner", None),
            P(("dp", "tensor"), None, "owner", None),
            P(("dp", "tensor"), "owner", None),
            P(("dp", "tensor"), "owner", None),
            P("owner", "tensor", None),
            P("owner", None, "tensor", None),
            P("owner", None, "tensor"),
            P(),
            P("dp", None),
            P("dp"),
        ),
        out_specs=P("dp", ("tensor", "owner")),
        check_vma=False,
    )
```

time: 343 us -> 108 us (0.31)
  blocking collectives: 266 us -> 63.2 us
  waiting for transfers between devices: 28.8 us -> 1.76 us
  between operations: 13.9 us -> 0.09 us
  Pallas kernels: 0 us -> 12.5 us
  starting transfers between devices: 0.09 us -> 12 us
  other arithmetic: 7.3 us -> 1.07 us
  local copies, waits for them, and re-layouts: 19 us -> 13.4 us
  matrix products: 7.57 us -> 3.27 us
    psum x1 -> x0, blocking collectives: 250 us -> none  [shards(): rank_code = lax.psum(rank_part, ('tensor', 'owner')).astype(jnp.bfloat16)]
    all_to_all x1 -> x3, blocking collectives: 16.2 us -> 63.2 us  [the longest x1 31.3 us: shards(): lax.all_to_all(weight, 'owner', split_axis=0, concat_axis=0, tiled=True)]
    unnamed x5 -> x0, waiting for transfers between devices: 28.8 us -> none
    pallas_call x0 -> x4, Pallas kernels: none -> 12.5 us  [the longest x1 5.46 us: shards(): pl.pallas_call(project_kernel, name='project', out_shape=(jax.ShapeDtypeS...]
    all_to_all x0 -> x1, starting transfers between devices: none -> 11.9 us  [shards(): lax.all_to_all(outgoing, ('owner', 'tensor'), split_axis=0, concat_axis=0...]
    reshape x1 -> x5, local copies, waits for them, and re-layouts: 0.3 us -> 11.9 us  [the longest x2 7.58 us: shards(): output_weight.reshape(feats, tensors, owners, block).transpose(2, 0, 1, 3)]
    unnamed x22 -> x8, local copies, waits for them, and re-layouts: 10.8 us -> 0.73 us
    gather x2 -> x0, local copies, waits for them, and re-layouts: 7.54 us -> none  [the longest x1 4.35 us: shards(): adapter_down_weight[clamped_index]]
  transfers between devices with their start and end apart: 3 -> 2, of which waited for: 1 -> 1; matrix products, arithmetic and copies ran while one was open for 7% -> 11% of each run, Pallas kernels for 0% -> 0%
where the time goes in v1:
time: 108 us; the launch traced here: 107 us
  blocking collectives  63.2 us (59%)
  local copies, waits for them, and re-layouts  13.4 us (12%)
  Pallas kernels  12.5 us (12%)
  starting transfers between devices  12 us (11%)
  matrix products  3.27 us (3%)
  waiting for transfers between devices  1.76 us (2%)
    all_to_all x1, blocking collectives, shards(): lax.all_to_all(weight, 'owner', split_axis=0, concat_axis=0, tiled=True)  31.3 us
    all_to_all x1, blocking collectives, shards(): lax.all_to_all(pieces, 'tensor', split_axis=0, concat_axis=0, tiled=True,...  21.9 us
    all_to_all x1, starting transfers between devices, shards(): lax.all_to_all(outgoing, ('owner', 'tensor'), split_axis=0, concat_axis=0...  11.9 us
    all_to_all x1, blocking collectives, shards(): lax.all_to_all(update, 'owner', split_axis=0, concat_axis=0, tiled=True)  9.99 us
    reshape x2, local copies, waits for them, and re-layouts, shards(): output_weight.reshape(feats, tensors, owners, block).transpose(2, 0, 1, 3)  7.58 us
    pallas_call x1, Pallas kernels, shards(): pl.pallas_call(project_kernel, name='project', out_shape=(jax.ShapeDtypeS...  5.46 us
    reshape x1, local copies, waits for them, and re-layouts, shards(): weight = weight.reshape(owners, feats, tensors * block)  4.14 us
    pallas_call x1, Pallas kernels, shards(): pl.pallas_call(update_kernel, name='update', out_shape=(jax.ShapeDtypeStr...  3.55 us
  transfers between devices with their start and end apart: 2, of which 1 were waited for; matrix products, arithmetic and copies ran while one was open for 11% of the time, Pallas kernels for 0%

profile of v1, /device:TPU:24, one launch (start us, length us, event | category | flops | bytes accessed | tf_op | source)
XLA Modules:
  0.0 107.3 jit_solution(15315684715255902298)
XLA Ops:
  0.0 0.8 convert_element_type.6
  0.8 1.3 %fusion.18 = f32[8,2,1,8]{3,2,1,0:T(1,128)S(1)} fusion(bf16[8,2,8,128]{3,0,2,1:T(8,128)(2,1)} %bitcast.20, bf16[8,2,128,1]{2,1,0,3:T(2,128)(2,1)} %bitcast.26), kind=kOutput, calls=%fused_computation.13 | convolution fusion | flops 32768 | bytes 37376 | tf_op jit(solution)/shard_map/rkgh,rkh->rkg/dot_general | solution.py:134
  2.2 1.5 %fusion.23 = (f32[8,2,8]{2,1,0:T(2,128)S(1)}, f32[8,2,8,512]{3,2,1,0:T(8,128)S(1)}) fusion(bf16[8,512,2,128]{3,2,1,0:T(2,128)(2,1)S(1)} %copy-done, bf16[8,2,8,128]{3,0,2,1:T(8,128)(2,1)} %bitcast.21), kind=kOutput, calls=%fused_computation.20 | convolution fusion | flops 16908160 | bytes 2392576 | tf_op jit(solution)/shard_map/rkgh,rckh->rkgc/dot_general | solution.py:128
  3.7 0.2 fusion.16
  3.9 0.5 fusion.13
  4.4 0.1 reshape.29
  4.5 0.1 copy.48
  4.6 0.1 broadcast_in_dim.4
  4.7 0.7 broadcast_in_dim.5
  5.3 11.9 %all-to-all-start = ((bf16[64,8,128]{2,1,0:T(8,128)(2,1)}), bf16[64,8,128]{2,1,0:T(8,128)(2,1)S(1)}, u32[]{:S(2)}, u32[]{:S(2)}) async-start(bf16[64,8,128]{2,1,0:T(8,128)(2,1)} %bitcast.6), calls=%async_computation | async-start | bytes 262144 | tf_op jit(solution)/shard_map/all_to_all | solution.py:183
  17.3 4.4 %reshape.32 = bf16[128,16,4,128]{3,2,1,0:T(4,128)(2,1)} reshape(bf16[2,64,8192]{2,1,0:T(8,128)(2,1)} %param.16) | data formatting | bytes 4194304 | tf_op jit(solution)/shard_map/reshape | solution.py:173
  21.7 3.2 %copy.47 = bf16[128,16,4,128]{3,1,0,2:T(8,128)(2,1)} copy(bf16[128,16,4,128]{3,2,1,0:T(4,128)(2,1)} %reshape.32) | data formatting | bytes 4194304 | tf_op jit(solution)/shard_map/reshape | solution.py:173
  24.8 4.1 %reshape.33 = bf16[4,128,2048]{2,1,0:T(8,128)(2,1)} reshape(bf16[4,128,16,128]{3,2,1,0:T(8,128)(2,1)} %bitcast.17) | data formatting | bytes 4194304 | tf_op jit(solution)/shard_map/reshape | solution.py:174
  29.0 0.0 all-to-all-done
  29.0 31.3 %all_to_all.20.w_ref = bf16[4,128,2048]{2,1,0:T(8,128)(2,1)} all-to-all(bf16[4,128,2048]{2,1,0:T(8,128)(2,1)} %reshape.33), channel_id=1, replica_groups=mesh['dp'=4,'tensor'=16,'owner'=4] {'owner'}, dimensions={0} | all-to-all | bytes 4194304 | tf_op jit(solution)/shard_map/all_to_all | solution.py:175
  60.3 5.5 %project.1 = (f32[1088,128]{1,0:T(8,128)}, bf16[1088,128]{1,0:T(8,128)(2,1)}) custom-call(s32[1,16]{1,0:T(1,128)} %group_ref.3, s32[128]{0:T(128)} %store_ref.3, s32[1,128]{1,0:T(1,128)} %bitcast.24, bf16[4,128,128]{2,1,0:T(8,128)(2,1)} %bitcast.18, bf16[4,128,2048]{2,1,0:T(8,128)(2,1)} %all_to_all.20.w_ref, bf16[32,8,64,64]{3,2,1,0:T(8,128)(2,1)} %down_ref.1), custom_call_target="tpu_custom_call" | custom-call | tf_op jit(solution)/shard_map/project/pallas_call | solution.py:189
  65.8 0.1 collective-permute-start
  65.9 1.8 %collective-permute-done.got_ref = bf16[1088,128]{1,0:T(8,128)(2,1)S(1)} collective-permute-done((bf16[1088,128]{1,0:T(8,128)(2,1)}, bf16[1088,128]{1,0:T(8,128)(2,1)S(1)}, u32[]{:S(2)}, u32[]{:S(2)}) %collective-permute-start) | collective-permute-done | bytes 278560 | tf_op jit(solution)/shard_map/ppermute | solution.py:204
  67.6 0.7 copy-done.2
  68.3 1.9 %pair.1 = bf16[8,192,128]{2,1,0:T(8,128)(2,1)} custom-call(f32[1088,128]{1,0:T(8,128)} %get-tuple-element.9.keep_ref, bf16[1088,128]{1,0:T(8,128)(2,1)} %copy-done.2), custom_call_target="tpu_custom_call" | custom-call | tf_op jit(solution)/shard_map/pair/pallas_call | solution.py:205
  70.3 21.9 %all_to_all.21.parts_ref = bf16[8,192,128]{2,1,0:T(8,128)(2,1)} all-to-all(bf16[8,192,128]{2,1,0:T(8,128)(2,1)} %pair.1), channel_id=1, replica_groups={{0,8,16,24,32,40,48,56},{4,12,20,28,36,44,52,60},{1,9,17,25,33,41,49,57..., dimensions={0} | all-to-all | bytes 786432 | tf_op jit(solution)/shard_map/all_to_all | solution.py:213
  92.2 3.6 %update.1 = (f32[128,128]{1,0:T(8,128)}, bf16[4,128,128]{2,1,0:T(8,128)(2,1)}) custom-call(s32[1,16]{1,0:T(1,128)} %group_ref.3, s32[128]{0:T(128)} %store_ref.3, s32[1,128]{1,0:T(1,128)} %bitcast.25, bf16[8,192,128]{2,1,0:T(8,128)(2,1)} %all_to_all.21.parts_ref, bf16[32,64,512]{2,1,0:T(8,128)(2,1)} %up_ref.1), custom_call_target="tpu_custom_call" | custom-call | tf_op jit(solution)/shard_map/update/pallas_call | solution.py:216
  95.7 10.0 %all_to_all.22.got_ref = bf16[4,128,128]{2,1,0:T(8,128)(2,1)} all-to-all(bf16[4,128,128]{2,1,0:T(8,128)(2,1)} %get-tuple-element.12), channel_id=1, replica_groups=mesh['dp'=4,'tensor'=16,'owner'=4] {'owner'}, dimensions={0} | all-to-all | bytes 262144 | tf_op jit(solution)/shard_map/all_to_all | solution.py:231
  105.7 1.6 %final.1 = bf16[128,128]{1,0:T(8,128)(2,1)} custom-call(f32[128,128]{1,0:T(8,128)} %get-tuple-element.11.base_ref, bf16[4,128,128]{2,1,0:T(8,128)(2,1)} %all_to_all.22.got_ref), custom_call_target="tpu_custom_call" | custom-call | tf_op jit(solution)/shard_map/final/pallas_call | solution.py:232
  (9 shorter events, 0.0 us)
Async XLA Ops:
  0.0 2.2 %copy-start = (bf16[8,512,2,128]{3,2,1,0:T(2,128)(2,1)S(1)}, bf16[8,512,2,128]{3,2,1,0:T(2,128)(2,1)}, u32[]{:S(2)}) copy-start(bf16[8,512,2,128]{3,2,1,0:T(2,128)(2,1)} %param.12) | copy-start | bytes 6291460
  0.0 3.9 %copy-start.3 = (bf16[8,512,2,128]{3,2,1,0:T(2,128)(2,1)S(1)}, bf16[8,512,2,128]{3,2,1,0:T(2,128)(2,1)}, u32[]{:S(2)}) copy-start(bf16[8,512,2,128]{3,2,1,0:T(2,128)(2,1)} %param.13) | copy-start | bytes 6291460
  5.3 23.7 %all-to-all-start = ((bf16[64,8,128]{2,1,0:T(8,128)(2,1)}), bf16[64,8,128]{2,1,0:T(8,128)(2,1)S(1)}, u32[]{:S(2)}, u32[]{:S(2)}) async-start(bf16[64,8,128]{2,1,0:T(8,128)(2,1)} %bitcast.6), calls=%async_computation | async-start | bytes 262144 | tf_op jit(solution)/shard_map/all_to_all | solution.py:183
  29.0 31.3 %copy-start.1 = (bf16[64,8,128]{2,1,0:T(8,128)(2,1)}, bf16[64,8,128]{2,1,0:T(8,128)(2,1)S(1)}, u32[]{:S(2)}) copy-start(bf16[64,8,128]{2,1,0:T(8,128)(2,1)S(1)} %all-to-all-done) | copy-start | bytes 393220
  65.8 1.9 %collective-permute-start = (bf16[1088,128]{1,0:T(8,128)(2,1)}, bf16[1088,128]{1,0:T(8,128)(2,1)S(1)}, u32[]{:S(2)}, u32[]{:S(2)}) collective-permute-start(bf16[1088,128]{1,0:T(8,128)(2,1)} %get-tuple-element.10), channel_id=1, source_target_pairs={{0,4},{4,0},{8,12},{12,8},{16,20},{20,16},{24,28},{28,24},{32,36},... | collective-permute-start | bytes 835592 | tf_op jit(solution)/shard_map/ppermute | solution.py:204
  67.6 0.7 copy-start.2

commit v2 on v1

--- a/solution.py
+++ b/solution.py
@@ -12,6 +12,11 @@
 VMEM = pl.BlockSpec(memory_space=pltpu.VMEM)
 SMEM = pl.BlockSpec(memory_space=pltpu.SMEM)
 ANY = pl.BlockSpec(memory_space=pl.ANY)
+LIMIT = pltpu.CompilerParams(vmem_limit_bytes=16 * 1024 * 1024)
+
+
+def near(array):
+    return pltpu.with_memory_space_constraint(array, pltpu.VMEM)
 
 
 def slot_position(slot, group_ref, store_ref, stored):
@@ -37,16 +42,22 @@
         copy.start()
         copies.append(copy)
     owners, rows, feats = att_ref.shape
+    mine = att_ref[lax.axis_index("owner")]
+    first = lax.rem(lax.axis_index("tensor"), 2) == 0
+    rank = dbuf.shape[-1]
+    block = keep_ref.shape[1]
+    planes = w_ref.shape[1] // (2 * owners * block)
+    wide = owners * block
+    for z in range(planes):
+        columns = w_ref[:, 2 * wide * z : 2 * wide * (z + 1)]
+        part = jnp.dot(mine, columns, preferred_element_type=F32)
+        for o in range(owners):
+            even = part[:, o * block : (o + 1) * block]
+            odd = part[:, wide + o * block : wide + (o + 1) * block]
+            span = pl.ds((z * owners + o) * rows, rows)
+            keep_ref[span, :] = jnp.where(first, even, odd)
+            send_ref[span, :] = jnp.where(first, odd, even).astype(BF16)
     att = jnp.concatenate([att_ref[o] for o in range(owners)], axis=1)
-    weight = w_ref[...].reshape(owners * feats, w_ref.shape[2])
-    first = lax.rem(lax.axis_index("tensor"), 2) == 0
-    planes = w_ref.shape[2] // 256
-    for z in range(planes):
-        part = jnp.dot(att, weight[:, 256 * z : 256 * z + 256], preferred_element_type=F32)
-        even, odd = part[:, :128], part[:, 128:]
-        keep_ref[z * rows : (z + 1) * rows, :] = jnp.where(first, even, odd)
-        send_ref[z * rows : (z + 1) * rows, :] = jnp.where(first, odd, even).astype(BF16)
-    rank = dbuf.shape[-1]
     ids = row_adapters(rows_ref, rank)
     acc[...] = jnp.zeros_like(acc)
     for s in range(slots):
@@ -61,23 +72,22 @@
 
     half = rows // 2
     code = jnp.concatenate([acc[:half, :], acc[half:, :]], axis=1)
-    keep_ref[planes * rows :, :] = code
-    send_ref[planes * rows :, :] = code.astype(BF16)
+    keep_ref[planes * owners * rows :, :] = code
+    send_ref[planes * owners * rows :, :] = code.astype(BF16)
 
 
 def pair_kernel(keep_ref, got_ref, out_ref):
     planes, total, _ = out_ref.shape
-    rows = (keep_ref.shape[0] - total) // (planes - 1)
-    code = (keep_ref[planes * rows :, :] + got_ref[planes * rows :, :].astype(F32)).astype(BF16)
+    tall = (keep_ref.shape[0] - total) // (planes - 1)
+    code = keep_ref[planes * tall :, :] + got_ref[planes * tall :, :].astype(F32)
+    code = code.astype(BF16)
     for z in range(planes):
-        span = pl.ds(z * rows, rows)
-        out_ref[z, :rows, :] = (keep_ref[span, :] + got_ref[span, :].astype(F32)).astype(BF16)
-        out_ref[z, rows:, :] = code
-
-
-def update_kernel(
-    group_ref, store_ref, rows_ref, parts_ref, up_ref, base_ref, send_ref, ubuf, acc, sems
-):
+        span = pl.ds(z * tall, tall)
+        out_ref[z, :tall, :] = (keep_ref[span, :] + got_ref[span, :].astype(F32)).astype(BF16)
+        out_ref[z, tall:, :] = code
+
+
+def update_kernel(group_ref, store_ref, rows_ref, parts_ref, up_ref, send_ref, ubuf, acc, sems):
     slots = ubuf.shape[0]
     stored = up_ref.shape[0]
     copies = []
@@ -86,14 +96,18 @@
         copy = pltpu.make_async_copy(up_ref.at[spot], ubuf.at[s], sems.at[s])
         copy.start()
         copies.append(copy)
-    total = parts_ref[0].astype(F32)
-    for z in range(1, parts_ref.shape[0]):
-        total = total + parts_ref[z].astype(F32)
-    rows = base_ref.shape[0]
-    base_ref[...] = total[:rows]
+    owners, rows, block = send_ref.shape
     rank = ubuf.shape[1]
-    packed = total[rows:]
-    code = jnp.concatenate([packed[:, :rank], packed[:, rank:]], axis=0).astype(BF16)
+    tall = owners * rows
+
+    def total(start, size):
+        part = parts_ref[0, start : start + size, :].astype(F32)
+        for z in range(1, parts_ref.shape[0]):
+            part = part + parts_ref[z, start : start + size, :].astype(F32)
+        return part
+
+    packed = total(tall, rows // 2)
+    code = jnp.concatenate([packed[:, :rank], packed[:, rank:]], axis=0).astype(BF16).astype(F32)
     ids = row_adapters(rows_ref, rank)
     acc[...] = jnp.zeros_like(acc)
     for s in range(slots):
@@ -102,19 +116,19 @@
 
         @pl.when(here)
         def _(s=s):
-            chosen = jnp.where(ids == group_ref[0, s], code.astype(F32), 0.0).astype(BF16)
+            chosen = jnp.where(ids == group_ref[0, s], code, 0.0).astype(BF16)
             acc[...] += jnp.dot(chosen, ubuf[s], preferred_element_type=F32)
 
-    width = send_ref.shape[2]
-    for o in range(send_ref.shape[0]):
-        send_ref[o] = acc[:, o * width : (o + 1) * width].astype(BF16)
-
-
-def final_kernel(base_ref, got_ref, out_ref):
-    update = got_ref[0].astype(F32)
+    for o in range(owners):
+        update = acc[:, o * block : (o + 1) * block]
+        send_ref[o] = (total(o * rows, rows) + ADAPTER_SCALE * update).astype(BF16)
+
+
+def final_kernel(got_ref, out_ref):
+    total = got_ref[0].astype(F32)
     for o in range(1, got_ref.shape[0]):
-        update = update + got_ref[o].astype(F32)
-    out_ref[...] = (base_ref[...] + ADAPTER_SCALE * update).astype(BF16)
+        total = total + got_ref[o].astype(F32)
+    out_ref[...] = total.astype(BF16)
 
 
 def attend(queries, cached_key_rows, cached_value_rows, newest_key, newest_value):
@@ -170,10 +184,6 @@
     rank = adapter_down_weight.shape[-1]
     row_ids = adapter_per_row.reshape(1, rows)
 
-    weight = output_weight.reshape(feats, tensors, owners, block).transpose(2, 0, 1, 3)
-    weight = weight.reshape(owners, feats, tensors * block)
-    weight = lax.all_to_all(weight, "owner", split_axis=0, concat_axis=0, tiled=True)
-
     mixed = attend(queries, cached_key_rows, cached_value_rows, newest_key, newest_value)
     part = output_weight.shape[1]
     outgoing = mixed.reshape(row_count, local_heads, tensors, part).transpose(2, 0, 1, 3)
@@ -185,14 +195,12 @@
     )
     attention = attention.reshape(owners, rows, feats)
 
-    tall = planes * rows + rows // 2
+    weight = output_weight.reshape(feats, columns)
+    tall = planes * owners * rows + rows // 2
     keep, send = pl.pallas_call(
         project_kernel,
         name="project",
-        out_shape=(
-            jax.ShapeDtypeStruct((tall, block), F32),
-            jax.ShapeDtypeStruct((tall, block), BF16),
-        ),
+        out_shape=(pltpu.VMEM((tall, block), F32), pltpu.VMEM((tall, block), BF16)),
         in_specs=[SMEM, SMEM, VMEM, VMEM, VMEM, ANY],
         out_specs=(VMEM, VMEM),
         scratch_shapes=[
@@ -200,42 +208,50 @@
             pltpu.VMEM((rows, rank), F32),
             pltpu.SemaphoreType.DMA((slots,)),
         ],
-    )(adapters_by_group, adapter_store_row, row_ids, attention, weight, adapter_down_weight)
+        compiler_params=LIMIT,
+    )(
+        adapters_by_group,
+        adapter_store_row,
+        row_ids,
+        near(attention),
+        near(weight),
+        adapter_down_weight,
+    )
     got = lax.ppermute(send, "tensor", [(t, t ^ 1) for t in range(tensors)])
     pieces = pl.pallas_call(
         pair_kernel,
         name="pair",
-        out_shape=jax.ShapeDtypeStruct((planes, rows + rows // 2, block), BF16),
+        out_shape=pltpu.VMEM((planes, owners * rows + rows // 2, block), BF16),
         in_specs=[VMEM, VMEM],
         out_specs=VMEM,
-    )(keep, got)
+        compiler_params=LIMIT,
+    )(near(keep), near(got))
     groups = [[2 * z + c for z in range(planes)] for c in range(2)]
     parts = lax.all_to_all(
         pieces, "tensor", split_axis=0, concat_axis=0, tiled=True, axis_index_groups=groups
     )
-    base, update = pl.pallas_call(
+    sums = pl.pallas_call(
         update_kernel,
         name="update",
-        out_shape=(
-            jax.ShapeDtypeStruct((rows, block), F32),
-            jax.ShapeDtypeStruct((owners, rows, block), BF16),
-        ),
+        out_shape=pltpu.VMEM((owners, rows, block), BF16),
         in_specs=[SMEM, SMEM, VMEM, VMEM, ANY],
-        out_specs=(VMEM, VMEM),
+        out_specs=VMEM,
         scratch_shapes=[
             pltpu.VMEM((slots,) + adapter_up_weight.shape[1:], BF16),
             pltpu.VMEM((rows, owners * block), F32),
             pltpu.SemaphoreType.DMA((slots,)),
         ],
-    )(adapters_by_group, adapter_store_row, row_ids, parts, adapter_up_weight)
-    update = lax.all_to_all(update, "owner", split_axis=0, concat_axis=0, tiled=True)
+        compiler_params=LIMIT,
+    )(adapters_by_group, adapter_store_row, row_ids, near(parts), adapter_up_weight)
+    sums = lax.all_to_all(sums, "owner", split_axis=0, concat_axis=0, tiled=True)
     return pl.pallas_call(
         final_kernel,
         name="final",
         out_shape=jax.ShapeDtypeStruct((rows, block), BF16),
-        in_specs=[VMEM, VMEM],
+        in_specs=[VMEM],
         out_specs=VMEM,
-    )(base, update)
+        compiler_params=LIMIT,
+    )(near(sums))
 
 
 def solution(mesh):

time: 108 us -> 87.4 us (0.81)
  starting transfers between devices: 12 us -> 0.19 us
  local copies, waits for them, and re-layouts: 13.4 us -> 4.08 us
  Pallas kernels: 12.5 us -> 9.46 us
  blocking collectives: 63.2 us -> 65.9 us
    all_to_all x1, blocking collectives: 21.9 us -> 34.8 us  [shards(): lax.all_to_all(pieces, 'tensor', split_axis=0, concat_axis=0, tiled=True,...]
    all_to_all x1 -> x0, starting transfers between devices: 11.9 us -> none  [shards(): lax.all_to_all(outgoing, ('owner', 'tensor'), split_axis=0, concat_axis=0...]
    reshape x3 -> x0, local copies, waits for them, and re-layouts: 11.7 us -> none  [the longest x2 7.58 us: shards(): output_weight.reshape(feats, tensors, owners, block).transpose(2, 0, 1, 3)]
    all_to_all x2, blocking collectives: 41.3 us -> 31.1 us  [the longest x1 22 us: shards(): lax.all_to_all(outgoing, ('owner', 'tensor'), split_axis=0, concat_axis=0...]
    unnamed x8 -> x16, local copies, waits for them, and re-layouts: 0.73 us -> 3.81 us
    pallas_call x3, Pallas kernels: 10.9 us -> 8.82 us  [the longest x1 5.22 us: shards(): pl.pallas_call(project_kernel, name='project', out_shape=(pltpu.VMEM((tal...]
  transfers between devices with their start and end apart: 2 -> 1, of which waited for: 1 -> 1; matrix products, arithmetic and copies ran while one was open for 11% -> 0% of each run, Pallas kernels for 0% -> 0%
where the time goes in v2:
time: 87.4 us; the launch traced here: 86.7 us
  blocking collectives  65.9 us (75%)
  Pallas kernels  9.46 us (11%)
  local copies, waits for them, and re-layouts  4.08 us (5%)
  matrix products  3.27 us (4%)
  waiting for transfers between devices  2.58 us (3%)
  other arithmetic  1.07 us (1%)
    all_to_all x1, blocking collectives, shards(): lax.all_to_all(pieces, 'tensor', split_axis=0, concat_axis=0, tiled=True,...  34.8 us
    all_to_all x1, blocking collectives, shards(): lax.all_to_all(outgoing, ('owner', 'tensor'), split_axis=0, concat_axis=0...  22 us
    all_to_all x1, blocking collectives, shards(): lax.all_to_all(sums, 'owner', split_axis=0, concat_axis=0, tiled=True)  9.05 us
    pallas_call x1, Pallas kernels, shards(): pl.pallas_call(project_kernel, name='project', out_shape=(pltpu.VMEM((tal...  5.22 us
    unnamed x16, local copies, waits for them, and re-layouts  3.81 us
    pallas_call x1, Pallas kernels, shards(): pl.pallas_call(update_kernel, name='update', out_shape=pltpu.VMEM((owners...  3.31 us
    ppermute x1, waiting for transfers between devices, shards(): got = lax.ppermute(send, 'tensor', [(t, t ^ 1) for t in range(tensors)])  2.58 us
  transfers between devices with their start and end apart: 1, of which 1 were waited for; matrix products, arithmetic and copies ran while one was open for 0% of the time, Pallas kernels for 0%

profile of v2, /device:TPU:24, one launch (start us, length us, event | category | flops | bytes accessed | tf_op | source)
XLA Modules:
  0.0 86.7 jit_solution(8733315687404416866)
XLA Ops:
  0.0 0.0 copy-start
  0.0 0.8 convert_element_type.6
  0.8 1.3 %fusion.18 = f32[8,2,1,8]{3,2,1,0:T(1,128)S(1)} fusion(bf16[8,2,8,128]{3,0,2,1:T(8,128)(2,1)} %bitcast.19, bf16[8,2,128,1]{2,1,0,3:T(2,128)(2,1)} %bitcast.23), kind=kOutput, calls=%fused_computation.12 | convolution fusion | flops 32768 | bytes 37376 | tf_op jit(solution)/shard_map/rkgh,rkh->rkg/dot_general | solution.py:148
  2.2 1.5 %fusion.23 = (f32[8,2,8]{2,1,0:T(2,128)S(1)}, f32[8,2,8,512]{3,2,1,0:T(8,128)S(1)}) fusion(bf16[8,512,2,128]{3,2,1,0:T(2,128)(2,1)S(1)} %copy-done, bf16[8,2,8,128]{3,0,2,1:T(8,128)(2,1)} %bitcast.20), kind=kOutput, calls=%fused_computation.19 | convolution fusion | flops 16908160 | bytes 2392576 | tf_op jit(solution)/shard_map/rkgh,rckh->rkgc/dot_general | solution.py:142
  3.7 0.0 copy-start.5
  3.7 0.0 copy-start.6
  3.7 0.2 fusion.16
  4.0 0.5 fusion.13
  4.4 0.1 reshape.26
  4.5 0.1 copy.44
  4.6 0.1 broadcast_in_dim.4
  4.7 22.0 %all_to_all.15 = bf16[64,8,128]{2,1,0:T(8,128)(2,1)S(1)} all-to-all(bf16[64,8,128]{2,1,0:T(8,128)(2,1)S(1)} %bitcast.17), channel_id=1, replica_groups=mesh['dp'=4,'tensor'=16,'owner'=4] {'owner','tensor'}, dimensions={0} | all-to-all | bytes 262144 | tf_op jit(solution)/shard_map/all_to_all | solution.py:193
  26.8 0.0 copy-start.1
  26.8 2.2 %copy-done.1 = bf16[32,8,64,64]{3,2,1,0:T(8,128)(2,1)S(1)} copy-done((bf16[32,8,64,64]{3,2,1,0:T(8,128)(2,1)S(1)}, bf16[32,8,64,64]{3,2,1,0:T(8,128)(2,1)}, u32[]{:S(2)}) %copy-start.1) | copy-done | bytes 2097176
  28.9 1.6 %copy-done.2 = bf16[2,64,8192]{2,1,0:T(8,128)(2,1)S(1)} copy-done((bf16[2,64,8192]{2,1,0:T(8,128)(2,1)S(1)}, bf16[2,64,8192]{2,1,0:T(8,128)(2,1)}, u32[]{:S(2)}) %copy-start.2) | copy-done | bytes 2097176
  30.5 5.2 %project.1 = (f32[4160,128]{1,0:T(8,128)S(1)}, bf16[4160,128]{1,0:T(8,128)(2,1)S(1)}) custom-call(s32[1,16]{1,0:T(1,128)S(1)} %copy-done.4, s32[128]{0:T(128)S(1)} %copy-done.5, s32[1,128]{1,0:T(1,128)S(1)} %bitcast.15, bf16[4,128,128]{2,1,0:T(8,128)(2,1)S(1)} %bitcast.14, bf16[128,8192]{1,0:T(8,128)(2,1)S(1)} %bitcast.13, bf16[32,8,64,64]{3,2,1,0:T(8,128)(2,1)S(1)} %copy-done.1), custom_call_target="tpu_custom_call" | custom-call | tf_op jit(solution)/shard_map/project/pallas_call | solution.py:200
  35.8 0.2 collective-permute-start
  36.0 2.6 %collective-permute-done.got_ref = bf16[4160,128]{1,0:T(8,128)(2,1)S(1)} collective-permute-done((bf16[4160,128]{1,0:T(8,128)(2,1)S(1)}, bf16[4160,128]{1,0:T(8,128)(2,1)S(1)}, u32[]{:S(2)}, u32[]{:S(2)}) %collective-permute-start) | collective-permute-done | bytes 1064992 | tf_op jit(solution)/shard_map/ppermute | solution.py:220
  38.5 0.3 pair.1
  38.8 0.0 copy-start.3
  38.8 34.8 %all_to_all.16.parts_ref = bf16[8,576,128]{2,1,0:T(8,128)(2,1)S(1)} all-to-all(bf16[8,576,128]{2,1,0:T(8,128)(2,1)S(1)} %pair.1), channel_id=1, replica_groups={{0,8,16,24,32,40,48,56},{4,12,20,28,36,44,52,60},{1,9,17,25,33,41,49,57..., dimensions={0} | all-to-all | bytes 2359296 | tf_op jit(solution)/shard_map/all_to_all | solution.py:230
  73.7 3.3 %update.1 = bf16[4,128,128]{2,1,0:T(8,128)(2,1)S(1)} custom-call(s32[1,16]{1,0:T(1,128)S(1)} %copy-done.4, s32[128]{0:T(128)S(1)} %copy-done.5, s32[1,128]{1,0:T(1,128)S(1)} %bitcast.16, bf16[8,576,128]{2,1,0:T(8,128)(2,1)S(1)} %all_to_all.16.parts_ref, bf16[32,64,512]{2,1,0:T(8,128)(2,1)S(1)} %copy-done.3), custom_call_target="tpu_custom_call" | custom-call | tf_op jit(solution)/shard_map/update/pallas_call | solution.py:233
  77.0 9.0 %all_to_all.17.got_ref = bf16[4,128,128]{2,1,0:T(8,128)(2,1)S(1)} all-to-all(bf16[4,128,128]{2,1,0:T(8,128)(2,1)S(1)} %update.1), channel_id=1, replica_groups=mesh['dp'=4,'tensor'=16,'owner'=4] {'owner'}, dimensions={0} | all-to-all | bytes 262144 | tf_op jit(solution)/shard_map/all_to_all | solution.py:246
  86.0 0.6 final.1
  (12 shorter events, 0.1 us)
Async XLA Ops:
  0.0 2.2 %copy-start = (bf16[8,512,2,128]{3,2,1,0:T(2,128)(2,1)S(1)}, bf16[8,512,2,128]{3,2,1,0:T(2,128)(2,1)}, u32[]{:S(2)}) copy-start(bf16[8,512,2,128]{3,2,1,0:T(2,128)(2,1)} %param.12) | copy-start | bytes 6291460
  0.0 3.9 %copy-start.7 = (bf16[8,512,2,128]{3,2,1,0:T(2,128)(2,1)S(1)}, bf16[8,512,2,128]{3,2,1,0:T(2,128)(2,1)}, u32[]{:S(2)}) copy-start(bf16[8,512,2,128]{3,2,1,0:T(2,128)(2,1)} %param.13) | copy-start | bytes 6291460
  3.7 23.1 %copy-start.4 = (s32[1,16]{1,0:T(1,128)S(1)}, s32[1,16]{1,0:T(1,128)}, u32[]{:S(2)}) copy-start(s32[1,16]{1,0:T(1,128)} %group_ref.3) | copy-start | bytes 196
  3.7 23.1 %copy-start.5 = (s32[128]{0:T(128)S(1)}, s32[128]{0:T(128)}, u32[]{:S(2)}) copy-start(s32[128]{0:T(128)} %store_ref.3) | copy-start | bytes 1540
  3.7 23.1 %copy-start.6 = (s32[128]{0:T(128)S(1)}, s32[128]{0:T(128)}, u32[]{:S(2)}) copy-start(s32[128]{0:T(128)} %param.21) | copy-start | bytes 1540
  26.8 2.2 %copy-start.1 = (bf16[32,8,64,64]{3,2,1,0:T(8,128)(2,1)S(1)}, bf16[32,8,64,64]{3,2,1,0:T(8,128)(2,1)}, u32[]{:S(2)}) copy-start(bf16[32,8,64,64]{3,2,1,0:T(8,128)(2,1)} %down_ref.1) | copy-start | bytes 6291460
  28.9 1.6 %copy-start.2 = (bf16[2,64,8192]{2,1,0:T(8,128)(2,1)S(1)}, bf16[2,64,8192]{2,1,0:T(8,128)(2,1)}, u32[]{:S(2)}) copy-start(bf16[2,64,8192]{2,1,0:T(8,128)(2,1)} %param.16) | copy-start | bytes 6291460
  35.8 2.8 %collective-permute-start = (bf16[4160,128]{1,0:T(8,128)(2,1)S(1)}, bf16[4160,128]{1,0:T(8,128)(2,1)S(1)}, u32[]{:S(2)}, u32[]{:S(2)}) collective-permute-start(bf16[4160,128]{1,0:T(8,128)(2,1)S(1)} %get-tuple-element.8), channel_id=1, source_target_pairs={{0,4},{4,0},{8,12},{12,8},{16,20},{20,16},{24,28},{28,24},{32,36},... | collective-permute-start | bytes 3194888 | tf_op jit(solution)/shard_map/ppermute | solution.py:220
  38.8 34.8 %copy-start.3 = (bf16[32,64,512]{2,1,0:T(8,128)(2,1)S(1)}, bf16[32,64,512]{2,1,0:T(8,128)(2,1)}, u32[]{:S(2)}) copy-start(bf16[32,64,512]{2,1,0:T(8,128)(2,1)} %up_ref.1) | copy-start | bytes 6291460

commit v3 on v2

v3 whole, which is shorter than its diff:
```python
import jax
import jax.numpy as jnp
from jax import lax
from jax.experimental import pallas as pl
from jax.experimental.pallas import tpu as pltpu
from jax.sharding import PartitionSpec as P

ADAPTER_SCALE = 2.0
BF16 = jnp.bfloat16
F32 = jnp.float32

VMEM = pl.BlockSpec(memory_space=pltpu.VMEM)
SMEM = pl.BlockSpec(memory_space=pltpu.SMEM)
HBM = pl.BlockSpec(memory_space=pltpu.HBM)
LIMIT = pltpu.CompilerParams(vmem_limit_bytes=16 * 1024 * 1024)


def near(array):
    return pltpu.with_memory_space_constraint(array, pltpu.VMEM)


def far(array):
    return pltpu.with_memory_space_constraint(array, pltpu.HBM)


def slot_position(slot, group_ref, store_ref, stored):
    spot = store_ref[group_ref[0, slot]] - lax.axis_index("owner") * stored
    here = jnp.logical_and(spot >= 0, spot < stored)
    return jnp.clip(spot, 0, stored - 1), here


def row_adapters(rows_ref, width):
    rows = rows_ref.shape[1]
    return jnp.transpose(jnp.broadcast_to(rows_ref[...], (rows, rows)))[:, :width]


def column_copies(w_ref, out_ref, step, sems, base):
    owners = lax.axis_size("owner")
    target = lax.rem(lax.axis_index("owner") + step, owners)
    copies = []
    for block in range(out_ref.shape[1] // 128):
        at = pl.multiple_of((block * owners + target) * 128, 128)
        copies.append(
            pltpu.make_async_copy(
                w_ref.at[:, pl.ds(at, 128)],
                out_ref.at[:, pl.ds(block * 128, 128)],
                sems.at[base + block],
            )
        )
    return copies


def slab_kernel(w_ref, right_ref, left_ref, sems):
    owners = lax.axis_size("owner")
    blocks = right_ref.shape[1] // 128
    copies = column_copies(w_ref, right_ref, 1, sems, 0)
    copies += column_copies(w_ref, left_ref, owners - 1, sems, blocks)
    for copy in copies:
        copy.start()
    for copy in copies:
        copy.wait()


def attend_kernel(
    group_ref,
    store_ref,
    queries_ref,
    keys_ref,
    values_hbm_ref,
    key_ref,
    value_ref,
    w_ref,
    down_ref,
    out_ref,
    mine_ref,
    across_ref,
    slots_ref,
    values_ref,
    value_sems,
    sems,
):
    stored = down_ref.shape[0]
    blocks = mine_ref.shape[1] // 128
    value_copies = [
        pltpu.make_async_copy(values_hbm_ref.at[r], values_ref.at[r], value_sems.at[r])
        for r in range(values_ref.shape[0])
    ]
    for copy in value_copies:
        copy.start()
    copies = column_copies(w_ref, mine_ref, 0, sems, 0)
    copies += column_copies(w_ref, across_ref, 2, sems, blocks)
    for s in range(slots_ref.shape[0]):
        spot, _ = slot_position(s, group_ref, store_ref, stored)
        copies.append(
            pltpu.make_async_copy(down_ref.at[spot], slots_ref.at[s], sems.at[2 * blocks + s])
        )
    for copy in copies:
        copy.start()

    heads, rows, width = queries_ref.shape
    _, local, _ = key_ref.shape
    grouped = heads // local
    positions = keys_ref.shape[1]
    scale = width ** (-0.5)
    queries = jnp.swapaxes(queries_ref[...].astype(F32), 0, 1)
    row_head = lax.broadcasted_iota(jnp.int32, (heads, positions), 0) // grouped
    place_head = lax.broadcasted_iota(jnp.int32, (heads, positions), 1) % local
    same = row_head == place_head

    def spread(ref, r):
        fresh = ref[r].astype(F32)
        parts = [jnp.broadcast_to(fresh[k : k + 1], (grouped, width)) for k in range(local)]
        return jnp.concatenate(parts, axis=0)

    mixed = []
    for r in range(rows):
        query = queries[r]
        scores = lax.dot_general(
            query.astype(BF16), keys_ref[r], (((1,), (1,)), ((), ())), preferred_element_type=F32
        )
        scores = jnp.where(same, scores * scale, -jnp.inf)
        fresh_score = jnp.sum(query * spread(key_ref, r), axis=1, keepdims=True) * scale
        overall = jnp.maximum(jnp.max(scores, axis=1, keepdims=True), fresh_score)
        weights = jnp.exp(scores - overall)
        fresh_weight = jnp.exp(fresh_score - overall)
        denominator = jnp.sum(weights, axis=1, keepdims=True) + fresh_weight
        value_copies[r].wait()
        total = jnp.dot(weights.astype(BF16), values_ref[r], preferred_element_type=F32)
        total = total + fresh_weight * spread(value_ref, r)
        mixed.append(total / denominator)
    mixed = jnp.swapaxes(jnp.stack(mixed), 0, 1)

    half = width // 2
    low = lax.broadcasted_iota(jnp.int32, (rows, width), 1) < half
    for g in range(grouped):
        one, two = mixed[g], mixed[grouped + g]
        pair = (
            jnp.where(low, one, pltpu.roll(two, half, 1)),
            jnp.where(low, pltpu.roll(one, half, 1), two),
        )
        for i, part in enumerate(pair):
            for o in range(out_ref.shape[0]):
                out_ref[o, 2 * g + i] = part.astype(BF16)
    for copy in copies:
        copy.wait()


def project_kernel(
    group_ref,
    store_ref,
    rows_ref,
    att_ref,
    mine_ref,
    across_ref,
    before_ref,
    after_ref,
    slots_ref,
    keep_ref,
    send_ref,
    acc,
):
    slots, _, _, rank = slots_ref.shape
    stored = store_ref.shape[0] // lax.axis_size("owner")
    owners, rows, feats = att_ref.shape
    owner = lax.axis_index("owner")
    mine = att_ref[owner]
    beside = jnp.concatenate(
        [att_ref[lax.rem(owner + owners - 1, owners)], att_ref[lax.rem(owner + 1, owners)]], axis=1
    )
    first = lax.rem(lax.axis_index("tensor"), 2) == 0
    block = keep_ref.shape[1]
    planes = before_ref.shape[1] // (2 * block)

    for z in range(planes):
        span = pl.ds(z * 2 * block, 2 * block)
        near_rows = jnp.concatenate([before_ref[:, span], after_ref[:, span]], axis=0)
        here = jnp.dot(beside, near_rows, preferred_element_type=F32)
        here = here + jnp.dot(mine, mine_ref[:, span], preferred_element_type=F32)
        there = jnp.dot(mine, across_ref[:, span], preferred_element_type=F32)
        for i, part in enumerate((here, there)):
            even, odd = part[:, :block], part[:, block:]
            rows_span = pl.ds((2 * z + i) * rows, rows)
            keep_ref[rows_span, :] = jnp.where(first, even, odd)
            send_ref[rows_span, :] = jnp.where(first, odd, even).astype(BF16)
    att = jnp.concatenate([att_ref[o] for o in range(owners)], axis=1)
    ids = row_adapters(rows_ref, rank)
    acc[...] = jnp.zeros_like(acc)
    for s in range(slots):
        _, here = slot_position(s, group_ref, store_ref, stored)

        @pl.when(here)
        def _(s=s):
            table = slots_ref[s].reshape(owners * feats, rank)
            code = jnp.dot(att, table, preferred_element_type=F32)
            acc[...] += jnp.where(ids == group_ref[0, s], code, 0.0)

    half = rows // 2
    code = jnp.concatenate([acc[:half, :], acc[half:, :]], axis=1)
    keep_ref[2 * planes * rows :, :] = code
    send_ref[2 * planes * rows :, :] = code.astype(BF16)


def pair_kernel(keep_ref, got_ref, out_ref):
    planes, total, _ = out_ref.shape
    tall = (keep_ref.shape[0] - total) // (planes - 1)
    code = keep_ref[planes * tall :, :] + got_ref[planes * tall :, :].astype(F32)
    code = code.astype(BF16)
    for z in range(planes):
        span = pl.ds(z * tall, tall)
        out_ref[z, :tall, :] = (keep_ref[span, :] + got_ref[span, :].astype(F32)).astype(BF16)
        out_ref[z, tall:, :] = code


def update_kernel(group_ref, store_ref, rows_ref, parts_ref, up_ref, send_ref, acc):
    slots = group_ref.shape[1]
    stored, rank, _ = up_ref.shape
    owners, rows, block = send_ref.shape
    owner = lax.axis_index("owner")

    def total(start, size):
        part = parts_ref[0, start : start + size, :].astype(F32)
        for z in range(1, parts_ref.shape[0]):
            part = part + parts_ref[z, start : start + size, :].astype(F32)
        return part

    packed = total(2 * rows, rows // 2)
    code = jnp.concatenate([packed[:, :rank], packed[:, rank:]], axis=0).astype(BF16).astype(F32)
    ids = row_adapters(rows_ref, rank)
    acc[...] = jnp.zeros_like(acc)
    for s in range(slots):
        spot, here = slot_position(s, group_ref, store_ref, stored)

        @pl.when(here)
        def _(s=s, spot=spot):
            chosen = jnp.where(ids == group_ref[0, s], code, 0.0).astype(BF16)
            acc[...] += jnp.dot(chosen, up_ref[spot], preferred_element_type=F32)

    own, across = total(0, rows), total(rows, rows)
    for o in range(owners):
        update = ADAPTER_SCALE * acc[:, o * block : (o + 1) * block]
        base = jnp.where(owner == o, own, jnp.where(owner == (o + 2) % owners, across, 0.0))
        send_ref[o] = (base + update).astype(BF16)


def final_kernel(got_ref, out_ref):
    total = got_ref[0].astype(F32)
    for o in range(1, got_ref.shape[0]):
        total = total + got_ref[o].astype(F32)
    out_ref[...] = total.astype(BF16)


def shards(
    queries,
    cached_key_rows,
    cached_value_rows,
    newest_key,
    newest_value,
    output_weight,
    adapter_down_weight,
    adapter_up_weight,
    adapter_store_row,
    adapters_by_group,
    adapter_per_row,
):
    owners = lax.axis_size("owner")
    tensors = lax.axis_size("tensor")
    planes = tensors // 2
    slots = adapters_by_group.shape[1]
    row_count, local_heads, head_width = newest_key.shape
    rows = adapter_per_row.shape[0]
    feats = local_heads * output_weight.shape[1]
    columns = output_weight.shape[2]
    block = columns // (tensors * owners)
    rank = adapter_down_weight.shape[-1]
    row_ids = adapter_per_row.reshape(1, rows)

    weight = far(output_weight.reshape(feats, columns))
    slab = pltpu.VMEM((feats, columns // owners), BF16)
    blocks = columns // owners // 128
    right, left = pl.pallas_call(
        slab_kernel,
        name="slabs",
        out_shape=(slab, slab),
        in_specs=[HBM],
        out_specs=(VMEM, VMEM),
        scratch_shapes=[pltpu.SemaphoreType.DMA((2 * blocks,))],
        compiler_params=LIMIT,
    )(weight)
    before = lax.ppermute(right, "owner", [(o, (o + 1) % owners) for o in range(owners)])
    after = lax.ppermute(left, "owner", [(o, (o - 1) % owners) for o in range(owners)])

    heads = queries.shape[1] // head_width
    grouped = queries.reshape(row_count, heads, head_width).transpose(1, 0, 2)
    outgoing, mine, across, tables = pl.pallas_call(
        attend_kernel,
        name="attend",
        out_shape=(
            pltpu.VMEM((owners, tensors, row_count, feats), BF16),
            slab,
            slab,
            pltpu.VMEM((slots,) + adapter_down_weight.shape[1:], BF16),
        ),
        in_specs=[SMEM, SMEM, VMEM, VMEM, HBM, VMEM, VMEM, HBM, HBM],
        out_specs=(VMEM, VMEM, VMEM, VMEM),
        scratch_shapes=[
            pltpu.VMEM((row_count, cached_value_rows.shape[1] * local_heads, head_width), BF16),
            pltpu.SemaphoreType.DMA((row_count,)),
            pltpu.SemaphoreType.DMA((2 * blocks + slots,)),
        ],
        compiler_params=LIMIT,
    )(
        adapters_by_group,
        adapter_store_row,
        grouped,
        near(cached_key_rows.reshape(row_count, -1, head_width)),
        far(cached_value_rows.reshape(row_count, -1, head_width)),
        newest_key,
        newest_value,
        weight,
        far(adapter_down_weight),
    )
    outgoing = outgoing.reshape(owners * tensors, row_count, feats)
    attention = lax.all_to_all(
        outgoing, ("owner", "tensor"), split_axis=0, concat_axis=0, tiled=True
    )
    attention = attention.reshape(owners, rows, feats)

    tall = 2 * planes * rows + rows // 2
    keep, send = pl.pallas_call(
        project_kernel,
        name="project",
        out_shape=(pltpu.VMEM((tall, block), F32), pltpu.VMEM((tall, block), BF16)),
        in_specs=[SMEM, SMEM] + [VMEM] * 7,
        out_specs=(VMEM, VMEM),
        scratch_shapes=[pltpu.VMEM((rows, rank), F32)],
        compiler_params=LIMIT,
    )(
        adapters_by_group,
        adapter_store_row,
        row_ids,
        near(attention),
        near(mine),
        near(across),
        near(before),
        near(after),
        near(tables),
    )
    got = lax.ppermute(send, "tensor", [(t, t ^ 1) for t in range(tensors)])
    pieces = pl.pallas_call(
        pair_kernel,
        name="pair",
        out_shape=pltpu.VMEM((planes, 2 * rows + rows // 2, block), BF16),
        in_specs=[VMEM, VMEM],
        out_specs=VMEM,
        compiler_params=LIMIT,
    )(near(keep), near(got))
    groups = [[2 * z + c for z in range(planes)] for c in range(2)]
    parts = lax.all_to_all(
        pieces, "tensor", split_axis=0, concat_axis=0, tiled=True, axis_index_groups=groups
    )
    sums = pl.pallas_call(
        update_kernel,
        name="update",
        out_shape=pltpu.VMEM((owners, rows, block), BF16),
        in_specs=[SMEM, SMEM, VMEM, VMEM, VMEM],
        out_specs=VMEM,
        scratch_shapes=[pltpu.VMEM((rows, owners * block), F32)],
        compiler_params=LIMIT,
    )(adapters_by_group, adapter_store_row, row_ids, near(parts), near(adapter_up_weight))
    sums = lax.all_to_all(sums, "owner", split_axis=0, concat_axis=0, tiled=True)
    return pl.pallas_call(
        final_kernel,
        name="final",
        out_shape=jax.ShapeDtypeStruct((rows, block), BF16),
        in_specs=[VMEM],
        out_specs=VMEM,
        compiler_params=LIMIT,
    )(near(sums))


def solution(mesh):
    return jax.shard_map(
        shards,
        mesh=mesh,
        in_specs=(
            P(("dp", "tensor"), "owner"),
            P(("dp", "tensor"), None, "owner", None),
            P(("dp", "tensor"), None, "owner", None),
            P(("dp", "tensor"), "owner", None),
            P(("dp", "tensor"), "owner", None),
            P("owner", "tensor", None),
            P("owner", None, "tensor", None),
            P("owner", None, "tensor"),
            P(),
            P("dp", None),
            P("dp"),
        ),
        out_specs=P("dp", ("tensor", "owner")),
        check_vma=False,
    )
```

time: 87.4 us -> 71.7 us (0.82)
  blocking collectives: 65.9 us -> 53 us
  starting transfers between devices: 0.19 us -> 3.51 us
  local copies, waits for them, and re-layouts: 4.08 us -> 0.78 us
  matrix products: 3.27 us -> 0 us
  Pallas kernels: 9.46 us -> 11.9 us
  other arithmetic: 1.07 us -> 0 us
    all_to_all x1, blocking collectives: 34.8 us -> 23.5 us  [shards(): lax.all_to_all(pieces, 'tensor', split_axis=0, concat_axis=0, tiled=True,...]
    pallas_call x1 -> x3, Pallas kernels: 0.29 us -> 7.61 us  [the longest x1 5.84 us: shards(): pl.pallas_call(attend_kernel, name='attend', out_shape=(pltpu.VMEM((owner...]
    ppermute x0 -> x2, starting transfers between devices: none -> 3.31 us  [the longest x1 1.75 us: shards(): lax.ppermute(left, 'owner', [(o, (o - 1) % owners) for o in range(owners)])]
    dot_general x3 -> x0, matrix products: 3.27 us -> none  [the longest x1 1.49 us: attend(): jnp.einsum('rkgh,rckh->rkgc', query_heads, cached_key_rows, preferred_ele...]
    pallas_call x1, Pallas kernels: 5.22 us -> 2.04 us  [shards(): pl.pallas_call(project_kernel, name='project', out_shape=(pltpu.VMEM((tal...]
    unnamed x16, local copies, waits for them, and re-layouts: 3.81 us -> 0.78 us
    pallas_call x1, Pallas kernels: 3.31 us -> 1.59 us  [shards(): pl.pallas_call(update_kernel, name='update', out_shape=pltpu.VMEM((owners...]
    all_to_all x1, blocking collectives: 22 us -> 20.8 us  [shards(): lax.all_to_all(outgoing, ('owner', 'tensor'), split_axis=0, concat_axis=0...]
  transfers between devices with their start and end apart: 1 -> 3, of which waited for: 1 -> 1; matrix products, arithmetic and copies ran while one was open for 0% -> 0% of each run, Pallas kernels for 0% -> 8%
where the time goes in v3:
time: 71.7 us; the launch traced here: 71.1 us
  blocking collectives  53 us (74%)
  Pallas kernels  11.9 us (17%)
  starting transfers between devices  3.51 us (5%)
  waiting for transfers between devices  1.82 us (3%)
  local copies, waits for them, and re-layouts  0.78 us (1%)
    all_to_all x1, blocking collectives, shards(): lax.all_to_all(pieces, 'tensor', split_axis=0, concat_axis=0, tiled=True,...  23.5 us
    all_to_all x1, blocking collectives, shards(): lax.all_to_all(outgoing, ('owner', 'tensor'), split_axis=0, concat_axis=0...  20.8 us
    all_to_all x1, blocking collectives, shards(): lax.all_to_all(sums, 'owner', split_axis=0, concat_axis=0, tiled=True)  8.71 us
    pallas_call x1, Pallas kernels, shards(): pl.pallas_call(attend_kernel, name='attend', out_shape=(pltpu.VMEM((owner...  5.84 us
    pallas_call x1, Pallas kernels, shards(): pl.pallas_call(project_kernel, name='project', out_shape=(pltpu.VMEM((tal...  2.04 us
    ppermute x1, waiting for transfers between devices, shards(): got = lax.ppermute(send, 'tensor', [(t, t ^ 1) for t in range(tensors)])  1.82 us
    ppermute x1, starting transfers between devices, shards(): lax.ppermute(left, 'owner', [(o, (o - 1) % owners) for o in range(owners)])  1.75 us
    pallas_call x1, Pallas kernels, shards(): pl.pallas_call(slab_kernel, name='slabs', out_shape=(slab, slab), in_spec...  1.63 us
  transfers between devices with their start and end apart: 3, of which 1 were waited for; matrix products, arithmetic and copies ran while one was open for 0% of the time, Pallas kernels for 8%

profile of v3, /device:TPU:24, one launch (start us, length us, event | category | flops | bytes accessed | tf_op | source)
XLA Modules:
  0.0 71.1 jit_solution(11687818359663706202)
XLA Ops:
  0.0 0.0 copy-start.5
  0.0 0.0 copy-start.1
  0.0 1.6 %slabs.1 = (bf16[128,2048]{1,0:T(8,128)(2,1)S(1)}, bf16[128,2048]{1,0:T(8,128)(2,1)S(1)}) custom-call(bf16[128,8192]{1,0:T(8,128)(2,1)} %bitcast.15), custom_call_target="tpu_custom_call" | custom-call | tf_op jit(solution)/shard_map/slabs/pallas_call | solution.py:280
  1.7 1.6 %collective-permute-start = (bf16[128,2048]{1,0:T(8,128)(2,1)S(1)}, bf16[128,2048]{1,0:T(8,128)(2,1)S(1)}, u32[]{:S(2)}, u32[]{:S(2)}) collective-permute-start(bf16[128,2048]{1,0:T(8,128)(2,1)S(1)} %get-tuple-element.16), channel_id=1, source_target_pairs={{0,1},{1,2},{2,3},{3,0},{4,5},{5,6},{6,7},{7,4},{8,9},{9,10},{10,1... | collective-permute-start | bytes 1572872 | tf_op jit(solution)/shard_map/ppermute | solution.py:289
  3.2 1.7 %collective-permute-start.1 = (bf16[128,2048]{1,0:T(8,128)(2,1)S(1)}, bf16[128,2048]{1,0:T(8,128)(2,1)S(1)}, u32[]{:S(2)}, u32[]{:S(2)}) collective-permute-start(bf16[128,2048]{1,0:T(8,128)(2,1)S(1)} %get-tuple-element.17), channel_id=1, source_target_pairs={{0,3},{1,0},{2,1},{3,2},{4,7},{5,4},{6,5},{7,6},{8,11},{9,8},{10,9... | collective-permute-start | bytes 1572872 | tf_op jit(solution)/shard_map/ppermute | solution.py:290
  5.0 0.0 copy-done.3
  5.0 0.0 copy-done.4
  5.0 0.0 copy-done.6
  5.0 0.0 copy-done.5
  5.0 0.0 copy-done.1
  5.0 0.0 copy-start.2
  5.0 0.7 %copy-done.2 = bf16[8,2048]{1,0:T(8,128)(2,1)S(1)} copy-done((bf16[8,2048]{1,0:T(8,128)(2,1)S(1)}, bf16[8,2048]{1,0:T(8,128)(2,1)}, u32[]{:S(2)}) %copy-start.2) | copy-done | bytes 32792
  5.8 5.8 %attend.1 = (bf16[4,16,8,128]{3,2,1,0:T(8,128)(2,1)S(1)}, bf16[128,2048]{1,0:T(8,128)(2,1)S(1)}, bf16[128,2048]{1,0:T(8,128)(2,1)S(1)}, bf16[16,8,64,64]{3,2,1,0:T(8,128)(2,1)S(1)}) custom-call(s32[1,16]{1,0:T(1,128)S(1)} %copy-done.3, s32[128]{0:T(128)S(1)} %copy-done.4, bf16[16,8,128]{2,1,0:T(8,128)(2,1)S(1)} %bitcast.12, ...), custom_call_target="tpu_custom_call" | custom-call | tf_op jit(solution)/shard_map/attend/pallas_call | solution.py:294
  11.6 20.8 %all_to_all.15 = bf16[64,8,128]{2,1,0:T(8,128)(2,1)S(1)} all-to-all(bf16[64,8,128]{2,1,0:T(8,128)(2,1)S(1)} %bitcast.11), channel_id=1, replica_groups=mesh['dp'=4,'tensor'=16,'owner'=4] {'owner','tensor'}, dimensions={0} | all-to-all | bytes 262144 | tf_op jit(solution)/shard_map/all_to_all | solution.py:323
  32.4 0.0 collective-permute-done.before_ref
  32.4 0.0 collective-permute-done.1.after_ref
  32.5 2.0 %project.1 = (f32[2112,128]{1,0:T(8,128)S(1)}, bf16[2112,128]{1,0:T(8,128)(2,1)S(1)}) custom-call(s32[1,16]{1,0:T(1,128)S(1)} %copy-done.3, s32[128]{0:T(128)S(1)} %copy-done.4, s32[1,128]{1,0:T(1,128)S(1)} %bitcast.13, bf16[4,128,128]{2,1,0:T(8,128)(2,1)S(1)} %bitcast.10, bf16[128,2048]{1,0:T(8,128)(2,1)S(1)} %get-tuple-element.14.mine_ref, ...), custom_call_target="tpu_custom_call" | custom-call | tf_op jit(solution)/shard_map/project/pallas_call | solution.py:329
  34.5 0.2 collective-permute-start.2
  34.7 1.8 %collective-permute-done.2.got_ref = bf16[2112,128]{1,0:T(8,128)(2,1)S(1)} collective-permute-done((bf16[2112,128]{1,0:T(8,128)(2,1)S(1)}, bf16[2112,128]{1,0:T(8,128)(2,1)S(1)}, u32[]{:S(2)}, u32[]{:S(2)}) %collective-permute-start.2) | collective-permute-done | bytes 540704 | tf_op jit(solution)/shard_map/ppermute | solution.py:348
  36.5 0.1 pair.1
  36.7 23.5 %all_to_all.16.parts_ref = bf16[8,320,128]{2,1,0:T(8,128)(2,1)S(1)} all-to-all(bf16[8,320,128]{2,1,0:T(8,128)(2,1)S(1)} %pair.1), channel_id=1, replica_groups={{0,8,16,24,32,40,48,56},{4,12,20,28,36,44,52,60},{1,9,17,25,33,41,49,57..., dimensions={0} | all-to-all | bytes 1310720 | tf_op jit(solution)/shard_map/all_to_all | solution.py:358
  60.1 1.6 %update.1 = bf16[4,128,128]{2,1,0:T(8,128)(2,1)S(1)} custom-call(s32[1,16]{1,0:T(1,128)S(1)} %copy-done.3, s32[128]{0:T(128)S(1)} %copy-done.4, s32[1,128]{1,0:T(1,128)S(1)} %bitcast.14, bf16[8,320,128]{2,1,0:T(8,128)(2,1)S(1)} %all_to_all.16.parts_ref, bf16[32,64,512]{2,1,0:T(8,128)(2,1)S(1)} %copy-done), custom_call_target="tpu_custom_call" | custom-call | tf_op jit(solution)/shard_map/update/pallas_call | solution.py:361
  61.7 8.7 %all_to_all.17.got_ref = bf16[4,128,128]{2,1,0:T(8,128)(2,1)S(1)} all-to-all(bf16[4,128,128]{2,1,0:T(8,128)(2,1)S(1)} %update.1), channel_id=1, replica_groups=mesh['dp'=4,'tensor'=16,'owner'=4] {'owner'}, dimensions={0} | all-to-all | bytes 262144 | tf_op jit(solution)/shard_map/all_to_all | solution.py:370
  70.4 0.6 final.1
  (7 shorter events, 0.0 us)
Async XLA Ops:
  0.0 5.0 %copy-start.3 = (s32[1,16]{1,0:T(1,128)S(1)}, s32[1,16]{1,0:T(1,128)}, u32[]{:S(2)}) copy-start(s32[1,16]{1,0:T(1,128)} %group_ref.5) | copy-start | bytes 196
  0.0 5.0 %copy-start.4 = (s32[128]{0:T(128)S(1)}, s32[128]{0:T(128)}, u32[]{:S(2)}) copy-start(s32[128]{0:T(128)} %store_ref.5) | copy-start | bytes 1540
  0.0 5.0 %copy-start.6 = (bf16[8,2,128]{2,1,0:T(2,128)(2,1)S(1)}, bf16[8,2,128]{2,1,0:T(2,128)(2,1)}, u32[]{:S(2)}) copy-start(bf16[8,2,128]{2,1,0:T(2,128)(2,1)} %value_ref.1) | copy-start | bytes 12292
  0.0 5.0 %copy-start.5 = (bf16[8,2,128]{2,1,0:T(2,128)(2,1)S(1)}, bf16[8,2,128]{2,1,0:T(2,128)(2,1)}, u32[]{:S(2)}) copy-start(bf16[8,2,128]{2,1,0:T(2,128)(2,1)} %key_ref.1) | copy-start | bytes 12292
  0.0 5.0 %copy-start.1 = (bf16[8,512,2,128]{3,2,1,0:T(2,128)(2,1)S(1)}, bf16[8,512,2,128]{3,2,1,0:T(2,128)(2,1)}, u32[]{:S(2)}) copy-start(bf16[8,512,2,128]{3,2,1,0:T(2,128)(2,1)} %param.12) | copy-start | bytes 6291460
  1.7 30.8 %collective-permute-start = (bf16[128,2048]{1,0:T(8,128)(2,1)S(1)}, bf16[128,2048]{1,0:T(8,128)(2,1)S(1)}, u32[]{:S(2)}, u32[]{:S(2)}) collective-permute-start(bf16[128,2048]{1,0:T(8,128)(2,1)S(1)} %get-tuple-element.16), channel_id=1, source_target_pairs={{0,1},{1,2},{2,3},{3,0},{4,5},{5,6},{6,7},{7,4},{8,9},{9,10},{10,1... | collective-permute-start | bytes 1572872 | tf_op jit(solution)/shard_map/ppermute | solution.py:289
  3.2 29.2 %collective-permute-start.1 = (bf16[128,2048]{1,0:T(8,128)(2,1)S(1)}, bf16[128,2048]{1,0:T(8,128)(2,1)S(1)}, u32[]{:S(2)}, u32[]{:S(2)}) collective-permute-start(bf16[128,2048]{1,0:T(8,128)(2,1)S(1)} %get-tuple-element.17), channel_id=1, source_target_pairs={{0,3},{1,0},{2,1},{3,2},{4,7},{5,4},{6,5},{7,6},{8,11},{9,8},{10,9... | collective-permute-start | bytes 1572872 | tf_op jit(solution)/shard_map/ppermute | solution.py:290
  5.0 0.8 %copy-start.2 = (bf16[8,2048]{1,0:T(8,128)(2,1)S(1)}, bf16[8,2048]{1,0:T(8,128)(2,1)}, u32[]{:S(2)}) copy-start(bf16[8,2048]{1,0:T(8,128)(2,1)} %param.11) | copy-start | bytes 98308
  5.8 26.7 %copy-start.7 = (s32[128]{0:T(128)S(1)}, s32[128]{0:T(128)}, u32[]{:S(2)}) copy-start(s32[128]{0:T(128)} %param.21) | copy-start | bytes 1540
  34.5 25.6 %copy-start = (bf16[32,64,512]{2,1,0:T(8,128)(2,1)S(1)}, bf16[32,64,512]{2,1,0:T(8,128)(2,1)}, u32[]{:S(2)}) copy-start(bf16[32,64,512]{2,1,0:T(8,128)(2,1)} %up_ref.1) | copy-start | bytes 6291460
  34.5 2.0 %collective-permute-start.2 = (bf16[2112,128]{1,0:T(8,128)(2,1)S(1)}, bf16[2112,128]{1,0:T(8,128)(2,1)S(1)}, u32[]{:S(2)}, u32[]{:S(2)}) collective-permute-start(bf16[2112,128]{1,0:T(8,128)(2,1)S(1)} %get-tuple-element.20), channel_id=1, source_target_pairs={{0,4},{4,0},{8,12},{12,8},{16,20},{20,16},{24,28},{28,24},{32,36},... | collective-permute-start | bytes 1622024 | tf_op jit(solution)/shard_map/ppermute | solution.py:348

commit v4 on v3

--- a/solution.py
+++ b/solution.py
@@ -34,31 +34,28 @@
     return jnp.transpose(jnp.broadcast_to(rows_ref[...], (rows, rows)))[:, :width]
 
 
-def column_copies(w_ref, out_ref, step, sems, base):
-    owners = lax.axis_size("owner")
-    target = lax.rem(lax.axis_index("owner") + step, owners)
-    copies = []
-    for block in range(out_ref.shape[1] // 128):
-        at = pl.multiple_of((block * owners + target) * 128, 128)
-        copies.append(
-            pltpu.make_async_copy(
-                w_ref.at[:, pl.ds(at, 128)],
-                out_ref.at[:, pl.ds(block * 128, 128)],
-                sems.at[base + block],
-            )
+def slab_kernel(w_hbm_ref, queries_hbm_ref, w_ref, queries_ref, right_ref, left_ref, sems):
+    chunks = sems.shape[0] - 1
+    step = w_ref.shape[0] // chunks
+    copies = [
+        pltpu.make_async_copy(
+            w_hbm_ref.at[pl.ds(i * step, step)], w_ref.at[pl.ds(i * step, step)], sems.at[i]
         )
-    return copies
-
-
-def slab_kernel(w_ref, right_ref, left_ref, sems):
-    owners = lax.axis_size("owner")
-    blocks = right_ref.shape[1] // 128
-    copies = column_copies(w_ref, right_ref, 1, sems, 0)
-    copies += column_copies(w_ref, left_ref, owners - 1, sems, blocks)
+        for i in range(chunks)
+    ]
+    copies.append(pltpu.make_async_copy(queries_hbm_ref, queries_ref, sems.at[chunks]))
     for copy in copies:
         copy.start()
-    for copy in copies:
-        copy.wait()
+    owner, owners = lax.axis_index("owner"), lax.axis_size("owner")
+    targets = [lax.rem(owner + 1, owners), lax.rem(owner + owners - 1, owners)]
+    for i in range(chunks):
+        copies[i].wait()
+        rows = pl.ds(i * step, step)
+        for out_ref, target in zip((right_ref, left_ref), targets):
+            for block in range(out_ref.shape[1] // 128):
+                at = pl.multiple_of((block * owners + target) * 128, 128)
+                out_ref[rows, block * 128 : (block + 1) * 128] = w_ref[rows, pl.ds(at, 128)]
+    copies[chunks].wait()
 
 
 def attend_kernel(
@@ -69,40 +66,30 @@
     values_hbm_ref,
     key_ref,
     value_ref,
-    w_ref,
     down_ref,
     out_ref,
-    mine_ref,
-    across_ref,
     slots_ref,
     values_ref,
-    value_sems,
+    value_sem,
     sems,
 ):
     stored = down_ref.shape[0]
-    blocks = mine_ref.shape[1] // 128
-    value_copies = [
-        pltpu.make_async_copy(values_hbm_ref.at[r], values_ref.at[r], value_sems.at[r])
-        for r in range(values_ref.shape[0])
-    ]
-    for copy in value_copies:
-        copy.start()
-    copies = column_copies(w_ref, mine_ref, 0, sems, 0)
-    copies += column_copies(w_ref, across_ref, 2, sems, blocks)
+    values_copy = pltpu.make_async_copy(values_hbm_ref, values_ref, value_sem)
+    values_copy.start()
+    copies = []
     for s in range(slots_ref.shape[0]):
         spot, _ = slot_position(s, group_ref, store_ref, stored)
-        copies.append(
-            pltpu.make_async_copy(down_ref.at[spot], slots_ref.at[s], sems.at[2 * blocks + s])
-        )
+        copies.append(pltpu.make_async_copy(down_ref.at[spot], slots_ref.at[s], sems.at[s]))
     for copy in copies:
         copy.start()
 
-    heads, rows, width = queries_ref.shape
-    _, local, _ = key_ref.shape
+    rows, local, width = key_ref.shape
+    heads = queries_ref.shape[1] // width
     grouped = heads // local
     positions = keys_ref.shape[1]
     scale = width ** (-0.5)
-    queries = jnp.swapaxes(queries_ref[...].astype(F32), 0, 1)
+    queries = [queries_ref[:, h * width : (h + 1) * width].astype(F32) for h in range(heads)]
+    queries = jnp.swapaxes(jnp.stack(queries), 0, 1)
     row_head = lax.broadcasted_iota(jnp.int32, (heads, positions), 0) // grouped
     place_head = lax.broadcasted_iota(jnp.int32, (heads, positions), 1) % local
     same = row_head == place_head
@@ -112,7 +99,7 @@
         parts = [jnp.broadcast_to(fresh[k : k + 1], (grouped, width)) for k in range(local)]
         return jnp.concatenate(parts, axis=0)
 
-    mixed = []
+    weights, fresh_weights, denominators = [], [], []
     for r in range(rows):
         query = queries[r]
         scores = lax.dot_general(
@@ -121,13 +108,17 @@
         scores = jnp.where(same, scores * scale, -jnp.inf)
         fresh_score = jnp.sum(query * spread(key_ref, r), axis=1, keepdims=True) * scale
         overall = jnp.maximum(jnp.max(scores, axis=1, keepdims=True), fresh_score)
-        weights = jnp.exp(scores - overall)
+        weight = jnp.exp(scores - overall)
         fresh_weight = jnp.exp(fresh_score - overall)
-        denominator = jnp.sum(weights, axis=1, keepdims=True) + fresh_weight
-        value_copies[r].wait()
-        total = jnp.dot(weights.astype(BF16), values_ref[r], preferred_element_type=F32)
-        total = total + fresh_weight * spread(value_ref, r)
-        mixed.append(total / denominator)
+        denominators.append(jnp.sum(weight, axis=1, keepdims=True) + fresh_weight)
+        weights.append(weight.astype(BF16))
+        fresh_weights.append(fresh_weight)
+    values_copy.wait()
+    mixed = []
+    for r in range(rows):
+        total = jnp.dot(weights[r], values_ref[r], preferred_element_type=F32)
+        total = total + fresh_weights[r] * spread(value_ref, r)
+        mixed.append(total / denominators[r])
     mixed = jnp.swapaxes(jnp.stack(mixed), 0, 1)
 
     half = width // 2
@@ -139,8 +130,9 @@
             jnp.where(low, pltpu.roll(one, half, 1), two),
         )
         for i, part in enumerate(pair):
+            part = part.astype(BF16)
             for o in range(out_ref.shape[0]):
-                out_ref[o, 2 * g + i] = part.astype(BF16)
+                out_ref[o, 2 * g + i] = part
     for copy in copies:
         copy.wait()
 
@@ -150,8 +142,7 @@
     store_ref,
     rows_ref,
     att_ref,
-    mine_ref,
-    across_ref,
+    w_ref,
     before_ref,
     after_ref,
     slots_ref,
@@ -171,12 +162,18 @@
     block = keep_ref.shape[1]
     planes = before_ref.shape[1] // (2 * block)
 
+    across = lax.rem(owner + 2, owners)
+
+    def columns(z, target):
+        at = [pl.multiple_of(((2 * z + c) * owners + target) * block, block) for c in range(2)]
+        return jnp.concatenate([w_ref[:, pl.ds(a, block)] for a in at], axis=1)
+
     for z in range(planes):
         span = pl.ds(z * 2 * block, 2 * block)
         near_rows = jnp.concatenate([before_ref[:, span], after_ref[:, span]], axis=0)
         here = jnp.dot(beside, near_rows, preferred_element_type=F32)
-        here = here + jnp.dot(mine, mine_ref[:, span], preferred_element_type=F32)
-        there = jnp.dot(mine, across_ref[:, span], preferred_element_type=F32)
+        here = here + jnp.dot(mine, columns(z, owner), preferred_element_type=F32)
+        there = jnp.dot(mine, columns(z, across), preferred_element_type=F32)
         for i, part in enumerate((here, there)):
             even, odd = part[:, :block], part[:, block:]
             rows_span = pl.ds((2 * z + i) * rows, rows)
@@ -274,49 +271,47 @@
     rank = adapter_down_weight.shape[-1]
     row_ids = adapter_per_row.reshape(1, rows)
 
-    weight = far(output_weight.reshape(feats, columns))
     slab = pltpu.VMEM((feats, columns // owners), BF16)
-    blocks = columns // owners // 128
-    right, left = pl.pallas_call(
+    weight, local_queries, right, left = pl.pallas_call(
         slab_kernel,
         name="slabs",
-        out_shape=(slab, slab),
-        in_specs=[HBM],
-        out_specs=(VMEM, VMEM),
-        scratch_shapes=[pltpu.SemaphoreType.DMA((2 * blocks,))],
-        compiler_params=LIMIT,
-    )(weight)
+        out_shape=(
+            pltpu.VMEM((feats, columns), BF16),
+            pltpu.VMEM(queries.shape, BF16),
+            slab,
+            slab,
+        ),
+        in_specs=[HBM, HBM],
+        out_specs=(VMEM, VMEM, VMEM, VMEM),
+        scratch_shapes=[pltpu.SemaphoreType.DMA((5,))],
+        compiler_params=LIMIT,
+    )(far(output_weight.reshape(feats, columns)), far(queries))
     before = lax.ppermute(right, "owner", [(o, (o + 1) % owners) for o in range(owners)])
     after = lax.ppermute(left, "owner", [(o, (o - 1) % owners) for o in range(owners)])
 
-    heads = queries.shape[1] // head_width
-    grouped = queries.reshape(row_count, heads, head_width).transpose(1, 0, 2)
-    outgoing, mine, across, tables = pl.pallas_call(
+    outgoing, tables = pl.pallas_call(
         attend_kernel,
         name="attend",
         out_shape=(
             pltpu.VMEM((owners, tensors, row_count, feats), BF16),
-            slab,
-            slab,
             pltpu.VMEM((slots,) + adapter_down_weight.shape[1:], BF16),
         ),
-        in_specs=[SMEM, SMEM, VMEM, VMEM, HBM, VMEM, VMEM, HBM, HBM],
-        out_specs=(VMEM, VMEM, VMEM, VMEM),
+        in_specs=[SMEM, SMEM, VMEM, VMEM, HBM, VMEM, VMEM, HBM],
+        out_specs=(VMEM, VMEM),
         scratch_shapes=[
             pltpu.VMEM((row_count, cached_value_rows.shape[1] * local_heads, head_width), BF16),
-            pltpu.SemaphoreType.DMA((row_count,)),
-            pltpu.SemaphoreType.DMA((2 * blocks + slots,)),
+            pltpu.SemaphoreType.DMA,
+            pltpu.SemaphoreType.DMA((slots,)),
         ],
         compiler_params=LIMIT,
     )(
         adapters_by_group,
         adapter_store_row,
-        grouped,
+        near(local_queries),
         near(cached_key_rows.reshape(row_count, -1, head_width)),
         far(cached_value_rows.reshape(row_count, -1, head_width)),
         newest_key,
         newest_value,
-        weight,
         far(adapter_down_weight),
     )
     outgoing = outgoing.reshape(owners * tensors, row_count, feats)
@@ -330,7 +325,7 @@
         project_kernel,
         name="project",
         out_shape=(pltpu.VMEM((tall, block), F32), pltpu.VMEM((tall, block), BF16)),
-        in_specs=[SMEM, SMEM] + [VMEM] * 7,
+        in_specs=[SMEM, SMEM] + [VMEM] * 6,
         out_specs=(VMEM, VMEM),
         scratch_shapes=[pltpu.VMEM((rows, rank), F32)],
         compiler_params=LIMIT,
@@ -339,8 +334,7 @@
         adapter_store_row,
         row_ids,
         near(attention),
-        near(mine),
-        near(across),
+        near(weight),
         near(before),
         near(after),
         near(tables),

time: 71.7 us -> 69.9 us (0.975)
  Pallas kernels: 11.9 us -> 10.8 us
  local copies, waits for them, and re-layouts: 0.78 us -> 0.03 us
    pallas_call x1, Pallas kernels: 5.84 us -> 4.32 us  [shards(): pl.pallas_call(attend_kernel, name='attend', out_shape=(pltpu.VMEM((owner...]
    unnamed x16 -> x14, local copies, waits for them, and re-layouts: 0.78 us -> 0.03 us
  transfers between devices with their start and end apart: 3 -> 3, of which waited for: 1 -> 1; matrix products, arithmetic and copies ran while one was open for 0% -> 0% of each run, Pallas kernels for 8% -> 6%
where the time goes in v4:
time: 69.9 us; the launch traced here: 69.4 us
  blocking collectives  53.1 us (76%)
  Pallas kernels  10.8 us (15%)
  starting transfers between devices  3.51 us (5%)
  waiting for transfers between devices  1.82 us (3%)
    all_to_all x1, blocking collectives, shards(): lax.all_to_all(pieces, 'tensor', split_axis=0, concat_axis=0, tiled=True,...  23.5 us
    all_to_all x1, blocking collectives, shards(): lax.all_to_all(outgoing, ('owner', 'tensor'), split_axis=0, concat_axis=0...  20.9 us
    all_to_all x1, blocking collectives, shards(): lax.all_to_all(sums, 'owner', split_axis=0, concat_axis=0, tiled=True)  8.72 us
    pallas_call x1, Pallas kernels, shards(): pl.pallas_call(attend_kernel, name='attend', out_shape=(pltpu.VMEM((owner...  4.32 us
    pallas_call x1, Pallas kernels, shards(): pl.pallas_call(project_kernel, name='project', out_shape=(pltpu.VMEM((tal...  2.26 us
    ppermute x1, waiting for transfers between devices, shards(): got = lax.ppermute(send, 'tensor', [(t, t ^ 1) for t in range(tensors)])  1.82 us
    pallas_call x1, Pallas kernels, shards(): pl.pallas_call(slab_kernel, name='slabs', out_shape=(pltpu.VMEM((feats, c...  1.78 us
    ppermute x1, starting transfers between devices, shards(): lax.ppermute(left, 'owner', [(o, (o - 1) % owners) for o in range(owners)])  1.75 us
  transfers between devices with their start and end apart: 3, of which 1 were waited for; matrix products, arithmetic and copies ran while one was open for 0% of the time, Pallas kernels for 6%

profile of v4, /device:TPU:24, one launch (start us, length us, event | category | flops | bytes accessed | tf_op | source)
XLA Modules:
  0.0 69.4 jit_solution(2231356163272892203)
XLA Ops:
  0.0 0.0 copy-start.4
  0.0 0.0 copy-start
  0.0 1.8 %slabs.1 = (bf16[128,8192]{1,0:T(8,128)(2,1)S(1)}, bf16[8,2048]{1,0:T(8,128)(2,1)S(1)}, bf16[128,2048]{1,0:T(8,128)(2,1)S(1)}, bf16[128,2048]{1,0:T(8,128)(2,1)S(1)}) custom-call(bf16[128,8192]{1,0:T(8,128)(2,1)} %bitcast.12, bf16[8,2048]{1,0:T(8,128)(2,1)} %queries_hbm_ref.1), custom_call_target="tpu_custom_call" | custom-call | tf_op jit(solution)/shard_map/slabs/pallas_call | solution.py:275
  1.8 1.6 %collective-permute-start = (bf16[128,2048]{1,0:T(8,128)(2,1)S(1)}, bf16[128,2048]{1,0:T(8,128)(2,1)S(1)}, u32[]{:S(2)}, u32[]{:S(2)}) collective-permute-start(bf16[128,2048]{1,0:T(8,128)(2,1)S(1)} %get-tuple-element.16), channel_id=1, source_target_pairs={{0,1},{1,2},{2,3},{3,0},{4,5},{5,6},{6,7},{7,4},{8,9},{9,10},{10,1... | collective-permute-start | bytes 1572872 | tf_op jit(solution)/shard_map/ppermute | solution.py:289
  3.4 1.7 %collective-permute-start.1 = (bf16[128,2048]{1,0:T(8,128)(2,1)S(1)}, bf16[128,2048]{1,0:T(8,128)(2,1)S(1)}, u32[]{:S(2)}, u32[]{:S(2)}) collective-permute-start(bf16[128,2048]{1,0:T(8,128)(2,1)S(1)} %get-tuple-element.17), channel_id=1, source_target_pairs={{0,3},{1,0},{2,1},{3,2},{4,7},{5,4},{6,5},{7,6},{8,11},{9,8},{10,9... | collective-permute-start | bytes 1572872 | tf_op jit(solution)/shard_map/ppermute | solution.py:290
  5.1 0.0 copy-done.2
  5.1 0.0 copy-done.3
  5.1 0.0 copy-done.5
  5.1 0.0 copy-done.4
  5.1 0.0 copy-done
  5.2 0.0 copy-start.6
  5.2 4.3 %attend.1 = (bf16[4,16,8,128]{3,2,1,0:T(8,128)(2,1)S(1)}, bf16[16,8,64,64]{3,2,1,0:T(8,128)(2,1)S(1)}) custom-call(s32[1,16]{1,0:T(1,128)S(1)} %copy-done.2, s32[128]{0:T(128)S(1)} %copy-done.3, bf16[8,2048]{1,0:T(8,128)(2,1)S(1)} %get-tuple-element.13.queries_ref, bf16[8,1024,128]{2,1,0:T(8,128)(2,1)S(1)} %bitcast.6, bf16[8,1024,128]{2,1,0:T(8,128)(2,1)} %bitcast.11, ...), custom_call_target="tpu_custom_call" | custom-call | tf_op jit(solution)/shard_map/attend/pallas_call | solution.py:292
  9.5 20.9 %all_to_all.15 = bf16[64,8,128]{2,1,0:T(8,128)(2,1)S(1)} all-to-all(bf16[64,8,128]{2,1,0:T(8,128)(2,1)S(1)} %bitcast.8), channel_id=1, replica_groups=mesh['dp'=4,'tensor'=16,'owner'=4] {'owner','tensor'}, dimensions={0} | all-to-all | bytes 262144 | tf_op jit(solution)/shard_map/all_to_all | solution.py:318
  30.4 0.0 collective-permute-done.before_ref
  30.4 0.0 collective-permute-done.1.after_ref
  30.4 0.0 copy-done.6
  30.4 2.3 %project.1 = (f32[2112,128]{1,0:T(8,128)S(1)}, bf16[2112,128]{1,0:T(8,128)(2,1)S(1)}) custom-call(s32[1,16]{1,0:T(1,128)S(1)} %copy-done.2, s32[128]{0:T(128)S(1)} %copy-done.3, s32[1,128]{1,0:T(1,128)S(1)} %bitcast.9, bf16[4,128,128]{2,1,0:T(8,128)(2,1)S(1)} %bitcast.7, bf16[128,8192]{1,0:T(8,128)(2,1)S(1)} %get-tuple-element.15.w_ref, ...), custom_call_target="tpu_custom_call" | custom-call | tf_op jit(solution)/shard_map/project/pallas_call | solution.py:324
  32.7 0.2 collective-permute-start.2
  32.9 1.8 %collective-permute-done.2.got_ref = bf16[2112,128]{1,0:T(8,128)(2,1)S(1)} collective-permute-done((bf16[2112,128]{1,0:T(8,128)(2,1)S(1)}, bf16[2112,128]{1,0:T(8,128)(2,1)S(1)}, u32[]{:S(2)}, u32[]{:S(2)}) %collective-permute-start.2) | collective-permute-done | bytes 540704 | tf_op jit(solution)/shard_map/ppermute | solution.py:342
  34.7 0.1 pair.1
  34.8 23.5 %all_to_all.16.parts_ref = bf16[8,320,128]{2,1,0:T(8,128)(2,1)S(1)} all-to-all(bf16[8,320,128]{2,1,0:T(8,128)(2,1)S(1)} %pair.1), channel_id=1, replica_groups={{0,8,16,24,32,40,48,56},{4,12,20,28,36,44,52,60},{1,9,17,25,33,41,49,57..., dimensions={0} | all-to-all | bytes 1310720 | tf_op jit(solution)/shard_map/all_to_all | solution.py:352
  58.3 1.7 %update.1 = bf16[4,128,128]{2,1,0:T(8,128)(2,1)S(1)} custom-call(s32[1,16]{1,0:T(1,128)S(1)} %copy-done.2, s32[128]{0:T(128)S(1)} %copy-done.3, s32[1,128]{1,0:T(1,128)S(1)} %bitcast.10, bf16[8,320,128]{2,1,0:T(8,128)(2,1)S(1)} %all_to_all.16.parts_ref, bf16[32,64,512]{2,1,0:T(8,128)(2,1)S(1)} %copy-done.1), custom_call_target="tpu_custom_call" | custom-call | tf_op jit(solution)/shard_map/update/pallas_call | solution.py:355
  60.0 8.7 %all_to_all.17.got_ref = bf16[4,128,128]{2,1,0:T(8,128)(2,1)S(1)} all-to-all(bf16[4,128,128]{2,1,0:T(8,128)(2,1)S(1)} %update.1), channel_id=1, replica_groups=mesh['dp'=4,'tensor'=16,'owner'=4] {'owner'}, dimensions={0} | all-to-all | bytes 262144 | tf_op jit(solution)/shard_map/all_to_all | solution.py:364
  68.7 0.6 final.1
  (5 shorter events, 0.0 us)
Async XLA Ops:
  0.0 5.1 %copy-start.2 = (s32[1,16]{1,0:T(1,128)S(1)}, s32[1,16]{1,0:T(1,128)}, u32[]{:S(2)}) copy-start(s32[1,16]{1,0:T(1,128)} %group_ref.5) | copy-start | bytes 196
  0.0 5.1 %copy-start.3 = (s32[128]{0:T(128)S(1)}, s32[128]{0:T(128)}, u32[]{:S(2)}) copy-start(s32[128]{0:T(128)} %store_ref.5) | copy-start | bytes 1540
  0.0 5.1 %copy-start.5 = (bf16[8,2,128]{2,1,0:T(2,128)(2,1)S(1)}, bf16[8,2,128]{2,1,0:T(2,128)(2,1)}, u32[]{:S(2)}) copy-start(bf16[8,2,128]{2,1,0:T(2,128)(2,1)} %value_ref.1) | copy-start | bytes 12292
  0.0 5.1 %copy-start.4 = (bf16[8,2,128]{2,1,0:T(2,128)(2,1)S(1)}, bf16[8,2,128]{2,1,0:T(2,128)(2,1)}, u32[]{:S(2)}) copy-start(bf16[8,2,128]{2,1,0:T(2,128)(2,1)} %key_ref.1) | copy-start | bytes 12292
  0.0 5.1 %copy-start = (bf16[8,512,2,128]{3,2,1,0:T(2,128)(2,1)S(1)}, bf16[8,512,2,128]{3,2,1,0:T(2,128)(2,1)}, u32[]{:S(2)}) copy-start(bf16[8,512,2,128]{3,2,1,0:T(2,128)(2,1)} %param.12) | copy-start | bytes 6291460
  1.8 28.6 %collective-permute-start = (bf16[128,2048]{1,0:T(8,128)(2,1)S(1)}, bf16[128,2048]{1,0:T(8,128)(2,1)S(1)}, u32[]{:S(2)}, u32[]{:S(2)}) collective-permute-start(bf16[128,2048]{1,0:T(8,128)(2,1)S(1)} %get-tuple-element.16), channel_id=1, source_target_pairs={{0,1},{1,2},{2,3},{3,0},{4,5},{5,6},{6,7},{7,4},{8,9},{9,10},{10,1... | collective-permute-start | bytes 1572872 | tf_op jit(solution)/shard_map/ppermute | solution.py:289
  3.4 27.0 %collective-permute-start.1 = (bf16[128,2048]{1,0:T(8,128)(2,1)S(1)}, bf16[128,2048]{1,0:T(8,128)(2,1)S(1)}, u32[]{:S(2)}, u32[]{:S(2)}) collective-permute-start(bf16[128,2048]{1,0:T(8,128)(2,1)S(1)} %get-tuple-element.17), channel_id=1, source_target_pairs={{0,3},{1,0},{2,1},{3,2},{4,7},{5,4},{6,5},{7,6},{8,11},{9,8},{10,9... | collective-permute-start | bytes 1572872 | tf_op jit(solution)/shard_map/ppermute | solution.py:290
  5.2 25.2 %copy-start.6 = (s32[128]{0:T(128)S(1)}, s32[128]{0:T(128)}, u32[]{:S(2)}) copy-start(s32[128]{0:T(128)} %param.21) | copy-start | bytes 1540
  32.7 25.6 %copy-start.1 = (bf16[32,64,512]{2,1,0:T(8,128)(2,1)S(1)}, bf16[32,64,512]{2,1,0:T(8,128)(2,1)}, u32[]{:S(2)}) copy-start(bf16[32,64,512]{2,1,0:T(8,128)(2,1)} %up_ref.1) | copy-start | bytes 6291460
  32.7 2.0 %collective-permute-start.2 = (bf16[2112,128]{1,0:T(8,128)(2,1)S(1)}, bf16[2112,128]{1,0:T(8,128)(2,1)S(1)}, u32[]{:S(2)}, u32[]{:S(2)}) collective-permute-start(bf16[2112,128]{1,0:T(8,128)(2,1)S(1)} %get-tuple-element.20), channel_id=1, source_target_pairs={{0,4},{4,0},{8,12},{12,8},{16,20},{20,16},{24,28},{28,24},{32,36},... | collective-permute-start | bytes 1622024 | tf_op jit(solution)/shard_map/ppermute | solution.py:342

commit v5 on v4

--- a/solution.py
+++ b/solution.py
@@ -197,53 +197,70 @@
     send_ref[2 * planes * rows :, :] = code.astype(BF16)
 
 
-def pair_kernel(keep_ref, got_ref, out_ref):
-    planes, total, _ = out_ref.shape
-    tall = (keep_ref.shape[0] - total) // (planes - 1)
-    code = keep_ref[planes * tall :, :] + got_ref[planes * tall :, :].astype(F32)
-    code = code.astype(BF16)
+def pair_kernel(keep_ref, got_ref, own_ref, across_ref, codes_ref):
+    planes, rows, _ = own_ref.shape
     for z in range(planes):
-        span = pl.ds(z * tall, tall)
-        out_ref[z, :tall, :] = (keep_ref[span, :] + got_ref[span, :].astype(F32)).astype(BF16)
-        out_ref[z, tall:, :] = code
-
-
-def update_kernel(group_ref, store_ref, rows_ref, parts_ref, up_ref, send_ref, acc):
-    slots = group_ref.shape[1]
-    stored, rank, _ = up_ref.shape
-    owners, rows, block = send_ref.shape
+        span = pl.ds(2 * z * rows, rows)
+        own_ref[z] = keep_ref[span, :] + got_ref[span, :].astype(F32)
+        span = pl.ds((2 * z + 1) * rows, rows)
+        across_ref[z] = (keep_ref[span, :] + got_ref[span, :].astype(F32)).astype(BF16)
+    span = pl.ds(2 * planes * rows, codes_ref.shape[1])
+    code = (keep_ref[span, :] + got_ref[span, :].astype(F32)).astype(BF16)
+    for z in range(planes):
+        codes_ref[z] = code
+
+
+def add_kernel(one_ref, two_ref, out_ref):
+    out_ref[...] = (one_ref[...] + two_ref[...].astype(F32)).astype(BF16)
+
+
+def update_kernel(
+    group_ref, store_ref, rows_ref, codes_ref, up_ref, own_ref, *rest
+):
+    send_refs, (ubuf, acc, sems) = rest[:-3], rest[-3:]
+    slots, rank, _ = ubuf.shape
+    stored = up_ref.shape[0]
+    copies = []
+    for s in range(slots):
+        spot, _ = slot_position(s, group_ref, store_ref, stored)
+        copy = pltpu.make_async_copy(up_ref.at[spot], ubuf.at[s], sems.at[s])
+        copy.start()
+        copies.append(copy)
+    rows, block = own_ref.shape
+    owners = lax.axis_size("owner")
     owner = lax.axis_index("owner")
-
-    def total(start, size):
-        part = parts_ref[0, start : start + size, :].astype(F32)
-        for z in range(1, parts_ref.shape[0]):
-            part = part + parts_ref[z, start : start + size, :].astype(F32)
-        return part
-
-    packed = total(2 * rows, rows // 2)
+    packed = codes_ref[0].astype(F32)
+    for z in range(1, codes_ref.shape[0]):
+        packed = packed + codes_ref[z].astype(F32)
     code = jnp.concatenate([packed[:, :rank], packed[:, rank:]], axis=0).astype(BF16).astype(F32)
     ids = row_adapters(rows_ref, rank)
     acc[...] = jnp.zeros_like(acc)
     for s in range(slots):
-        spot, here = slot_position(s, group_ref, store_ref, stored)
+        copies[s].wait()
+        _, here = slot_position(s, group_ref, store_ref, stored)
 
         @pl.when(here)
-        def _(s=s, spot=spot):
+        def _(s=s):
             chosen = jnp.where(ids == group_ref[0, s], code, 0.0).astype(BF16)
-            acc[...] += jnp.dot(chosen, up_ref[spot], preferred_element_type=F32)
-
-    own, across = total(0, rows), total(rows, rows)
-    for o in range(owners):
-        update = ADAPTER_SCALE * acc[:, o * block : (o + 1) * block]
-        base = jnp.where(owner == o, own, jnp.where(owner == (o + 2) % owners, across, 0.0))
-        send_ref[o] = (base + update).astype(BF16)
-
-
-def final_kernel(got_ref, out_ref):
-    total = got_ref[0].astype(F32)
-    for o in range(1, got_ref.shape[0]):
-        total = total + got_ref[o].astype(F32)
-    out_ref[...] = total.astype(BF16)
+            acc[...] += jnp.dot(chosen, ubuf[s], preferred_element_type=F32)
+
+    def columns(target):
+        return acc[:, pl.ds(pl.multiple_of(target * block, block), block)]
+
+    own_ref[...] = columns(owner)
+    for i, send_ref in enumerate(send_refs):
+        send_ref[...] = columns(lax.rem(owner + i + 1, owners)).astype(BF16)
+
+
+def final_kernel(parts_ref, own_ref, *rest):
+    got_refs, out_ref = rest[:-1], rest[-1]
+    base = parts_ref[0].astype(F32)
+    for z in range(1, parts_ref.shape[0]):
+        base = base + parts_ref[z].astype(F32)
+    update = own_ref[...]
+    for got_ref in got_refs:
+        update = update + got_ref[...].astype(F32)
+    out_ref[...] = (base + ADAPTER_SCALE * update).astype(BF16)
 
 
 def shards(
@@ -340,36 +357,63 @@
         near(tables),
     )
     got = lax.ppermute(send, "tensor", [(t, t ^ 1) for t in range(tensors)])
-    pieces = pl.pallas_call(
+    own_part, across, codes = pl.pallas_call(
         pair_kernel,
         name="pair",
-        out_shape=pltpu.VMEM((planes, 2 * rows + rows // 2, block), BF16),
+        out_shape=(
+            pltpu.VMEM((planes, rows, block), F32),
+            pltpu.VMEM((planes, rows, block), BF16),
+            pltpu.VMEM((planes, rows // 2, 2 * rank), BF16),
+        ),
         in_specs=[VMEM, VMEM],
-        out_specs=VMEM,
+        out_specs=(VMEM, VMEM, VMEM),
         compiler_params=LIMIT,
     )(near(keep), near(got))
     groups = [[2 * z + c for z in range(planes)] for c in range(2)]
-    parts = lax.all_to_all(
-        pieces, "tensor", split_axis=0, concat_axis=0, tiled=True, axis_index_groups=groups
-    )
-    sums = pl.pallas_call(
+
+    def over_z(pieces):
+        return lax.all_to_all(
+            pieces, "tensor", split_axis=0, concat_axis=0, tiled=True, axis_index_groups=groups
+        )
+
+    across = lax.ppermute(across, "owner", [(o, (o + 2) % owners) for o in range(owners)])
+    codes = over_z(codes)
+    strip = pltpu.VMEM((rows, block), BF16)
+    own_update, *updates = pl.pallas_call(
         update_kernel,
         name="update",
-        out_shape=pltpu.VMEM((owners, rows, block), BF16),
-        in_specs=[SMEM, SMEM, VMEM, VMEM, VMEM],
-        out_specs=VMEM,
-        scratch_shapes=[pltpu.VMEM((rows, owners * block), F32)],
-        compiler_params=LIMIT,
-    )(adapters_by_group, adapter_store_row, row_ids, near(parts), near(adapter_up_weight))
-    sums = lax.all_to_all(sums, "owner", split_axis=0, concat_axis=0, tiled=True)
+        out_shape=(pltpu.VMEM((rows, block), F32),) + (strip,) * (owners - 1),
+        in_specs=[SMEM, SMEM] + [VMEM] * 2 + [HBM],
+        out_specs=(VMEM,) * owners,
+        scratch_shapes=[
+            pltpu.VMEM((slots,) + adapter_up_weight.shape[1:], BF16),
+            pltpu.VMEM((rows, owners * block), F32),
+            pltpu.SemaphoreType.DMA((slots,)),
+        ],
+        compiler_params=LIMIT,
+    )(adapters_by_group, adapter_store_row, row_ids, near(codes), far(adapter_up_weight))
+    updates = [
+        lax.ppermute(update, "owner", [(o, (o + i + 1) % owners) for o in range(owners)])
+        for i, update in enumerate(updates)
+    ]
+    parts = over_z(
+        pl.pallas_call(
+            add_kernel,
+            name="add",
+            out_shape=pltpu.VMEM((planes, rows, block), BF16),
+            in_specs=[VMEM, VMEM],
+            out_specs=VMEM,
+            compiler_params=LIMIT,
+        )(near(own_part), near(across))
+    )
     return pl.pallas_call(
         final_kernel,
         name="final",
         out_shape=jax.ShapeDtypeStruct((rows, block), BF16),
-        in_specs=[VMEM],
+        in_specs=[VMEM] * (owners + 1),
         out_specs=VMEM,
         compiler_params=LIMIT,
-    )(near(sums))
+    )(near(parts), near(own_update), *[near(update) for update in updates])
 
 
 def solution(mesh):

time: 69.9 us -> 65.1 us (0.931)
  blocking collectives: 53.1 us -> 20.2 us
  starting transfers between devices: 3.51 us -> 16.8 us
  waiting for transfers between devices: 1.82 us -> 14.7 us
  Pallas kernels: 10.8 us -> 13 us
    all_to_all x2 -> x0, blocking collectives: 32.2 us -> none  [the longest x1 23.5 us: shards(): lax.all_to_all(pieces, 'tensor', split_axis=0, concat_axis=0, tiled=True,...]
    all_to_all x0 -> x2, starting transfers between devices: none -> 6.78 us  [over_z(): lax.all_to_all(pieces, 'tensor', split_axis=0, concat_axis=0, tiled=True,...]
    ppermute x0 -> x4, starting transfers between devices: none -> 6.51 us  [the longest x3 3.63 us: shards(): lax.ppermute(update, 'owner', [(o, (o + i + 1) % owners) for o in range(o...]
    ppermute x0 -> x4, waiting for transfers between devices: none -> 6.45 us  [the longest x1 3.59 us: shards(): lax.ppermute(across, 'owner', [(o, (o + 2) % owners) for o in range(owner...]
    all_to_all x0 -> x2, waiting for transfers between devices: none -> 6.42 us  [over_z(): lax.all_to_all(pieces, 'tensor', split_axis=0, concat_axis=0, tiled=True,...]
    pallas_call x2 -> x3, Pallas kernels: 1.82 us -> 4.07 us  [the longest x1 2.61 us: shards(): pl.pallas_call(update_kernel, name='update', out_shape=(pltpu.VMEM((rows,...]
  transfers between devices with their start and end apart: 3 -> 9, of which waited for: 1 -> 7; matrix products, arithmetic and copies ran while one was open for 0% -> 0% of each run, Pallas kernels for 6% -> 13%
where the time goes in v5:
time: 65.1 us; the launch traced here: 64.8 us
  blocking collectives  20.2 us (31%)
  starting transfers between devices  16.8 us (26%)
  waiting for transfers between devices  14.7 us (23%)
  Pallas kernels  13 us (20%)
    all_to_all x1, blocking collectives, shards(): lax.all_to_all(outgoing, ('owner', 'tensor'), split_axis=0, concat_axis=0...  20.2 us
    all_to_all x2, starting transfers between devices, over_z(): lax.all_to_all(pieces, 'tensor', split_axis=0, concat_axis=0, tiled=True,...  6.78 us
    all_to_all x2, waiting for transfers between devices, over_z(): lax.all_to_all(pieces, 'tensor', split_axis=0, concat_axis=0, tiled=True,...  6.42 us
    pallas_call x1, Pallas kernels, shards(): pl.pallas_call(attend_kernel, name='attend', out_shape=(pltpu.VMEM((owner...  4.86 us
    ppermute x3, starting transfers between devices, shards(): lax.ppermute(update, 'owner', [(o, (o + i + 1) % owners) for o in range(o...  3.63 us
    ppermute x1, waiting for transfers between devices, shards(): lax.ppermute(across, 'owner', [(o, (o + 2) % owners) for o in range(owner...  3.59 us
    ppermute x1, starting transfers between devices, shards(): lax.ppermute(across, 'owner', [(o, (o + 2) % owners) for o in range(owner...  2.89 us
    ppermute x3, waiting for transfers between devices, shards(): lax.ppermute(update, 'owner', [(o, (o + i + 1) % owners) for o in range(o...  2.86 us
  transfers between devices with their start and end apart: 9, of which 7 were waited for; matrix products, arithmetic and copies ran while one was open for 0% of the time, Pallas kernels for 13%

profile of v5, /device:TPU:24, one launch (start us, length us, event | category | flops | bytes accessed | tf_op | source)
XLA Modules:
  0.0 64.8 jit_solution(13726540603182222959)
XLA Ops:
  0.0 1.8 %slabs.1 = (bf16[128,8192]{1,0:T(8,128)(2,1)S(1)}, bf16[8,2048]{1,0:T(8,128)(2,1)S(1)}, bf16[128,2048]{1,0:T(8,128)(2,1)S(1)}, bf16[128,2048]{1,0:T(8,128)(2,1)S(1)}) custom-call(bf16[128,8192]{1,0:T(8,128)(2,1)} %bitcast.12, bf16[8,2048]{1,0:T(8,128)(2,1)} %queries_hbm_ref.1), custom_call_target="tpu_custom_call" | custom-call | tf_op jit(solution)/shard_map/slabs/pallas_call | solution.py:292
  1.8 1.6 %collective-permute-start = (bf16[128,2048]{1,0:T(8,128)(2,1)S(1)}, bf16[128,2048]{1,0:T(8,128)(2,1)S(1)}, u32[]{:S(2)}, u32[]{:S(2)}) collective-permute-start(bf16[128,2048]{1,0:T(8,128)(2,1)S(1)} %get-tuple-element.23), channel_id=1, source_target_pairs={{0,1},{1,2},{2,3},{3,0},{4,5},{5,6},{6,7},{7,4},{8,9},{9,10},{10,1... | collective-permute-start | bytes 1572872 | tf_op jit(solution)/shard_map/ppermute | solution.py:306
  3.4 1.7 %collective-permute-start.1 = (bf16[128,2048]{1,0:T(8,128)(2,1)S(1)}, bf16[128,2048]{1,0:T(8,128)(2,1)S(1)}, u32[]{:S(2)}, u32[]{:S(2)}) collective-permute-start(bf16[128,2048]{1,0:T(8,128)(2,1)S(1)} %get-tuple-element.24), channel_id=1, source_target_pairs={{0,3},{1,0},{2,1},{3,2},{4,7},{5,4},{6,5},{7,6},{8,11},{9,8},{10,9... | collective-permute-start | bytes 1572872 | tf_op jit(solution)/shard_map/ppermute | solution.py:307
  5.2 4.9 %attend.1 = (bf16[4,16,8,128]{3,2,1,0:T(8,128)(2,1)S(1)}, bf16[16,8,64,64]{3,2,1,0:T(8,128)(2,1)S(1)}) custom-call(s32[1,16]{1,0:T(1,128)S(1)} %copy-done.1, s32[128]{0:T(128)S(1)} %copy-done.2, bf16[8,2048]{1,0:T(8,128)(2,1)S(1)} %get-tuple-element.20.queries_ref, bf16[8,1024,128]{2,1,0:T(8,128)(2,1)S(1)} %bitcast.6, bf16[8,1024,128]{2,1,0:T(8,128)(2,1)} %bitcast.11, ...), custom_call_target="tpu_custom_call" | custom-call | tf_op jit(solution)/shard_map/attend/pallas_call | solution.py:309
  10.0 20.2 %all_to_all.15 = bf16[64,8,128]{2,1,0:T(8,128)(2,1)S(1)} all-to-all(bf16[64,8,128]{2,1,0:T(8,128)(2,1)S(1)} %bitcast.8), channel_id=1, replica_groups=mesh['dp'=4,'tensor'=16,'owner'=4] {'owner','tensor'}, dimensions={0} | all-to-all | bytes 262144 | tf_op jit(solution)/shard_map/all_to_all | solution.py:335
  30.2 1.6 %project.1 = (f32[2112,128]{1,0:T(8,128)S(1)}, bf16[2112,128]{1,0:T(8,128)(2,1)S(1)}) custom-call(s32[1,16]{1,0:T(1,128)S(1)} %copy-done.1, s32[128]{0:T(128)S(1)} %copy-done.2, s32[1,128]{1,0:T(1,128)S(1)} %bitcast.9, bf16[4,128,128]{2,1,0:T(8,128)(2,1)S(1)} %bitcast.7, bf16[128,8192]{1,0:T(8,128)(2,1)S(1)} %get-tuple-element.22.w_ref, ...), custom_call_target="tpu_custom_call" | custom-call | tf_op jit(solution)/shard_map/project/pallas_call | solution.py:341
  31.8 0.2 collective-permute-start.2
  32.0 1.8 %collective-permute-done.2.got_ref = bf16[2112,128]{1,0:T(8,128)(2,1)S(1)} collective-permute-done((bf16[2112,128]{1,0:T(8,128)(2,1)S(1)}, bf16[2112,128]{1,0:T(8,128)(2,1)S(1)}, u32[]{:S(2)}, u32[]{:S(2)}) %collective-permute-start.2) | collective-permute-done | bytes 540704 | tf_op jit(solution)/shard_map/ppermute | solution.py:359
  33.8 0.7 %pair.1 = (f32[8,128,128]{2,1,0:T(8,128)S(1)}, bf16[8,128,128]{2,1,0:T(8,128)(2,1)S(1)}, bf16[8,64,128]{2,1,0:T(8,128)(2,1)}) custom-call(f32[2112,128]{1,0:T(8,128)S(1)} %get-tuple-element.26.keep_ref, bf16[2112,128]{1,0:T(8,128)(2,1)S(1)} %collective-permute-done.2.got_ref), custom_call_target="tpu_custom_call" | custom-call | tf_op jit(solution)/shard_map/pair/pallas_call | solution.py:360
  34.5 2.9 %collective-permute-start.3 = (bf16[8,128,128]{2,1,0:T(8,128)(2,1)S(1)}, bf16[8,128,128]{2,1,0:T(8,128)(2,1)S(1)}, u32[]{:S(2)}, u32[]{:S(2)}) collective-permute-start(bf16[8,128,128]{2,1,0:T(8,128)(2,1)S(1)} %get-tuple-element.29), channel_id=1, source_target_pairs={{0,2},{1,3},{2,0},{3,1},{4,6},{5,7},{6,4},{7,5},{8,10},{9,11},{10,... | collective-permute-start | bytes 786440 | tf_op jit(solution)/shard_map/ppermute | solution.py:379
  37.4 3.4 %all-to-all-start.2 = ((bf16[8,64,128]{2,1,0:T(8,128)(2,1)}), bf16[8,64,128]{2,1,0:T(8,128)(2,1)S(1)}, u32[]{:S(2)}, u32[]{:S(2)}) async-start(bf16[8,64,128]{2,1,0:T(8,128)(2,1)} %get-tuple-element.30), calls=%async_computation.2 | async-start | bytes 262144 | tf_op jit(solution)/shard_map/all_to_all | solution.py:375
  40.8 3.6 %collective-permute-done.3.two_ref = bf16[8,128,128]{2,1,0:T(8,128)(2,1)S(1)} collective-permute-done((bf16[8,128,128]{2,1,0:T(8,128)(2,1)S(1)}, bf16[8,128,128]{2,1,0:T(8,128)(2,1)S(1)}, u32[]{:S(2)}, u32[]{:S(2)}) %collective-permute-start.3) | collective-permute-done | bytes 262176 | tf_op jit(solution)/shard_map/ppermute | solution.py:379
  44.4 0.7 %add.1 = bf16[8,128,128]{2,1,0:T(8,128)(2,1)} custom-call(f32[8,128,128]{2,1,0:T(8,128)S(1)} %get-tuple-element.28.one_ref, bf16[8,128,128]{2,1,0:T(8,128)(2,1)S(1)} %collective-permute-done.3.two_ref), custom_call_target="tpu_custom_call" | custom-call | tf_op jit(solution)/shard_map/add/pallas_call | solution.py:400
  45.1 4.9 %all-to-all-done.2.codes_ref = bf16[8,64,128]{2,1,0:T(8,128)(2,1)S(1)} async-done(((bf16[8,64,128]{2,1,0:T(8,128)(2,1)}), bf16[8,64,128]{2,1,0:T(8,128)(2,1)S(1)}, u32[]{:S(2)}, u32[]{:S(2)}) %all-to-all-start.2) | async-done | bytes 131104 | tf_op jit(solution)/shard_map/all_to_all | solution.py:375
  50.1 3.4 %all-to-all-start.1 = ((bf16[8,128,128]{2,1,0:T(8,128)(2,1)}), bf16[8,128,128]{2,1,0:T(8,128)(2,1)S(1)}, u32[]{:S(2)}, u32[]{:S(2)}) async-start(bf16[8,128,128]{2,1,0:T(8,128)(2,1)} %add.1), calls=%async_computation.1 | async-start | bytes 524288 | tf_op jit(solution)/shard_map/all_to_all | solution.py:375
  53.5 2.6 %update.1 = (f32[128,128]{1,0:T(8,128)S(1)}, bf16[128,128]{1,0:T(8,128)(2,1)S(1)}, bf16[128,128]{1,0:T(8,128)(2,1)S(1)}, bf16[128,128]{1,0:T(8,128)(2,1)S(1)}) custom-call(s32[1,16]{1,0:T(1,128)S(1)} %copy-done.1, s32[128]{0:T(128)S(1)} %copy-done.2, s32[1,128]{1,0:T(1,128)S(1)} %bitcast.10, bf16[8,64,128]{2,1,0:T(8,128)(2,1)S(1)} %all-to-all-done.2.codes_ref, ...), custom_call_target="tpu_custom_call" | custom-call | tf_op jit(solution)/shard_map/update/pallas_call | solution.py:382
  56.1 0.1 collective-permute-start.4
  56.2 2.5 %collective-permute-start.5 = (bf16[128,128]{1,0:T(8,128)(2,1)S(1)}, bf16[128,128]{1,0:T(8,128)(2,1)S(1)}, u32[]{:S(2)}, u32[]{:S(2)}) collective-permute-start(bf16[128,128]{1,0:T(8,128)(2,1)S(1)} %get-tuple-element.33), channel_id=1, source_target_pairs={{0,2},{1,3},{2,0},{3,1},{4,6},{5,7},{6,4},{7,5},{8,10},{9,11},{10,... | collective-permute-start | bytes 98312 | tf_op jit(solution)/shard_map/ppermute | solution.py:396
  58.7 1.1 %collective-permute-start.6 = (bf16[128,128]{1,0:T(8,128)(2,1)S(1)}, bf16[128,128]{1,0:T(8,128)(2,1)S(1)}, u32[]{:S(2)}, u32[]{:S(2)}) collective-permute-start(bf16[128,128]{1,0:T(8,128)(2,1)S(1)} %get-tuple-element.34), channel_id=1, source_target_pairs={{0,3},{1,0},{2,1},{3,2},{4,7},{5,4},{6,5},{7,6},{8,11},{9,8},{10,9... | collective-permute-start | bytes 98312 | tf_op jit(solution)/shard_map/ppermute | solution.py:396
  59.7 1.6 %collective-permute-done.4.rest_0_ = bf16[128,128]{1,0:T(8,128)(2,1)S(1)} collective-permute-done((bf16[128,128]{1,0:T(8,128)(2,1)S(1)}, bf16[128,128]{1,0:T(8,128)(2,1)S(1)}, u32[]{:S(2)}, u32[]{:S(2)}) %collective-permute-start.4) | collective-permute-done | bytes 32800 | tf_op jit(solution)/shard_map/ppermute | solution.py:396
  61.3 0.4 collective-permute-done.5.rest_1_
  61.7 0.9 %collective-permute-done.6.rest_2_ = bf16[128,128]{1,0:T(8,128)(2,1)S(1)} collective-permute-done((bf16[128,128]{1,0:T(8,128)(2,1)S(1)}, bf16[128,128]{1,0:T(8,128)(2,1)S(1)}, u32[]{:S(2)}, u32[]{:S(2)}) %collective-permute-start.6) | collective-permute-done | bytes 32800 | tf_op jit(solution)/shard_map/ppermute | solution.py:396
  62.6 1.5 %all-to-all-done.1.parts_ref = bf16[8,128,128]{2,1,0:T(8,128)(2,1)S(1)} async-done(((bf16[8,128,128]{2,1,0:T(8,128)(2,1)}), bf16[8,128,128]{2,1,0:T(8,128)(2,1)S(1)}, u32[]{:S(2)}, u32[]{:S(2)}) %all-to-all-start.1) | async-done | bytes 262176 | tf_op jit(solution)/shard_map/all_to_all | solution.py:375
  64.1 0.7 %final.1 = bf16[128,128]{1,0:T(8,128)(2,1)} custom-call(bf16[8,128,128]{2,1,0:T(8,128)(2,1)S(1)} %all-to-all-done.1.parts_ref, f32[128,128]{1,0:T(8,128)S(1)} %get-tuple-element.31.own_ref, bf16[128,128]{1,0:T(8,128)(2,1)S(1)} %collective-permute-done.4.rest_0_, bf16[128,128]{1,0:T(8,128)(2,1)S(1)} %collective-permute-done.5.rest_1_, ...), custom_call_target="tpu_custom_call" | custom-call | tf_op jit(solution)/shard_map/final/pallas_call | solution.py:409
  (14 shorter events, 0.0 us)
Async XLA Ops:
  0.0 5.1 %copy-start.1 = (s32[1,16]{1,0:T(1,128)S(1)}, s32[1,16]{1,0:T(1,128)}, u32[]{:S(2)}) copy-start(s32[1,16]{1,0:T(1,128)} %group_ref.5) | copy-start | bytes 196
  0.0 5.1 %copy-start.2 = (s32[128]{0:T(128)S(1)}, s32[128]{0:T(128)}, u32[]{:S(2)}) copy-start(s32[128]{0:T(128)} %store_ref.5) | copy-start | bytes 1540
  0.0 5.1 %copy-start.4 = (bf16[8,2,128]{2,1,0:T(2,128)(2,1)S(1)}, bf16[8,2,128]{2,1,0:T(2,128)(2,1)}, u32[]{:S(2)}) copy-start(bf16[8,2,128]{2,1,0:T(2,128)(2,1)} %value_ref.1) | copy-start | bytes 12292
  0.0 5.1 %copy-start.3 = (bf16[8,2,128]{2,1,0:T(2,128)(2,1)S(1)}, bf16[8,2,128]{2,1,0:T(2,128)(2,1)}, u32[]{:S(2)}) copy-start(bf16[8,2,128]{2,1,0:T(2,128)(2,1)} %key_ref.1) | copy-start | bytes 12292
  0.0 5.1 %copy-start = (bf16[8,512,2,128]{3,2,1,0:T(2,128)(2,1)S(1)}, bf16[8,512,2,128]{3,2,1,0:T(2,128)(2,1)}, u32[]{:S(2)}) copy-start(bf16[8,512,2,128]{3,2,1,0:T(2,128)(2,1)} %param.12) | copy-start | bytes 6291460
  1.8 28.4 %collective-permute-start = (bf16[128,2048]{1,0:T(8,128)(2,1)S(1)}, bf16[128,2048]{1,0:T(8,128)(2,1)S(1)}, u32[]{:S(2)}, u32[]{:S(2)}) collective-permute-start(bf16[128,2048]{1,0:T(8,128)(2,1)S(1)} %get-tuple-element.23), channel_id=1, source_target_pairs={{0,1},{1,2},{2,3},{3,0},{4,5},{5,6},{6,7},{7,4},{8,9},{9,10},{10,1... | collective-permute-start | bytes 1572872 | tf_op jit(solution)/shard_map/ppermute | solution.py:306
  3.4 26.9 %collective-permute-start.1 = (bf16[128,2048]{1,0:T(8,128)(2,1)S(1)}, bf16[128,2048]{1,0:T(8,128)(2,1)S(1)}, u32[]{:S(2)}, u32[]{:S(2)}) collective-permute-start(bf16[128,2048]{1,0:T(8,128)(2,1)S(1)} %get-tuple-element.24), channel_id=1, source_target_pairs={{0,3},{1,0},{2,1},{3,2},{4,7},{5,4},{6,5},{7,6},{8,11},{9,8},{10,9... | collective-permute-start | bytes 1572872 | tf_op jit(solution)/shard_map/ppermute | solution.py:307
  5.2 25.1 %copy-start.5 = (s32[128]{0:T(128)S(1)}, s32[128]{0:T(128)}, u32[]{:S(2)}) copy-start(s32[128]{0:T(128)} %param.21) | copy-start | bytes 1540
  31.8 2.0 %collective-permute-start.2 = (bf16[2112,128]{1,0:T(8,128)(2,1)S(1)}, bf16[2112,128]{1,0:T(8,128)(2,1)S(1)}, u32[]{:S(2)}, u32[]{:S(2)}) collective-permute-start(bf16[2112,128]{1,0:T(8,128)(2,1)S(1)} %get-tuple-element.27), channel_id=1, source_target_pairs={{0,4},{4,0},{8,12},{12,8},{16,20},{20,16},{24,28},{28,24},{32,36},... | collective-permute-start | bytes 1622024 | tf_op jit(solution)/shard_map/ppermute | solution.py:359
  34.5 9.9 %collective-permute-start.3 = (bf16[8,128,128]{2,1,0:T(8,128)(2,1)S(1)}, bf16[8,128,128]{2,1,0:T(8,128)(2,1)S(1)}, u32[]{:S(2)}, u32[]{:S(2)}) collective-permute-start(bf16[8,128,128]{2,1,0:T(8,128)(2,1)S(1)} %get-tuple-element.29), channel_id=1, source_target_pairs={{0,2},{1,3},{2,0},{3,1},{4,6},{5,7},{6,4},{7,5},{8,10},{9,11},{10,... | collective-permute-start | bytes 786440 | tf_op jit(solution)/shard_map/ppermute | solution.py:379
  37.4 12.7 %all-to-all-start.2 = ((bf16[8,64,128]{2,1,0:T(8,128)(2,1)}), bf16[8,64,128]{2,1,0:T(8,128)(2,1)S(1)}, u32[]{:S(2)}, u32[]{:S(2)}) async-start(bf16[8,64,128]{2,1,0:T(8,128)(2,1)} %get-tuple-element.30), calls=%async_computation.2 | async-start | bytes 262144 | tf_op jit(solution)/shard_map/all_to_all | solution.py:375
  50.1 14.0 %all-to-all-start.1 = ((bf16[8,128,128]{2,1,0:T(8,128)(2,1)}), bf16[8,128,128]{2,1,0:T(8,128)(2,1)S(1)}, u32[]{:S(2)}, u32[]{:S(2)}) async-start(bf16[8,128,128]{2,1,0:T(8,128)(2,1)} %add.1), calls=%async_computation.1 | async-start | bytes 524288 | tf_op jit(solution)/shard_map/all_to_all | solution.py:375
  56.1 5.2 %collective-permute-start.4 = (bf16[128,128]{1,0:T(8,128)(2,1)S(1)}, bf16[128,128]{1,0:T(8,128)(2,1)S(1)}, u32[]{:S(2)}, u32[]{:S(2)}) collective-permute-start(bf16[128,128]{1,0:T(8,128)(2,1)S(1)} %get-tuple-element.32), channel_id=1, source_target_pairs={{0,1},{1,2},{2,3},{3,0},{4,5},{5,6},{6,7},{7,4},{8,9},{9,10},{10,1... | collective-permute-start | bytes 98312 | tf_op jit(solution)/shard_map/ppermute | solution.py:396
  56.2 5.5 %collective-permute-start.5 = (bf16[128,128]{1,0:T(8,128)(2,1)S(1)}, bf16[128,128]{1,0:T(8,128)(2,1)S(1)}, u32[]{:S(2)}, u32[]{:S(2)}) collective-permute-start(bf16[128,128]{1,0:T(8,128)(2,1)S(1)} %get-tuple-element.33), channel_id=1, source_target_pairs={{0,2},{1,3},{2,0},{3,1},{4,6},{5,7},{6,4},{7,5},{8,10},{9,11},{10,... | collective-permute-start | bytes 98312 | tf_op jit(solution)/shard_map/ppermute | solution.py:396
  58.7 3.9 %collective-permute-start.6 = (bf16[128,128]{1,0:T(8,128)(2,1)S(1)}, bf16[128,128]{1,0:T(8,128)(2,1)S(1)}, u32[]{:S(2)}, u32[]{:S(2)}) collective-permute-start(bf16[128,128]{1,0:T(8,128)(2,1)S(1)} %get-tuple-element.34), channel_id=1, source_target_pairs={{0,3},{1,0},{2,1},{3,2},{4,7},{5,4},{6,5},{7,6},{8,11},{9,8},{10,9... | collective-permute-start | bytes 98312 | tf_op jit(solution)/shard_map/ppermute | solution.py:396

commit v6 on v5

--- a/solution.py
+++ b/solution.py
@@ -70,12 +70,22 @@
     out_ref,
     slots_ref,
     values_ref,
-    value_sem,
+    value_sems,
     sems,
 ):
     stored = down_ref.shape[0]
-    values_copy = pltpu.make_async_copy(values_hbm_ref, values_ref, value_sem)
-    values_copy.start()
+    part = values_ref.shape[1] // 2
+    value_copies = [
+        pltpu.make_async_copy(
+            values_hbm_ref.at[r, pl.ds(i * part, part)],
+            values_ref.at[r, pl.ds(i * part, part)],
+            value_sems.at[2 * r + i],
+        )
+        for r in range(values_ref.shape[0])
+        for i in range(2)
+    ]
+    for copy in value_copies:
+        copy.start()
     copies = []
     for s in range(slots_ref.shape[0]):
         spot, _ = slot_position(s, group_ref, store_ref, stored)
@@ -113,7 +123,8 @@
         denominators.append(jnp.sum(weight, axis=1, keepdims=True) + fresh_weight)
         weights.append(weight.astype(BF16))
         fresh_weights.append(fresh_weight)
-    values_copy.wait()
+    for copy in value_copies:
+        copy.wait()
     mixed = []
     for r in range(rows):
         total = jnp.dot(weights[r], values_ref[r], preferred_element_type=F32)
@@ -214,18 +225,10 @@
     out_ref[...] = (one_ref[...] + two_ref[...].astype(F32)).astype(BF16)
 
 
-def update_kernel(
-    group_ref, store_ref, rows_ref, codes_ref, up_ref, own_ref, *rest
-):
-    send_refs, (ubuf, acc, sems) = rest[:-3], rest[-3:]
-    slots, rank, _ = ubuf.shape
-    stored = up_ref.shape[0]
-    copies = []
-    for s in range(slots):
-        spot, _ = slot_position(s, group_ref, store_ref, stored)
-        copy = pltpu.make_async_copy(up_ref.at[spot], ubuf.at[s], sems.at[s])
-        copy.start()
-        copies.append(copy)
+def update_kernel(group_ref, store_ref, rows_ref, codes_ref, up_ref, own_ref, *rest):
+    send_refs, acc = rest[:-1], rest[-1]
+    slots = group_ref.shape[1]
+    stored, rank, _ = up_ref.shape
     rows, block = own_ref.shape
     owners = lax.axis_size("owner")
     owner = lax.axis_index("owner")
@@ -236,13 +239,12 @@
     ids = row_adapters(rows_ref, rank)
     acc[...] = jnp.zeros_like(acc)
     for s in range(slots):
-        copies[s].wait()
-        _, here = slot_position(s, group_ref, store_ref, stored)
+        spot, here = slot_position(s, group_ref, store_ref, stored)
 
         @pl.when(here)
-        def _(s=s):
+        def _(s=s, spot=spot):
             chosen = jnp.where(ids == group_ref[0, s], code, 0.0).astype(BF16)
-            acc[...] += jnp.dot(chosen, ubuf[s], preferred_element_type=F32)
+            acc[...] += jnp.dot(chosen, up_ref[spot], preferred_element_type=F32)
 
     def columns(target):
         return acc[:, pl.ds(pl.multiple_of(target * block, block), block)]
@@ -300,7 +302,7 @@
         ),
         in_specs=[HBM, HBM],
         out_specs=(VMEM, VMEM, VMEM, VMEM),
-        scratch_shapes=[pltpu.SemaphoreType.DMA((5,))],
+        scratch_shapes=[pltpu.SemaphoreType.DMA((feats // 8 + 1,))],
         compiler_params=LIMIT,
     )(far(output_weight.reshape(feats, columns)), far(queries))
     before = lax.ppermute(right, "owner", [(o, (o + 1) % owners) for o in range(owners)])
@@ -317,7 +319,7 @@
         out_specs=(VMEM, VMEM),
         scratch_shapes=[
             pltpu.VMEM((row_count, cached_value_rows.shape[1] * local_heads, head_width), BF16),
-            pltpu.SemaphoreType.DMA,
+            pltpu.SemaphoreType.DMA((2 * row_count,)),
             pltpu.SemaphoreType.DMA((slots,)),
         ],
         compiler_params=LIMIT,
@@ -383,15 +385,11 @@
         update_kernel,
         name="update",
         out_shape=(pltpu.VMEM((rows, block), F32),) + (strip,) * (owners - 1),
-        in_specs=[SMEM, SMEM] + [VMEM] * 2 + [HBM],
+        in_specs=[SMEM, SMEM] + [VMEM] * 3,
         out_specs=(VMEM,) * owners,
-        scratch_shapes=[
-            pltpu.VMEM((slots,) + adapter_up_weight.shape[1:], BF16),
-            pltpu.VMEM((rows, owners * block), F32),
-            pltpu.SemaphoreType.DMA((slots,)),
-        ],
-        compiler_params=LIMIT,
-    )(adapters_by_group, adapter_store_row, row_ids, near(codes), far(adapter_up_weight))
+        scratch_shapes=[pltpu.VMEM((rows, owners * block), F32)],
+        compiler_params=LIMIT,
+    )(adapters_by_group, adapter_store_row, row_ids, near(codes), near(adapter_up_weight))
     updates = [
         lax.ppermute(update, "owner", [(o, (o + i + 1) % owners) for o in range(owners)])
         for i, update in enumerate(updates)

time: 65.1 us -> 64.8 us (level)
  Pallas kernels: 13 us -> 11.7 us
  waiting for transfers between devices: 14.7 us -> 15.4 us
    pallas_call x1, Pallas kernels: 2.61 us -> 1.19 us  [shards(): pl.pallas_call(update_kernel, name='update', out_shape=(pltpu.VMEM((rows,...]
    ppermute x3, starting transfers between devices: 3.63 us -> 4.32 us  [shards(): lax.ppermute(update, 'owner', [(o, (o + i + 1) % owners) for o in range(o...]
  transfers between devices with their start and end apart: 9 -> 9, of which waited for: 7 -> 7; matrix products, arithmetic and copies ran while one was open for 0% -> 0% of each run, Pallas kernels for 13% -> 10%
where the time goes in v6:
time: 64.8 us; the launch traced here: 64.5 us
  blocking collectives  20.2 us (31%)
  starting transfers between devices  17 us (26%)
  waiting for transfers between devices  15.4 us (24%)
  Pallas kernels  11.7 us (18%)
    all_to_all x1, blocking collectives, shards(): lax.all_to_all(outgoing, ('owner', 'tensor'), split_axis=0, concat_axis=0...  20.2 us
    all_to_all x2, starting transfers between devices, over_z(): lax.all_to_all(pieces, 'tensor', split_axis=0, concat_axis=0, tiled=True,...  6.78 us
    all_to_all x2, waiting for transfers between devices, over_z(): lax.all_to_all(pieces, 'tensor', split_axis=0, concat_axis=0, tiled=True,...  6.58 us
    pallas_call x1, Pallas kernels, shards(): pl.pallas_call(attend_kernel, name='attend', out_shape=(pltpu.VMEM((owner...  4.69 us
    ppermute x3, starting transfers between devices, shards(): lax.ppermute(update, 'owner', [(o, (o + i + 1) % owners) for o in range(o...  4.32 us
    ppermute x1, waiting for transfers between devices, shards(): lax.ppermute(across, 'owner', [(o, (o + 2) % owners) for o in range(owner...  4.09 us
    ppermute x3, waiting for transfers between devices, shards(): lax.ppermute(update, 'owner', [(o, (o + i + 1) % owners) for o in range(o...  2.92 us
    ppermute x1, starting transfers between devices, shards(): lax.ppermute(across, 'owner', [(o, (o + 2) % owners) for o in range(owner...  2.38 us
  transfers between devices with their start and end apart: 9, of which 7 were waited for; matrix products, arithmetic and copies ran while one was open for 0% of the time, Pallas kernels for 10%

profile of v6, /device:TPU:24, one launch (start us, length us, event | category | flops | bytes accessed | tf_op | source)
XLA Modules:
  0.0 64.5 jit_solution(682132984236540768)
XLA Ops:
  0.0 1.9 %slabs.1 = (bf16[128,8192]{1,0:T(8,128)(2,1)S(1)}, bf16[8,2048]{1,0:T(8,128)(2,1)S(1)}, bf16[128,2048]{1,0:T(8,128)(2,1)S(1)}, bf16[128,2048]{1,0:T(8,128)(2,1)S(1)}) custom-call(bf16[128,8192]{1,0:T(8,128)(2,1)} %bitcast.12, bf16[8,2048]{1,0:T(8,128)(2,1)} %queries_hbm_ref.1), custom_call_target="tpu_custom_call" | custom-call | tf_op jit(solution)/shard_map/slabs/pallas_call | solution.py:294
  1.9 1.6 %collective-permute-start = (bf16[128,2048]{1,0:T(8,128)(2,1)S(1)}, bf16[128,2048]{1,0:T(8,128)(2,1)S(1)}, u32[]{:S(2)}, u32[]{:S(2)}) collective-permute-start(bf16[128,2048]{1,0:T(8,128)(2,1)S(1)} %get-tuple-element.23), channel_id=1, source_target_pairs={{0,1},{1,2},{2,3},{3,0},{4,5},{5,6},{6,7},{7,4},{8,9},{9,10},{10,1... | collective-permute-start | bytes 1572872 | tf_op jit(solution)/shard_map/ppermute | solution.py:308
  3.5 1.7 %collective-permute-start.1 = (bf16[128,2048]{1,0:T(8,128)(2,1)S(1)}, bf16[128,2048]{1,0:T(8,128)(2,1)S(1)}, u32[]{:S(2)}, u32[]{:S(2)}) collective-permute-start(bf16[128,2048]{1,0:T(8,128)(2,1)S(1)} %get-tuple-element.24), channel_id=1, source_target_pairs={{0,3},{1,0},{2,1},{3,2},{4,7},{5,4},{6,5},{7,6},{8,11},{9,8},{10,9... | collective-permute-start | bytes 1572872 | tf_op jit(solution)/shard_map/ppermute | solution.py:309
  5.3 4.7 %attend.1 = (bf16[4,16,8,128]{3,2,1,0:T(8,128)(2,1)S(1)}, bf16[16,8,64,64]{3,2,1,0:T(8,128)(2,1)S(1)}) custom-call(s32[1,16]{1,0:T(1,128)S(1)} %copy-done.2, s32[128]{0:T(128)S(1)} %copy-done.3, bf16[8,2048]{1,0:T(8,128)(2,1)S(1)} %get-tuple-element.20.queries_ref, bf16[8,1024,128]{2,1,0:T(8,128)(2,1)S(1)} %bitcast.6, bf16[8,1024,128]{2,1,0:T(8,128)(2,1)} %bitcast.11, ...), custom_call_target="tpu_custom_call" | custom-call | tf_op jit(solution)/shard_map/attend/pallas_call | solution.py:311
  10.0 20.2 %all_to_all.15 = bf16[64,8,128]{2,1,0:T(8,128)(2,1)S(1)} all-to-all(bf16[64,8,128]{2,1,0:T(8,128)(2,1)S(1)} %bitcast.8), channel_id=1, replica_groups=mesh['dp'=4,'tensor'=16,'owner'=4] {'owner','tensor'}, dimensions={0} | all-to-all | bytes 262144 | tf_op jit(solution)/shard_map/all_to_all | solution.py:337
  30.2 1.8 %project.1 = (f32[2112,128]{1,0:T(8,128)S(1)}, bf16[2112,128]{1,0:T(8,128)(2,1)S(1)}) custom-call(s32[1,16]{1,0:T(1,128)S(1)} %copy-done.2, s32[128]{0:T(128)S(1)} %copy-done.3, s32[1,128]{1,0:T(1,128)S(1)} %bitcast.9, bf16[4,128,128]{2,1,0:T(8,128)(2,1)S(1)} %bitcast.7, bf16[128,8192]{1,0:T(8,128)(2,1)S(1)} %get-tuple-element.22.w_ref, ...), custom_call_target="tpu_custom_call" | custom-call | tf_op jit(solution)/shard_map/project/pallas_call | solution.py:343
  32.0 0.2 collective-permute-start.2
  32.2 1.8 %collective-permute-done.2.got_ref = bf16[2112,128]{1,0:T(8,128)(2,1)S(1)} collective-permute-done((bf16[2112,128]{1,0:T(8,128)(2,1)S(1)}, bf16[2112,128]{1,0:T(8,128)(2,1)S(1)}, u32[]{:S(2)}, u32[]{:S(2)}) %collective-permute-start.2) | collective-permute-done | bytes 540704 | tf_op jit(solution)/shard_map/ppermute | solution.py:361
  34.0 0.7 %pair.1 = (f32[8,128,128]{2,1,0:T(8,128)S(1)}, bf16[8,128,128]{2,1,0:T(8,128)(2,1)S(1)}, bf16[8,64,128]{2,1,0:T(8,128)(2,1)}) custom-call(f32[2112,128]{1,0:T(8,128)S(1)} %get-tuple-element.26.keep_ref, bf16[2112,128]{1,0:T(8,128)(2,1)S(1)} %collective-permute-done.2.got_ref), custom_call_target="tpu_custom_call" | custom-call | tf_op jit(solution)/shard_map/pair/pallas_call | solution.py:362
  34.8 2.4 %collective-permute-start.3 = (bf16[8,128,128]{2,1,0:T(8,128)(2,1)S(1)}, bf16[8,128,128]{2,1,0:T(8,128)(2,1)S(1)}, u32[]{:S(2)}, u32[]{:S(2)}) collective-permute-start(bf16[8,128,128]{2,1,0:T(8,128)(2,1)S(1)} %get-tuple-element.29), channel_id=1, source_target_pairs={{0,2},{1,3},{2,0},{3,1},{4,6},{5,7},{6,4},{7,5},{8,10},{9,11},{10,... | collective-permute-start | bytes 786440 | tf_op jit(solution)/shard_map/ppermute | solution.py:381
  37.1 3.4 %all-to-all-start.2 = ((bf16[8,64,128]{2,1,0:T(8,128)(2,1)}), bf16[8,64,128]{2,1,0:T(8,128)(2,1)S(1)}, u32[]{:S(2)}, u32[]{:S(2)}) async-start(bf16[8,64,128]{2,1,0:T(8,128)(2,1)} %get-tuple-element.30), calls=%async_computation.2 | async-start | bytes 262144 | tf_op jit(solution)/shard_map/all_to_all | solution.py:377
  40.5 4.1 %collective-permute-done.3.two_ref = bf16[8,128,128]{2,1,0:T(8,128)(2,1)S(1)} collective-permute-done((bf16[8,128,128]{2,1,0:T(8,128)(2,1)S(1)}, bf16[8,128,128]{2,1,0:T(8,128)(2,1)S(1)}, u32[]{:S(2)}, u32[]{:S(2)}) %collective-permute-start.3) | collective-permute-done | bytes 262176 | tf_op jit(solution)/shard_map/ppermute | solution.py:381
  44.6 0.7 %add.1 = bf16[8,128,128]{2,1,0:T(8,128)(2,1)} custom-call(f32[8,128,128]{2,1,0:T(8,128)S(1)} %get-tuple-element.28.one_ref, bf16[8,128,128]{2,1,0:T(8,128)(2,1)S(1)} %collective-permute-done.3.two_ref), custom_call_target="tpu_custom_call" | custom-call | tf_op jit(solution)/shard_map/add/pallas_call | solution.py:398
  45.4 4.4 %all-to-all-done.2.codes_ref = bf16[8,64,128]{2,1,0:T(8,128)(2,1)S(1)} async-done(((bf16[8,64,128]{2,1,0:T(8,128)(2,1)}), bf16[8,64,128]{2,1,0:T(8,128)(2,1)S(1)}, u32[]{:S(2)}, u32[]{:S(2)}) %all-to-all-start.2) | async-done | bytes 131104 | tf_op jit(solution)/shard_map/all_to_all | solution.py:377
  49.8 3.4 %all-to-all-start.1 = ((bf16[8,128,128]{2,1,0:T(8,128)(2,1)}), bf16[8,128,128]{2,1,0:T(8,128)(2,1)S(1)}, u32[]{:S(2)}, u32[]{:S(2)}) async-start(bf16[8,128,128]{2,1,0:T(8,128)(2,1)} %add.1), calls=%async_computation.1 | async-start | bytes 524288 | tf_op jit(solution)/shard_map/all_to_all | solution.py:377
  53.2 1.2 %update.1 = (f32[128,128]{1,0:T(8,128)S(1)}, bf16[128,128]{1,0:T(8,128)(2,1)S(1)}, bf16[128,128]{1,0:T(8,128)(2,1)S(1)}, bf16[128,128]{1,0:T(8,128)(2,1)S(1)}) custom-call(s32[1,16]{1,0:T(1,128)S(1)} %copy-done.2, s32[128]{0:T(128)S(1)} %copy-done.3, s32[1,128]{1,0:T(1,128)S(1)} %bitcast.10, bf16[8,64,128]{2,1,0:T(8,128)(2,1)S(1)} %all-to-all-done.2.codes_ref, ...), custom_call_target="tpu_custom_call" | custom-call | tf_op jit(solution)/shard_map/update/pallas_call | solution.py:384
  54.4 1.0 %collective-permute-start.4 = (bf16[128,128]{1,0:T(8,128)(2,1)S(1)}, bf16[128,128]{1,0:T(8,128)(2,1)S(1)}, u32[]{:S(2)}, u32[]{:S(2)}) collective-permute-start(bf16[128,128]{1,0:T(8,128)(2,1)S(1)} %get-tuple-element.32), channel_id=1, source_target_pairs={{0,1},{1,2},{2,3},{3,0},{4,5},{5,6},{6,7},{7,4},{8,9},{9,10},{10,1... | collective-permute-start | bytes 98312 | tf_op jit(solution)/shard_map/ppermute | solution.py:394
  55.4 2.4 %collective-permute-start.5 = (bf16[128,128]{1,0:T(8,128)(2,1)S(1)}, bf16[128,128]{1,0:T(8,128)(2,1)S(1)}, u32[]{:S(2)}, u32[]{:S(2)}) collective-permute-start(bf16[128,128]{1,0:T(8,128)(2,1)S(1)} %get-tuple-element.33), channel_id=1, source_target_pairs={{0,2},{1,3},{2,0},{3,1},{4,6},{5,7},{6,4},{7,5},{8,10},{9,11},{10,... | collective-permute-start | bytes 98312 | tf_op jit(solution)/shard_map/ppermute | solution.py:394
  57.7 1.0 %collective-permute-start.6 = (bf16[128,128]{1,0:T(8,128)(2,1)S(1)}, bf16[128,128]{1,0:T(8,128)(2,1)S(1)}, u32[]{:S(2)}, u32[]{:S(2)}) collective-permute-start(bf16[128,128]{1,0:T(8,128)(2,1)S(1)} %get-tuple-element.34), channel_id=1, source_target_pairs={{0,3},{1,0},{2,1},{3,2},{4,7},{5,4},{6,5},{7,6},{8,11},{9,8},{10,9... | collective-permute-start | bytes 98312 | tf_op jit(solution)/shard_map/ppermute | solution.py:394
  58.7 0.9 %collective-permute-done.4.rest_0_ = bf16[128,128]{1,0:T(8,128)(2,1)S(1)} collective-permute-done((bf16[128,128]{1,0:T(8,128)(2,1)S(1)}, bf16[128,128]{1,0:T(8,128)(2,1)S(1)}, u32[]{:S(2)}, u32[]{:S(2)}) %collective-permute-start.4) | collective-permute-done | bytes 32800 | tf_op jit(solution)/shard_map/ppermute | solution.py:394
  59.6 1.2 %collective-permute-done.5.rest_1_ = bf16[128,128]{1,0:T(8,128)(2,1)S(1)} collective-permute-done((bf16[128,128]{1,0:T(8,128)(2,1)S(1)}, bf16[128,128]{1,0:T(8,128)(2,1)S(1)}, u32[]{:S(2)}, u32[]{:S(2)}) %collective-permute-start.5) | collective-permute-done | bytes 32800 | tf_op jit(solution)/shard_map/ppermute | solution.py:394
  60.8 0.9 %collective-permute-done.6.rest_2_ = bf16[128,128]{1,0:T(8,128)(2,1)S(1)} collective-permute-done((bf16[128,128]{1,0:T(8,128)(2,1)S(1)}, bf16[128,128]{1,0:T(8,128)(2,1)S(1)}, u32[]{:S(2)}, u32[]{:S(2)}) %collective-permute-start.6) | collective-permute-done | bytes 32800 | tf_op jit(solution)/shard_map/ppermute | solution.py:394
  61.7 2.1 %all-to-all-done.1.parts_ref = bf16[8,128,128]{2,1,0:T(8,128)(2,1)S(1)} async-done(((bf16[8,128,128]{2,1,0:T(8,128)(2,1)}), bf16[8,128,128]{2,1,0:T(8,128)(2,1)S(1)}, u32[]{:S(2)}, u32[]{:S(2)}) %all-to-all-start.1) | async-done | bytes 262176 | tf_op jit(solution)/shard_map/all_to_all | solution.py:377
  63.8 0.7 %final.1 = bf16[128,128]{1,0:T(8,128)(2,1)} custom-call(bf16[8,128,128]{2,1,0:T(8,128)(2,1)S(1)} %all-to-all-done.1.parts_ref, f32[128,128]{1,0:T(8,128)S(1)} %get-tuple-element.31.own_ref, bf16[128,128]{1,0:T(8,128)(2,1)S(1)} %collective-permute-done.4.rest_0_, bf16[128,128]{1,0:T(8,128)(2,1)S(1)} %collective-permute-done.5.rest_1_, ...), custom_call_target="tpu_custom_call" | custom-call | tf_op jit(solution)/shard_map/final/pallas_call | solution.py:407
  (16 shorter events, 0.0 us)
Async XLA Ops:
  0.0 5.3 %copy-start.2 = (s32[1,16]{1,0:T(1,128)S(1)}, s32[1,16]{1,0:T(1,128)}, u32[]{:S(2)}) copy-start(s32[1,16]{1,0:T(1,128)} %group_ref.5) | copy-start | bytes 196
  0.0 5.3 %copy-start.3 = (s32[128]{0:T(128)S(1)}, s32[128]{0:T(128)}, u32[]{:S(2)}) copy-start(s32[128]{0:T(128)} %store_ref.5) | copy-start | bytes 1540
  0.0 5.3 %copy-start.5 = (bf16[8,2,128]{2,1,0:T(2,128)(2,1)S(1)}, bf16[8,2,128]{2,1,0:T(2,128)(2,1)}, u32[]{:S(2)}) copy-start(bf16[8,2,128]{2,1,0:T(2,128)(2,1)} %value_ref.1) | copy-start | bytes 12292
  0.0 5.3 %copy-start.4 = (bf16[8,2,128]{2,1,0:T(2,128)(2,1)S(1)}, bf16[8,2,128]{2,1,0:T(2,128)(2,1)}, u32[]{:S(2)}) copy-start(bf16[8,2,128]{2,1,0:T(2,128)(2,1)} %key_ref.1) | copy-start | bytes 12292
  0.0 5.3 %copy-start = (bf16[8,512,2,128]{3,2,1,0:T(2,128)(2,1)S(1)}, bf16[8,512,2,128]{3,2,1,0:T(2,128)(2,1)}, u32[]{:S(2)}) copy-start(bf16[8,512,2,128]{3,2,1,0:T(2,128)(2,1)} %param.12) | copy-start | bytes 6291460
  1.9 28.3 %collective-permute-start = (bf16[128,2048]{1,0:T(8,128)(2,1)S(1)}, bf16[128,2048]{1,0:T(8,128)(2,1)S(1)}, u32[]{:S(2)}, u32[]{:S(2)}) collective-permute-start(bf16[128,2048]{1,0:T(8,128)(2,1)S(1)} %get-tuple-element.23), channel_id=1, source_target_pairs={{0,1},{1,2},{2,3},{3,0},{4,5},{5,6},{6,7},{7,4},{8,9},{9,10},{10,1... | collective-permute-start | bytes 1572872 | tf_op jit(solution)/shard_map/ppermute | solution.py:308
  3.5 26.7 %collective-permute-start.1 = (bf16[128,2048]{1,0:T(8,128)(2,1)S(1)}, bf16[128,2048]{1,0:T(8,128)(2,1)S(1)}, u32[]{:S(2)}, u32[]{:S(2)}) collective-permute-start(bf16[128,2048]{1,0:T(8,128)(2,1)S(1)} %get-tuple-element.24), channel_id=1, source_target_pairs={{0,3},{1,0},{2,1},{3,2},{4,7},{5,4},{6,5},{7,6},{8,11},{9,8},{10,9... | collective-permute-start | bytes 1572872 | tf_op jit(solution)/shard_map/ppermute | solution.py:309
  5.3 25.0 %copy-start.6 = (s32[128]{0:T(128)S(1)}, s32[128]{0:T(128)}, u32[]{:S(2)}) copy-start(s32[128]{0:T(128)} %param.21) | copy-start | bytes 1540
  32.0 21.2 %copy-start.1 = (bf16[32,64,512]{2,1,0:T(8,128)(2,1)S(1)}, bf16[32,64,512]{2,1,0:T(8,128)(2,1)}, u32[]{:S(2)}) copy-start(bf16[32,64,512]{2,1,0:T(8,128)(2,1)} %up_ref.1) | copy-start | bytes 6291460
  32.0 2.0 %collective-permute-start.2 = (bf16[2112,128]{1,0:T(8,128)(2,1)S(1)}, bf16[2112,128]{1,0:T(8,128)(2,1)S(1)}, u32[]{:S(2)}, u32[]{:S(2)}) collective-permute-start(bf16[2112,128]{1,0:T(8,128)(2,1)S(1)} %get-tuple-element.27), channel_id=1, source_target_pairs={{0,4},{4,0},{8,12},{12,8},{16,20},{20,16},{24,28},{28,24},{32,36},... | collective-permute-start | bytes 1622024 | tf_op jit(solution)/shard_map/ppermute | solution.py:361
  34.8 9.9 %collective-permute-start.3 = (bf16[8,128,128]{2,1,0:T(8,128)(2,1)S(1)}, bf16[8,128,128]{2,1,0:T(8,128)(2,1)S(1)}, u32[]{:S(2)}, u32[]{:S(2)}) collective-permute-start(bf16[8,128,128]{2,1,0:T(8,128)(2,1)S(1)} %get-tuple-element.29), channel_id=1, source_target_pairs={{0,2},{1,3},{2,0},{3,1},{4,6},{5,7},{6,4},{7,5},{8,10},{9,11},{10,... | collective-permute-start | bytes 786440 | tf_op jit(solution)/shard_map/ppermute | solution.py:381
  37.1 12.7 %all-to-all-start.2 = ((bf16[8,64,128]{2,1,0:T(8,128)(2,1)}), bf16[8,64,128]{2,1,0:T(8,128)(2,1)S(1)}, u32[]{:S(2)}, u32[]{:S(2)}) async-start(bf16[8,64,128]{2,1,0:T(8,128)(2,1)} %get-tuple-element.30), calls=%async_computation.2 | async-start | bytes 262144 | tf_op jit(solution)/shard_map/all_to_all | solution.py:377
  49.8 14.0 %all-to-all-start.1 = ((bf16[8,128,128]{2,1,0:T(8,128)(2,1)}), bf16[8,128,128]{2,1,0:T(8,128)(2,1)S(1)}, u32[]{:S(2)}, u32[]{:S(2)}) async-start(bf16[8,128,128]{2,1,0:T(8,128)(2,1)} %add.1), calls=%async_computation.1 | async-start | bytes 524288 | tf_op jit(solution)/shard_map/all_to_all | solution.py:377
  54.4 5.2 %collective-permute-start.4 = (bf16[128,128]{1,0:T(8,128)(2,1)S(1)}, bf16[128,128]{1,0:T(8,128)(2,1)S(1)}, u32[]{:S(2)}, u32[]{:S(2)}) collective-permute-start(bf16[128,128]{1,0:T(8,128)(2,1)S(1)} %get-tuple-element.32), channel_id=1, source_target_pairs={{0,1},{1,2},{2,3},{3,0},{4,5},{5,6},{6,7},{7,4},{8,9},{9,10},{10,1... | collective-permute-start | bytes 98312 | tf_op jit(solution)/shard_map/ppermute | solution.py:394
  55.4 5.4 %collective-permute-start.5 = (bf16[128,128]{1,0:T(8,128)(2,1)S(1)}, bf16[128,128]{1,0:T(8,128)(2,1)S(1)}, u32[]{:S(2)}, u32[]{:S(2)}) collective-permute-start(bf16[128,128]{1,0:T(8,128)(2,1)S(1)} %get-tuple-element.33), channel_id=1, source_target_pairs={{0,2},{1,3},{2,0},{3,1},{4,6},{5,7},{6,4},{7,5},{8,10},{9,11},{10,... | collective-permute-start | bytes 98312 | tf_op jit(solution)/shard_map/ppermute | solution.py:394
  57.7 3.9 %collective-permute-start.6 = (bf16[128,128]{1,0:T(8,128)(2,1)S(1)}, bf16[128,128]{1,0:T(8,128)(2,1)S(1)}, u32[]{:S(2)}, u32[]{:S(2)}) collective-permute-start(bf16[128,128]{1,0:T(8,128)(2,1)S(1)} %get-tuple-element.34), channel_id=1, source_target_pairs={{0,3},{1,0},{2,1},{3,2},{4,7},{5,4},{6,5},{7,6},{8,11},{9,8},{10,9... | collective-permute-start | bytes 98312 | tf_op jit(solution)/shard_map/ppermute | solution.py:394

commit v7 on v6

--- a/solution.py
+++ b/solution.py
@@ -10,7 +10,6 @@
 F32 = jnp.float32
 
 VMEM = pl.BlockSpec(memory_space=pltpu.VMEM)
-SMEM = pl.BlockSpec(memory_space=pltpu.SMEM)
 HBM = pl.BlockSpec(memory_space=pltpu.HBM)
 LIMIT = pltpu.CompilerParams(vmem_limit_bytes=16 * 1024 * 1024)
 
@@ -24,9 +23,19 @@
 
 
 def slot_position(slot, group_ref, store_ref, stored):
-    spot = store_ref[group_ref[0, slot]] - lax.axis_index("owner") * stored
+    spot = store_ref[0, group_ref[0, slot]] - lax.axis_index("owner") * stored
     here = jnp.logical_and(spot >= 0, spot < stored)
     return jnp.clip(spot, 0, stored - 1), here
+
+
+def index_copies(group_ref, store_ref, group, store, sems):
+    copies = (
+        pltpu.make_async_copy(group_ref, group, sems.at[0]),
+        pltpu.make_async_copy(store_ref, store, sems.at[1]),
+    )
+    for copy in copies:
+        copy.start()
+    return copies
 
 
 def row_adapters(rows_ref, width):
@@ -34,7 +43,18 @@
     return jnp.transpose(jnp.broadcast_to(rows_ref[...], (rows, rows)))[:, :width]
 
 
-def slab_kernel(w_hbm_ref, queries_hbm_ref, w_ref, queries_ref, right_ref, left_ref, sems):
+def slab_kernel(
+    w_hbm_ref,
+    queries_hbm_ref,
+    values_hbm_ref,
+    w_ref,
+    queries_ref,
+    values_ref,
+    right_ref,
+    left_ref,
+    sems,
+    value_sems,
+):
     chunks = sems.shape[0] - 1
     step = w_ref.shape[0] // chunks
     copies = [
@@ -43,8 +63,12 @@
         )
         for i in range(chunks)
     ]
-    copies.append(pltpu.make_async_copy(queries_hbm_ref, queries_ref, sems.at[chunks]))
-    for copy in copies:
+    rest = [pltpu.make_async_copy(queries_hbm_ref, queries_ref, sems.at[chunks])]
+    rest += [
+        pltpu.make_async_copy(values_hbm_ref.at[r], values_ref.at[r], value_sems.at[r])
+        for r in range(values_ref.shape[0])
+    ]
+    for copy in copies + rest:
         copy.start()
     owner, owners = lax.axis_index("owner"), lax.axis_size("owner")
     targets = [lax.rem(owner + 1, owners), lax.rem(owner + owners - 1, owners)]
@@ -55,7 +79,8 @@
             for block in range(out_ref.shape[1] // 128):
                 at = pl.multiple_of((block * owners + target) * 128, 128)
                 out_ref[rows, block * 128 : (block + 1) * 128] = w_ref[rows, pl.ds(at, 128)]
-    copies[chunks].wait()
+    for copy in rest:
+        copy.wait()
 
 
 def attend_kernel(
@@ -63,35 +88,19 @@
     store_ref,
     queries_ref,
     keys_ref,
-    values_hbm_ref,
+    values_ref,
     key_ref,
     value_ref,
     down_ref,
     out_ref,
     slots_ref,
-    values_ref,
-    value_sems,
+    group,
+    store,
+    index_sems,
     sems,
 ):
     stored = down_ref.shape[0]
-    part = values_ref.shape[1] // 2
-    value_copies = [
-        pltpu.make_async_copy(
-            values_hbm_ref.at[r, pl.ds(i * part, part)],
-            values_ref.at[r, pl.ds(i * part, part)],
-            value_sems.at[2 * r + i],
-        )
-        for r in range(values_ref.shape[0])
-        for i in range(2)
-    ]
-    for copy in value_copies:
-        copy.start()
-    copies = []
-    for s in range(slots_ref.shape[0]):
-        spot, _ = slot_position(s, group_ref, store_ref, stored)
-        copies.append(pltpu.make_async_copy(down_ref.at[spot], slots_ref.at[s], sems.at[s]))
-    for copy in copies:
-        copy.start()
+    indices = index_copies(group_ref, store_ref, group, store, index_sems)
 
     rows, local, width = key_ref.shape
     heads = queries_ref.shape[1] // width
@@ -123,8 +132,13 @@
         denominators.append(jnp.sum(weight, axis=1, keepdims=True) + fresh_weight)
         weights.append(weight.astype(BF16))
         fresh_weights.append(fresh_weight)
-    for copy in value_copies:
+    for copy in indices:
         copy.wait()
+    copies = []
+    for s in range(slots_ref.shape[0]):
+        spot, _ = slot_position(s, group, store, stored)
+        copies.append(pltpu.make_async_copy(down_ref.at[spot], slots_ref.at[s], sems.at[s]))
+        copies[s].start()
     mixed = []
     for r in range(rows):
         total = jnp.dot(weights[r], values_ref[r], preferred_element_type=F32)
@@ -160,9 +174,13 @@
     keep_ref,
     send_ref,
     acc,
+    group,
+    store,
+    index_sems,
 ):
+    indices = index_copies(group_ref, store_ref, group, store, index_sems)
     slots, _, _, rank = slots_ref.shape
-    stored = store_ref.shape[0] // lax.axis_size("owner")
+    stored = store_ref.shape[1] // lax.axis_size("owner")
     owners, rows, feats = att_ref.shape
     owner = lax.axis_index("owner")
     mine = att_ref[owner]
@@ -193,14 +211,16 @@
     att = jnp.concatenate([att_ref[o] for o in range(owners)], axis=1)
     ids = row_adapters(rows_ref, rank)
     acc[...] = jnp.zeros_like(acc)
+    for copy in indices:
+        copy.wait()
     for s in range(slots):
-        _, here = slot_position(s, group_ref, store_ref, stored)
+        _, here = slot_position(s, group, store, stored)
 
         @pl.when(here)
         def _(s=s):
             table = slots_ref[s].reshape(owners * feats, rank)
             code = jnp.dot(att, table, preferred_element_type=F32)
-            acc[...] += jnp.where(ids == group_ref[0, s], code, 0.0)
+            acc[...] += jnp.where(ids == group[0, s], code, 0.0)
 
     half = rows // 2
     code = jnp.concatenate([acc[:half, :], acc[half:, :]], axis=1)
@@ -226,8 +246,9 @@
 
 
 def update_kernel(group_ref, store_ref, rows_ref, codes_ref, up_ref, own_ref, *rest):
-    send_refs, acc = rest[:-1], rest[-1]
-    slots = group_ref.shape[1]
+    send_refs, (acc, group, store, index_sems) = rest[:-4], rest[-4:]
+    indices = index_copies(group_ref, store_ref, group, store, index_sems)
+    slots = group.shape[1]
     stored, rank, _ = up_ref.shape
     rows, block = own_ref.shape
     owners = lax.axis_size("owner")
@@ -238,12 +259,14 @@
     code = jnp.concatenate([packed[:, :rank], packed[:, rank:]], axis=0).astype(BF16).astype(F32)
     ids = row_adapters(rows_ref, rank)
     acc[...] = jnp.zeros_like(acc)
+    for copy in indices:
+        copy.wait()
     for s in range(slots):
-        spot, here = slot_position(s, group_ref, store_ref, stored)
+        spot, here = slot_position(s, group, store, stored)
 
         @pl.when(here)
         def _(s=s, spot=spot):
-            chosen = jnp.where(ids == group_ref[0, s], code, 0.0).astype(BF16)
+            chosen = jnp.where(ids == group[0, s], code, 0.0).astype(BF16)
             acc[...] += jnp.dot(chosen, up_ref[spot], preferred_element_type=F32)
 
     def columns(target):
@@ -289,22 +312,37 @@
     block = columns // (tensors * owners)
     rank = adapter_down_weight.shape[-1]
     row_ids = adapter_per_row.reshape(1, rows)
+    group, store = far(adapters_by_group), far(adapter_store_row.reshape(1, -1))
+    indices = [
+        pltpu.SMEM(group.shape, jnp.int32),
+        pltpu.SMEM(store.shape, jnp.int32),
+        pltpu.SemaphoreType.DMA((2,)),
+    ]
 
     slab = pltpu.VMEM((feats, columns // owners), BF16)
-    weight, local_queries, right, left = pl.pallas_call(
+    positions = cached_value_rows.shape[1] * local_heads
+    weight, local_queries, values, right, left = pl.pallas_call(
         slab_kernel,
         name="slabs",
         out_shape=(
             pltpu.VMEM((feats, columns), BF16),
             pltpu.VMEM(queries.shape, BF16),
+            pltpu.VMEM((row_count, positions, head_width), BF16),
             slab,
             slab,
         ),
-        in_specs=[HBM, HBM],
-        out_specs=(VMEM, VMEM, VMEM, VMEM),
-        scratch_shapes=[pltpu.SemaphoreType.DMA((feats // 8 + 1,))],
-        compiler_params=LIMIT,
-    )(far(output_weight.reshape(feats, columns)), far(queries))
+        in_specs=[HBM, HBM, HBM],
+        out_specs=(VMEM,) * 5,
+        scratch_shapes=[
+            pltpu.SemaphoreType.DMA((feats // 16 + 1,)),
+            pltpu.SemaphoreType.DMA((row_count,)),
+        ],
+        compiler_params=LIMIT,
+    )(
+        far(output_weight.reshape(feats, columns)),
+        far(queries),
+        far(cached_value_rows.reshape(row_count, positions, head_width)),
+    )
     before = lax.ppermute(right, "owner", [(o, (o + 1) % owners) for o in range(owners)])
     after = lax.ppermute(left, "owner", [(o, (o - 1) % owners) for o in range(owners)])
 
@@ -315,20 +353,16 @@
             pltpu.VMEM((owners, tensors, row_count, feats), BF16),
             pltpu.VMEM((slots,) + adapter_down_weight.shape[1:], BF16),
         ),
-        in_specs=[SMEM, SMEM, VMEM, VMEM, HBM, VMEM, VMEM, HBM],
+        in_specs=[HBM, HBM] + [VMEM] * 5 + [HBM],
         out_specs=(VMEM, VMEM),
-        scratch_shapes=[
-            pltpu.VMEM((row_count, cached_value_rows.shape[1] * local_heads, head_width), BF16),
-            pltpu.SemaphoreType.DMA((2 * row_count,)),
-            pltpu.SemaphoreType.DMA((slots,)),
-        ],
+        scratch_shapes=indices + [pltpu.SemaphoreType.DMA((slots,))],
         compiler_params=LIMIT,
     )(
-        adapters_by_group,
-        adapter_store_row,
+        group,
+        store,
         near(local_queries),
         near(cached_key_rows.reshape(row_count, -1, head_width)),
-        far(cached_value_rows.reshape(row_count, -1, head_width)),
+        near(values),
         newest_key,
         newest_value,
         far(adapter_down_weight),
@@ -344,13 +378,13 @@
         project_kernel,
         name="project",
         out_shape=(pltpu.VMEM((tall, block), F32), pltpu.VMEM((tall, block), BF16)),
-        in_specs=[SMEM, SMEM] + [VMEM] * 6,
+        in_specs=[HBM, HBM] + [VMEM] * 6,
         out_specs=(VMEM, VMEM),
-        scratch_shapes=[pltpu.VMEM((rows, rank), F32)],
+        scratch_shapes=[pltpu.VMEM((rows, rank), F32)] + indices,
         compiler_params=LIMIT,
     )(
-        adapters_by_group,
-        adapter_store_row,
+        group,
+        store,
         row_ids,
         near(attention),
         near(weight),
@@ -385,11 +419,11 @@
         update_kernel,
         name="update",
         out_shape=(pltpu.VMEM((rows, block), F32),) + (strip,) * (owners - 1),
-        in_specs=[SMEM, SMEM] + [VMEM] * 3,
+        in_specs=[HBM, HBM] + [VMEM] * 3,
         out_specs=(VMEM,) * owners,
-        scratch_shapes=[pltpu.VMEM((rows, owners * block), F32)],
-        compiler_params=LIMIT,
-    )(adapters_by_group, adapter_store_row, row_ids, near(codes), near(adapter_up_weight))
+        scratch_shapes=[pltpu.VMEM((rows, owners * block), F32)] + indices,
+        compiler_params=LIMIT,
+    )(group, store, row_ids, near(codes), near(adapter_up_weight))
     updates = [
         lax.ppermute(update, "owner", [(o, (o + i + 1) % owners) for o in range(owners)])
         for i, update in enumerate(updates)

time: 64.8 us -> 65 us (level)
  Pallas kernels: 11.7 us -> 12.6 us
  starting transfers between devices: 17 us -> 16.2 us
    all_to_all x2, waiting for transfers between devices: 6.58 us -> 5.49 us  [over_z(): lax.all_to_all(pieces, 'tensor', split_axis=0, concat_axis=0, tiled=True,...]
    ppermute x1, waiting for transfers between devices: 4.09 us -> 4.95 us  [shards(): lax.ppermute(across, 'owner', [(o, (o + 2) % owners) for o in range(owner...]
    ppermute x1, starting transfers between devices: 2.38 us -> 1.53 us  [shards(): lax.ppermute(across, 'owner', [(o, (o + 2) % owners) for o in range(owner...]
    pallas_call x1, Pallas kernels: 4.69 us -> 3.97 us  [shards(): pl.pallas_call(attend_kernel, name='attend', out_shape=(pltpu.VMEM((owner...]
where the time goes in v7:
time: 65 us; the launch traced here: 64.5 us
  blocking collectives  20.8 us (32%)
  starting transfers between devices  16.2 us (25%)
  waiting for transfers between devices  14.8 us (23%)
  Pallas kernels  12.6 us (19%)
    all_to_all x1, blocking collectives, shards(): lax.all_to_all(outgoing, ('owner', 'tensor'), split_axis=0, concat_axis=0...  20.8 us
    all_to_all x2, starting transfers between devices, over_z(): lax.all_to_all(pieces, 'tensor', split_axis=0, concat_axis=0, tiled=True,...  6.78 us
    all_to_all x2, waiting for transfers between devices, over_z(): lax.all_to_all(pieces, 'tensor', split_axis=0, concat_axis=0, tiled=True,...  5.49 us
    ppermute x1, waiting for transfers between devices, shards(): lax.ppermute(across, 'owner', [(o, (o + 2) % owners) for o in range(owner...  4.95 us
    ppermute x3, starting transfers between devices, shards(): lax.ppermute(update, 'owner', [(o, (o + i + 1) % owners) for o in range(o...  4.39 us
    pallas_call x1, Pallas kernels, shards(): pl.pallas_call(attend_kernel, name='attend', out_shape=(pltpu.VMEM((owner...  3.97 us
    ppermute x3, waiting for transfers between devices, shards(): lax.ppermute(update, 'owner', [(o, (o + i + 1) % owners) for o in range(o...  2.54 us
    pallas_call x1, Pallas kernels, shards(): pl.pallas_call(slab_kernel, name='slabs', out_shape=(pltpu.VMEM((feats, c...  2.44 us
  transfers between devices with their start and end apart: 9, of which 7 were waited for; matrix products, arithmetic and copies ran while one was open for 0% of the time, Pallas kernels for 10%

profile of v7, /device:TPU:24, one launch (start us, length us, event | category | flops | bytes accessed | tf_op | source)
XLA Modules:
  0.0 64.5 jit_solution(5087067543883140909)
XLA Ops:
  0.0 2.4 %slabs.1 = (bf16[128,8192]{1,0:T(8,128)(2,1)S(1)}, bf16[8,2048]{1,0:T(8,128)(2,1)S(1)}, bf16[8,1024,128]{2,1,0:T(8,128)(2,1)S(1)}, bf16[128,2048]{1,0:T(8,128)(2,1)S(1)}, bf16[128,2048]{1,0:T(8,128)(2,1)S(1)}) custom-call(bf16[128,8192]{1,0:T(8,128)(2,1)} %bitcast.12, bf16[8,2048]{1,0:T(8,128)(2,1)} %queries_hbm_ref.1, bf16[8,1024,128]{2,1,0:T(8,128)(2,1)} %bitcast.13), custom_call_target="tpu_custom_call" | custom-call | tf_op jit(solution)/shard_map/slabs/pallas_call | solution.py:324
  2.5 1.6 %collective-permute-start = (bf16[128,2048]{1,0:T(8,128)(2,1)S(1)}, bf16[128,2048]{1,0:T(8,128)(2,1)S(1)}, u32[]{:S(2)}, u32[]{:S(2)}) collective-permute-start(bf16[128,2048]{1,0:T(8,128)(2,1)S(1)} %get-tuple-element.25), channel_id=1, source_target_pairs={{0,1},{1,2},{2,3},{3,0},{4,5},{5,6},{6,7},{7,4},{8,9},{9,10},{10,1... | collective-permute-start | bytes 1572872 | tf_op jit(solution)/shard_map/ppermute | solution.py:346
  4.0 1.7 %collective-permute-start.1 = (bf16[128,2048]{1,0:T(8,128)(2,1)S(1)}, bf16[128,2048]{1,0:T(8,128)(2,1)S(1)}, u32[]{:S(2)}, u32[]{:S(2)}) collective-permute-start(bf16[128,2048]{1,0:T(8,128)(2,1)S(1)} %get-tuple-element.26), channel_id=1, source_target_pairs={{0,3},{1,0},{2,1},{3,2},{4,7},{5,4},{6,5},{7,6},{8,11},{9,8},{10,9... | collective-permute-start | bytes 1572872 | tf_op jit(solution)/shard_map/ppermute | solution.py:347
  5.8 4.0 %attend.1 = (bf16[4,16,8,128]{3,2,1,0:T(8,128)(2,1)S(1)}, bf16[16,8,64,64]{3,2,1,0:T(8,128)(2,1)S(1)}) custom-call(s32[1,16]{1,0:T(1,128)} %group_ref.5, s32[1,128]{1,0:T(1,128)} %bitcast.14, bf16[8,2048]{1,0:T(8,128)(2,1)S(1)} %get-tuple-element.21.queries_ref, bf16[8,1024,128]{2,1,0:T(8,128)(2,1)S(1)} %bitcast.7, ...), custom_call_target="tpu_custom_call" | custom-call | tf_op jit(solution)/shard_map/attend/pallas_call | solution.py:349
  9.8 20.8 %all_to_all.15 = bf16[64,8,128]{2,1,0:T(8,128)(2,1)S(1)} all-to-all(bf16[64,8,128]{2,1,0:T(8,128)(2,1)S(1)} %bitcast.9), channel_id=1, replica_groups=mesh['dp'=4,'tensor'=16,'owner'=4] {'owner','tensor'}, dimensions={0} | all-to-all | bytes 262144 | tf_op jit(solution)/shard_map/all_to_all | solution.py:371
  30.6 2.3 %project.1 = (f32[2112,128]{1,0:T(8,128)S(1)}, bf16[2112,128]{1,0:T(8,128)(2,1)S(1)}) custom-call(s32[1,16]{1,0:T(1,128)} %group_ref.5, s32[1,128]{1,0:T(1,128)} %bitcast.15, s32[1,128]{1,0:T(1,128)S(1)} %bitcast.10, bf16[4,128,128]{2,1,0:T(8,128)(2,1)S(1)} %bitcast.8, bf16[128,8192]{1,0:T(8,128)(2,1)S(1)} %get-tuple-element.24.w_ref, ...), custom_call_target="tpu_custom_call" | custom-call | tf_op jit(solution)/shard_map/project/pallas_call | solution.py:377
  32.8 0.2 collective-permute-start.2
  33.0 1.8 %collective-permute-done.2.got_ref = bf16[2112,128]{1,0:T(8,128)(2,1)S(1)} collective-permute-done((bf16[2112,128]{1,0:T(8,128)(2,1)S(1)}, bf16[2112,128]{1,0:T(8,128)(2,1)S(1)}, u32[]{:S(2)}, u32[]{:S(2)}) %collective-permute-start.2) | collective-permute-done | bytes 540704 | tf_op jit(solution)/shard_map/ppermute | solution.py:395
  34.9 0.7 %pair.1 = (f32[8,128,128]{2,1,0:T(8,128)S(1)}, bf16[8,128,128]{2,1,0:T(8,128)(2,1)S(1)}, bf16[8,64,128]{2,1,0:T(8,128)(2,1)}) custom-call(f32[2112,128]{1,0:T(8,128)S(1)} %get-tuple-element.28.keep_ref, bf16[2112,128]{1,0:T(8,128)(2,1)S(1)} %collective-permute-done.2.got_ref), custom_call_target="tpu_custom_call" | custom-call | tf_op jit(solution)/shard_map/pair/pallas_call | solution.py:396
  35.6 1.5 %collective-permute-start.3 = (bf16[8,128,128]{2,1,0:T(8,128)(2,1)S(1)}, bf16[8,128,128]{2,1,0:T(8,128)(2,1)S(1)}, u32[]{:S(2)}, u32[]{:S(2)}) collective-permute-start(bf16[8,128,128]{2,1,0:T(8,128)(2,1)S(1)} %get-tuple-element.31), channel_id=1, source_target_pairs={{0,2},{1,3},{2,0},{3,1},{4,6},{5,7},{6,4},{7,5},{8,10},{9,11},{10,... | collective-permute-start | bytes 786440 | tf_op jit(solution)/shard_map/ppermute | solution.py:415
  37.1 3.4 %all-to-all-start.2 = ((bf16[8,64,128]{2,1,0:T(8,128)(2,1)}), bf16[8,64,128]{2,1,0:T(8,128)(2,1)S(1)}, u32[]{:S(2)}, u32[]{:S(2)}) async-start(bf16[8,64,128]{2,1,0:T(8,128)(2,1)} %get-tuple-element.32), calls=%async_computation.2 | async-start | bytes 262144 | tf_op jit(solution)/shard_map/all_to_all | solution.py:411
  40.5 4.9 %collective-permute-done.3.two_ref = bf16[8,128,128]{2,1,0:T(8,128)(2,1)S(1)} collective-permute-done((bf16[8,128,128]{2,1,0:T(8,128)(2,1)S(1)}, bf16[8,128,128]{2,1,0:T(8,128)(2,1)S(1)}, u32[]{:S(2)}, u32[]{:S(2)}) %collective-permute-start.3) | collective-permute-done | bytes 262176 | tf_op jit(solution)/shard_map/ppermute | solution.py:415
  45.5 0.7 %add.1 = bf16[8,128,128]{2,1,0:T(8,128)(2,1)} custom-call(f32[8,128,128]{2,1,0:T(8,128)S(1)} %get-tuple-element.30.one_ref, bf16[8,128,128]{2,1,0:T(8,128)(2,1)S(1)} %collective-permute-done.3.two_ref), custom_call_target="tpu_custom_call" | custom-call | tf_op jit(solution)/shard_map/add/pallas_call | solution.py:432
  46.2 3.6 %all-to-all-done.2.codes_ref = bf16[8,64,128]{2,1,0:T(8,128)(2,1)S(1)} async-done(((bf16[8,64,128]{2,1,0:T(8,128)(2,1)}), bf16[8,64,128]{2,1,0:T(8,128)(2,1)S(1)}, u32[]{:S(2)}, u32[]{:S(2)}) %all-to-all-start.2) | async-done | bytes 131104 | tf_op jit(solution)/shard_map/all_to_all | solution.py:411
  49.8 3.4 %all-to-all-start.1 = ((bf16[8,128,128]{2,1,0:T(8,128)(2,1)}), bf16[8,128,128]{2,1,0:T(8,128)(2,1)S(1)}, u32[]{:S(2)}, u32[]{:S(2)}) async-start(bf16[8,128,128]{2,1,0:T(8,128)(2,1)} %add.1), calls=%async_computation.1 | async-start | bytes 524288 | tf_op jit(solution)/shard_map/all_to_all | solution.py:411
  53.2 1.7 %update.1 = (f32[128,128]{1,0:T(8,128)S(1)}, bf16[128,128]{1,0:T(8,128)(2,1)S(1)}, bf16[128,128]{1,0:T(8,128)(2,1)S(1)}, bf16[128,128]{1,0:T(8,128)(2,1)S(1)}) custom-call(s32[1,16]{1,0:T(1,128)} %group_ref.5, s32[1,128]{1,0:T(1,128)} %bitcast.16, s32[1,128]{1,0:T(1,128)S(1)} %bitcast.11, bf16[8,64,128]{2,1,0:T(8,128)(2,1)S(1)} %all-to-all-done.2.codes_ref, ...), custom_call_target="tpu_custom_call" | custom-call | tf_op jit(solution)/shard_map/update/pallas_call | solution.py:418
  55.0 0.6 collective-permute-start.4
  55.6 2.4 %collective-permute-start.5 = (bf16[128,128]{1,0:T(8,128)(2,1)S(1)}, bf16[128,128]{1,0:T(8,128)(2,1)S(1)}, u32[]{:S(2)}, u32[]{:S(2)}) collective-permute-start(bf16[128,128]{1,0:T(8,128)(2,1)S(1)} %get-tuple-element.35), channel_id=1, source_target_pairs={{0,2},{1,3},{2,0},{3,1},{4,6},{5,7},{6,4},{7,5},{8,10},{9,11},{10,... | collective-permute-start | bytes 98312 | tf_op jit(solution)/shard_map/ppermute | solution.py:428
  58.0 1.4 %collective-permute-start.6 = (bf16[128,128]{1,0:T(8,128)(2,1)S(1)}, bf16[128,128]{1,0:T(8,128)(2,1)S(1)}, u32[]{:S(2)}, u32[]{:S(2)}) collective-permute-start(bf16[128,128]{1,0:T(8,128)(2,1)S(1)} %get-tuple-element.36), channel_id=1, source_target_pairs={{0,3},{1,0},{2,1},{3,2},{4,7},{5,4},{6,5},{7,6},{8,11},{9,8},{10,9... | collective-permute-start | bytes 98312 | tf_op jit(solution)/shard_map/ppermute | solution.py:428
  59.4 0.8 %collective-permute-done.4.rest_0_ = bf16[128,128]{1,0:T(8,128)(2,1)S(1)} collective-permute-done((bf16[128,128]{1,0:T(8,128)(2,1)S(1)}, bf16[128,128]{1,0:T(8,128)(2,1)S(1)}, u32[]{:S(2)}, u32[]{:S(2)}) %collective-permute-start.4) | collective-permute-done | bytes 32800 | tf_op jit(solution)/shard_map/ppermute | solution.py:428
  60.2 0.8 %collective-permute-done.5.rest_1_ = bf16[128,128]{1,0:T(8,128)(2,1)S(1)} collective-permute-done((bf16[128,128]{1,0:T(8,128)(2,1)S(1)}, bf16[128,128]{1,0:T(8,128)(2,1)S(1)}, u32[]{:S(2)}, u32[]{:S(2)}) %collective-permute-start.5) | collective-permute-done | bytes 32800 | tf_op jit(solution)/shard_map/ppermute | solution.py:428
  61.0 0.9 %collective-permute-done.6.rest_2_ = bf16[128,128]{1,0:T(8,128)(2,1)S(1)} collective-permute-done((bf16[128,128]{1,0:T(8,128)(2,1)S(1)}, bf16[128,128]{1,0:T(8,128)(2,1)S(1)}, u32[]{:S(2)}, u32[]{:S(2)}) %collective-permute-start.6) | collective-permute-done | bytes 32800 | tf_op jit(solution)/shard_map/ppermute | solution.py:428
  61.9 1.9 %all-to-all-done.1.parts_ref = bf16[8,128,128]{2,1,0:T(8,128)(2,1)S(1)} async-done(((bf16[8,128,128]{2,1,0:T(8,128)(2,1)}), bf16[8,128,128]{2,1,0:T(8,128)(2,1)S(1)}, u32[]{:S(2)}, u32[]{:S(2)}) %all-to-all-start.1) | async-done | bytes 262176 | tf_op jit(solution)/shard_map/all_to_all | solution.py:411
  63.8 0.7 %final.1 = bf16[128,128]{1,0:T(8,128)(2,1)} custom-call(bf16[8,128,128]{2,1,0:T(8,128)(2,1)S(1)} %all-to-all-done.1.parts_ref, f32[128,128]{1,0:T(8,128)S(1)} %get-tuple-element.33.own_ref, bf16[128,128]{1,0:T(8,128)(2,1)S(1)} %collective-permute-done.4.rest_0_, bf16[128,128]{1,0:T(8,128)(2,1)S(1)} %collective-permute-done.5.rest_1_, ...), custom_call_target="tpu_custom_call" | custom-call | tf_op jit(solution)/shard_map/final/pallas_call | solution.py:441
  (12 shorter events, 0.0 us)
Async XLA Ops:
  0.0 5.8 %copy-start = (bf16[8,512,2,128]{3,2,1,0:T(2,128)(2,1)S(1)}, bf16[8,512,2,128]{3,2,1,0:T(2,128)(2,1)}, u32[]{:S(2)}) copy-start(bf16[8,512,2,128]{3,2,1,0:T(2,128)(2,1)} %param.12) | copy-start | bytes 6291460
  0.0 5.8 %copy-start.2 = (bf16[8,2,128]{2,1,0:T(2,128)(2,1)S(1)}, bf16[8,2,128]{2,1,0:T(2,128)(2,1)}, u32[]{:S(2)}) copy-start(bf16[8,2,128]{2,1,0:T(2,128)(2,1)} %key_ref.1) | copy-start | bytes 12292
  0.0 5.8 %copy-start.3 = (bf16[8,2,128]{2,1,0:T(2,128)(2,1)S(1)}, bf16[8,2,128]{2,1,0:T(2,128)(2,1)}, u32[]{:S(2)}) copy-start(bf16[8,2,128]{2,1,0:T(2,128)(2,1)} %value_ref.1) | copy-start | bytes 12292
  2.5 28.1 %collective-permute-start = (bf16[128,2048]{1,0:T(8,128)(2,1)S(1)}, bf16[128,2048]{1,0:T(8,128)(2,1)S(1)}, u32[]{:S(2)}, u32[]{:S(2)}) collective-permute-start(bf16[128,2048]{1,0:T(8,128)(2,1)S(1)} %get-tuple-element.25), channel_id=1, source_target_pairs={{0,1},{1,2},{2,3},{3,0},{4,5},{5,6},{6,7},{7,4},{8,9},{9,10},{10,1... | collective-permute-start | bytes 1572872 | tf_op jit(solution)/shard_map/ppermute | solution.py:346
  4.0 26.5 %collective-permute-start.1 = (bf16[128,2048]{1,0:T(8,128)(2,1)S(1)}, bf16[128,2048]{1,0:T(8,128)(2,1)S(1)}, u32[]{:S(2)}, u32[]{:S(2)}) collective-permute-start(bf16[128,2048]{1,0:T(8,128)(2,1)S(1)} %get-tuple-element.26), channel_id=1, source_target_pairs={{0,3},{1,0},{2,1},{3,2},{4,7},{5,4},{6,5},{7,6},{8,11},{9,8},{10,9... | collective-permute-start | bytes 1572872 | tf_op jit(solution)/shard_map/ppermute | solution.py:347
  5.8 24.8 %copy-start.4 = (s32[128]{0:T(128)S(1)}, s32[128]{0:T(128)}, u32[]{:S(2)}) copy-start(s32[128]{0:T(128)} %param.21) | copy-start | bytes 1540
  32.8 20.4 %copy-start.1 = (bf16[32,64,512]{2,1,0:T(8,128)(2,1)S(1)}, bf16[32,64,512]{2,1,0:T(8,128)(2,1)}, u32[]{:S(2)}) copy-start(bf16[32,64,512]{2,1,0:T(8,128)(2,1)} %up_ref.1) | copy-start | bytes 6291460
  32.8 2.0 %collective-permute-start.2 = (bf16[2112,128]{1,0:T(8,128)(2,1)S(1)}, bf16[2112,128]{1,0:T(8,128)(2,1)S(1)}, u32[]{:S(2)}, u32[]{:S(2)}) collective-permute-start(bf16[2112,128]{1,0:T(8,128)(2,1)S(1)} %get-tuple-element.29), channel_id=1, source_target_pairs={{0,4},{4,0},{8,12},{12,8},{16,20},{20,16},{24,28},{28,24},{32,36},... | collective-permute-start | bytes 1622024 | tf_op jit(solution)/shard_map/ppermute | solution.py:395
  35.6 9.9 %collective-permute-start.3 = (bf16[8,128,128]{2,1,0:T(8,128)(2,1)S(1)}, bf16[8,128,128]{2,1,0:T(8,128)(2,1)S(1)}, u32[]{:S(2)}, u32[]{:S(2)}) collective-permute-start(bf16[8,128,128]{2,1,0:T(8,128)(2,1)S(1)} %get-tuple-element.31), channel_id=1, source_target_pairs={{0,2},{1,3},{2,0},{3,1},{4,6},{5,7},{6,4},{7,5},{8,10},{9,11},{10,... | collective-permute-start | bytes 786440 | tf_op jit(solution)/shard_map/ppermute | solution.py:415
  37.1 12.7 %all-to-all-start.2 = ((bf16[8,64,128]{2,1,0:T(8,128)(2,1)}), bf16[8,64,128]{2,1,0:T(8,128)(2,1)S(1)}, u32[]{:S(2)}, u32[]{:S(2)}) async-start(bf16[8,64,128]{2,1,0:T(8,128)(2,1)} %get-tuple-element.32), calls=%async_computation.2 | async-start | bytes 262144 | tf_op jit(solution)/shard_map/all_to_all | solution.py:411
  49.8 14.0 %all-to-all-start.1 = ((bf16[8,128,128]{2,1,0:T(8,128)(2,1)}), bf16[8,128,128]{2,1,0:T(8,128)(2,1)S(1)}, u32[]{:S(2)}, u32[]{:S(2)}) async-start(bf16[8,128,128]{2,1,0:T(8,128)(2,1)} %add.1), calls=%async_computation.1 | async-start | bytes 524288 | tf_op jit(solution)/shard_map/all_to_all | solution.py:411
  55.0 5.2 %collective-permute-start.4 = (bf16[128,128]{1,0:T(8,128)(2,1)S(1)}, bf16[128,128]{1,0:T(8,128)(2,1)S(1)}, u32[]{:S(2)}, u32[]{:S(2)}) collective-permute-start(bf16[128,128]{1,0:T(8,128)(2,1)S(1)} %get-tuple-element.34), channel_id=1, source_target_pairs={{0,1},{1,2},{2,3},{3,0},{4,5},{5,6},{6,7},{7,4},{8,9},{9,10},{10,1... | collective-permute-start | bytes 98312 | tf_op jit(solution)/shard_map/ppermute | solution.py:428
  55.6 5.4 %collective-permute-start.5 = (bf16[128,128]{1,0:T(8,128)(2,1)S(1)}, bf16[128,128]{1,0:T(8,128)(2,1)S(1)}, u32[]{:S(2)}, u32[]{:S(2)}) collective-permute-start(bf16[128,128]{1,0:T(8,128)(2,1)S(1)} %get-tuple-element.35), channel_id=1, source_target_pairs={{0,2},{1,3},{2,0},{3,1},{4,6},{5,7},{6,4},{7,5},{8,10},{9,11},{10,... | collective-permute-start | bytes 98312 | tf_op jit(solution)/shard_map/ppermute | solution.py:428
  58.0 3.9 %collective-permute-start.6 = (bf16[128,128]{1,0:T(8,128)(2,1)S(1)}, bf16[128,128]{1,0:T(8,128)(2,1)S(1)}, u32[]{:S(2)}, u32[]{:S(2)}) collective-permute-start(bf16[128,128]{1,0:T(8,128)(2,1)S(1)} %get-tuple-element.36), channel_id=1, source_target_pairs={{0,3},{1,0},{2,1},{3,2},{4,7},{5,4},{6,5},{7,6},{8,11},{9,8},{10,9... | collective-permute-start | bytes 98312 | tf_op jit(solution)/shard_map/ppermute | solution.py:428

commit v8 on v7

--- a/solution.py
+++ b/solution.py
@@ -83,25 +83,7 @@
         copy.wait()
 
 
-def attend_kernel(
-    group_ref,
-    store_ref,
-    queries_ref,
-    keys_ref,
-    values_ref,
-    key_ref,
-    value_ref,
-    down_ref,
-    out_ref,
-    slots_ref,
-    group,
-    store,
-    index_sems,
-    sems,
-):
-    stored = down_ref.shape[0]
-    indices = index_copies(group_ref, store_ref, group, store, index_sems)
-
+def attend_kernel(queries_ref, keys_ref, values_ref, key_ref, value_ref, out_ref):
     rows, local, width = key_ref.shape
     heads = queries_ref.shape[1] // width
     grouped = heads // local
@@ -132,13 +114,6 @@
         denominators.append(jnp.sum(weight, axis=1, keepdims=True) + fresh_weight)
         weights.append(weight.astype(BF16))
         fresh_weights.append(fresh_weight)
-    for copy in indices:
-        copy.wait()
-    copies = []
-    for s in range(slots_ref.shape[0]):
-        spot, _ = slot_position(s, group, store, stored)
-        copies.append(pltpu.make_async_copy(down_ref.at[spot], slots_ref.at[s], sems.at[s]))
-        copies[s].start()
     mixed = []
     for r in range(rows):
         total = jnp.dot(weights[r], values_ref[r], preferred_element_type=F32)
@@ -158,8 +133,6 @@
             part = part.astype(BF16)
             for o in range(out_ref.shape[0]):
                 out_ref[o, 2 * g + i] = part
-    for copy in copies:
-        copy.wait()
 
 
 def project_kernel(
@@ -170,7 +143,7 @@
     w_ref,
     before_ref,
     after_ref,
-    slots_ref,
+    down_ref,
     keep_ref,
     send_ref,
     acc,
@@ -179,8 +152,8 @@
     index_sems,
 ):
     indices = index_copies(group_ref, store_ref, group, store, index_sems)
-    slots, _, _, rank = slots_ref.shape
-    stored = store_ref.shape[1] // lax.axis_size("owner")
+    slots = group.shape[1]
+    stored, _, _, rank = down_ref.shape
     owners, rows, feats = att_ref.shape
     owner = lax.axis_index("owner")
     mine = att_ref[owner]
@@ -214,11 +187,11 @@
     for copy in indices:
         copy.wait()
     for s in range(slots):
-        _, here = slot_position(s, group, store, stored)
+        spot, here = slot_position(s, group, store, stored)
 
         @pl.when(here)
-        def _(s=s):
-            table = slots_ref[s].reshape(owners * feats, rank)
+        def _(s=s, spot=spot):
+            table = down_ref[spot].reshape(owners * feats, rank)
             code = jnp.dot(att, table, preferred_element_type=F32)
             acc[...] += jnp.where(ids == group[0, s], code, 0.0)
 
@@ -346,26 +319,19 @@
     before = lax.ppermute(right, "owner", [(o, (o + 1) % owners) for o in range(owners)])
     after = lax.ppermute(left, "owner", [(o, (o - 1) % owners) for o in range(owners)])
 
-    outgoing, tables = pl.pallas_call(
+    outgoing = pl.pallas_call(
         attend_kernel,
         name="attend",
-        out_shape=(
-            pltpu.VMEM((owners, tensors, row_count, feats), BF16),
-            pltpu.VMEM((slots,) + adapter_down_weight.shape[1:], BF16),
-        ),
-        in_specs=[HBM, HBM] + [VMEM] * 5 + [HBM],
-        out_specs=(VMEM, VMEM),
-        scratch_shapes=indices + [pltpu.SemaphoreType.DMA((slots,))],
+        out_shape=pltpu.VMEM((owners, tensors, row_count, feats), BF16),
+        in_specs=[VMEM] * 5,
+        out_specs=VMEM,
         compiler_params=LIMIT,
     )(
-        group,
-        store,
         near(local_queries),
-        near(cached_key_rows.reshape(row_count, -1, head_width)),
+        near(cached_key_rows.reshape(row_count, positions, head_width)),
         near(values),
         newest_key,
         newest_value,
-        far(adapter_down_weight),
     )
     outgoing = outgoing.reshape(owners * tensors, row_count, feats)
     attention = lax.all_to_all(
@@ -390,7 +356,7 @@
         near(weight),
         near(before),
         near(after),
-        near(tables),
+        near(adapter_down_weight),
     )
     got = lax.ppermute(send, "tensor", [(t, t ^ 1) for t in range(tensors)])
     own_part, across, codes = pl.pallas_call(

time: 65 us -> 62.6 us (0.963)
  Pallas kernels: 12.6 us -> 9.29 us
    pallas_call x1, Pallas kernels: 3.97 us -> 1.03 us  [shards(): pl.pallas_call(attend_kernel, name='attend', out_shape=pltpu.VMEM((owners...]
  transfers between devices with their start and end apart: 9 -> 9, of which waited for: 7 -> 7; matrix products, arithmetic and copies ran while one was open for 0% -> 0% of each run, Pallas kernels for 10% -> 5%
where the time goes in v8:
time: 62.6 us; the launch traced here: 61.7 us
  blocking collectives  21 us (34%)
  starting transfers between devices  16.4 us (26%)
  waiting for transfers between devices  15 us (24%)
  Pallas kernels  9.29 us (15%)
    all_to_all x1, blocking collectives, shards(): lax.all_to_all(outgoing, ('owner', 'tensor'), split_axis=0, concat_axis=0...  21 us
    all_to_all x2, starting transfers between devices, over_z(): lax.all_to_all(pieces, 'tensor', split_axis=0, concat_axis=0, tiled=True,...  6.78 us
    all_to_all x2, waiting for transfers between devices, over_z(): lax.all_to_all(pieces, 'tensor', split_axis=0, concat_axis=0, tiled=True,...  5.53 us
    ppermute x1, waiting for transfers between devices, shards(): lax.ppermute(across, 'owner', [(o, (o + 2) % owners) for o in range(owner...  4.76 us
    ppermute x3, starting transfers between devices, shards(): lax.ppermute(update, 'owner', [(o, (o + i + 1) % owners) for o in range(o...  4.36 us
    ppermute x3, waiting for transfers between devices, shards(): lax.ppermute(update, 'owner', [(o, (o + i + 1) % owners) for o in range(o...  2.87 us
    pallas_call x1, Pallas kernels, shards(): pl.pallas_call(slab_kernel, name='slabs', out_shape=(pltpu.VMEM((feats, c...  2.44 us
    pallas_call x1, Pallas kernels, shards(): pl.pallas_call(project_kernel, name='project', out_shape=(pltpu.VMEM((tal...  2.11 us
  transfers between devices with their start and end apart: 9, of which 7 were waited for; matrix products, arithmetic and copies ran while one was open for 0% of the time, Pallas kernels for 5%

profile of v8, /device:TPU:24, one launch (start us, length us, event | category | flops | bytes accessed | tf_op | source)
XLA Modules:
  0.0 61.7 jit_solution(13128904055601115964)
XLA Ops:
  0.0 2.4 %slabs.1 = (bf16[128,8192]{1,0:T(8,128)(2,1)S(1)}, bf16[8,2048]{1,0:T(8,128)(2,1)S(1)}, bf16[8,1024,128]{2,1,0:T(8,128)(2,1)S(1)}, bf16[128,2048]{1,0:T(8,128)(2,1)S(1)}, bf16[128,2048]{1,0:T(8,128)(2,1)S(1)}) custom-call(bf16[128,8192]{1,0:T(8,128)(2,1)} %bitcast.12, bf16[8,2048]{1,0:T(8,128)(2,1)} %queries_hbm_ref.1, bf16[8,1024,128]{2,1,0:T(8,128)(2,1)} %bitcast.13), custom_call_target="tpu_custom_call" | custom-call | tf_op jit(solution)/shard_map/slabs/pallas_call | solution.py:297
  2.5 1.6 %collective-permute-start = (bf16[128,2048]{1,0:T(8,128)(2,1)S(1)}, bf16[128,2048]{1,0:T(8,128)(2,1)S(1)}, u32[]{:S(2)}, u32[]{:S(2)}) collective-permute-start(bf16[128,2048]{1,0:T(8,128)(2,1)S(1)} %get-tuple-element.22), channel_id=1, source_target_pairs={{0,1},{1,2},{2,3},{3,0},{4,5},{5,6},{6,7},{7,4},{8,9},{9,10},{10,1... | collective-permute-start | bytes 1572872 | tf_op jit(solution)/shard_map/ppermute | solution.py:319
  4.0 1.7 %collective-permute-start.1 = (bf16[128,2048]{1,0:T(8,128)(2,1)S(1)}, bf16[128,2048]{1,0:T(8,128)(2,1)S(1)}, u32[]{:S(2)}, u32[]{:S(2)}) collective-permute-start(bf16[128,2048]{1,0:T(8,128)(2,1)S(1)} %get-tuple-element.23), channel_id=1, source_target_pairs={{0,3},{1,0},{2,1},{3,2},{4,7},{5,4},{6,5},{7,6},{8,11},{9,8},{10,9... | collective-permute-start | bytes 1572872 | tf_op jit(solution)/shard_map/ppermute | solution.py:320
  5.8 1.0 %attend.1 = bf16[4,16,8,128]{3,2,1,0:T(8,128)(2,1)S(1)} custom-call(bf16[8,2048]{1,0:T(8,128)(2,1)S(1)} %get-tuple-element.19.queries_ref, bf16[8,1024,128]{2,1,0:T(8,128)(2,1)S(1)} %bitcast.7, bf16[8,1024,128]{2,1,0:T(8,128)(2,1)S(1)} %get-tuple-element.20.values_ref, bf16[8,2,128]{2,1,0:T(2,128)(2,1)S(1)} %copy-done.3, bf16[8,2,128]{2,1,0:T(2,128)(2,1)S(1)} %copy-done.4), custom_call_target="tpu_custom_call" | custom-call | tf_op jit(solution)/shard_map/attend/pallas_call | solution.py:322
  6.8 21.0 %all_to_all.15 = bf16[64,8,128]{2,1,0:T(8,128)(2,1)S(1)} all-to-all(bf16[64,8,128]{2,1,0:T(8,128)(2,1)S(1)} %bitcast.9), channel_id=1, replica_groups=mesh['dp'=4,'tensor'=16,'owner'=4] {'owner','tensor'}, dimensions={0} | all-to-all | bytes 262144 | tf_op jit(solution)/shard_map/all_to_all | solution.py:337
  27.8 2.1 %project.1 = (f32[2112,128]{1,0:T(8,128)S(1)}, bf16[2112,128]{1,0:T(8,128)(2,1)S(1)}) custom-call(s32[1,16]{1,0:T(1,128)} %group_ref.3, s32[1,128]{1,0:T(1,128)} %bitcast.14, s32[1,128]{1,0:T(1,128)S(1)} %bitcast.10, bf16[4,128,128]{2,1,0:T(8,128)(2,1)S(1)} %bitcast.8, bf16[128,8192]{1,0:T(8,128)(2,1)S(1)} %get-tuple-element.21.w_ref, ...), custom_call_target="tpu_custom_call" | custom-call | tf_op jit(solution)/shard_map/project/pallas_call | solution.py:343
  29.9 0.2 collective-permute-start.2
  30.1 1.8 %collective-permute-done.2.got_ref = bf16[2112,128]{1,0:T(8,128)(2,1)S(1)} collective-permute-done((bf16[2112,128]{1,0:T(8,128)(2,1)S(1)}, bf16[2112,128]{1,0:T(8,128)(2,1)S(1)}, u32[]{:S(2)}, u32[]{:S(2)}) %collective-permute-start.2) | collective-permute-done | bytes 540704 | tf_op jit(solution)/shard_map/ppermute | solution.py:361
  32.0 0.7 %pair.1 = (f32[8,128,128]{2,1,0:T(8,128)S(1)}, bf16[8,128,128]{2,1,0:T(8,128)(2,1)S(1)}, bf16[8,64,128]{2,1,0:T(8,128)(2,1)}) custom-call(f32[2112,128]{1,0:T(8,128)S(1)} %get-tuple-element.24.keep_ref, bf16[2112,128]{1,0:T(8,128)(2,1)S(1)} %collective-permute-done.2.got_ref), custom_call_target="tpu_custom_call" | custom-call | tf_op jit(solution)/shard_map/pair/pallas_call | solution.py:362
  32.7 1.7 %collective-permute-start.3 = (bf16[8,128,128]{2,1,0:T(8,128)(2,1)S(1)}, bf16[8,128,128]{2,1,0:T(8,128)(2,1)S(1)}, u32[]{:S(2)}, u32[]{:S(2)}) collective-permute-start(bf16[8,128,128]{2,1,0:T(8,128)(2,1)S(1)} %get-tuple-element.27), channel_id=1, source_target_pairs={{0,2},{1,3},{2,0},{3,1},{4,6},{5,7},{6,4},{7,5},{8,10},{9,11},{10,... | collective-permute-start | bytes 786440 | tf_op jit(solution)/shard_map/ppermute | solution.py:381
  34.4 3.4 %all-to-all-start.2 = ((bf16[8,64,128]{2,1,0:T(8,128)(2,1)}), bf16[8,64,128]{2,1,0:T(8,128)(2,1)S(1)}, u32[]{:S(2)}, u32[]{:S(2)}) async-start(bf16[8,64,128]{2,1,0:T(8,128)(2,1)} %get-tuple-element.28), calls=%async_computation.2 | async-start | bytes 262144 | tf_op jit(solution)/shard_map/all_to_all | solution.py:377
  37.8 4.8 %collective-permute-done.3.two_ref = bf16[8,128,128]{2,1,0:T(8,128)(2,1)S(1)} collective-permute-done((bf16[8,128,128]{2,1,0:T(8,128)(2,1)S(1)}, bf16[8,128,128]{2,1,0:T(8,128)(2,1)S(1)}, u32[]{:S(2)}, u32[]{:S(2)}) %collective-permute-start.3) | collective-permute-done | bytes 262176 | tf_op jit(solution)/shard_map/ppermute | solution.py:381
  42.5 0.7 %add.1 = bf16[8,128,128]{2,1,0:T(8,128)(2,1)} custom-call(f32[8,128,128]{2,1,0:T(8,128)S(1)} %get-tuple-element.26.one_ref, bf16[8,128,128]{2,1,0:T(8,128)(2,1)S(1)} %collective-permute-done.3.two_ref), custom_call_target="tpu_custom_call" | custom-call | tf_op jit(solution)/shard_map/add/pallas_call | solution.py:398
  43.3 3.8 %all-to-all-done.2.codes_ref = bf16[8,64,128]{2,1,0:T(8,128)(2,1)S(1)} async-done(((bf16[8,64,128]{2,1,0:T(8,128)(2,1)}), bf16[8,64,128]{2,1,0:T(8,128)(2,1)S(1)}, u32[]{:S(2)}, u32[]{:S(2)}) %all-to-all-start.2) | async-done | bytes 131104 | tf_op jit(solution)/shard_map/all_to_all | solution.py:377
  47.1 3.4 %all-to-all-start.1 = ((bf16[8,128,128]{2,1,0:T(8,128)(2,1)}), bf16[8,128,128]{2,1,0:T(8,128)(2,1)S(1)}, u32[]{:S(2)}, u32[]{:S(2)}) async-start(bf16[8,128,128]{2,1,0:T(8,128)(2,1)} %add.1), calls=%async_computation.1 | async-start | bytes 524288 | tf_op jit(solution)/shard_map/all_to_all | solution.py:377
  50.5 1.6 %update.1 = (f32[128,128]{1,0:T(8,128)S(1)}, bf16[128,128]{1,0:T(8,128)(2,1)S(1)}, bf16[128,128]{1,0:T(8,128)(2,1)S(1)}, bf16[128,128]{1,0:T(8,128)(2,1)S(1)}) custom-call(s32[1,16]{1,0:T(1,128)} %group_ref.3, s32[1,128]{1,0:T(1,128)} %bitcast.15, s32[1,128]{1,0:T(1,128)S(1)} %bitcast.11, bf16[8,64,128]{2,1,0:T(8,128)(2,1)S(1)} %all-to-all-done.2.codes_ref, ...), custom_call_target="tpu_custom_call" | custom-call | tf_op jit(solution)/shard_map/update/pallas_call | solution.py:384
  52.1 1.0 %collective-permute-start.4 = (bf16[128,128]{1,0:T(8,128)(2,1)S(1)}, bf16[128,128]{1,0:T(8,128)(2,1)S(1)}, u32[]{:S(2)}, u32[]{:S(2)}) collective-permute-start(bf16[128,128]{1,0:T(8,128)(2,1)S(1)} %get-tuple-element.30), channel_id=1, source_target_pairs={{0,1},{1,2},{2,3},{3,0},{4,5},{5,6},{6,7},{7,4},{8,9},{9,10},{10,1... | collective-permute-start | bytes 98312 | tf_op jit(solution)/shard_map/ppermute | solution.py:394
  53.0 2.4 %collective-permute-start.5 = (bf16[128,128]{1,0:T(8,128)(2,1)S(1)}, bf16[128,128]{1,0:T(8,128)(2,1)S(1)}, u32[]{:S(2)}, u32[]{:S(2)}) collective-permute-start(bf16[128,128]{1,0:T(8,128)(2,1)S(1)} %get-tuple-element.31), channel_id=1, source_target_pairs={{0,2},{1,3},{2,0},{3,1},{4,6},{5,7},{6,4},{7,5},{8,10},{9,11},{10,... | collective-permute-start | bytes 98312 | tf_op jit(solution)/shard_map/ppermute | solution.py:394
  55.4 1.0 %collective-permute-start.6 = (bf16[128,128]{1,0:T(8,128)(2,1)S(1)}, bf16[128,128]{1,0:T(8,128)(2,1)S(1)}, u32[]{:S(2)}, u32[]{:S(2)}) collective-permute-start(bf16[128,128]{1,0:T(8,128)(2,1)S(1)} %get-tuple-element.32), channel_id=1, source_target_pairs={{0,3},{1,0},{2,1},{3,2},{4,7},{5,4},{6,5},{7,6},{8,11},{9,8},{10,9... | collective-permute-start | bytes 98312 | tf_op jit(solution)/shard_map/ppermute | solution.py:394
  56.4 0.8 %collective-permute-done.4.rest_0_ = bf16[128,128]{1,0:T(8,128)(2,1)S(1)} collective-permute-done((bf16[128,128]{1,0:T(8,128)(2,1)S(1)}, bf16[128,128]{1,0:T(8,128)(2,1)S(1)}, u32[]{:S(2)}, u32[]{:S(2)}) %collective-permute-start.4) | collective-permute-done | bytes 32800 | tf_op jit(solution)/shard_map/ppermute | solution.py:394
  57.3 1.2 %collective-permute-done.5.rest_1_ = bf16[128,128]{1,0:T(8,128)(2,1)S(1)} collective-permute-done((bf16[128,128]{1,0:T(8,128)(2,1)S(1)}, bf16[128,128]{1,0:T(8,128)(2,1)S(1)}, u32[]{:S(2)}, u32[]{:S(2)}) %collective-permute-start.5) | collective-permute-done | bytes 32800 | tf_op jit(solution)/shard_map/ppermute | solution.py:394
  58.4 0.9 %collective-permute-done.6.rest_2_ = bf16[128,128]{1,0:T(8,128)(2,1)S(1)} collective-permute-done((bf16[128,128]{1,0:T(8,128)(2,1)S(1)}, bf16[128,128]{1,0:T(8,128)(2,1)S(1)}, u32[]{:S(2)}, u32[]{:S(2)}) %collective-permute-start.6) | collective-permute-done | bytes 32800 | tf_op jit(solution)/shard_map/ppermute | solution.py:394
  59.3 1.8 %all-to-all-done.1.parts_ref = bf16[8,128,128]{2,1,0:T(8,128)(2,1)S(1)} async-done(((bf16[8,128,128]{2,1,0:T(8,128)(2,1)}), bf16[8,128,128]{2,1,0:T(8,128)(2,1)S(1)}, u32[]{:S(2)}, u32[]{:S(2)}) %all-to-all-start.1) | async-done | bytes 262176 | tf_op jit(solution)/shard_map/all_to_all | solution.py:377
  61.1 0.7 %final.1 = bf16[128,128]{1,0:T(8,128)(2,1)} custom-call(bf16[8,128,128]{2,1,0:T(8,128)(2,1)S(1)} %all-to-all-done.1.parts_ref, f32[128,128]{1,0:T(8,128)S(1)} %get-tuple-element.29.own_ref, bf16[128,128]{1,0:T(8,128)(2,1)S(1)} %collective-permute-done.4.rest_0_, bf16[128,128]{1,0:T(8,128)(2,1)S(1)} %collective-permute-done.5.rest_1_, ...), custom_call_target="tpu_custom_call" | custom-call | tf_op jit(solution)/shard_map/final/pallas_call | solution.py:407
  (14 shorter events, 0.0 us)
Async XLA Ops:
  0.0 5.8 %copy-start.1 = (bf16[8,512,2,128]{3,2,1,0:T(2,128)(2,1)S(1)}, bf16[8,512,2,128]{3,2,1,0:T(2,128)(2,1)}, u32[]{:S(2)}) copy-start(bf16[8,512,2,128]{3,2,1,0:T(2,128)(2,1)} %param.12) | copy-start | bytes 6291460
  0.0 5.8 %copy-start.3 = (bf16[8,2,128]{2,1,0:T(2,128)(2,1)S(1)}, bf16[8,2,128]{2,1,0:T(2,128)(2,1)}, u32[]{:S(2)}) copy-start(bf16[8,2,128]{2,1,0:T(2,128)(2,1)} %key_ref.1) | copy-start | bytes 12292
  0.0 5.8 %copy-start.4 = (bf16[8,2,128]{2,1,0:T(2,128)(2,1)S(1)}, bf16[8,2,128]{2,1,0:T(2,128)(2,1)}, u32[]{:S(2)}) copy-start(bf16[8,2,128]{2,1,0:T(2,128)(2,1)} %value_ref.1) | copy-start | bytes 12292
  2.5 25.3 %collective-permute-start = (bf16[128,2048]{1,0:T(8,128)(2,1)S(1)}, bf16[128,2048]{1,0:T(8,128)(2,1)S(1)}, u32[]{:S(2)}, u32[]{:S(2)}) collective-permute-start(bf16[128,2048]{1,0:T(8,128)(2,1)S(1)} %get-tuple-element.22), channel_id=1, source_target_pairs={{0,1},{1,2},{2,3},{3,0},{4,5},{5,6},{6,7},{7,4},{8,9},{9,10},{10,1... | collective-permute-start | bytes 1572872 | tf_op jit(solution)/shard_map/ppermute | solution.py:319
  4.0 23.8 %collective-permute-start.1 = (bf16[128,2048]{1,0:T(8,128)(2,1)S(1)}, bf16[128,2048]{1,0:T(8,128)(2,1)S(1)}, u32[]{:S(2)}, u32[]{:S(2)}) collective-permute-start(bf16[128,2048]{1,0:T(8,128)(2,1)S(1)} %get-tuple-element.23), channel_id=1, source_target_pairs={{0,3},{1,0},{2,1},{3,2},{4,7},{5,4},{6,5},{7,6},{8,11},{9,8},{10,9... | collective-permute-start | bytes 1572872 | tf_op jit(solution)/shard_map/ppermute | solution.py:320
  5.8 22.0 %copy-start = (bf16[32,8,64,64]{3,2,1,0:T(8,128)(2,1)S(1)}, bf16[32,8,64,64]{3,2,1,0:T(8,128)(2,1)}, u32[]{:S(2)}) copy-start(bf16[32,8,64,64]{3,2,1,0:T(8,128)(2,1)} %down_ref.1) | copy-start | bytes 6291460
  5.8 22.0 %copy-start.5 = (s32[128]{0:T(128)S(1)}, s32[128]{0:T(128)}, u32[]{:S(2)}) copy-start(s32[128]{0:T(128)} %param.21) | copy-start | bytes 1540
  29.9 20.5 %copy-start.2 = (bf16[32,64,512]{2,1,0:T(8,128)(2,1)S(1)}, bf16[32,64,512]{2,1,0:T(8,128)(2,1)}, u32[]{:S(2)}) copy-start(bf16[32,64,512]{2,1,0:T(8,128)(2,1)} %up_ref.1) | copy-start | bytes 6291460
  29.9 2.0 %collective-permute-start.2 = (bf16[2112,128]{1,0:T(8,128)(2,1)S(1)}, bf16[2112,128]{1,0:T(8,128)(2,1)S(1)}, u32[]{:S(2)}, u32[]{:S(2)}) collective-permute-start(bf16[2112,128]{1,0:T(8,128)(2,1)S(1)} %get-tuple-element.25), channel_id=1, source_target_pairs={{0,4},{4,0},{8,12},{12,8},{16,20},{20,16},{24,28},{28,24},{32,36},... | collective-permute-start | bytes 1622024 | tf_op jit(solution)/shard_map/ppermute | solution.py:361
  32.7 9.9 %collective-permute-start.3 = (bf16[8,128,128]{2,1,0:T(8,128)(2,1)S(1)}, bf16[8,128,128]{2,1,0:T(8,128)(2,1)S(1)}, u32[]{:S(2)}, u32[]{:S(2)}) collective-permute-start(bf16[8,128,128]{2,1,0:T(8,128)(2,1)S(1)} %get-tuple-element.27), channel_id=1, source_target_pairs={{0,2},{1,3},{2,0},{3,1},{4,6},{5,7},{6,4},{7,5},{8,10},{9,11},{10,... | collective-permute-start | bytes 786440 | tf_op jit(solution)/shard_map/ppermute | solution.py:381
  34.4 12.7 %all-to-all-start.2 = ((bf16[8,64,128]{2,1,0:T(8,128)(2,1)}), bf16[8,64,128]{2,1,0:T(8,128)(2,1)S(1)}, u32[]{:S(2)}, u32[]{:S(2)}) async-start(bf16[8,64,128]{2,1,0:T(8,128)(2,1)} %get-tuple-element.28), calls=%async_computation.2 | async-start | bytes 262144 | tf_op jit(solution)/shard_map/all_to_all | solution.py:377
  47.1 14.0 %all-to-all-start.1 = ((bf16[8,128,128]{2,1,0:T(8,128)(2,1)}), bf16[8,128,128]{2,1,0:T(8,128)(2,1)S(1)}, u32[]{:S(2)}, u32[]{:S(2)}) async-start(bf16[8,128,128]{2,1,0:T(8,128)(2,1)} %add.1), calls=%async_computation.1 | async-start | bytes 524288 | tf_op jit(solution)/shard_map/all_to_all | solution.py:377
  52.1 5.2 %collective-permute-start.4 = (bf16[128,128]{1,0:T(8,128)(2,1)S(1)}, bf16[128,128]{1,0:T(8,128)(2,1)S(1)}, u32[]{:S(2)}, u32[]{:S(2)}) collective-permute-start(bf16[128,128]{1,0:T(8,128)(2,1)S(1)} %get-tuple-element.30), channel_id=1, source_target_pairs={{0,1},{1,2},{2,3},{3,0},{4,5},{5,6},{6,7},{7,4},{8,9},{9,10},{10,1... | collective-permute-start | bytes 98312 | tf_op jit(solution)/shard_map/ppermute | solution.py:394
  53.0 5.4 %collective-permute-start.5 = (bf16[128,128]{1,0:T(8,128)(2,1)S(1)}, bf16[128,128]{1,0:T(8,128)(2,1)S(1)}, u32[]{:S(2)}, u32[]{:S(2)}) collective-permute-start(bf16[128,128]{1,0:T(8,128)(2,1)S(1)} %get-tuple-element.31), channel_id=1, source_target_pairs={{0,2},{1,3},{2,0},{3,1},{4,6},{5,7},{6,4},{7,5},{8,10},{9,11},{10,... | collective-permute-start | bytes 98312 | tf_op jit(solution)/shard_map/ppermute | solution.py:394
  55.4 3.9 %collective-permute-start.6 = (bf16[128,128]{1,0:T(8,128)(2,1)S(1)}, bf16[128,128]{1,0:T(8,128)(2,1)S(1)}, u32[]{:S(2)}, u32[]{:S(2)}) collective-permute-start(bf16[128,128]{1,0:T(8,128)(2,1)S(1)} %get-tuple-element.32), channel_id=1, source_target_pairs={{0,3},{1,0},{2,1},{3,2},{4,7},{5,4},{6,5},{7,6},{8,11},{9,8},{10,9... | collective-permute-start | bytes 98312 | tf_op jit(solution)/shard_map/ppermute | solution.py:394

commit v9 on v8

--- a/solution.py
+++ b/solution.py
@@ -136,51 +136,64 @@
 
 
 def project_kernel(
-    group_ref,
-    store_ref,
-    rows_ref,
+    order_ref,
     att_ref,
     w_ref,
     before_ref,
     after_ref,
+    own_ref,
+    send_own_ref,
+    across_ref,
+    send_across_ref,
+):
+    del order_ref
+    owners, rows, _ = att_ref.shape
+    owner = lax.axis_index("owner")
+    mine = att_ref[owner]
+    beside = jnp.concatenate(
+        [att_ref[lax.rem(owner + owners - 1, owners)], att_ref[lax.rem(owner + 1, owners)]], axis=1
+    )
+    first = lax.rem(lax.axis_index("tensor"), 2) == 0
+    planes, _, block = own_ref.shape
+    opposite = lax.rem(owner + 2, owners)
+
+    def columns(z, target):
+        at = [pl.multiple_of(((2 * z + c) * owners + target) * block, block) for c in range(2)]
+        return jnp.concatenate([w_ref[:, pl.ds(a, block)] for a in at], axis=1)
+
+    for z in range(planes):
+        span = pl.ds(z * 2 * block, 2 * block)
+        near_rows = jnp.concatenate([before_ref[:, span], after_ref[:, span]], axis=0)
+        here = jnp.dot(beside, near_rows, preferred_element_type=F32)
+        here = here + jnp.dot(mine, columns(z, owner), preferred_element_type=F32)
+        there = jnp.dot(mine, columns(z, opposite), preferred_element_type=F32)
+        for part, keep, send in (
+            (here, own_ref, send_own_ref),
+            (there, across_ref, send_across_ref),
+        ):
+            even, odd = part[:, :block], part[:, block:]
+            keep[z] = jnp.where(first, even, odd)
+            send[z] = jnp.where(first, odd, even).astype(BF16)
+
+
+def rank_kernel(
+    group_ref,
+    store_ref,
+    rows_ref,
+    order_ref,
+    att_ref,
     down_ref,
-    keep_ref,
-    send_ref,
+    codes_ref,
     acc,
     group,
     store,
     index_sems,
 ):
+    del order_ref
     indices = index_copies(group_ref, store_ref, group, store, index_sems)
     slots = group.shape[1]
     stored, _, _, rank = down_ref.shape
     owners, rows, feats = att_ref.shape
-    owner = lax.axis_index("owner")
-    mine = att_ref[owner]
-    beside = jnp.concatenate(
-        [att_ref[lax.rem(owner + owners - 1, owners)], att_ref[lax.rem(owner + 1, owners)]], axis=1
-    )
-    first = lax.rem(lax.axis_index("tensor"), 2) == 0
-    block = keep_ref.shape[1]
-    planes = before_ref.shape[1] // (2 * block)
-
-    across = lax.rem(owner + 2, owners)
-
-    def columns(z, target):
-        at = [pl.multiple_of(((2 * z + c) * owners + target) * block, block) for c in range(2)]
-        return jnp.concatenate([w_ref[:, pl.ds(a, block)] for a in at], axis=1)
-
-    for z in range(planes):
-        span = pl.ds(z * 2 * block, 2 * block)
-        near_rows = jnp.concatenate([before_ref[:, span], after_ref[:, span]], axis=0)
-        here = jnp.dot(beside, near_rows, preferred_element_type=F32)
-        here = here + jnp.dot(mine, columns(z, owner), preferred_element_type=F32)
-        there = jnp.dot(mine, columns(z, across), preferred_element_type=F32)
-        for i, part in enumerate((here, there)):
-            even, odd = part[:, :block], part[:, block:]
-            rows_span = pl.ds((2 * z + i) * rows, rows)
-            keep_ref[rows_span, :] = jnp.where(first, even, odd)
-            send_ref[rows_span, :] = jnp.where(first, odd, even).astype(BF16)
     att = jnp.concatenate([att_ref[o] for o in range(owners)], axis=1)
     ids = row_adapters(rows_ref, rank)
     acc[...] = jnp.zeros_like(acc)
@@ -196,29 +209,24 @@
             acc[...] += jnp.where(ids == group[0, s], code, 0.0)
 
     half = rows // 2
-    code = jnp.concatenate([acc[:half, :], acc[half:, :]], axis=1)
-    keep_ref[2 * planes * rows :, :] = code
-    send_ref[2 * planes * rows :, :] = code.astype(BF16)
-
-
-def pair_kernel(keep_ref, got_ref, own_ref, across_ref, codes_ref):
-    planes, rows, _ = own_ref.shape
-    for z in range(planes):
-        span = pl.ds(2 * z * rows, rows)
-        own_ref[z] = keep_ref[span, :] + got_ref[span, :].astype(F32)
-        span = pl.ds((2 * z + 1) * rows, rows)
-        across_ref[z] = (keep_ref[span, :] + got_ref[span, :].astype(F32)).astype(BF16)
-    span = pl.ds(2 * planes * rows, codes_ref.shape[1])
-    code = (keep_ref[span, :] + got_ref[span, :].astype(F32)).astype(BF16)
-    for z in range(planes):
+    code = jnp.concatenate([acc[:half, :], acc[half:, :]], axis=1).astype(BF16)
+    for z in range(codes_ref.shape[0]):
         codes_ref[z] = code
 
 
-def add_kernel(one_ref, two_ref, out_ref):
-    out_ref[...] = (one_ref[...] + two_ref[...].astype(F32)).astype(BF16)
-
-
-def update_kernel(group_ref, store_ref, rows_ref, codes_ref, up_ref, own_ref, *rest):
+def pair_kernel(order_ref, keep_ref, got_ref, out_ref):
+    del order_ref
+    out_ref[...] = (keep_ref[...] + got_ref[...].astype(F32)).astype(BF16)
+
+
+def add_kernel(keep_ref, got_ref, across_ref, out_ref):
+    total = keep_ref[...] + got_ref[...].astype(F32) + across_ref[...].astype(F32)
+    out_ref[...] = total.astype(BF16)
+
+
+def update_kernel(
+    group_ref, store_ref, rows_ref, codes_ref, others_ref, up_ref, own_ref, *rest
+):
     send_refs, (acc, group, store, index_sems) = rest[:-4], rest[-4:]
     indices = index_copies(group_ref, store_ref, group, store, index_sems)
     slots = group.shape[1]
@@ -226,9 +234,9 @@
     rows, block = own_ref.shape
     owners = lax.axis_size("owner")
     owner = lax.axis_index("owner")
-    packed = codes_ref[0].astype(F32)
+    packed = codes_ref[0].astype(F32) + others_ref[0].astype(F32)
     for z in range(1, codes_ref.shape[0]):
-        packed = packed + codes_ref[z].astype(F32)
+        packed = packed + codes_ref[z].astype(F32) + others_ref[z].astype(F32)
     code = jnp.concatenate([packed[:, :rank], packed[:, rank:]], axis=0).astype(BF16).astype(F32)
     ids = row_adapters(rows_ref, rank)
     acc[...] = jnp.zeros_like(acc)
@@ -339,38 +347,38 @@
     )
     attention = attention.reshape(owners, rows, feats)
 
-    tall = 2 * planes * rows + rows // 2
-    keep, send = pl.pallas_call(
+    attention, down = near(attention), near(adapter_down_weight)
+    swap = [(t, t ^ 1) for t in range(tensors)]
+    kept, sent = pltpu.VMEM((planes, rows, block), F32), pltpu.VMEM((planes, rows, block), BF16)
+    own_part, send_own, across_part, send_across = pl.pallas_call(
         project_kernel,
         name="project",
-        out_shape=(pltpu.VMEM((tall, block), F32), pltpu.VMEM((tall, block), BF16)),
-        in_specs=[HBM, HBM] + [VMEM] * 6,
-        out_specs=(VMEM, VMEM),
+        out_shape=(kept, sent, kept, sent),
+        in_specs=[VMEM] * 5,
+        out_specs=(VMEM,) * 4,
+        compiler_params=LIMIT,
+    )(down, attention, near(weight), near(before), near(after))
+    got_across = lax.ppermute(send_across, "tensor", swap)
+    codes = pl.pallas_call(
+        rank_kernel,
+        name="rank",
+        out_shape=pltpu.VMEM((planes, rows // 2, 2 * rank), BF16),
+        in_specs=[HBM, HBM] + [VMEM] * 4,
+        out_specs=VMEM,
         scratch_shapes=[pltpu.VMEM((rows, rank), F32)] + indices,
         compiler_params=LIMIT,
-    )(
-        group,
-        store,
-        row_ids,
-        near(attention),
-        near(weight),
-        near(before),
-        near(after),
-        near(adapter_down_weight),
-    )
-    got = lax.ppermute(send, "tensor", [(t, t ^ 1) for t in range(tensors)])
-    own_part, across, codes = pl.pallas_call(
+    )(group, store, row_ids, near(send_across), attention, down)
+    across = pl.pallas_call(
         pair_kernel,
         name="pair",
-        out_shape=(
-            pltpu.VMEM((planes, rows, block), F32),
-            pltpu.VMEM((planes, rows, block), BF16),
-            pltpu.VMEM((planes, rows // 2, 2 * rank), BF16),
-        ),
-        in_specs=[VMEM, VMEM],
-        out_specs=(VMEM, VMEM, VMEM),
-        compiler_params=LIMIT,
-    )(near(keep), near(got))
+        out_shape=sent,
+        in_specs=[HBM, VMEM, VMEM],
+        out_specs=VMEM,
+        compiler_params=LIMIT,
+    )(codes, near(across_part), near(got_across))
+    across, send_own = lax.optimization_barrier((across, send_own))
+    across = lax.ppermute(across, "owner", [(o, (o + 2) % owners) for o in range(owners)])
+    got_own = lax.ppermute(send_own, "tensor", swap)
     groups = [[2 * z + c for z in range(planes)] for c in range(2)]
 
     def over_z(pieces):
@@ -378,18 +386,18 @@
             pieces, "tensor", split_axis=0, concat_axis=0, tiled=True, axis_index_groups=groups
         )
 
-    across = lax.ppermute(across, "owner", [(o, (o + 2) % owners) for o in range(owners)])
     codes = over_z(codes)
+    other_codes = lax.ppermute(codes, "tensor", swap)
     strip = pltpu.VMEM((rows, block), BF16)
     own_update, *updates = pl.pallas_call(
         update_kernel,
         name="update",
         out_shape=(pltpu.VMEM((rows, block), F32),) + (strip,) * (owners - 1),
-        in_specs=[HBM, HBM] + [VMEM] * 3,
+        in_specs=[HBM, HBM] + [VMEM] * 4,
         out_specs=(VMEM,) * owners,
         scratch_shapes=[pltpu.VMEM((rows, owners * block), F32)] + indices,
         compiler_params=LIMIT,
-    )(group, store, row_ids, near(codes), near(adapter_up_weight))
+    )(group, store, row_ids, near(codes), near(other_codes), near(adapter_up_weight))
     updates = [
         lax.ppermute(update, "owner", [(o, (o + i + 1) % owners) for o in range(owners)])
         for i, update in enumerate(updates)
@@ -399,10 +407,10 @@
             add_kernel,
             name="add",
             out_shape=pltpu.VMEM((planes, rows, block), BF16),
-            in_specs=[VMEM, VMEM],
+            in_specs=[VMEM] * 3,
             out_specs=VMEM,
             compiler_params=LIMIT,
-        )(near(own_part), near(across))
+        )(near(own_part), near(got_own), near(across))
     )
     return pl.pallas_call(
         final_kernel,

time: 62.6 us -> 61.8 us (0.987)
  waiting for transfers between devices: 15 us -> 13.4 us
  starting transfers between devices: 16.4 us -> 17.5 us
    all_to_all x2, waiting for transfers between devices: 5.53 us -> 3.74 us  [over_z(): lax.all_to_all(pieces, 'tensor', split_axis=0, concat_axis=0, tiled=True,...]
    ppermute x3, waiting for transfers between devices: 2.87 us -> 3.6 us  [shards(): lax.ppermute(update, 'owner', [(o, (o + i + 1) % owners) for o in range(o...]
    pallas_call x2 -> x3, Pallas kernels: 2.84 us -> 3.34 us  [the longest x1 1.97 us: shards(): pl.pallas_call(rank_kernel, name='rank', out_shape=pltpu.VMEM((planes, ro...]
    ppermute x1 -> x3, waiting for transfers between devices: 1.82 us -> 1.34 us  [the longest x1 1.33 us: shards(): other_codes = lax.ppermute(codes, 'tensor', swap)]
  transfers between devices with their start and end apart: 9 -> 11, of which waited for: 7 -> 6; matrix products, arithmetic and copies ran while one was open for 0% -> 0% of each run, Pallas kernels for 5% -> 8%
where the time goes in v9:
time: 61.8 us; the launch traced here: 61.5 us
  blocking collectives  21 us (34%)
  starting transfers between devices  17.5 us (28%)
  waiting for transfers between devices  13.4 us (22%)
  Pallas kernels  9.5 us (15%)
    all_to_all x1, blocking collectives, shards(): lax.all_to_all(outgoing, ('owner', 'tensor'), split_axis=0, concat_axis=0...  21 us
    all_to_all x2, starting transfers between devices, over_z(): lax.all_to_all(pieces, 'tensor', split_axis=0, concat_axis=0, tiled=True,...  6.78 us
    ppermute x3, starting transfers between devices, shards(): lax.ppermute(update, 'owner', [(o, (o + i + 1) % owners) for o in range(o...  4.98 us
    ppermute x1, waiting for transfers between devices, shards(): lax.ppermute(across, 'owner', [(o, (o + 2) % owners) for o in range(owner...  4.73 us
    all_to_all x2, waiting for transfers between devices, over_z(): lax.all_to_all(pieces, 'tensor', split_axis=0, concat_axis=0, tiled=True,...  3.74 us
    ppermute x3, waiting for transfers between devices, shards(): lax.ppermute(update, 'owner', [(o, (o + i + 1) % owners) for o in range(o...  3.6 us
    pallas_call x1, Pallas kernels, shards(): pl.pallas_call(slab_kernel, name='slabs', out_shape=(pltpu.VMEM((feats, c...  2.44 us
    pallas_call x1, Pallas kernels, shards(): pl.pallas_call(rank_kernel, name='rank', out_shape=pltpu.VMEM((planes, ro...  1.97 us
  transfers between devices with their start and end apart: 11, of which 6 were waited for; matrix products, arithmetic and copies ran while one was open for 0% of the time, Pallas kernels for 8%

profile of v9, /device:TPU:24, one launch (start us, length us, event | category | flops | bytes accessed | tf_op | source)
XLA Modules:
  0.0 61.5 jit_solution(1113018805006560360)
XLA Ops:
  0.0 2.4 %slabs.1 = (bf16[128,8192]{1,0:T(8,128)(2,1)S(1)}, bf16[8,2048]{1,0:T(8,128)(2,1)S(1)}, bf16[8,1024,128]{2,1,0:T(8,128)(2,1)S(1)}, bf16[128,2048]{1,0:T(8,128)(2,1)S(1)}, bf16[128,2048]{1,0:T(8,128)(2,1)S(1)}) custom-call(bf16[128,8192]{1,0:T(8,128)(2,1)} %bitcast.13, bf16[8,2048]{1,0:T(8,128)(2,1)} %queries_hbm_ref.1, bf16[8,1024,128]{2,1,0:T(8,128)(2,1)} %bitcast.14), custom_call_target="tpu_custom_call" | custom-call | tf_op jit(solution)/shard_map/slabs/pallas_call | solution.py:305
  2.5 1.6 %collective-permute-start = (bf16[128,2048]{1,0:T(8,128)(2,1)S(1)}, bf16[128,2048]{1,0:T(8,128)(2,1)S(1)}, u32[]{:S(2)}, u32[]{:S(2)}) collective-permute-start(bf16[128,2048]{1,0:T(8,128)(2,1)S(1)} %get-tuple-element.23), channel_id=1, source_target_pairs={{0,1},{1,2},{2,3},{3,0},{4,5},{5,6},{6,7},{7,4},{8,9},{9,10},{10,1... | collective-permute-start | bytes 1572872 | tf_op jit(solution)/shard_map/ppermute | solution.py:327
  4.0 1.7 %collective-permute-start.1 = (bf16[128,2048]{1,0:T(8,128)(2,1)S(1)}, bf16[128,2048]{1,0:T(8,128)(2,1)S(1)}, u32[]{:S(2)}, u32[]{:S(2)}) collective-permute-start(bf16[128,2048]{1,0:T(8,128)(2,1)S(1)} %get-tuple-element.24), channel_id=1, source_target_pairs={{0,3},{1,0},{2,1},{3,2},{4,7},{5,4},{6,5},{7,6},{8,11},{9,8},{10,9... | collective-permute-start | bytes 1572872 | tf_op jit(solution)/shard_map/ppermute | solution.py:328
  5.8 1.0 %attend.1 = bf16[4,16,8,128]{3,2,1,0:T(8,128)(2,1)S(1)} custom-call(bf16[8,2048]{1,0:T(8,128)(2,1)S(1)} %get-tuple-element.20.queries_ref, bf16[8,1024,128]{2,1,0:T(8,128)(2,1)S(1)} %bitcast.7, bf16[8,1024,128]{2,1,0:T(8,128)(2,1)S(1)} %get-tuple-element.21.values_ref, bf16[8,2,128]{2,1,0:T(2,128)(2,1)S(1)} %copy-done.3, bf16[8,2,128]{2,1,0:T(2,128)(2,1)S(1)} %copy-done.4), custom_call_target="tpu_custom_call" | custom-call | tf_op jit(solution)/shard_map/attend/pallas_call | solution.py:330
  6.8 21.0 %all_to_all.15 = bf16[64,8,128]{2,1,0:T(8,128)(2,1)S(1)} all-to-all(bf16[64,8,128]{2,1,0:T(8,128)(2,1)S(1)} %bitcast.10), channel_id=1, replica_groups=mesh['dp'=4,'tensor'=16,'owner'=4] {'owner','tensor'}, dimensions={0} | all-to-all | bytes 262144 | tf_op jit(solution)/shard_map/all_to_all | solution.py:345
  27.8 1.3 %project.1 = (f32[8,128,128]{2,1,0:T(8,128)S(1)}, bf16[8,128,128]{2,1,0:T(8,128)(2,1)}, f32[8,128,128]{2,1,0:T(8,128)S(1)}, bf16[8,128,128]{2,1,0:T(8,128)(2,1)S(1)}) custom-call(bf16[32,8,64,64]{3,2,1,0:T(8,128)(2,1)S(1)} %copy-done, bf16[4,128,128]{2,1,0:T(8,128)(2,1)S(1)} %bitcast.8, bf16[128,8192]{1,0:T(8,128)(2,1)S(1)} %get-tuple-element.22.w_ref, ...), custom_call_target="tpu_custom_call" | custom-call | tf_op jit(solution)/shard_map/project/pallas_call | solution.py:353
  29.1 0.1 collective-permute-start.2
  29.2 2.0 %rank.1.order_ref = bf16[8,64,128]{2,1,0:T(8,128)(2,1)} custom-call(s32[1,16]{1,0:T(1,128)} %group_ref.3, s32[1,128]{1,0:T(1,128)} %bitcast.15, s32[1,128]{1,0:T(1,128)S(1)} %bitcast.11, bf16[8,128,128]{2,1,0:T(8,128)(2,1)S(1)} %get-tuple-element.26.order_ref, bf16[4,128,128]{2,1,0:T(8,128)(2,1)S(1)} %bitcast.9, bf16[32,8,64,64]{3,2,1,0:T(8,128)(2,1)S(1)} %copy-done), custom_call_target="tpu_custom_call" | custom-call | tf_op jit(solution)/shard_map/rank/pallas_call | solution.py:362
  31.3 0.5 collective-permute-start.3
  31.8 1.7 %collective-permute-start.4 = (bf16[8,128,128]{2,1,0:T(8,128)(2,1)S(1)}, bf16[8,128,128]{2,1,0:T(8,128)(2,1)S(1)}, u32[]{:S(2)}, u32[]{:S(2)}) collective-permute-start(bf16[8,128,128]{2,1,0:T(8,128)(2,1)S(1)} %pair.1), channel_id=1, source_target_pairs={{0,2},{1,3},{2,0},{3,1},{4,6},{5,7},{6,4},{7,5},{8,10},{9,11},{10,... | collective-permute-start | bytes 786440 | tf_op jit(solution)/shard_map/ppermute | solution.py:380
  33.5 3.4 %all-to-all-start.2 = ((bf16[8,64,128]{2,1,0:T(8,128)(2,1)}), bf16[8,64,128]{2,1,0:T(8,128)(2,1)S(1)}, u32[]{:S(2)}, u32[]{:S(2)}) async-start(bf16[8,64,128]{2,1,0:T(8,128)(2,1)} %rank.1.order_ref), calls=%async_computation.2 | async-start | bytes 262144 | tf_op jit(solution)/shard_map/all_to_all | solution.py:385
  36.9 4.7 %collective-permute-done.4.across_ref = bf16[8,128,128]{2,1,0:T(8,128)(2,1)S(1)} collective-permute-done((bf16[8,128,128]{2,1,0:T(8,128)(2,1)S(1)}, bf16[8,128,128]{2,1,0:T(8,128)(2,1)S(1)}, u32[]{:S(2)}, u32[]{:S(2)}) %collective-permute-start.4) | collective-permute-done | bytes 262176 | tf_op jit(solution)/shard_map/ppermute | solution.py:380
  41.6 0.8 %add.1 = bf16[8,128,128]{2,1,0:T(8,128)(2,1)} custom-call(f32[8,128,128]{2,1,0:T(8,128)S(1)} %get-tuple-element.25.keep_ref, bf16[8,128,128]{2,1,0:T(8,128)(2,1)S(1)} %collective-permute-done.3.got_ref, bf16[8,128,128]{2,1,0:T(8,128)(2,1)S(1)} %collective-permute-done.4.across_ref), custom_call_target="tpu_custom_call" | custom-call | tf_op jit(solution)/shard_map/add/pallas_call | solution.py:406
  42.4 3.7 %all-to-all-done.2.codes_ref = bf16[8,64,128]{2,1,0:T(8,128)(2,1)S(1)} async-done(((bf16[8,64,128]{2,1,0:T(8,128)(2,1)}), bf16[8,64,128]{2,1,0:T(8,128)(2,1)S(1)}, u32[]{:S(2)}, u32[]{:S(2)}) %all-to-all-start.2) | async-done | bytes 131104 | tf_op jit(solution)/shard_map/all_to_all | solution.py:385
  46.1 3.4 %all-to-all-start.1 = ((bf16[8,128,128]{2,1,0:T(8,128)(2,1)}), bf16[8,128,128]{2,1,0:T(8,128)(2,1)S(1)}, u32[]{:S(2)}, u32[]{:S(2)}) async-start(bf16[8,128,128]{2,1,0:T(8,128)(2,1)} %add.1), calls=%async_computation.1 | async-start | bytes 524288 | tf_op jit(solution)/shard_map/all_to_all | solution.py:385
  49.7 1.3 %collective-permute-done.5.others_ref = bf16[8,64,128]{2,1,0:T(8,128)(2,1)S(1)} collective-permute-done((bf16[8,64,128]{2,1,0:T(8,128)(2,1)S(1)}, bf16[8,64,128]{2,1,0:T(8,128)(2,1)S(1)}, u32[]{:S(2)}, u32[]{:S(2)}) %collective-permute-start.5) | collective-permute-done | bytes 131104 | tf_op jit(solution)/shard_map/ppermute | solution.py:390
  51.0 1.2 %update.1 = (f32[128,128]{1,0:T(8,128)S(1)}, bf16[128,128]{1,0:T(8,128)(2,1)S(1)}, bf16[128,128]{1,0:T(8,128)(2,1)S(1)}, bf16[128,128]{1,0:T(8,128)(2,1)S(1)}) custom-call(s32[1,16]{1,0:T(1,128)} %group_ref.3, s32[1,128]{1,0:T(1,128)} %bitcast.16, s32[1,128]{1,0:T(1,128)S(1)} %bitcast.12, bf16[8,64,128]{2,1,0:T(8,128)(2,1)S(1)} %all-to-all-done.2.codes_ref, ...), custom_call_target="tpu_custom_call" | custom-call | tf_op jit(solution)/shard_map/update/pallas_call | solution.py:392
  52.2 2.2 %collective-permute-start.6 = (bf16[128,128]{1,0:T(8,128)(2,1)S(1)}, bf16[128,128]{1,0:T(8,128)(2,1)S(1)}, u32[]{:S(2)}, u32[]{:S(2)}) collective-permute-start(bf16[128,128]{1,0:T(8,128)(2,1)S(1)} %get-tuple-element.32), channel_id=1, source_target_pairs={{0,1},{1,2},{2,3},{3,0},{4,5},{5,6},{6,7},{7,4},{8,9},{9,10},{10,1... | collective-permute-start | bytes 98312 | tf_op jit(solution)/shard_map/ppermute | solution.py:402
  54.5 2.5 %collective-permute-start.7 = (bf16[128,128]{1,0:T(8,128)(2,1)S(1)}, bf16[128,128]{1,0:T(8,128)(2,1)S(1)}, u32[]{:S(2)}, u32[]{:S(2)}) collective-permute-start(bf16[128,128]{1,0:T(8,128)(2,1)S(1)} %get-tuple-element.33), channel_id=1, source_target_pairs={{0,2},{1,3},{2,0},{3,1},{4,6},{5,7},{6,4},{7,5},{8,10},{9,11},{10,... | collective-permute-start | bytes 98312 | tf_op jit(solution)/shard_map/ppermute | solution.py:402
  56.9 0.3 collective-permute-start.8
  57.2 0.2 collective-permute-done.6.rest_0_
  57.5 2.4 %collective-permute-done.7.rest_1_ = bf16[128,128]{1,0:T(8,128)(2,1)S(1)} collective-permute-done((bf16[128,128]{1,0:T(8,128)(2,1)S(1)}, bf16[128,128]{1,0:T(8,128)(2,1)S(1)}, u32[]{:S(2)}, u32[]{:S(2)}) %collective-permute-start.7) | collective-permute-done | bytes 32800 | tf_op jit(solution)/shard_map/ppermute | solution.py:402
  59.9 1.0 %collective-permute-done.8.rest_2_ = bf16[128,128]{1,0:T(8,128)(2,1)S(1)} collective-permute-done((bf16[128,128]{1,0:T(8,128)(2,1)S(1)}, bf16[128,128]{1,0:T(8,128)(2,1)S(1)}, u32[]{:S(2)}, u32[]{:S(2)}) %collective-permute-start.8) | collective-permute-done | bytes 32800 | tf_op jit(solution)/shard_map/ppermute | solution.py:402
  60.8 0.7 %final.1 = bf16[128,128]{1,0:T(8,128)(2,1)} custom-call(bf16[8,128,128]{2,1,0:T(8,128)(2,1)S(1)} %all-to-all-done.1.parts_ref, f32[128,128]{1,0:T(8,128)S(1)} %get-tuple-element.31.own_ref, bf16[128,128]{1,0:T(8,128)(2,1)S(1)} %collective-permute-done.6.rest_0_, bf16[128,128]{1,0:T(8,128)(2,1)S(1)} %collective-permute-done.7.rest_1_, ...), custom_call_target="tpu_custom_call" | custom-call | tf_op jit(solution)/shard_map/final/pallas_call | solution.py:415
  (19 shorter events, 0.2 us)
Async XLA Ops:
  0.0 5.8 %copy-start.2 = (bf16[8,512,2,128]{3,2,1,0:T(2,128)(2,1)S(1)}, bf16[8,512,2,128]{3,2,1,0:T(2,128)(2,1)}, u32[]{:S(2)}) copy-start(bf16[8,512,2,128]{3,2,1,0:T(2,128)(2,1)} %param.12) | copy-start | bytes 6291460
  0.0 5.8 %copy-start.3 = (bf16[8,2,128]{2,1,0:T(2,128)(2,1)S(1)}, bf16[8,2,128]{2,1,0:T(2,128)(2,1)}, u32[]{:S(2)}) copy-start(bf16[8,2,128]{2,1,0:T(2,128)(2,1)} %key_ref.1) | copy-start | bytes 12292
  0.0 5.8 %copy-start.4 = (bf16[8,2,128]{2,1,0:T(2,128)(2,1)S(1)}, bf16[8,2,128]{2,1,0:T(2,128)(2,1)}, u32[]{:S(2)}) copy-start(bf16[8,2,128]{2,1,0:T(2,128)(2,1)} %value_ref.1) | copy-start | bytes 12292
  2.5 25.3 %collective-permute-start = (bf16[128,2048]{1,0:T(8,128)(2,1)S(1)}, bf16[128,2048]{1,0:T(8,128)(2,1)S(1)}, u32[]{:S(2)}, u32[]{:S(2)}) collective-permute-start(bf16[128,2048]{1,0:T(8,128)(2,1)S(1)} %get-tuple-element.23), channel_id=1, source_target_pairs={{0,1},{1,2},{2,3},{3,0},{4,5},{5,6},{6,7},{7,4},{8,9},{9,10},{10,1... | collective-permute-start | bytes 1572872 | tf_op jit(solution)/shard_map/ppermute | solution.py:327
  4.0 23.8 %collective-permute-start.1 = (bf16[128,2048]{1,0:T(8,128)(2,1)S(1)}, bf16[128,2048]{1,0:T(8,128)(2,1)S(1)}, u32[]{:S(2)}, u32[]{:S(2)}) collective-permute-start(bf16[128,2048]{1,0:T(8,128)(2,1)S(1)} %get-tuple-element.24), channel_id=1, source_target_pairs={{0,3},{1,0},{2,1},{3,2},{4,7},{5,4},{6,5},{7,6},{8,11},{9,8},{10,9... | collective-permute-start | bytes 1572872 | tf_op jit(solution)/shard_map/ppermute | solution.py:328
  5.8 22.0 %copy-start = (bf16[32,8,64,64]{3,2,1,0:T(8,128)(2,1)S(1)}, bf16[32,8,64,64]{3,2,1,0:T(8,128)(2,1)}, u32[]{:S(2)}) copy-start(bf16[32,8,64,64]{3,2,1,0:T(8,128)(2,1)} %down_ref.1) | copy-start | bytes 6291460
  27.8 1.5 %copy-start.5 = (s32[128]{0:T(128)S(1)}, s32[128]{0:T(128)}, u32[]{:S(2)}) copy-start(s32[128]{0:T(128)} %param.21) | copy-start | bytes 1540
  29.1 2.1 %collective-permute-start.2 = (bf16[8,128,128]{2,1,0:T(8,128)(2,1)S(1)}, bf16[8,128,128]{2,1,0:T(8,128)(2,1)S(1)}, u32[]{:S(2)}, u32[]{:S(2)}) collective-permute-start(bf16[8,128,128]{2,1,0:T(8,128)(2,1)S(1)} %get-tuple-element.26.order_ref), channel_id=1, source_target_pairs={{0,4},{4,0},{8,12},{12,8},{16,20},{20,16},{24,28},{28,24},{32,36},... | collective-permute-start | bytes 786440 | tf_op jit(solution)/shard_map/ppermute | solution.py:361
  31.2 19.8 %copy-start.1 = (bf16[32,64,512]{2,1,0:T(8,128)(2,1)S(1)}, bf16[32,64,512]{2,1,0:T(8,128)(2,1)}, u32[]{:S(2)}) copy-start(bf16[32,64,512]{2,1,0:T(8,128)(2,1)} %up_ref.1) | copy-start | bytes 6291460
  31.3 5.6 %collective-permute-start.3 = (bf16[8,128,128]{2,1,0:T(8,128)(2,1)}, bf16[8,128,128]{2,1,0:T(8,128)(2,1)S(1)}, u32[]{:S(2)}, u32[]{:S(2)}) collective-permute-start(bf16[8,128,128]{2,1,0:T(8,128)(2,1)} %get-tuple-element.29), channel_id=1, source_target_pairs={{0,4},{4,0},{8,12},{12,8},{16,20},{20,16},{24,28},{28,24},{32,36},... | collective-permute-start | bytes 786440 | tf_op jit(solution)/shard_map/ppermute | solution.py:381
  31.8 9.8 %collective-permute-start.4 = (bf16[8,128,128]{2,1,0:T(8,128)(2,1)S(1)}, bf16[8,128,128]{2,1,0:T(8,128)(2,1)S(1)}, u32[]{:S(2)}, u32[]{:S(2)}) collective-permute-start(bf16[8,128,128]{2,1,0:T(8,128)(2,1)S(1)} %pair.1), channel_id=1, source_target_pairs={{0,2},{1,3},{2,0},{3,1},{4,6},{5,7},{6,4},{7,5},{8,10},{9,11},{10,... | collective-permute-start | bytes 786440 | tf_op jit(solution)/shard_map/ppermute | solution.py:380
  33.5 12.6 %all-to-all-start.2 = ((bf16[8,64,128]{2,1,0:T(8,128)(2,1)}), bf16[8,64,128]{2,1,0:T(8,128)(2,1)S(1)}, u32[]{:S(2)}, u32[]{:S(2)}) async-start(bf16[8,64,128]{2,1,0:T(8,128)(2,1)} %rank.1.order_ref), calls=%async_computation.2 | async-start | bytes 262144 | tf_op jit(solution)/shard_map/all_to_all | solution.py:385
  46.1 14.7 %all-to-all-start.1 = ((bf16[8,128,128]{2,1,0:T(8,128)(2,1)}), bf16[8,128,128]{2,1,0:T(8,128)(2,1)S(1)}, u32[]{:S(2)}, u32[]{:S(2)}) async-start(bf16[8,128,128]{2,1,0:T(8,128)(2,1)} %add.1), calls=%async_computation.1 | async-start | bytes 524288 | tf_op jit(solution)/shard_map/all_to_all | solution.py:385
  49.6 1.4 %collective-permute-start.5 = (bf16[8,64,128]{2,1,0:T(8,128)(2,1)S(1)}, bf16[8,64,128]{2,1,0:T(8,128)(2,1)S(1)}, u32[]{:S(2)}, u32[]{:S(2)}) collective-permute-start(bf16[8,64,128]{2,1,0:T(8,128)(2,1)S(1)} %all-to-all-done.2.codes_ref), channel_id=1, source_target_pairs={{0,4},{4,0},{8,12},{12,8},{16,20},{20,16},{24,28},{28,24},{32,36},... | collective-permute-start | bytes 393224 | tf_op jit(solution)/shard_map/ppermute | solution.py:390
  52.2 5.2 %collective-permute-start.6 = (bf16[128,128]{1,0:T(8,128)(2,1)S(1)}, bf16[128,128]{1,0:T(8,128)(2,1)S(1)}, u32[]{:S(2)}, u32[]{:S(2)}) collective-permute-start(bf16[128,128]{1,0:T(8,128)(2,1)S(1)} %get-tuple-element.32), channel_id=1, source_target_pairs={{0,1},{1,2},{2,3},{3,0},{4,5},{5,6},{6,7},{7,4},{8,9},{9,10},{10,1... | collective-permute-start | bytes 98312 | tf_op jit(solution)/shard_map/ppermute | solution.py:402
  54.5 5.4 %collective-permute-start.7 = (bf16[128,128]{1,0:T(8,128)(2,1)S(1)}, bf16[128,128]{1,0:T(8,128)(2,1)S(1)}, u32[]{:S(2)}, u32[]{:S(2)}) collective-permute-start(bf16[128,128]{1,0:T(8,128)(2,1)S(1)} %get-tuple-element.33), channel_id=1, source_target_pairs={{0,2},{1,3},{2,0},{3,1},{4,6},{5,7},{6,4},{7,5},{8,10},{9,11},{10,... | collective-permute-start | bytes 98312 | tf_op jit(solution)/shard_map/ppermute | solution.py:402
  56.9 3.9 %collective-permute-start.8 = (bf16[128,128]{1,0:T(8,128)(2,1)S(1)}, bf16[128,128]{1,0:T(8,128)(2,1)S(1)}, u32[]{:S(2)}, u32[]{:S(2)}) collective-permute-start(bf16[128,128]{1,0:T(8,128)(2,1)S(1)} %get-tuple-element.34), channel_id=1, source_target_pairs={{0,3},{1,0},{2,1},{3,2},{4,7},{5,4},{6,5},{7,6},{8,11},{9,8},{10,9... | collective-permute-start | bytes 98312 | tf_op jit(solution)/shard_map/ppermute | solution.py:402

commit v10 on v8

--- a/solution.py
+++ b/solution.py
@@ -43,47 +43,60 @@
     return jnp.transpose(jnp.broadcast_to(rows_ref[...], (rows, rows)))[:, :width]
 
 
-def slab_kernel(
-    w_hbm_ref,
+def column_copies(w_ref, out_ref, step, sems):
+    owners = lax.axis_size("owner")
+    target = lax.rem(lax.axis_index("owner") + step, owners)
+    copies = []
+    for block in range(out_ref.shape[1] // 128):
+        at = pl.multiple_of((block * owners + target) * 128, 128)
+        copies.append(
+            pltpu.make_async_copy(
+                w_ref.at[:, pl.ds(at, 128)],
+                out_ref.at[:, pl.ds(block * 128, 128)],
+                sems.at[block],
+            )
+        )
+    return copies
+
+
+def front_kernel(
     queries_hbm_ref,
+    keys_hbm_ref,
     values_hbm_ref,
     w_ref,
-    queries_ref,
-    values_ref,
+    key_hbm_ref,
+    value_hbm_ref,
+    out_ref,
     right_ref,
     left_ref,
-    sems,
+    queries_ref,
+    keys_ref,
+    values_ref,
+    key_ref,
+    value_ref,
+    small_sems,
+    key_sems,
     value_sems,
+    right_sems,
+    left_sems,
 ):
-    chunks = sems.shape[0] - 1
-    step = w_ref.shape[0] // chunks
     copies = [
-        pltpu.make_async_copy(
-            w_hbm_ref.at[pl.ds(i * step, step)], w_ref.at[pl.ds(i * step, step)], sems.at[i]
-        )
-        for i in range(chunks)
+        pltpu.make_async_copy(queries_hbm_ref, queries_ref, small_sems.at[0]),
+        pltpu.make_async_copy(key_hbm_ref, key_ref, small_sems.at[1]),
+        pltpu.make_async_copy(value_hbm_ref, value_ref, small_sems.at[2]),
     ]
-    rest = [pltpu.make_async_copy(queries_hbm_ref, queries_ref, sems.at[chunks])]
-    rest += [
+    for r in range(keys_ref.shape[0]):
+        copies.append(pltpu.make_async_copy(keys_hbm_ref.at[r], keys_ref.at[r], key_sems.at[r]))
+    later = [
         pltpu.make_async_copy(values_hbm_ref.at[r], values_ref.at[r], value_sems.at[r])
         for r in range(values_ref.shape[0])
     ]
-    for copy in copies + rest:
+    last = column_copies(w_ref, right_ref, 1, right_sems)
+    last += column_copies(w_ref, left_ref, lax.axis_size("owner") - 1, left_sems)
+    for copy in copies + later + last:
         copy.start()
-    owner, owners = lax.axis_index("owner"), lax.axis_size("owner")
-    targets = [lax.rem(owner + 1, owners), lax.rem(owner + owners - 1, owners)]
-    for i in range(chunks):
-        copies[i].wait()
-        rows = pl.ds(i * step, step)
-        for out_ref, target in zip((right_ref, left_ref), targets):
-            for block in range(out_ref.shape[1] // 128):
-                at = pl.multiple_of((block * owners + target) * 128, 128)
-                out_ref[rows, block * 128 : (block + 1) * 128] = w_ref[rows, pl.ds(at, 128)]
-    for copy in rest:
+    for copy in copies:
         copy.wait()
-
-
-def attend_kernel(queries_ref, keys_ref, values_ref, key_ref, value_ref, out_ref):
     rows, local, width = key_ref.shape
     heads = queries_ref.shape[1] // width
     grouped = heads // local
@@ -114,6 +127,8 @@
         denominators.append(jnp.sum(weight, axis=1, keepdims=True) + fresh_weight)
         weights.append(weight.astype(BF16))
         fresh_weights.append(fresh_weight)
+    for copy in later:
+        copy.wait()
     mixed = []
     for r in range(rows):
         total = jnp.dot(weights[r], values_ref[r], preferred_element_type=F32)
@@ -133,6 +148,8 @@
             part = part.astype(BF16)
             for o in range(out_ref.shape[0]):
                 out_ref[o, 2 * g + i] = part
+    for copy in last:
+        copy.wait()
 
 
 def project_kernel(
@@ -293,46 +310,39 @@
     ]
 
     slab = pltpu.VMEM((feats, columns // owners), BF16)
+    blocks = columns // owners // 128
     positions = cached_value_rows.shape[1] * local_heads
-    weight, local_queries, values, right, left = pl.pallas_call(
-        slab_kernel,
-        name="slabs",
-        out_shape=(
-            pltpu.VMEM((feats, columns), BF16),
+    cache = (row_count, positions, head_width)
+    weight = output_weight.reshape(feats, columns)
+    outgoing, right, left = pl.pallas_call(
+        front_kernel,
+        name="front",
+        out_shape=(pltpu.VMEM((owners, tensors, row_count, feats), BF16), slab, slab),
+        in_specs=[HBM] * 6,
+        out_specs=(VMEM,) * 3,
+        scratch_shapes=[
             pltpu.VMEM(queries.shape, BF16),
-            pltpu.VMEM((row_count, positions, head_width), BF16),
-            slab,
-            slab,
-        ),
-        in_specs=[HBM, HBM, HBM],
-        out_specs=(VMEM,) * 5,
-        scratch_shapes=[
-            pltpu.SemaphoreType.DMA((feats // 16 + 1,)),
+            pltpu.VMEM(cache, BF16),
+            pltpu.VMEM(cache, BF16),
+            pltpu.VMEM(newest_key.shape, BF16),
+            pltpu.VMEM(newest_value.shape, BF16),
+            pltpu.SemaphoreType.DMA((3,)),
             pltpu.SemaphoreType.DMA((row_count,)),
+            pltpu.SemaphoreType.DMA((row_count,)),
+            pltpu.SemaphoreType.DMA((blocks,)),
+            pltpu.SemaphoreType.DMA((blocks,)),
         ],
         compiler_params=LIMIT,
     )(
-        far(output_weight.reshape(feats, columns)),
         far(queries),
-        far(cached_value_rows.reshape(row_count, positions, head_width)),
+        far(cached_key_rows.reshape(cache)),
+        far(cached_value_rows.reshape(cache)),
+        far(weight),
+        far(newest_key),
+        far(newest_value),
     )
     before = lax.ppermute(right, "owner", [(o, (o + 1) % owners) for o in range(owners)])
     after = lax.ppermute(left, "owner", [(o, (o - 1) % owners) for o in range(owners)])
-
-    outgoing = pl.pallas_call(
-        attend_kernel,
-        name="attend",
-        out_shape=pltpu.VMEM((owners, tensors, row_count, feats), BF16),
-        in_specs=[VMEM] * 5,
-        out_specs=VMEM,
-        compiler_params=LIMIT,
-    )(
-        near(local_queries),
-        near(cached_key_rows.reshape(row_count, positions, head_width)),
-        near(values),
-        newest_key,
-        newest_value,
-    )
     outgoing = outgoing.reshape(owners * tensors, row_count, feats)
     attention = lax.all_to_all(
         outgoing, ("owner", "tensor"), split_axis=0, concat_axis=0, tiled=True
@@ -353,7 +363,7 @@
         store,
         row_ids,
         near(attention),
-        near(weight),
+        weight,
         near(before),
         near(after),
         near(adapter_down_weight),

time: 62.6 us -> 63.1 us (level)
  Pallas kernels: 9.29 us -> 10.3 us
    pallas_call x2 -> x1, Pallas kernels: 3.47 us -> 4.49 us  [shards(): pl.pallas_call(front_kernel, name='front', out_shape=(pltpu.VMEM((owners,...]
  transfers between devices with their start and end apart: 9 -> 9, of which waited for: 7 -> 7; matrix products, arithmetic and copies ran while one was open for 0% -> 0% of each run, Pallas kernels for 5% -> 4%
where the time goes in v10:
time: 63.1 us; the launch traced here: 62.6 us
  blocking collectives  20.8 us (33%)
  starting transfers between devices  16.4 us (26%)
  waiting for transfers between devices  15 us (24%)
  Pallas kernels  10.3 us (16%)
    all_to_all x1, blocking collectives, shards(): lax.all_to_all(outgoing, ('owner', 'tensor'), split_axis=0, concat_axis=0...  20.8 us
    all_to_all x2, starting transfers between devices, over_z(): lax.all_to_all(pieces, 'tensor', split_axis=0, concat_axis=0, tiled=True,...  6.78 us
    all_to_all x2, waiting for transfers between devices, over_z(): lax.all_to_all(pieces, 'tensor', split_axis=0, concat_axis=0, tiled=True,...  5.55 us
    ppermute x1, waiting for transfers between devices, shards(): lax.ppermute(across, 'owner', [(o, (o + 2) % owners) for o in range(owner...  4.76 us
    pallas_call x1, Pallas kernels, shards(): pl.pallas_call(front_kernel, name='front', out_shape=(pltpu.VMEM((owners,...  4.49 us
    ppermute x3, starting transfers between devices, shards(): lax.ppermute(update, 'owner', [(o, (o + i + 1) % owners) for o in range(o...  4.36 us
    ppermute x3, waiting for transfers between devices, shards(): lax.ppermute(update, 'owner', [(o, (o + i + 1) % owners) for o in range(o...  2.85 us
    pallas_call x1, Pallas kernels, shards(): pl.pallas_call(project_kernel, name='project', out_shape=(pltpu.VMEM((tal...  2.12 us
  transfers between devices with their start and end apart: 9, of which 7 were waited for; matrix products, arithmetic and copies ran while one was open for 0% of the time, Pallas kernels for 4%

profile of v10, /device:TPU:24, one launch (start us, length us, event | category | flops | bytes accessed | tf_op | source)
XLA Modules:
  0.0 62.6 jit_solution(12941319786492379813)
XLA Ops:
  0.0 4.5 %front.1 = (bf16[4,16,8,128]{3,2,1,0:T(8,128)(2,1)S(1)}, bf16[128,2048]{1,0:T(8,128)(2,1)S(1)}, bf16[128,2048]{1,0:T(8,128)(2,1)S(1)}) custom-call(bf16[8,2048]{1,0:T(8,128)(2,1)} %queries_hbm_ref.1, bf16[8,1024,128]{2,1,0:T(8,128)(2,1)} %bitcast.13, bf16[8,1024,128]{2,1,0:T(8,128)(2,1)} %bitcast.14, bf16[128,8192]{1,0:T(8,128)(2,1)} %bitcast.7, ...), custom_call_target="tpu_custom_call" | custom-call | tf_op jit(solution)/shard_map/front/pallas_call | solution.py:317
  4.5 1.6 %collective-permute-start = (bf16[128,2048]{1,0:T(8,128)(2,1)S(1)}, bf16[128,2048]{1,0:T(8,128)(2,1)S(1)}, u32[]{:S(2)}, u32[]{:S(2)}) collective-permute-start(bf16[128,2048]{1,0:T(8,128)(2,1)S(1)} %get-tuple-element.18), channel_id=1, source_target_pairs={{0,1},{1,2},{2,3},{3,0},{4,5},{5,6},{6,7},{7,4},{8,9},{9,10},{10,1... | collective-permute-start | bytes 1572872 | tf_op jit(solution)/shard_map/ppermute | solution.py:344
  6.1 1.7 %collective-permute-start.1 = (bf16[128,2048]{1,0:T(8,128)(2,1)S(1)}, bf16[128,2048]{1,0:T(8,128)(2,1)S(1)}, u32[]{:S(2)}, u32[]{:S(2)}) collective-permute-start(bf16[128,2048]{1,0:T(8,128)(2,1)S(1)} %get-tuple-element.19), channel_id=1, source_target_pairs={{0,3},{1,0},{2,1},{3,2},{4,7},{5,4},{6,5},{7,6},{8,11},{9,8},{10,9... | collective-permute-start | bytes 1572872 | tf_op jit(solution)/shard_map/ppermute | solution.py:345
  7.8 20.8 %all_to_all.15 = bf16[64,8,128]{2,1,0:T(8,128)(2,1)S(1)} all-to-all(bf16[64,8,128]{2,1,0:T(8,128)(2,1)S(1)} %bitcast.10), channel_id=1, replica_groups=mesh['dp'=4,'tensor'=16,'owner'=4] {'owner','tensor'}, dimensions={0} | all-to-all | bytes 262144 | tf_op jit(solution)/shard_map/all_to_all | solution.py:347
  28.7 2.1 %project.1 = (f32[2112,128]{1,0:T(8,128)S(1)}, bf16[2112,128]{1,0:T(8,128)(2,1)S(1)}) custom-call(s32[1,16]{1,0:T(1,128)} %group_ref.3, s32[1,128]{1,0:T(1,128)} %bitcast.15, s32[1,128]{1,0:T(1,128)S(1)} %bitcast.11, bf16[4,128,128]{2,1,0:T(8,128)(2,1)S(1)} %bitcast.9, bf16[128,8192]{1,0:T(8,128)(2,1)S(1)} %bitcast.8, ...), custom_call_target="tpu_custom_call" | custom-call | tf_op jit(solution)/shard_map/project/pallas_call | solution.py:353
  30.8 0.0 copy-start.2
  30.8 0.2 collective-permute-start.2
  31.0 1.8 %collective-permute-done.2.got_ref = bf16[2112,128]{1,0:T(8,128)(2,1)S(1)} collective-permute-done((bf16[2112,128]{1,0:T(8,128)(2,1)S(1)}, bf16[2112,128]{1,0:T(8,128)(2,1)S(1)}, u32[]{:S(2)}, u32[]{:S(2)}) %collective-permute-start.2) | collective-permute-done | bytes 540704 | tf_op jit(solution)/shard_map/ppermute | solution.py:371
  32.8 0.7 %pair.1 = (f32[8,128,128]{2,1,0:T(8,128)S(1)}, bf16[8,128,128]{2,1,0:T(8,128)(2,1)S(1)}, bf16[8,64,128]{2,1,0:T(8,128)(2,1)}) custom-call(f32[2112,128]{1,0:T(8,128)S(1)} %get-tuple-element.20.keep_ref, bf16[2112,128]{1,0:T(8,128)(2,1)S(1)} %collective-permute-done.2.got_ref), custom_call_target="tpu_custom_call" | custom-call | tf_op jit(solution)/shard_map/pair/pallas_call | solution.py:372
  33.5 1.7 %collective-permute-start.3 = (bf16[8,128,128]{2,1,0:T(8,128)(2,1)S(1)}, bf16[8,128,128]{2,1,0:T(8,128)(2,1)S(1)}, u32[]{:S(2)}, u32[]{:S(2)}) collective-permute-start(bf16[8,128,128]{2,1,0:T(8,128)(2,1)S(1)} %get-tuple-element.23), channel_id=1, source_target_pairs={{0,2},{1,3},{2,0},{3,1},{4,6},{5,7},{6,4},{7,5},{8,10},{9,11},{10,... | collective-permute-start | bytes 786440 | tf_op jit(solution)/shard_map/ppermute | solution.py:391
  35.3 3.4 %all-to-all-start.2 = ((bf16[8,64,128]{2,1,0:T(8,128)(2,1)}), bf16[8,64,128]{2,1,0:T(8,128)(2,1)S(1)}, u32[]{:S(2)}, u32[]{:S(2)}) async-start(bf16[8,64,128]{2,1,0:T(8,128)(2,1)} %get-tuple-element.24), calls=%async_computation.2 | async-start | bytes 262144 | tf_op jit(solution)/shard_map/all_to_all | solution.py:387
  38.6 4.8 %collective-permute-done.3.two_ref = bf16[8,128,128]{2,1,0:T(8,128)(2,1)S(1)} collective-permute-done((bf16[8,128,128]{2,1,0:T(8,128)(2,1)S(1)}, bf16[8,128,128]{2,1,0:T(8,128)(2,1)S(1)}, u32[]{:S(2)}, u32[]{:S(2)}) %collective-permute-start.3) | collective-permute-done | bytes 262176 | tf_op jit(solution)/shard_map/ppermute | solution.py:391
  43.4 0.8 %add.1 = bf16[8,128,128]{2,1,0:T(8,128)(2,1)} custom-call(f32[8,128,128]{2,1,0:T(8,128)S(1)} %get-tuple-element.22.one_ref, bf16[8,128,128]{2,1,0:T(8,128)(2,1)S(1)} %collective-permute-done.3.two_ref), custom_call_target="tpu_custom_call" | custom-call | tf_op jit(solution)/shard_map/add/pallas_call | solution.py:408
  44.2 3.8 %all-to-all-done.2.codes_ref = bf16[8,64,128]{2,1,0:T(8,128)(2,1)S(1)} async-done(((bf16[8,64,128]{2,1,0:T(8,128)(2,1)}), bf16[8,64,128]{2,1,0:T(8,128)(2,1)S(1)}, u32[]{:S(2)}, u32[]{:S(2)}) %all-to-all-start.2) | async-done | bytes 131104 | tf_op jit(solution)/shard_map/all_to_all | solution.py:387
  47.9 3.4 %all-to-all-start.1 = ((bf16[8,128,128]{2,1,0:T(8,128)(2,1)}), bf16[8,128,128]{2,1,0:T(8,128)(2,1)S(1)}, u32[]{:S(2)}, u32[]{:S(2)}) async-start(bf16[8,128,128]{2,1,0:T(8,128)(2,1)} %add.1), calls=%async_computation.1 | async-start | bytes 524288 | tf_op jit(solution)/shard_map/all_to_all | solution.py:387
  51.3 1.6 %update.1 = (f32[128,128]{1,0:T(8,128)S(1)}, bf16[128,128]{1,0:T(8,128)(2,1)S(1)}, bf16[128,128]{1,0:T(8,128)(2,1)S(1)}, bf16[128,128]{1,0:T(8,128)(2,1)S(1)}) custom-call(s32[1,16]{1,0:T(1,128)} %group_ref.3, s32[1,128]{1,0:T(1,128)} %bitcast.16, s32[1,128]{1,0:T(1,128)S(1)} %bitcast.12, bf16[8,64,128]{2,1,0:T(8,128)(2,1)S(1)} %all-to-all-done.2.codes_ref, ...), custom_call_target="tpu_custom_call" | custom-call | tf_op jit(solution)/shard_map/update/pallas_call | solution.py:394
  52.9 1.0 %collective-permute-start.4 = (bf16[128,128]{1,0:T(8,128)(2,1)S(1)}, bf16[128,128]{1,0:T(8,128)(2,1)S(1)}, u32[]{:S(2)}, u32[]{:S(2)}) collective-permute-start(bf16[128,128]{1,0:T(8,128)(2,1)S(1)} %get-tuple-element.26), channel_id=1, source_target_pairs={{0,1},{1,2},{2,3},{3,0},{4,5},{5,6},{6,7},{7,4},{8,9},{9,10},{10,1... | collective-permute-start | bytes 98312 | tf_op jit(solution)/shard_map/ppermute | solution.py:404
  53.9 2.3 %collective-permute-start.5 = (bf16[128,128]{1,0:T(8,128)(2,1)S(1)}, bf16[128,128]{1,0:T(8,128)(2,1)S(1)}, u32[]{:S(2)}, u32[]{:S(2)}) collective-permute-start(bf16[128,128]{1,0:T(8,128)(2,1)S(1)} %get-tuple-element.27), channel_id=1, source_target_pairs={{0,2},{1,3},{2,0},{3,1},{4,6},{5,7},{6,4},{7,5},{8,10},{9,11},{10,... | collective-permute-start | bytes 98312 | tf_op jit(solution)/shard_map/ppermute | solution.py:404
  56.2 1.1 %collective-permute-start.6 = (bf16[128,128]{1,0:T(8,128)(2,1)S(1)}, bf16[128,128]{1,0:T(8,128)(2,1)S(1)}, u32[]{:S(2)}, u32[]{:S(2)}) collective-permute-start(bf16[128,128]{1,0:T(8,128)(2,1)S(1)} %get-tuple-element.28), channel_id=1, source_target_pairs={{0,3},{1,0},{2,1},{3,2},{4,7},{5,4},{6,5},{7,6},{8,11},{9,8},{10,9... | collective-permute-start | bytes 98312 | tf_op jit(solution)/shard_map/ppermute | solution.py:404
  57.3 0.8 %collective-permute-done.4.rest_0_ = bf16[128,128]{1,0:T(8,128)(2,1)S(1)} collective-permute-done((bf16[128,128]{1,0:T(8,128)(2,1)S(1)}, bf16[128,128]{1,0:T(8,128)(2,1)S(1)}, u32[]{:S(2)}, u32[]{:S(2)}) %collective-permute-start.4) | collective-permute-done | bytes 32800 | tf_op jit(solution)/shard_map/ppermute | solution.py:404
  58.1 1.2 %collective-permute-done.5.rest_1_ = bf16[128,128]{1,0:T(8,128)(2,1)S(1)} collective-permute-done((bf16[128,128]{1,0:T(8,128)(2,1)S(1)}, bf16[128,128]{1,0:T(8,128)(2,1)S(1)}, u32[]{:S(2)}, u32[]{:S(2)}) %collective-permute-start.5) | collective-permute-done | bytes 32800 | tf_op jit(solution)/shard_map/ppermute | solution.py:404
  59.3 0.8 %collective-permute-done.6.rest_2_ = bf16[128,128]{1,0:T(8,128)(2,1)S(1)} collective-permute-done((bf16[128,128]{1,0:T(8,128)(2,1)S(1)}, bf16[128,128]{1,0:T(8,128)(2,1)S(1)}, u32[]{:S(2)}, u32[]{:S(2)}) %collective-permute-start.6) | collective-permute-done | bytes 32800 | tf_op jit(solution)/shard_map/ppermute | solution.py:404
  60.1 1.8 %all-to-all-done.1.parts_ref = bf16[8,128,128]{2,1,0:T(8,128)(2,1)S(1)} async-done(((bf16[8,128,128]{2,1,0:T(8,128)(2,1)}), bf16[8,128,128]{2,1,0:T(8,128)(2,1)S(1)}, u32[]{:S(2)}, u32[]{:S(2)}) %all-to-all-start.1) | async-done | bytes 262176 | tf_op jit(solution)/shard_map/all_to_all | solution.py:387
  61.9 0.7 %final.1 = bf16[128,128]{1,0:T(8,128)(2,1)} custom-call(bf16[8,128,128]{2,1,0:T(8,128)(2,1)S(1)} %all-to-all-done.1.parts_ref, f32[128,128]{1,0:T(8,128)S(1)} %get-tuple-element.25.own_ref, bf16[128,128]{1,0:T(8,128)(2,1)S(1)} %collective-permute-done.4.rest_0_, bf16[128,128]{1,0:T(8,128)(2,1)S(1)} %collective-permute-done.5.rest_1_, ...), custom_call_target="tpu_custom_call" | custom-call | tf_op jit(solution)/shard_map/final/pallas_call | solution.py:417
  (9 shorter events, 0.0 us)
Async XLA Ops:
  0.0 28.6 %copy-start = (bf16[2,64,8192]{2,1,0:T(8,128)(2,1)S(1)}, bf16[2,64,8192]{2,1,0:T(8,128)(2,1)}, u32[]{:S(2)}) copy-start(bf16[2,64,8192]{2,1,0:T(8,128)(2,1)} %param.16) | copy-start | bytes 6291460
  0.0 28.6 %copy-start.1 = (bf16[32,8,64,64]{3,2,1,0:T(8,128)(2,1)S(1)}, bf16[32,8,64,64]{3,2,1,0:T(8,128)(2,1)}, u32[]{:S(2)}) copy-start(bf16[32,8,64,64]{3,2,1,0:T(8,128)(2,1)} %down_ref.1) | copy-start | bytes 6291460
  0.0 28.7 %copy-start.3 = (s32[128]{0:T(128)S(1)}, s32[128]{0:T(128)}, u32[]{:S(2)}) copy-start(s32[128]{0:T(128)} %param.21) | copy-start | bytes 1540
  4.5 24.1 %collective-permute-start = (bf16[128,2048]{1,0:T(8,128)(2,1)S(1)}, bf16[128,2048]{1,0:T(8,128)(2,1)S(1)}, u32[]{:S(2)}, u32[]{:S(2)}) collective-permute-start(bf16[128,2048]{1,0:T(8,128)(2,1)S(1)} %get-tuple-element.18), channel_id=1, source_target_pairs={{0,1},{1,2},{2,3},{3,0},{4,5},{5,6},{6,7},{7,4},{8,9},{9,10},{10,1... | collective-permute-start | bytes 1572872 | tf_op jit(solution)/shard_map/ppermute | solution.py:344
  6.1 22.6 %collective-permute-start.1 = (bf16[128,2048]{1,0:T(8,128)(2,1)S(1)}, bf16[128,2048]{1,0:T(8,128)(2,1)S(1)}, u32[]{:S(2)}, u32[]{:S(2)}) collective-permute-start(bf16[128,2048]{1,0:T(8,128)(2,1)S(1)} %get-tuple-element.19), channel_id=1, source_target_pairs={{0,3},{1,0},{2,1},{3,2},{4,7},{5,4},{6,5},{7,6},{8,11},{9,8},{10,9... | collective-permute-start | bytes 1572872 | tf_op jit(solution)/shard_map/ppermute | solution.py:345
  30.8 20.5 %copy-start.2 = (bf16[32,64,512]{2,1,0:T(8,128)(2,1)S(1)}, bf16[32,64,512]{2,1,0:T(8,128)(2,1)}, u32[]{:S(2)}) copy-start(bf16[32,64,512]{2,1,0:T(8,128)(2,1)} %up_ref.1) | copy-start | bytes 6291460
  30.8 2.0 %collective-permute-start.2 = (bf16[2112,128]{1,0:T(8,128)(2,1)S(1)}, bf16[2112,128]{1,0:T(8,128)(2,1)S(1)}, u32[]{:S(2)}, u32[]{:S(2)}) collective-permute-start(bf16[2112,128]{1,0:T(8,128)(2,1)S(1)} %get-tuple-element.21), channel_id=1, source_target_pairs={{0,4},{4,0},{8,12},{12,8},{16,20},{20,16},{24,28},{28,24},{32,36},... | collective-permute-start | bytes 1622024 | tf_op jit(solution)/shard_map/ppermute | solution.py:371
  33.5 9.9 %collective-permute-start.3 = (bf16[8,128,128]{2,1,0:T(8,128)(2,1)S(1)}, bf16[8,128,128]{2,1,0:T(8,128)(2,1)S(1)}, u32[]{:S(2)}, u32[]{:S(2)}) collective-permute-start(bf16[8,128,128]{2,1,0:T(8,128)(2,1)S(1)} %get-tuple-element.23), channel_id=1, source_target_pairs={{0,2},{1,3},{2,0},{3,1},{4,6},{5,7},{6,4},{7,5},{8,10},{9,11},{10,... | collective-permute-start | bytes 786440 | tf_op jit(solution)/shard_map/ppermute | solution.py:391
  35.3 12.7 %all-to-all-start.2 = ((bf16[8,64,128]{2,1,0:T(8,128)(2,1)}), bf16[8,64,128]{2,1,0:T(8,128)(2,1)S(1)}, u32[]{:S(2)}, u32[]{:S(2)}) async-start(bf16[8,64,128]{2,1,0:T(8,128)(2,1)} %get-tuple-element.24), calls=%async_computation.2 | async-start | bytes 262144 | tf_op jit(solution)/shard_map/all_to_all | solution.py:387
  47.9 14.0 %all-to-all-start.1 = ((bf16[8,128,128]{2,1,0:T(8,128)(2,1)}), bf16[8,128,128]{2,1,0:T(8,128)(2,1)S(1)}, u32[]{:S(2)}, u32[]{:S(2)}) async-start(bf16[8,128,128]{2,1,0:T(8,128)(2,1)} %add.1), calls=%async_computation.1 | async-start | bytes 524288 | tf_op jit(solution)/shard_map/all_to_all | solution.py:387
  52.9 5.2 %collective-permute-start.4 = (bf16[128,128]{1,0:T(8,128)(2,1)S(1)}, bf16[128,128]{1,0:T(8,128)(2,1)S(1)}, u32[]{:S(2)}, u32[]{:S(2)}) collective-permute-start(bf16[128,128]{1,0:T(8,128)(2,1)S(1)} %get-tuple-element.26), channel_id=1, source_target_pairs={{0,1},{1,2},{2,3},{3,0},{4,5},{5,6},{6,7},{7,4},{8,9},{9,10},{10,1... | collective-permute-start | bytes 98312 | tf_op jit(solution)/shard_map/ppermute | solution.py:404
  53.9 5.4 %collective-permute-start.5 = (bf16[128,128]{1,0:T(8,128)(2,1)S(1)}, bf16[128,128]{1,0:T(8,128)(2,1)S(1)}, u32[]{:S(2)}, u32[]{:S(2)}) collective-permute-start(bf16[128,128]{1,0:T(8,128)(2,1)S(1)} %get-tuple-element.27), channel_id=1, source_target_pairs={{0,2},{1,3},{2,0},{3,1},{4,6},{5,7},{6,4},{7,5},{8,10},{9,11},{10,... | collective-permute-start | bytes 98312 | tf_op jit(solution)/shard_map/ppermute | solution.py:404
  56.2 3.9 %collective-permute-start.6 = (bf16[128,128]{1,0:T(8,128)(2,1)S(1)}, bf16[128,128]{1,0:T(8,128)(2,1)S(1)}, u32[]{:S(2)}, u32[]{:S(2)}) collective-permute-start(bf16[128,128]{1,0:T(8,128)(2,1)S(1)} %get-tuple-element.28), channel_id=1, source_target_pairs={{0,3},{1,0},{2,1},{3,2},{4,7},{5,4},{6,5},{7,6},{8,11},{9,8},{10,9... | collective-permute-start | bytes 98312 | tf_op jit(solution)/shard_map/ppermute | solution.py:404

commit v11 on v8

--- a/solution.py
+++ b/solution.py
@@ -144,6 +144,8 @@
     before_ref,
     after_ref,
     down_ref,
+    own_ref,
+    send_own_ref,
     keep_ref,
     send_ref,
     acc,
@@ -176,11 +178,13 @@
         here = jnp.dot(beside, near_rows, preferred_element_type=F32)
         here = here + jnp.dot(mine, columns(z, owner), preferred_element_type=F32)
         there = jnp.dot(mine, columns(z, across), preferred_element_type=F32)
-        for i, part in enumerate((here, there)):
-            even, odd = part[:, :block], part[:, block:]
-            rows_span = pl.ds((2 * z + i) * rows, rows)
-            keep_ref[rows_span, :] = jnp.where(first, even, odd)
-            send_ref[rows_span, :] = jnp.where(first, odd, even).astype(BF16)
+        span = pl.ds(z * rows, rows)
+        even, odd = here[:, :block], here[:, block:]
+        own_ref[z] = jnp.where(first, even, odd).astype(BF16)
+        send_own_ref[z] = jnp.where(first, odd, even).astype(BF16)
+        even, odd = there[:, :block], there[:, block:]
+        keep_ref[span, :] = jnp.where(first, even, odd)
+        send_ref[span, :] = jnp.where(first, odd, even).astype(BF16)
     att = jnp.concatenate([att_ref[o] for o in range(owners)], axis=1)
     ids = row_adapters(rows_ref, rank)
     acc[...] = jnp.zeros_like(acc)
@@ -197,25 +201,30 @@
 
     half = rows // 2
     code = jnp.concatenate([acc[:half, :], acc[half:, :]], axis=1)
-    keep_ref[2 * planes * rows :, :] = code
-    send_ref[2 * planes * rows :, :] = code.astype(BF16)
-
-
-def pair_kernel(keep_ref, got_ref, own_ref, across_ref, codes_ref):
-    planes, rows, _ = own_ref.shape
+    keep_ref[planes * rows :, :] = code
+    send_ref[planes * rows :, :] = code.astype(BF16)
+
+
+def pair_kernel(keep_ref, got_ref, across_ref, codes_ref, code_ref, sems):
+    planes, rows, _ = across_ref.shape
+    span = pl.ds(planes * rows, code_ref.shape[0])
+    code_ref[...] = (keep_ref[span, :] + got_ref[span, :].astype(F32)).astype(BF16)
+    copies = [
+        pltpu.make_async_copy(code_ref, codes_ref.at[z], sems.at[z]) for z in range(planes)
+    ]
+    for copy in copies:
+        copy.start()
     for z in range(planes):
-        span = pl.ds(2 * z * rows, rows)
-        own_ref[z] = keep_ref[span, :] + got_ref[span, :].astype(F32)
-        span = pl.ds((2 * z + 1) * rows, rows)
+        span = pl.ds(z * rows, rows)
         across_ref[z] = (keep_ref[span, :] + got_ref[span, :].astype(F32)).astype(BF16)
-    span = pl.ds(2 * planes * rows, codes_ref.shape[1])
-    code = (keep_ref[span, :] + got_ref[span, :].astype(F32)).astype(BF16)
-    for z in range(planes):
-        codes_ref[z] = code
-
-
-def add_kernel(one_ref, two_ref, out_ref):
-    out_ref[...] = (one_ref[...] + two_ref[...].astype(F32)).astype(BF16)
+    for copy in copies:
+        copy.wait()
+
+
+def add_kernel(keep_ref, got_ref, across_ref, out_ref):
+    total = keep_ref[...].astype(F32) + got_ref[...].astype(F32)
+    total = total + across_ref[...].astype(F32)
+    out_ref[...] = total.astype(BF16)
 
 
 def update_kernel(group_ref, store_ref, rows_ref, codes_ref, up_ref, own_ref, *rest):
@@ -339,13 +348,19 @@
     )
     attention = attention.reshape(owners, rows, feats)
 
-    tall = 2 * planes * rows + rows // 2
-    keep, send = pl.pallas_call(
+    tall = planes * rows + rows // 2
+    sent = pltpu.VMEM((planes, rows, block), BF16)
+    own_part, send_own, keep, send = pl.pallas_call(
         project_kernel,
         name="project",
-        out_shape=(pltpu.VMEM((tall, block), F32), pltpu.VMEM((tall, block), BF16)),
+        out_shape=(
+            sent,
+            sent,
+            pltpu.VMEM((tall, block), F32),
+            pltpu.VMEM((tall, block), BF16),
+        ),
         in_specs=[HBM, HBM] + [VMEM] * 6,
-        out_specs=(VMEM, VMEM),
+        out_specs=(VMEM,) * 4,
         scratch_shapes=[pltpu.VMEM((rows, rank), F32)] + indices,
         compiler_params=LIMIT,
     )(
@@ -358,17 +373,16 @@
         near(after),
         near(adapter_down_weight),
     )
-    got = lax.ppermute(send, "tensor", [(t, t ^ 1) for t in range(tensors)])
-    own_part, across, codes = pl.pallas_call(
+    swap = [(t, t ^ 1) for t in range(tensors)]
+    got = lax.ppermute(send, "tensor", swap)
+    lines = (rows // 2, 2 * rank)
+    across, codes = pl.pallas_call(
         pair_kernel,
         name="pair",
-        out_shape=(
-            pltpu.VMEM((planes, rows, block), F32),
-            pltpu.VMEM((planes, rows, block), BF16),
-            pltpu.VMEM((planes, rows // 2, 2 * rank), BF16),
-        ),
+        out_shape=(sent, pltpu.HBM((planes,) + lines, BF16)),
         in_specs=[VMEM, VMEM],
-        out_specs=(VMEM, VMEM, VMEM),
+        out_specs=(VMEM, HBM),
+        scratch_shapes=[pltpu.VMEM(lines, BF16), pltpu.SemaphoreType.DMA((planes,))],
         compiler_params=LIMIT,
     )(near(keep), near(got))
     groups = [[2 * z + c for z in range(planes)] for c in range(2)]
@@ -378,8 +392,10 @@
             pieces, "tensor", split_axis=0, concat_axis=0, tiled=True, axis_index_groups=groups
         )
 
+    across, send_own = lax.optimization_barrier((across, send_own))
     across = lax.ppermute(across, "owner", [(o, (o + 2) % owners) for o in range(owners)])
     codes = over_z(codes)
+    got_own = lax.ppermute(send_own, "tensor", swap)
     strip = pltpu.VMEM((rows, block), BF16)
     own_update, *updates = pl.pallas_call(
         update_kernel,
@@ -399,10 +415,10 @@
             add_kernel,
             name="add",
             out_shape=pltpu.VMEM((planes, rows, block), BF16),
-            in_specs=[VMEM, VMEM],
+            in_specs=[VMEM] * 3,
             out_specs=VMEM,
             compiler_params=LIMIT,
-        )(near(own_part), near(across))
+        )(near(own_part), near(got_own), near(across))
     )
     return pl.pallas_call(
         final_kernel,

time: 62.6 us -> 63 us (level)
  starting transfers between devices: 16.4 us -> 17.1 us
    all_to_all x2, waiting for transfers between devices: 5.53 us -> 7.21 us  [over_z(): lax.all_to_all(pieces, 'tensor', split_axis=0, concat_axis=0, tiled=True,...]
    ppermute x3, waiting for transfers between devices: 2.87 us -> 2.09 us  [shards(): lax.ppermute(update, 'owner', [(o, (o + i + 1) % owners) for o in range(o...]
    ppermute x1 -> x2, waiting for transfers between devices: 1.82 us -> 1.45 us  [the longest x1 1.44 us: shards(): got = lax.ppermute(send, 'tensor', swap)]
  transfers between devices with their start and end apart: 9 -> 10, of which waited for: 7 -> 7; matrix products, arithmetic and copies ran while one was open for 0% -> 0% of each run, Pallas kernels for 5% -> 5%
where the time goes in v11:
time: 63 us; the launch traced here: 62.7 us
  blocking collectives  21 us (33%)
  starting transfers between devices  17.1 us (27%)
  waiting for transfers between devices  15.2 us (24%)
  Pallas kernels  9.35 us (15%)
    all_to_all x1, blocking collectives, shards(): lax.all_to_all(outgoing, ('owner', 'tensor'), split_axis=0, concat_axis=0...  21 us
    all_to_all x2, waiting for transfers between devices, over_z(): lax.all_to_all(pieces, 'tensor', split_axis=0, concat_axis=0, tiled=True,...  7.21 us
    all_to_all x2, starting transfers between devices, over_z(): lax.all_to_all(pieces, 'tensor', split_axis=0, concat_axis=0, tiled=True,...  6.78 us
    ppermute x1, waiting for transfers between devices, shards(): lax.ppermute(across, 'owner', [(o, (o + 2) % owners) for o in range(owner...  4.45 us
    ppermute x3, starting transfers between devices, shards(): lax.ppermute(update, 'owner', [(o, (o + i + 1) % owners) for o in range(o...  4.31 us
    pallas_call x1, Pallas kernels, shards(): pl.pallas_call(slab_kernel, name='slabs', out_shape=(pltpu.VMEM((feats, c...  2.44 us
    ppermute x1, starting transfers between devices, shards(): lax.ppermute(across, 'owner', [(o, (o + 2) % owners) for o in range(owner...  2.25 us
    pallas_call x1, Pallas kernels, shards(): pl.pallas_call(project_kernel, name='project', out_shape=(sent, sent, plt...  2.13 us
  transfers between devices with their start and end apart: 10, of which 7 were waited for; matrix products, arithmetic and copies ran while one was open for 0% of the time, Pallas kernels for 5%

profile of v11, /device:TPU:24, one launch (start us, length us, event | category | flops | bytes accessed | tf_op | source)
XLA Modules:
  0.0 62.7 jit_solution(1971920138352851993)
XLA Ops:
  0.0 2.4 %slabs.1 = (bf16[128,8192]{1,0:T(8,128)(2,1)S(1)}, bf16[8,2048]{1,0:T(8,128)(2,1)S(1)}, bf16[8,1024,128]{2,1,0:T(8,128)(2,1)S(1)}, bf16[128,2048]{1,0:T(8,128)(2,1)S(1)}, bf16[128,2048]{1,0:T(8,128)(2,1)S(1)}) custom-call(bf16[128,8192]{1,0:T(8,128)(2,1)} %bitcast.12, bf16[8,2048]{1,0:T(8,128)(2,1)} %queries_hbm_ref.1, bf16[8,1024,128]{2,1,0:T(8,128)(2,1)} %bitcast.13), custom_call_target="tpu_custom_call" | custom-call | tf_op jit(solution)/shard_map/slabs/pallas_call | solution.py:306
  2.5 1.6 %collective-permute-start = (bf16[128,2048]{1,0:T(8,128)(2,1)S(1)}, bf16[128,2048]{1,0:T(8,128)(2,1)S(1)}, u32[]{:S(2)}, u32[]{:S(2)}) collective-permute-start(bf16[128,2048]{1,0:T(8,128)(2,1)S(1)} %get-tuple-element.25), channel_id=1, source_target_pairs={{0,1},{1,2},{2,3},{3,0},{4,5},{5,6},{6,7},{7,4},{8,9},{9,10},{10,1... | collective-permute-start | bytes 1572872 | tf_op jit(solution)/shard_map/ppermute | solution.py:328
  4.0 1.7 %collective-permute-start.1 = (bf16[128,2048]{1,0:T(8,128)(2,1)S(1)}, bf16[128,2048]{1,0:T(8,128)(2,1)S(1)}, u32[]{:S(2)}, u32[]{:S(2)}) collective-permute-start(bf16[128,2048]{1,0:T(8,128)(2,1)S(1)} %get-tuple-element.26), channel_id=1, source_target_pairs={{0,3},{1,0},{2,1},{3,2},{4,7},{5,4},{6,5},{7,6},{8,11},{9,8},{10,9... | collective-permute-start | bytes 1572872 | tf_op jit(solution)/shard_map/ppermute | solution.py:329
  5.8 1.0 %attend.1 = bf16[4,16,8,128]{3,2,1,0:T(8,128)(2,1)S(1)} custom-call(bf16[8,2048]{1,0:T(8,128)(2,1)S(1)} %get-tuple-element.22.queries_ref, bf16[8,1024,128]{2,1,0:T(8,128)(2,1)S(1)} %bitcast.7, bf16[8,1024,128]{2,1,0:T(8,128)(2,1)S(1)} %get-tuple-element.23.values_ref, bf16[8,2,128]{2,1,0:T(2,128)(2,1)S(1)} %copy-done.3, bf16[8,2,128]{2,1,0:T(2,128)(2,1)S(1)} %copy-done.4), custom_call_target="tpu_custom_call" | custom-call | tf_op jit(solution)/shard_map/attend/pallas_call | solution.py:331
  6.8 21.0 %all_to_all.15 = bf16[64,8,128]{2,1,0:T(8,128)(2,1)S(1)} all-to-all(bf16[64,8,128]{2,1,0:T(8,128)(2,1)S(1)} %bitcast.9), channel_id=1, replica_groups=mesh['dp'=4,'tensor'=16,'owner'=4] {'owner','tensor'}, dimensions={0} | all-to-all | bytes 262144 | tf_op jit(solution)/shard_map/all_to_all | solution.py:346
  27.8 2.1 %project.1 = (bf16[8,128,128]{2,1,0:T(8,128)(2,1)S(1)}, bf16[8,128,128]{2,1,0:T(8,128)(2,1)S(1)}, f32[1088,128]{1,0:T(8,128)S(1)}, bf16[1088,128]{1,0:T(8,128)(2,1)S(1)}) custom-call(s32[1,16]{1,0:T(1,128)} %group_ref.3, s32[1,128]{1,0:T(1,128)} %bitcast.14, s32[1,128]{1,0:T(1,128)S(1)} %bitcast.10, bf16[4,128,128]{2,1,0:T(8,128)(2,1)S(1)} %bitcast.8, ...), custom_call_target="tpu_custom_call" | custom-call | tf_op jit(solution)/shard_map/project/pallas_call | solution.py:353
  30.0 0.2 collective-permute-start.2
  30.2 1.4 %collective-permute-done.2.got_ref = bf16[1088,128]{1,0:T(8,128)(2,1)S(1)} collective-permute-done((bf16[1088,128]{1,0:T(8,128)(2,1)S(1)}, bf16[1088,128]{1,0:T(8,128)(2,1)S(1)}, u32[]{:S(2)}, u32[]{:S(2)}) %collective-permute-start.2) | collective-permute-done | bytes 278560 | tf_op jit(solution)/shard_map/ppermute | solution.py:377
  31.6 0.7 %pair.1 = (bf16[8,128,128]{2,1,0:T(8,128)(2,1)S(1)}, bf16[8,64,128]{2,1,0:T(8,128)(2,1)}) custom-call(f32[1088,128]{1,0:T(8,128)S(1)} %get-tuple-element.28.keep_ref, bf16[1088,128]{1,0:T(8,128)(2,1)S(1)} %collective-permute-done.2.got_ref), custom_call_target="tpu_custom_call" | custom-call | tf_op jit(solution)/shard_map/pair/pallas_call | solution.py:379
  32.3 0.2 collective-permute-start.3
  32.6 2.2 %collective-permute-start.4 = (bf16[8,128,128]{2,1,0:T(8,128)(2,1)S(1)}, bf16[8,128,128]{2,1,0:T(8,128)(2,1)S(1)}, u32[]{:S(2)}, u32[]{:S(2)}) collective-permute-start(bf16[8,128,128]{2,1,0:T(8,128)(2,1)S(1)} %get-tuple-element.33), channel_id=1, source_target_pairs={{0,2},{1,3},{2,0},{3,1},{4,6},{5,7},{6,4},{7,5},{8,10},{9,11},{10,... | collective-permute-start | bytes 786440 | tf_op jit(solution)/shard_map/ppermute | solution.py:396
  34.8 3.4 %all-to-all-start.2 = ((bf16[8,64,128]{2,1,0:T(8,128)(2,1)}), bf16[8,64,128]{2,1,0:T(8,128)(2,1)S(1)}, u32[]{:S(2)}, u32[]{:S(2)}) async-start(bf16[8,64,128]{2,1,0:T(8,128)(2,1)} %get-tuple-element.34), calls=%async_computation.2 | async-start | bytes 262144 | tf_op jit(solution)/shard_map/all_to_all | solution.py:391
  38.2 4.5 %collective-permute-done.4.across_ref = bf16[8,128,128]{2,1,0:T(8,128)(2,1)S(1)} collective-permute-done((bf16[8,128,128]{2,1,0:T(8,128)(2,1)S(1)}, bf16[8,128,128]{2,1,0:T(8,128)(2,1)S(1)}, u32[]{:S(2)}, u32[]{:S(2)}) %collective-permute-start.4) | collective-permute-done | bytes 262176 | tf_op jit(solution)/shard_map/ppermute | solution.py:396
  42.7 0.8 %add.1 = bf16[8,128,128]{2,1,0:T(8,128)(2,1)} custom-call(bf16[8,128,128]{2,1,0:T(8,128)(2,1)S(1)} %get-tuple-element.27.keep_ref, bf16[8,128,128]{2,1,0:T(8,128)(2,1)S(1)} %collective-permute-done.3.got_ref, bf16[8,128,128]{2,1,0:T(8,128)(2,1)S(1)} %collective-permute-done.4.across_ref), custom_call_target="tpu_custom_call" | custom-call | tf_op jit(solution)/shard_map/add/pallas_call | solution.py:414
  43.5 4.2 %all-to-all-done.2.codes_ref = bf16[8,64,128]{2,1,0:T(8,128)(2,1)S(1)} async-done(((bf16[8,64,128]{2,1,0:T(8,128)(2,1)}), bf16[8,64,128]{2,1,0:T(8,128)(2,1)S(1)}, u32[]{:S(2)}, u32[]{:S(2)}) %all-to-all-start.2) | async-done | bytes 131104 | tf_op jit(solution)/shard_map/all_to_all | solution.py:391
  47.7 3.4 %all-to-all-start.1 = ((bf16[8,128,128]{2,1,0:T(8,128)(2,1)}), bf16[8,128,128]{2,1,0:T(8,128)(2,1)S(1)}, u32[]{:S(2)}, u32[]{:S(2)}) async-start(bf16[8,128,128]{2,1,0:T(8,128)(2,1)} %add.1), calls=%async_computation.1 | async-start | bytes 524288 | tf_op jit(solution)/shard_map/all_to_all | solution.py:391
  51.1 1.6 %update.1 = (f32[128,128]{1,0:T(8,128)S(1)}, bf16[128,128]{1,0:T(8,128)(2,1)S(1)}, bf16[128,128]{1,0:T(8,128)(2,1)S(1)}, bf16[128,128]{1,0:T(8,128)(2,1)S(1)}) custom-call(s32[1,16]{1,0:T(1,128)} %group_ref.3, s32[1,128]{1,0:T(1,128)} %bitcast.15, s32[1,128]{1,0:T(1,128)S(1)} %bitcast.11, bf16[8,64,128]{2,1,0:T(8,128)(2,1)S(1)} %all-to-all-done.2.codes_ref, ...), custom_call_target="tpu_custom_call" | custom-call | tf_op jit(solution)/shard_map/update/pallas_call | solution.py:400
  52.8 2.2 %collective-permute-start.6 = (bf16[128,128]{1,0:T(8,128)(2,1)S(1)}, bf16[128,128]{1,0:T(8,128)(2,1)S(1)}, u32[]{:S(2)}, u32[]{:S(2)}) collective-permute-start(bf16[128,128]{1,0:T(8,128)(2,1)S(1)} %get-tuple-element.37), channel_id=1, source_target_pairs={{0,2},{1,3},{2,0},{3,1},{4,6},{5,7},{6,4},{7,5},{8,10},{9,11},{10,... | collective-permute-start | bytes 98312 | tf_op jit(solution)/shard_map/ppermute | solution.py:410
  55.0 2.0 %collective-permute-start.7 = (bf16[128,128]{1,0:T(8,128)(2,1)S(1)}, bf16[128,128]{1,0:T(8,128)(2,1)S(1)}, u32[]{:S(2)}, u32[]{:S(2)}) collective-permute-start(bf16[128,128]{1,0:T(8,128)(2,1)S(1)} %get-tuple-element.38), channel_id=1, source_target_pairs={{0,3},{1,0},{2,1},{3,2},{4,7},{5,4},{6,5},{7,6},{8,11},{9,8},{10,9... | collective-permute-start | bytes 98312 | tf_op jit(solution)/shard_map/ppermute | solution.py:410
  57.0 0.9 %collective-permute-done.5.rest_0_ = bf16[128,128]{1,0:T(8,128)(2,1)S(1)} collective-permute-done((bf16[128,128]{1,0:T(8,128)(2,1)S(1)}, bf16[128,128]{1,0:T(8,128)(2,1)S(1)}, u32[]{:S(2)}, u32[]{:S(2)}) %collective-permute-start.5) | collective-permute-done | bytes 32800 | tf_op jit(solution)/shard_map/ppermute | solution.py:410
  57.9 0.4 collective-permute-done.6.rest_1_
  58.3 0.8 %collective-permute-done.7.rest_2_ = bf16[128,128]{1,0:T(8,128)(2,1)S(1)} collective-permute-done((bf16[128,128]{1,0:T(8,128)(2,1)S(1)}, bf16[128,128]{1,0:T(8,128)(2,1)S(1)}, u32[]{:S(2)}, u32[]{:S(2)}) %collective-permute-start.7) | collective-permute-done | bytes 32800 | tf_op jit(solution)/shard_map/ppermute | solution.py:410
  59.1 3.0 %all-to-all-done.1.parts_ref = bf16[8,128,128]{2,1,0:T(8,128)(2,1)S(1)} async-done(((bf16[8,128,128]{2,1,0:T(8,128)(2,1)}), bf16[8,128,128]{2,1,0:T(8,128)(2,1)S(1)}, u32[]{:S(2)}, u32[]{:S(2)}) %all-to-all-start.1) | async-done | bytes 262176 | tf_op jit(solution)/shard_map/all_to_all | solution.py:391
  62.1 0.7 %final.1 = bf16[128,128]{1,0:T(8,128)(2,1)} custom-call(bf16[8,128,128]{2,1,0:T(8,128)(2,1)S(1)} %all-to-all-done.1.parts_ref, f32[128,128]{1,0:T(8,128)S(1)} %get-tuple-element.35.own_ref, bf16[128,128]{1,0:T(8,128)(2,1)S(1)} %collective-permute-done.5.rest_0_, bf16[128,128]{1,0:T(8,128)(2,1)S(1)} %collective-permute-done.6.rest_1_, ...), custom_call_target="tpu_custom_call" | custom-call | tf_op jit(solution)/shard_map/final/pallas_call | solution.py:423
  (16 shorter events, 0.1 us)
Async XLA Ops:
  0.0 5.8 %copy-start.1 = (bf16[8,512,2,128]{3,2,1,0:T(2,128)(2,1)S(1)}, bf16[8,512,2,128]{3,2,1,0:T(2,128)(2,1)}, u32[]{:S(2)}) copy-start(bf16[8,512,2,128]{3,2,1,0:T(2,128)(2,1)} %param.12) | copy-start | bytes 6291460
  0.0 5.8 %copy-start.3 = (bf16[8,2,128]{2,1,0:T(2,128)(2,1)S(1)}, bf16[8,2,128]{2,1,0:T(2,128)(2,1)}, u32[]{:S(2)}) copy-start(bf16[8,2,128]{2,1,0:T(2,128)(2,1)} %key_ref.1) | copy-start | bytes 12292
  0.0 5.8 %copy-start.4 = (bf16[8,2,128]{2,1,0:T(2,128)(2,1)S(1)}, bf16[8,2,128]{2,1,0:T(2,128)(2,1)}, u32[]{:S(2)}) copy-start(bf16[8,2,128]{2,1,0:T(2,128)(2,1)} %value_ref.1) | copy-start | bytes 12292
  2.5 25.3 %collective-permute-start = (bf16[128,2048]{1,0:T(8,128)(2,1)S(1)}, bf16[128,2048]{1,0:T(8,128)(2,1)S(1)}, u32[]{:S(2)}, u32[]{:S(2)}) collective-permute-start(bf16[128,2048]{1,0:T(8,128)(2,1)S(1)} %get-tuple-element.25), channel_id=1, source_target_pairs={{0,1},{1,2},{2,3},{3,0},{4,5},{5,6},{6,7},{7,4},{8,9},{9,10},{10,1... | collective-permute-start | bytes 1572872 | tf_op jit(solution)/shard_map/ppermute | solution.py:328
  4.0 23.8 %collective-permute-start.1 = (bf16[128,2048]{1,0:T(8,128)(2,1)S(1)}, bf16[128,2048]{1,0:T(8,128)(2,1)S(1)}, u32[]{:S(2)}, u32[]{:S(2)}) collective-permute-start(bf16[128,2048]{1,0:T(8,128)(2,1)S(1)} %get-tuple-element.26), channel_id=1, source_target_pairs={{0,3},{1,0},{2,1},{3,2},{4,7},{5,4},{6,5},{7,6},{8,11},{9,8},{10,9... | collective-permute-start | bytes 1572872 | tf_op jit(solution)/shard_map/ppermute | solution.py:329
  5.8 22.0 %copy-start = (bf16[32,8,64,64]{3,2,1,0:T(8,128)(2,1)S(1)}, bf16[32,8,64,64]{3,2,1,0:T(8,128)(2,1)}, u32[]{:S(2)}) copy-start(bf16[32,8,64,64]{3,2,1,0:T(8,128)(2,1)} %down_ref.1) | copy-start | bytes 6291460
  5.8 22.0 %copy-start.5 = (s32[128]{0:T(128)S(1)}, s32[128]{0:T(128)}, u32[]{:S(2)}) copy-start(s32[128]{0:T(128)} %param.21) | copy-start | bytes 1540
  30.0 21.2 %copy-start.2 = (bf16[32,64,512]{2,1,0:T(8,128)(2,1)S(1)}, bf16[32,64,512]{2,1,0:T(8,128)(2,1)}, u32[]{:S(2)}) copy-start(bf16[32,64,512]{2,1,0:T(8,128)(2,1)} %up_ref.1) | copy-start | bytes 6291460
  30.0 1.6 %collective-permute-start.2 = (bf16[1088,128]{1,0:T(8,128)(2,1)S(1)}, bf16[1088,128]{1,0:T(8,128)(2,1)S(1)}, u32[]{:S(2)}, u32[]{:S(2)}) collective-permute-start(bf16[1088,128]{1,0:T(8,128)(2,1)S(1)} %get-tuple-element.29), channel_id=1, source_target_pairs={{0,4},{4,0},{8,12},{12,8},{16,20},{20,16},{24,28},{28,24},{32,36},... | collective-permute-start | bytes 835592 | tf_op jit(solution)/shard_map/ppermute | solution.py:377
  32.3 5.8 %collective-permute-start.3 = (bf16[8,128,128]{2,1,0:T(8,128)(2,1)S(1)}, bf16[8,128,128]{2,1,0:T(8,128)(2,1)S(1)}, u32[]{:S(2)}, u32[]{:S(2)}) collective-permute-start(bf16[8,128,128]{2,1,0:T(8,128)(2,1)S(1)} %get-tuple-element.32), channel_id=1, source_target_pairs={{0,4},{4,0},{8,12},{12,8},{16,20},{20,16},{24,28},{28,24},{32,36},... | collective-permute-start | bytes 786440 | tf_op jit(solution)/shard_map/ppermute | solution.py:398
  32.6 10.1 %collective-permute-start.4 = (bf16[8,128,128]{2,1,0:T(8,128)(2,1)S(1)}, bf16[8,128,128]{2,1,0:T(8,128)(2,1)S(1)}, u32[]{:S(2)}, u32[]{:S(2)}) collective-permute-start(bf16[8,128,128]{2,1,0:T(8,128)(2,1)S(1)} %get-tuple-element.33), channel_id=1, source_target_pairs={{0,2},{1,3},{2,0},{3,1},{4,6},{5,7},{6,4},{7,5},{8,10},{9,11},{10,... | collective-permute-start | bytes 786440 | tf_op jit(solution)/shard_map/ppermute | solution.py:396
  34.8 12.9 %all-to-all-start.2 = ((bf16[8,64,128]{2,1,0:T(8,128)(2,1)}), bf16[8,64,128]{2,1,0:T(8,128)(2,1)S(1)}, u32[]{:S(2)}, u32[]{:S(2)}) async-start(bf16[8,64,128]{2,1,0:T(8,128)(2,1)} %get-tuple-element.34), calls=%async_computation.2 | async-start | bytes 262144 | tf_op jit(solution)/shard_map/all_to_all | solution.py:391
  47.7 14.4 %all-to-all-start.1 = ((bf16[8,128,128]{2,1,0:T(8,128)(2,1)}), bf16[8,128,128]{2,1,0:T(8,128)(2,1)S(1)}, u32[]{:S(2)}, u32[]{:S(2)}) async-start(bf16[8,128,128]{2,1,0:T(8,128)(2,1)} %add.1), calls=%async_computation.1 | async-start | bytes 524288 | tf_op jit(solution)/shard_map/all_to_all | solution.py:391
  52.7 5.2 %collective-permute-start.5 = (bf16[128,128]{1,0:T(8,128)(2,1)S(1)}, bf16[128,128]{1,0:T(8,128)(2,1)S(1)}, u32[]{:S(2)}, u32[]{:S(2)}) collective-permute-start(bf16[128,128]{1,0:T(8,128)(2,1)S(1)} %get-tuple-element.36), channel_id=1, source_target_pairs={{0,1},{1,2},{2,3},{3,0},{4,5},{5,6},{6,7},{7,4},{8,9},{9,10},{10,1... | collective-permute-start | bytes 98312 | tf_op jit(solution)/shard_map/ppermute | solution.py:410
  52.8 5.5 %collective-permute-start.6 = (bf16[128,128]{1,0:T(8,128)(2,1)S(1)}, bf16[128,128]{1,0:T(8,128)(2,1)S(1)}, u32[]{:S(2)}, u32[]{:S(2)}) collective-permute-start(bf16[128,128]{1,0:T(8,128)(2,1)S(1)} %get-tuple-element.37), channel_id=1, source_target_pairs={{0,2},{1,3},{2,0},{3,1},{4,6},{5,7},{6,4},{7,5},{8,10},{9,11},{10,... | collective-permute-start | bytes 98312 | tf_op jit(solution)/shard_map/ppermute | solution.py:410
  55.0 4.1 %collective-permute-start.7 = (bf16[128,128]{1,0:T(8,128)(2,1)S(1)}, bf16[128,128]{1,0:T(8,128)(2,1)S(1)}, u32[]{:S(2)}, u32[]{:S(2)}) collective-permute-start(bf16[128,128]{1,0:T(8,128)(2,1)S(1)} %get-tuple-element.38), channel_id=1, source_target_pairs={{0,3},{1,0},{2,1},{3,2},{4,7},{5,4},{6,5},{7,6},{8,11},{9,8},{10,9... | collective-permute-start | bytes 98312 | tf_op jit(solution)/shard_map/ppermute | solution.py:410

commit v12 on v8

--- a/solution.py
+++ b/solution.py
@@ -135,10 +135,27 @@
                 out_ref[o, 2 * g + i] = part
 
 
+def across_kernel(att_ref, w_ref, keep_ref, send_ref):
+    owners = att_ref.shape[0]
+    owner = lax.axis_index("owner")
+    target = lax.rem(owner + 2, owners)
+    mine = att_ref[owner]
+    first = lax.rem(lax.axis_index("tensor"), 2) == 0
+    planes, _, block = keep_ref.shape
+    for z in range(planes):
+        at = [pl.multiple_of(((2 * z + c) * owners + target) * block, block) for c in range(2)]
+        columns = jnp.concatenate([w_ref[:, pl.ds(a, block)] for a in at], axis=1)
+        part = jnp.dot(mine, columns, preferred_element_type=F32)
+        even, odd = part[:, :block], part[:, block:]
+        keep_ref[z] = jnp.where(first, even, odd)
+        send_ref[z] = jnp.where(first, odd, even).astype(BF16)
+
+
 def project_kernel(
     group_ref,
     store_ref,
     rows_ref,
+    order_ref,
     att_ref,
     w_ref,
     before_ref,
@@ -151,6 +168,7 @@
     store,
     index_sems,
 ):
+    del order_ref
     indices = index_copies(group_ref, store_ref, group, store, index_sems)
     slots = group.shape[1]
     stored, _, _, rank = down_ref.shape
@@ -164,7 +182,6 @@
     block = keep_ref.shape[1]
     planes = before_ref.shape[1] // (2 * block)
 
-    across = lax.rem(owner + 2, owners)
 
     def columns(z, target):
         at = [pl.multiple_of(((2 * z + c) * owners + target) * block, block) for c in range(2)]
@@ -175,12 +192,10 @@
         near_rows = jnp.concatenate([before_ref[:, span], after_ref[:, span]], axis=0)
         here = jnp.dot(beside, near_rows, preferred_element_type=F32)
         here = here + jnp.dot(mine, columns(z, owner), preferred_element_type=F32)
-        there = jnp.dot(mine, columns(z, across), preferred_element_type=F32)
-        for i, part in enumerate((here, there)):
-            even, odd = part[:, :block], part[:, block:]
-            rows_span = pl.ds((2 * z + i) * rows, rows)
-            keep_ref[rows_span, :] = jnp.where(first, even, odd)
-            send_ref[rows_span, :] = jnp.where(first, odd, even).astype(BF16)
+        even, odd = here[:, :block], here[:, block:]
+        span = pl.ds(z * rows, rows)
+        keep_ref[span, :] = jnp.where(first, even, odd)
+        send_ref[span, :] = jnp.where(first, odd, even).astype(BF16)
     att = jnp.concatenate([att_ref[o] for o in range(owners)], axis=1)
     ids = row_adapters(rows_ref, rank)
     acc[...] = jnp.zeros_like(acc)
@@ -197,18 +212,20 @@
 
     half = rows // 2
     code = jnp.concatenate([acc[:half, :], acc[half:, :]], axis=1)
-    keep_ref[2 * planes * rows :, :] = code
-    send_ref[2 * planes * rows :, :] = code.astype(BF16)
-
-
-def pair_kernel(keep_ref, got_ref, own_ref, across_ref, codes_ref):
+    keep_ref[planes * rows :, :] = code
+    send_ref[planes * rows :, :] = code.astype(BF16)
+
+
+def pair_across_kernel(keep_ref, got_ref, out_ref):
+    out_ref[...] = (keep_ref[...] + got_ref[...].astype(F32)).astype(BF16)
+
+
+def pair_kernel(keep_ref, got_ref, own_ref, codes_ref):
     planes, rows, _ = own_ref.shape
     for z in range(planes):
-        span = pl.ds(2 * z * rows, rows)
+        span = pl.ds(z * rows, rows)
         own_ref[z] = keep_ref[span, :] + got_ref[span, :].astype(F32)
-        span = pl.ds((2 * z + 1) * rows, rows)
-        across_ref[z] = (keep_ref[span, :] + got_ref[span, :].astype(F32)).astype(BF16)
-    span = pl.ds(2 * planes * rows, codes_ref.shape[1])
+    span = pl.ds(planes * rows, codes_ref.shape[1])
     code = (keep_ref[span, :] + got_ref[span, :].astype(F32)).astype(BF16)
     for z in range(planes):
         codes_ref[z] = code
@@ -339,12 +356,24 @@
     )
     attention = attention.reshape(owners, rows, feats)
 
-    tall = 2 * planes * rows + rows // 2
+    swap = [(t, t ^ 1) for t in range(tensors)]
+    attention = near(attention)
+    kept, sent = pltpu.VMEM((planes, rows, block), F32), pltpu.VMEM((planes, rows, block), BF16)
+    keep_across, send_across = pl.pallas_call(
+        across_kernel,
+        name="across",
+        out_shape=(kept, sent),
+        in_specs=[VMEM, VMEM],
+        out_specs=(VMEM, VMEM),
+        compiler_params=LIMIT,
+    )(attention, near(weight))
+    got_across = lax.ppermute(send_across, "tensor", swap)
+    tall = planes * rows + rows // 2
     keep, send = pl.pallas_call(
         project_kernel,
         name="project",
         out_shape=(pltpu.VMEM((tall, block), F32), pltpu.VMEM((tall, block), BF16)),
-        in_specs=[HBM, HBM] + [VMEM] * 6,
+        in_specs=[HBM, HBM] + [VMEM] * 7,
         out_specs=(VMEM, VMEM),
         scratch_shapes=[pltpu.VMEM((rows, rank), F32)] + indices,
         compiler_params=LIMIT,
@@ -352,23 +381,28 @@
         group,
         store,
         row_ids,
-        near(attention),
+        near(send_across),
+        attention,
         near(weight),
         near(before),
         near(after),
         near(adapter_down_weight),
     )
-    got = lax.ppermute(send, "tensor", [(t, t ^ 1) for t in range(tensors)])
-    own_part, across, codes = pl.pallas_call(
+    got = lax.ppermute(send, "tensor", swap)
+    across = pl.pallas_call(
+        pair_across_kernel,
+        name="pair_across",
+        out_shape=sent,
+        in_specs=[VMEM, VMEM],
+        out_specs=VMEM,
+        compiler_params=LIMIT,
+    )(near(keep_across), near(got_across))
+    own_part, codes = pl.pallas_call(
         pair_kernel,
         name="pair",
-        out_shape=(
-            pltpu.VMEM((planes, rows, block), F32),
-            pltpu.VMEM((planes, rows, block), BF16),
-            pltpu.VMEM((planes, rows // 2, 2 * rank), BF16),
-        ),
+        out_shape=(kept, pltpu.VMEM((planes, rows // 2, 2 * rank), BF16)),
         in_specs=[VMEM, VMEM],
-        out_specs=(VMEM, VMEM, VMEM),
+        out_specs=(VMEM, VMEM),
         compiler_params=LIMIT,
     )(near(keep), near(got))
     groups = [[2 * z + c for z in range(planes)] for c in range(2)]

time: 62.6 us -> 61.3 us (0.979)
  waiting for transfers between devices: 15 us -> 13.1 us
  starting transfers between devices: 16.4 us -> 17.3 us
    ppermute x1 -> x2, waiting for transfers between devices: 1.82 us -> 0.01 us  [the longest x1 0.01 us: shards(): got_across = lax.ppermute(send_across, 'tensor', swap)]
    all_to_all x2, waiting for transfers between devices: 5.53 us -> 7.18 us  [over_z(): lax.all_to_all(pieces, 'tensor', split_axis=0, concat_axis=0, tiled=True,...]
    ppermute x1, waiting for transfers between devices: 4.76 us -> 3.71 us  [shards(): lax.ppermute(across, 'owner', [(o, (o + 2) % owners) for o in range(owner...]
    ppermute x3, waiting for transfers between devices: 2.87 us -> 2.17 us  [shards(): lax.ppermute(update, 'owner', [(o, (o + i + 1) % owners) for o in range(o...]
  transfers between devices with their start and end apart: 9 -> 10, of which waited for: 7 -> 6; matrix products, arithmetic and copies ran while one was open for 0% -> 0% of each run, Pallas kernels for 5% -> 10%
where the time goes in v12:
time: 61.3 us; the launch traced here: 60.9 us
  blocking collectives  21 us (34%)
  starting transfers between devices  17.3 us (28%)
  waiting for transfers between devices  13.1 us (21%)
  Pallas kernels  9.43 us (15%)
    all_to_all x1, blocking collectives, shards(): lax.all_to_all(outgoing, ('owner', 'tensor'), split_axis=0, concat_axis=0...  21 us
    all_to_all x2, waiting for transfers between devices, over_z(): lax.all_to_all(pieces, 'tensor', split_axis=0, concat_axis=0, tiled=True,...  7.18 us
    all_to_all x2, starting transfers between devices, over_z(): lax.all_to_all(pieces, 'tensor', split_axis=0, concat_axis=0, tiled=True,...  6.78 us
    ppermute x3, starting transfers between devices, shards(): lax.ppermute(update, 'owner', [(o, (o + i + 1) % owners) for o in range(o...  4.43 us
    ppermute x1, waiting for transfers between devices, shards(): lax.ppermute(across, 'owner', [(o, (o + 2) % owners) for o in range(owner...  3.71 us
    pallas_call x1, Pallas kernels, shards(): pl.pallas_call(slab_kernel, name='slabs', out_shape=(pltpu.VMEM((feats, c...  2.44 us
    ppermute x3, waiting for transfers between devices, shards(): lax.ppermute(update, 'owner', [(o, (o + i + 1) % owners) for o in range(o...  2.17 us
    ppermute x1, starting transfers between devices, shards(): lax.ppermute(across, 'owner', [(o, (o + 2) % owners) for o in range(owner...  2.12 us
  transfers between devices with their start and end apart: 10, of which 6 were waited for; matrix products, arithmetic and copies ran while one was open for 0% of the time, Pallas kernels for 10%

profile of v12, /device:TPU:24, one launch (start us, length us, event | category | flops | bytes accessed | tf_op | source)
XLA Modules:
  0.0 60.9 jit_solution(12504173448688553125)
XLA Ops:
  0.0 2.4 %slabs.1 = (bf16[128,8192]{1,0:T(8,128)(2,1)S(1)}, bf16[8,2048]{1,0:T(8,128)(2,1)S(1)}, bf16[8,1024,128]{2,1,0:T(8,128)(2,1)S(1)}, bf16[128,2048]{1,0:T(8,128)(2,1)S(1)}, bf16[128,2048]{1,0:T(8,128)(2,1)S(1)}) custom-call(bf16[128,8192]{1,0:T(8,128)(2,1)} %bitcast.13, bf16[8,2048]{1,0:T(8,128)(2,1)} %queries_hbm_ref.1, bf16[8,1024,128]{2,1,0:T(8,128)(2,1)} %bitcast.14), custom_call_target="tpu_custom_call" | custom-call | tf_op jit(solution)/shard_map/slabs/pallas_call | solution.py:314
  2.5 1.6 %collective-permute-start = (bf16[128,2048]{1,0:T(8,128)(2,1)S(1)}, bf16[128,2048]{1,0:T(8,128)(2,1)S(1)}, u32[]{:S(2)}, u32[]{:S(2)}) collective-permute-start(bf16[128,2048]{1,0:T(8,128)(2,1)S(1)} %get-tuple-element.24), channel_id=1, source_target_pairs={{0,1},{1,2},{2,3},{3,0},{4,5},{5,6},{6,7},{7,4},{8,9},{9,10},{10,1... | collective-permute-start | bytes 1572872 | tf_op jit(solution)/shard_map/ppermute | solution.py:336
  4.0 1.7 %collective-permute-start.1 = (bf16[128,2048]{1,0:T(8,128)(2,1)S(1)}, bf16[128,2048]{1,0:T(8,128)(2,1)S(1)}, u32[]{:S(2)}, u32[]{:S(2)}) collective-permute-start(bf16[128,2048]{1,0:T(8,128)(2,1)S(1)} %get-tuple-element.25), channel_id=1, source_target_pairs={{0,3},{1,0},{2,1},{3,2},{4,7},{5,4},{6,5},{7,6},{8,11},{9,8},{10,9... | collective-permute-start | bytes 1572872 | tf_op jit(solution)/shard_map/ppermute | solution.py:337
  5.8 1.0 %attend.1 = bf16[4,16,8,128]{3,2,1,0:T(8,128)(2,1)S(1)} custom-call(bf16[8,2048]{1,0:T(8,128)(2,1)S(1)} %get-tuple-element.20.queries_ref, bf16[8,1024,128]{2,1,0:T(8,128)(2,1)S(1)} %bitcast.7, bf16[8,1024,128]{2,1,0:T(8,128)(2,1)S(1)} %get-tuple-element.21.values_ref, bf16[8,2,128]{2,1,0:T(2,128)(2,1)S(1)} %copy-done.3, bf16[8,2,128]{2,1,0:T(2,128)(2,1)S(1)} %copy-done.4), custom_call_target="tpu_custom_call" | custom-call | tf_op jit(solution)/shard_map/attend/pallas_call | solution.py:339
  6.8 21.0 %all_to_all.15 = bf16[64,8,128]{2,1,0:T(8,128)(2,1)S(1)} all-to-all(bf16[64,8,128]{2,1,0:T(8,128)(2,1)S(1)} %bitcast.10), channel_id=1, replica_groups=mesh['dp'=4,'tensor'=16,'owner'=4] {'owner','tensor'}, dimensions={0} | all-to-all | bytes 262144 | tf_op jit(solution)/shard_map/all_to_all | solution.py:354
  27.8 0.3 across.1
  28.4 1.9 %project.1 = (f32[1088,128]{1,0:T(8,128)S(1)}, bf16[1088,128]{1,0:T(8,128)(2,1)S(1)}) custom-call(s32[1,16]{1,0:T(1,128)} %group_ref.3, s32[1,128]{1,0:T(1,128)} %bitcast.15, s32[1,128]{1,0:T(1,128)S(1)} %bitcast.11, bf16[8,128,128]{2,1,0:T(8,128)(2,1)S(1)} %get-tuple-element.23.order_ref, bf16[4,128,128]{2,1,0:T(8,128)(2,1)S(1)} %bitcast.9, ...), custom_call_target="tpu_custom_call" | custom-call | tf_op jit(solution)/shard_map/project/pallas_call | solution.py:372
  30.3 0.5 collective-permute-start.2
  30.8 2.1 %collective-permute-start.4 = (bf16[8,128,128]{2,1,0:T(8,128)(2,1)S(1)}, bf16[8,128,128]{2,1,0:T(8,128)(2,1)S(1)}, u32[]{:S(2)}, u32[]{:S(2)}) collective-permute-start(bf16[8,128,128]{2,1,0:T(8,128)(2,1)S(1)} %pair_across.1), channel_id=1, source_target_pairs={{0,2},{1,3},{2,0},{3,1},{4,6},{5,7},{6,4},{7,5},{8,10},{9,11},{10,... | collective-permute-start | bytes 786440 | tf_op jit(solution)/shard_map/ppermute | solution.py:415
  32.9 0.7 %pair.1 = (f32[8,128,128]{2,1,0:T(8,128)S(1)}, bf16[8,64,128]{2,1,0:T(8,128)(2,1)}) custom-call(f32[1088,128]{1,0:T(8,128)S(1)} %get-tuple-element.26.keep_ref, bf16[1088,128]{1,0:T(8,128)(2,1)S(1)} %collective-permute-done.2.got_ref), custom_call_target="tpu_custom_call" | custom-call | tf_op jit(solution)/shard_map/pair/pallas_call | solution.py:400
  33.6 3.4 %all-to-all-start.2 = ((bf16[8,64,128]{2,1,0:T(8,128)(2,1)}), bf16[8,64,128]{2,1,0:T(8,128)(2,1)S(1)}, u32[]{:S(2)}, u32[]{:S(2)}) async-start(bf16[8,64,128]{2,1,0:T(8,128)(2,1)} %get-tuple-element.30), calls=%async_computation.2 | async-start | bytes 262144 | tf_op jit(solution)/shard_map/all_to_all | solution.py:411
  37.0 3.7 %collective-permute-done.4.two_ref = bf16[8,128,128]{2,1,0:T(8,128)(2,1)S(1)} collective-permute-done((bf16[8,128,128]{2,1,0:T(8,128)(2,1)S(1)}, bf16[8,128,128]{2,1,0:T(8,128)(2,1)S(1)}, u32[]{:S(2)}, u32[]{:S(2)}) %collective-permute-start.4) | collective-permute-done | bytes 262176 | tf_op jit(solution)/shard_map/ppermute | solution.py:415
  40.7 0.7 %add.1 = bf16[8,128,128]{2,1,0:T(8,128)(2,1)} custom-call(f32[8,128,128]{2,1,0:T(8,128)S(1)} %get-tuple-element.28.one_ref, bf16[8,128,128]{2,1,0:T(8,128)(2,1)S(1)} %collective-permute-done.4.two_ref), custom_call_target="tpu_custom_call" | custom-call | tf_op jit(solution)/shard_map/add/pallas_call | solution.py:432
  41.5 4.8 %all-to-all-done.2.codes_ref = bf16[8,64,128]{2,1,0:T(8,128)(2,1)S(1)} async-done(((bf16[8,64,128]{2,1,0:T(8,128)(2,1)}), bf16[8,64,128]{2,1,0:T(8,128)(2,1)S(1)}, u32[]{:S(2)}, u32[]{:S(2)}) %all-to-all-start.2) | async-done | bytes 131104 | tf_op jit(solution)/shard_map/all_to_all | solution.py:411
  46.3 3.4 %all-to-all-start.1 = ((bf16[8,128,128]{2,1,0:T(8,128)(2,1)}), bf16[8,128,128]{2,1,0:T(8,128)(2,1)S(1)}, u32[]{:S(2)}, u32[]{:S(2)}) async-start(bf16[8,128,128]{2,1,0:T(8,128)(2,1)} %add.1), calls=%async_computation.1 | async-start | bytes 524288 | tf_op jit(solution)/shard_map/all_to_all | solution.py:411
  49.7 1.6 %update.1 = (f32[128,128]{1,0:T(8,128)S(1)}, bf16[128,128]{1,0:T(8,128)(2,1)S(1)}, bf16[128,128]{1,0:T(8,128)(2,1)S(1)}, bf16[128,128]{1,0:T(8,128)(2,1)S(1)}) custom-call(s32[1,16]{1,0:T(1,128)} %group_ref.3, s32[1,128]{1,0:T(1,128)} %bitcast.16, s32[1,128]{1,0:T(1,128)S(1)} %bitcast.12, bf16[8,64,128]{2,1,0:T(8,128)(2,1)S(1)} %all-to-all-done.2.codes_ref, ...), custom_call_target="tpu_custom_call" | custom-call | tf_op jit(solution)/shard_map/update/pallas_call | solution.py:418
  51.3 0.9 %collective-permute-start.5 = (bf16[128,128]{1,0:T(8,128)(2,1)S(1)}, bf16[128,128]{1,0:T(8,128)(2,1)S(1)}, u32[]{:S(2)}, u32[]{:S(2)}) collective-permute-start(bf16[128,128]{1,0:T(8,128)(2,1)S(1)} %get-tuple-element.32), channel_id=1, source_target_pairs={{0,1},{1,2},{2,3},{3,0},{4,5},{5,6},{6,7},{7,4},{8,9},{9,10},{10,1... | collective-permute-start | bytes 98312 | tf_op jit(solution)/shard_map/ppermute | solution.py:428
  52.2 1.8 %collective-permute-start.6 = (bf16[128,128]{1,0:T(8,128)(2,1)S(1)}, bf16[128,128]{1,0:T(8,128)(2,1)S(1)}, u32[]{:S(2)}, u32[]{:S(2)}) collective-permute-start(bf16[128,128]{1,0:T(8,128)(2,1)S(1)} %get-tuple-element.33), channel_id=1, source_target_pairs={{0,2},{1,3},{2,0},{3,1},{4,6},{5,7},{6,4},{7,5},{8,10},{9,11},{10,... | collective-permute-start | bytes 98312 | tf_op jit(solution)/shard_map/ppermute | solution.py:428
  54.0 1.7 %collective-permute-start.7 = (bf16[128,128]{1,0:T(8,128)(2,1)S(1)}, bf16[128,128]{1,0:T(8,128)(2,1)S(1)}, u32[]{:S(2)}, u32[]{:S(2)}) collective-permute-start(bf16[128,128]{1,0:T(8,128)(2,1)S(1)} %get-tuple-element.34), channel_id=1, source_target_pairs={{0,3},{1,0},{2,1},{3,2},{4,7},{5,4},{6,5},{7,6},{8,11},{9,8},{10,9... | collective-permute-start | bytes 98312 | tf_op jit(solution)/shard_map/ppermute | solution.py:428
  55.7 0.8 %collective-permute-done.5.rest_0_ = bf16[128,128]{1,0:T(8,128)(2,1)S(1)} collective-permute-done((bf16[128,128]{1,0:T(8,128)(2,1)S(1)}, bf16[128,128]{1,0:T(8,128)(2,1)S(1)}, u32[]{:S(2)}, u32[]{:S(2)}) %collective-permute-start.5) | collective-permute-done | bytes 32800 | tf_op jit(solution)/shard_map/ppermute | solution.py:428
  56.5 1.1 %collective-permute-done.6.rest_1_ = bf16[128,128]{1,0:T(8,128)(2,1)S(1)} collective-permute-done((bf16[128,128]{1,0:T(8,128)(2,1)S(1)}, bf16[128,128]{1,0:T(8,128)(2,1)S(1)}, u32[]{:S(2)}, u32[]{:S(2)}) %collective-permute-start.6) | collective-permute-done | bytes 32800 | tf_op jit(solution)/shard_map/ppermute | solution.py:428
  57.6 0.3 collective-permute-done.7.rest_2_
  57.9 2.4 %all-to-all-done.1.parts_ref = bf16[8,128,128]{2,1,0:T(8,128)(2,1)S(1)} async-done(((bf16[8,128,128]{2,1,0:T(8,128)(2,1)}), bf16[8,128,128]{2,1,0:T(8,128)(2,1)S(1)}, u32[]{:S(2)}, u32[]{:S(2)}) %all-to-all-start.1) | async-done | bytes 262176 | tf_op jit(solution)/shard_map/all_to_all | solution.py:411
  60.3 0.7 %final.1 = bf16[128,128]{1,0:T(8,128)(2,1)} custom-call(bf16[8,128,128]{2,1,0:T(8,128)(2,1)S(1)} %all-to-all-done.1.parts_ref, f32[128,128]{1,0:T(8,128)S(1)} %get-tuple-element.31.own_ref, bf16[128,128]{1,0:T(8,128)(2,1)S(1)} %collective-permute-done.5.rest_0_, bf16[128,128]{1,0:T(8,128)(2,1)S(1)} %collective-permute-done.6.rest_1_, ...), custom_call_target="tpu_custom_call" | custom-call | tf_op jit(solution)/shard_map/final/pallas_call | solution.py:441
  (18 shorter events, 0.3 us)
Async XLA Ops:
  0.0 5.8 %copy-start.1 = (bf16[8,512,2,128]{3,2,1,0:T(2,128)(2,1)S(1)}, bf16[8,512,2,128]{3,2,1,0:T(2,128)(2,1)}, u32[]{:S(2)}) copy-start(bf16[8,512,2,128]{3,2,1,0:T(2,128)(2,1)} %param.12) | copy-start | bytes 6291460
  0.0 5.8 %copy-start.3 = (bf16[8,2,128]{2,1,0:T(2,128)(2,1)S(1)}, bf16[8,2,128]{2,1,0:T(2,128)(2,1)}, u32[]{:S(2)}) copy-start(bf16[8,2,128]{2,1,0:T(2,128)(2,1)} %key_ref.1) | copy-start | bytes 12292
  0.0 5.8 %copy-start.4 = (bf16[8,2,128]{2,1,0:T(2,128)(2,1)S(1)}, bf16[8,2,128]{2,1,0:T(2,128)(2,1)}, u32[]{:S(2)}) copy-start(bf16[8,2,128]{2,1,0:T(2,128)(2,1)} %value_ref.1) | copy-start | bytes 12292
  2.5 25.9 %collective-permute-start = (bf16[128,2048]{1,0:T(8,128)(2,1)S(1)}, bf16[128,2048]{1,0:T(8,128)(2,1)S(1)}, u32[]{:S(2)}, u32[]{:S(2)}) collective-permute-start(bf16[128,2048]{1,0:T(8,128)(2,1)S(1)} %get-tuple-element.24), channel_id=1, source_target_pairs={{0,1},{1,2},{2,3},{3,0},{4,5},{5,6},{6,7},{7,4},{8,9},{9,10},{10,1... | collective-permute-start | bytes 1572872 | tf_op jit(solution)/shard_map/ppermute | solution.py:336
  4.0 24.3 %collective-permute-start.1 = (bf16[128,2048]{1,0:T(8,128)(2,1)S(1)}, bf16[128,2048]{1,0:T(8,128)(2,1)S(1)}, u32[]{:S(2)}, u32[]{:S(2)}) collective-permute-start(bf16[128,2048]{1,0:T(8,128)(2,1)S(1)} %get-tuple-element.25), channel_id=1, source_target_pairs={{0,3},{1,0},{2,1},{3,2},{4,7},{5,4},{6,5},{7,6},{8,11},{9,8},{10,9... | collective-permute-start | bytes 1572872 | tf_op jit(solution)/shard_map/ppermute | solution.py:337
  5.8 22.6 %copy-start = (bf16[32,8,64,64]{3,2,1,0:T(8,128)(2,1)S(1)}, bf16[32,8,64,64]{3,2,1,0:T(8,128)(2,1)}, u32[]{:S(2)}) copy-start(bf16[32,8,64,64]{3,2,1,0:T(8,128)(2,1)} %down_ref.1) | copy-start | bytes 6291460
  6.8 21.5 %copy-start.5 = (s32[128]{0:T(128)S(1)}, s32[128]{0:T(128)}, u32[]{:S(2)}) copy-start(s32[128]{0:T(128)} %param.21) | copy-start | bytes 1540
  28.1 2.6 %collective-permute-start.3 = (bf16[8,128,128]{2,1,0:T(8,128)(2,1)S(1)}, bf16[8,128,128]{2,1,0:T(8,128)(2,1)S(1)}, u32[]{:S(2)}, u32[]{:S(2)}) collective-permute-start(bf16[8,128,128]{2,1,0:T(8,128)(2,1)S(1)} %get-tuple-element.23.order_ref), channel_id=1, source_target_pairs={{0,4},{4,0},{8,12},{12,8},{16,20},{20,16},{24,28},{28,24},{32,36},... | collective-permute-start | bytes 786440 | tf_op jit(solution)/shard_map/ppermute | solution.py:370
  30.3 19.4 %copy-start.2 = (bf16[32,64,512]{2,1,0:T(8,128)(2,1)S(1)}, bf16[32,64,512]{2,1,0:T(8,128)(2,1)}, u32[]{:S(2)}) copy-start(bf16[32,64,512]{2,1,0:T(8,128)(2,1)} %up_ref.1) | copy-start | bytes 6291460
  30.3 2.7 %collective-permute-start.2 = (bf16[1088,128]{1,0:T(8,128)(2,1)S(1)}, bf16[1088,128]{1,0:T(8,128)(2,1)S(1)}, u32[]{:S(2)}, u32[]{:S(2)}) collective-permute-start(bf16[1088,128]{1,0:T(8,128)(2,1)S(1)} %get-tuple-element.27), channel_id=1, source_target_pairs={{0,4},{4,0},{8,12},{12,8},{16,20},{20,16},{24,28},{28,24},{32,36},... | collective-permute-start | bytes 835592 | tf_op jit(solution)/shard_map/ppermute | solution.py:391
  30.8 9.9 %collective-permute-start.4 = (bf16[8,128,128]{2,1,0:T(8,128)(2,1)S(1)}, bf16[8,128,128]{2,1,0:T(8,128)(2,1)S(1)}, u32[]{:S(2)}, u32[]{:S(2)}) collective-permute-start(bf16[8,128,128]{2,1,0:T(8,128)(2,1)S(1)} %pair_across.1), channel_id=1, source_target_pairs={{0,2},{1,3},{2,0},{3,1},{4,6},{5,7},{6,4},{7,5},{8,10},{9,11},{10,... | collective-permute-start | bytes 786440 | tf_op jit(solution)/shard_map/ppermute | solution.py:415
  33.6 12.6 %all-to-all-start.2 = ((bf16[8,64,128]{2,1,0:T(8,128)(2,1)}), bf16[8,64,128]{2,1,0:T(8,128)(2,1)S(1)}, u32[]{:S(2)}, u32[]{:S(2)}) async-start(bf16[8,64,128]{2,1,0:T(8,128)(2,1)} %get-tuple-element.30), calls=%async_computation.2 | async-start | bytes 262144 | tf_op jit(solution)/shard_map/all_to_all | solution.py:411
  46.3 14.0 %all-to-all-start.1 = ((bf16[8,128,128]{2,1,0:T(8,128)(2,1)}), bf16[8,128,128]{2,1,0:T(8,128)(2,1)S(1)}, u32[]{:S(2)}, u32[]{:S(2)}) async-start(bf16[8,128,128]{2,1,0:T(8,128)(2,1)} %add.1), calls=%async_computation.1 | async-start | bytes 524288 | tf_op jit(solution)/shard_map/all_to_all | solution.py:411
  51.3 5.2 %collective-permute-start.5 = (bf16[128,128]{1,0:T(8,128)(2,1)S(1)}, bf16[128,128]{1,0:T(8,128)(2,1)S(1)}, u32[]{:S(2)}, u32[]{:S(2)}) collective-permute-start(bf16[128,128]{1,0:T(8,128)(2,1)S(1)} %get-tuple-element.32), channel_id=1, source_target_pairs={{0,1},{1,2},{2,3},{3,0},{4,5},{5,6},{6,7},{7,4},{8,9},{9,10},{10,1... | collective-permute-start | bytes 98312 | tf_op jit(solution)/shard_map/ppermute | solution.py:428
  52.2 5.4 %collective-permute-start.6 = (bf16[128,128]{1,0:T(8,128)(2,1)S(1)}, bf16[128,128]{1,0:T(8,128)(2,1)S(1)}, u32[]{:S(2)}, u32[]{:S(2)}) collective-permute-start(bf16[128,128]{1,0:T(8,128)(2,1)S(1)} %get-tuple-element.33), channel_id=1, source_target_pairs={{0,2},{1,3},{2,0},{3,1},{4,6},{5,7},{6,4},{7,5},{8,10},{9,11},{10,... | collective-permute-start | bytes 98312 | tf_op jit(solution)/shard_map/ppermute | solution.py:428
  54.0 3.9 %collective-permute-start.7 = (bf16[128,128]{1,0:T(8,128)(2,1)S(1)}, bf16[128,128]{1,0:T(8,128)(2,1)S(1)}, u32[]{:S(2)}, u32[]{:S(2)}) collective-permute-start(bf16[128,128]{1,0:T(8,128)(2,1)S(1)} %get-tuple-element.34), channel_id=1, source_target_pairs={{0,3},{1,0},{2,1},{3,2},{4,7},{5,4},{6,5},{7,6},{8,11},{9,8},{10,9... | collective-permute-start | bytes 98312 | tf_op jit(solution)/shard_map/ppermute | solution.py:428

commit v13 on v12

--- a/solution.py
+++ b/solution.py
@@ -194,7 +194,7 @@
         here = here + jnp.dot(mine, columns(z, owner), preferred_element_type=F32)
         even, odd = here[:, :block], here[:, block:]
         span = pl.ds(z * rows, rows)
-        keep_ref[span, :] = jnp.where(first, even, odd)
+        keep_ref[span, :] = jnp.where(first, even, odd).astype(BF16)
         send_ref[span, :] = jnp.where(first, odd, even).astype(BF16)
     att = jnp.concatenate([att_ref[o] for o in range(owners)], axis=1)
     ids = row_adapters(rows_ref, rank)
@@ -212,7 +212,7 @@
 
     half = rows // 2
     code = jnp.concatenate([acc[:half, :], acc[half:, :]], axis=1)
-    keep_ref[planes * rows :, :] = code
+    keep_ref[planes * rows :, :] = code.astype(BF16)
     send_ref[planes * rows :, :] = code.astype(BF16)
 
 
@@ -220,19 +220,19 @@
     out_ref[...] = (keep_ref[...] + got_ref[...].astype(F32)).astype(BF16)
 
 
-def pair_kernel(keep_ref, got_ref, own_ref, codes_ref):
-    planes, rows, _ = own_ref.shape
+def pair_kernel(keep_ref, got_ref, codes_ref):
+    span = pl.ds(keep_ref.shape[0] - codes_ref.shape[1], codes_ref.shape[1])
+    code = (keep_ref[span, :].astype(F32) + got_ref[span, :].astype(F32)).astype(BF16)
+    for z in range(codes_ref.shape[0]):
+        codes_ref[z] = code
+
+
+def add_kernel(keep_ref, got_ref, across_ref, out_ref):
+    planes, rows, _ = out_ref.shape
     for z in range(planes):
         span = pl.ds(z * rows, rows)
-        own_ref[z] = keep_ref[span, :] + got_ref[span, :].astype(F32)
-    span = pl.ds(planes * rows, codes_ref.shape[1])
-    code = (keep_ref[span, :] + got_ref[span, :].astype(F32)).astype(BF16)
-    for z in range(planes):
-        codes_ref[z] = code
-
-
-def add_kernel(one_ref, two_ref, out_ref):
-    out_ref[...] = (one_ref[...] + two_ref[...].astype(F32)).astype(BF16)
+        total = keep_ref[span, :].astype(F32) + got_ref[span, :].astype(F32)
+        out_ref[z] = (total + across_ref[z].astype(F32)).astype(BF16)
 
 
 def update_kernel(group_ref, store_ref, rows_ref, codes_ref, up_ref, own_ref, *rest):
@@ -372,7 +372,7 @@
     keep, send = pl.pallas_call(
         project_kernel,
         name="project",
-        out_shape=(pltpu.VMEM((tall, block), F32), pltpu.VMEM((tall, block), BF16)),
+        out_shape=(pltpu.VMEM((tall, block), BF16), pltpu.VMEM((tall, block), BF16)),
         in_specs=[HBM, HBM] + [VMEM] * 7,
         out_specs=(VMEM, VMEM),
         scratch_shapes=[pltpu.VMEM((rows, rank), F32)] + indices,
@@ -397,12 +397,12 @@
         out_specs=VMEM,
         compiler_params=LIMIT,
     )(near(keep_across), near(got_across))
-    own_part, codes = pl.pallas_call(
+    codes = pl.pallas_call(
         pair_kernel,
         name="pair",
-        out_shape=(kept, pltpu.VMEM((planes, rows // 2, 2 * rank), BF16)),
+        out_shape=pltpu.VMEM((planes, rows // 2, 2 * rank), BF16),
         in_specs=[VMEM, VMEM],
-        out_specs=(VMEM, VMEM),
+        out_specs=VMEM,
         compiler_params=LIMIT,
     )(near(keep), near(got))
     groups = [[2 * z + c for z in range(planes)] for c in range(2)]
@@ -433,10 +433,10 @@
             add_kernel,
             name="add",
             out_shape=pltpu.VMEM((planes, rows, block), BF16),
-            in_specs=[VMEM, VMEM],
+            in_specs=[VMEM] * 3,
             out_specs=VMEM,
             compiler_params=LIMIT,
-        )(near(own_part), near(across))
+        )(near(keep), near(got), near(across))
     )
     return pl.pallas_call(
         final_kernel,

time: 61.3 us -> 61.7 us (level)
  no operation moved by 1% of the time
where the time goes in v13:
time: 61.7 us; the launch traced here: 61.1 us
  blocking collectives  21 us (34%)
  starting transfers between devices  17.7 us (29%)
  waiting for transfers between devices  12.8 us (21%)
  Pallas kernels  9.44 us (15%)
    all_to_all x1, blocking collectives, shards(): lax.all_to_all(outgoing, ('owner', 'tensor'), split_axis=0, concat_axis=0...  21 us
    all_to_all x2, waiting for transfers between devices, over_z(): lax.all_to_all(pieces, 'tensor', split_axis=0, concat_axis=0, tiled=True,...  7.46 us
    all_to_all x2, starting transfers between devices, over_z(): lax.all_to_all(pieces, 'tensor', split_axis=0, concat_axis=0, tiled=True,...  6.78 us
    ppermute x3, starting transfers between devices, shards(): lax.ppermute(update, 'owner', [(o, (o + i + 1) % owners) for o in range(o...  4.59 us
    ppermute x1, waiting for transfers between devices, shards(): lax.ppermute(across, 'owner', [(o, (o + 2) % owners) for o in range(owner...  3.57 us
    pallas_call x1, Pallas kernels, shards(): pl.pallas_call(slab_kernel, name='slabs', out_shape=(pltpu.VMEM((feats, c...  2.44 us
    ppermute x1, starting transfers between devices, shards(): lax.ppermute(across, 'owner', [(o, (o + 2) % owners) for o in range(owner...  2.31 us
    pallas_call x1, Pallas kernels, shards(): pl.pallas_call(project_kernel, name='project', out_shape=(pltpu.VMEM((tal...  1.9 us
  transfers between devices with their start and end apart: 10, of which 6 were waited for; matrix products, arithmetic and copies ran while one was open for 0% of the time, Pallas kernels for 10%

profile of v13, /device:TPU:24, one launch (start us, length us, event | category | flops | bytes accessed | tf_op | source)
XLA Modules:
  0.0 61.1 jit_solution(8984975496542878921)
XLA Ops:
  0.0 2.4 %slabs.1 = (bf16[128,8192]{1,0:T(8,128)(2,1)S(1)}, bf16[8,2048]{1,0:T(8,128)(2,1)S(1)}, bf16[8,1024,128]{2,1,0:T(8,128)(2,1)S(1)}, bf16[128,2048]{1,0:T(8,128)(2,1)S(1)}, bf16[128,2048]{1,0:T(8,128)(2,1)S(1)}) custom-call(bf16[128,8192]{1,0:T(8,128)(2,1)} %bitcast.13, bf16[8,2048]{1,0:T(8,128)(2,1)} %queries_hbm_ref.1, bf16[8,1024,128]{2,1,0:T(8,128)(2,1)} %bitcast.14), custom_call_target="tpu_custom_call" | custom-call | tf_op jit(solution)/shard_map/slabs/pallas_call | solution.py:314
  2.5 1.6 %collective-permute-start = (bf16[128,2048]{1,0:T(8,128)(2,1)S(1)}, bf16[128,2048]{1,0:T(8,128)(2,1)S(1)}, u32[]{:S(2)}, u32[]{:S(2)}) collective-permute-start(bf16[128,2048]{1,0:T(8,128)(2,1)S(1)} %get-tuple-element.22), channel_id=1, source_target_pairs={{0,1},{1,2},{2,3},{3,0},{4,5},{5,6},{6,7},{7,4},{8,9},{9,10},{10,1... | collective-permute-start | bytes 1572872 | tf_op jit(solution)/shard_map/ppermute | solution.py:336
  4.0 1.7 %collective-permute-start.1 = (bf16[128,2048]{1,0:T(8,128)(2,1)S(1)}, bf16[128,2048]{1,0:T(8,128)(2,1)S(1)}, u32[]{:S(2)}, u32[]{:S(2)}) collective-permute-start(bf16[128,2048]{1,0:T(8,128)(2,1)S(1)} %get-tuple-element.23), channel_id=1, source_target_pairs={{0,3},{1,0},{2,1},{3,2},{4,7},{5,4},{6,5},{7,6},{8,11},{9,8},{10,9... | collective-permute-start | bytes 1572872 | tf_op jit(solution)/shard_map/ppermute | solution.py:337
  5.8 1.0 %attend.1 = bf16[4,16,8,128]{3,2,1,0:T(8,128)(2,1)S(1)} custom-call(bf16[8,2048]{1,0:T(8,128)(2,1)S(1)} %get-tuple-element.18.queries_ref, bf16[8,1024,128]{2,1,0:T(8,128)(2,1)S(1)} %bitcast.7, bf16[8,1024,128]{2,1,0:T(8,128)(2,1)S(1)} %get-tuple-element.19.values_ref, bf16[8,2,128]{2,1,0:T(2,128)(2,1)S(1)} %copy-done.3, bf16[8,2,128]{2,1,0:T(2,128)(2,1)S(1)} %copy-done.4), custom_call_target="tpu_custom_call" | custom-call | tf_op jit(solution)/shard_map/attend/pallas_call | solution.py:339
  6.8 21.0 %all_to_all.15 = bf16[64,8,128]{2,1,0:T(8,128)(2,1)S(1)} all-to-all(bf16[64,8,128]{2,1,0:T(8,128)(2,1)S(1)} %bitcast.10), channel_id=1, replica_groups=mesh['dp'=4,'tensor'=16,'owner'=4] {'owner','tensor'}, dimensions={0} | all-to-all | bytes 262144 | tf_op jit(solution)/shard_map/all_to_all | solution.py:354
  27.8 0.3 across.1
  28.1 0.2 collective-permute-start.3
  28.4 1.9 %project.1 = (bf16[1088,128]{1,0:T(8,128)(2,1)S(1)}, bf16[1088,128]{1,0:T(8,128)(2,1)S(1)}) custom-call(s32[1,16]{1,0:T(1,128)} %group_ref.3, s32[1,128]{1,0:T(1,128)} %bitcast.15, s32[1,128]{1,0:T(1,128)S(1)} %bitcast.11, bf16[8,128,128]{2,1,0:T(8,128)(2,1)S(1)} %get-tuple-element.21.order_ref, bf16[4,128,128]{2,1,0:T(8,128)(2,1)S(1)} %bitcast.9, ...), custom_call_target="tpu_custom_call" | custom-call | tf_op jit(solution)/shard_map/project/pallas_call | solution.py:372
  30.3 0.5 collective-permute-start.2
  30.8 2.3 %collective-permute-start.4 = (bf16[8,128,128]{2,1,0:T(8,128)(2,1)S(1)}, bf16[8,128,128]{2,1,0:T(8,128)(2,1)S(1)}, u32[]{:S(2)}, u32[]{:S(2)}) collective-permute-start(bf16[8,128,128]{2,1,0:T(8,128)(2,1)S(1)} %pair_across.1), channel_id=1, source_target_pairs={{0,2},{1,3},{2,0},{3,1},{4,6},{5,7},{6,4},{7,5},{8,10},{9,11},{10,... | collective-permute-start | bytes 786440 | tf_op jit(solution)/shard_map/ppermute | solution.py:415
  33.1 0.7 %pair.1 = bf16[8,64,128]{2,1,0:T(8,128)(2,1)} custom-call(bf16[1088,128]{1,0:T(8,128)(2,1)S(1)} %get-tuple-element.24.keep_ref, bf16[1088,128]{1,0:T(8,128)(2,1)S(1)} %collective-permute-done.2.got_ref), custom_call_target="tpu_custom_call" | custom-call | tf_op jit(solution)/shard_map/pair/pallas_call | solution.py:400
  33.8 3.4 %all-to-all-start.2 = ((bf16[8,64,128]{2,1,0:T(8,128)(2,1)}), bf16[8,64,128]{2,1,0:T(8,128)(2,1)S(1)}, u32[]{:S(2)}, u32[]{:S(2)}) async-start(bf16[8,64,128]{2,1,0:T(8,128)(2,1)} %pair.1), calls=%async_computation.2 | async-start | bytes 262144 | tf_op jit(solution)/shard_map/all_to_all | solution.py:411
  37.2 3.6 %collective-permute-done.4.across_ref = bf16[8,128,128]{2,1,0:T(8,128)(2,1)S(1)} collective-permute-done((bf16[8,128,128]{2,1,0:T(8,128)(2,1)S(1)}, bf16[8,128,128]{2,1,0:T(8,128)(2,1)S(1)}, u32[]{:S(2)}, u32[]{:S(2)}) %collective-permute-start.4) | collective-permute-done | bytes 262176 | tf_op jit(solution)/shard_map/ppermute | solution.py:415
  40.7 0.8 %add.1 = bf16[8,128,128]{2,1,0:T(8,128)(2,1)} custom-call(bf16[1088,128]{1,0:T(8,128)(2,1)S(1)} %get-tuple-element.24.keep_ref, bf16[1088,128]{1,0:T(8,128)(2,1)S(1)} %collective-permute-done.2.got_ref, bf16[8,128,128]{2,1,0:T(8,128)(2,1)S(1)} %collective-permute-done.4.across_ref), custom_call_target="tpu_custom_call" | custom-call | tf_op jit(solution)/shard_map/add/pallas_call | solution.py:432
  41.5 4.9 %all-to-all-done.2.codes_ref = bf16[8,64,128]{2,1,0:T(8,128)(2,1)S(1)} async-done(((bf16[8,64,128]{2,1,0:T(8,128)(2,1)}), bf16[8,64,128]{2,1,0:T(8,128)(2,1)S(1)}, u32[]{:S(2)}, u32[]{:S(2)}) %all-to-all-start.2) | async-done | bytes 131104 | tf_op jit(solution)/shard_map/all_to_all | solution.py:411
  46.4 3.4 %all-to-all-start.1 = ((bf16[8,128,128]{2,1,0:T(8,128)(2,1)}), bf16[8,128,128]{2,1,0:T(8,128)(2,1)S(1)}, u32[]{:S(2)}, u32[]{:S(2)}) async-start(bf16[8,128,128]{2,1,0:T(8,128)(2,1)} %add.1), calls=%async_computation.1 | async-start | bytes 524288 | tf_op jit(solution)/shard_map/all_to_all | solution.py:411
  49.9 1.6 %update.1 = (f32[128,128]{1,0:T(8,128)S(1)}, bf16[128,128]{1,0:T(8,128)(2,1)S(1)}, bf16[128,128]{1,0:T(8,128)(2,1)S(1)}, bf16[128,128]{1,0:T(8,128)(2,1)S(1)}) custom-call(s32[1,16]{1,0:T(1,128)} %group_ref.3, s32[1,128]{1,0:T(1,128)} %bitcast.16, s32[1,128]{1,0:T(1,128)S(1)} %bitcast.12, bf16[8,64,128]{2,1,0:T(8,128)(2,1)S(1)} %all-to-all-done.2.codes_ref, ...), custom_call_target="tpu_custom_call" | custom-call | tf_op jit(solution)/shard_map/update/pallas_call | solution.py:418
  51.5 2.2 %collective-permute-start.6 = (bf16[128,128]{1,0:T(8,128)(2,1)S(1)}, bf16[128,128]{1,0:T(8,128)(2,1)S(1)}, u32[]{:S(2)}, u32[]{:S(2)}) collective-permute-start(bf16[128,128]{1,0:T(8,128)(2,1)S(1)} %get-tuple-element.29), channel_id=1, source_target_pairs={{0,2},{1,3},{2,0},{3,1},{4,6},{5,7},{6,4},{7,5},{8,10},{9,11},{10,... | collective-permute-start | bytes 98312 | tf_op jit(solution)/shard_map/ppermute | solution.py:428
  53.8 2.3 %collective-permute-start.7 = (bf16[128,128]{1,0:T(8,128)(2,1)S(1)}, bf16[128,128]{1,0:T(8,128)(2,1)S(1)}, u32[]{:S(2)}, u32[]{:S(2)}) collective-permute-start(bf16[128,128]{1,0:T(8,128)(2,1)S(1)} %get-tuple-element.30), channel_id=1, source_target_pairs={{0,3},{1,0},{2,1},{3,2},{4,7},{5,4},{6,5},{7,6},{8,11},{9,8},{10,9... | collective-permute-start | bytes 98312 | tf_op jit(solution)/shard_map/ppermute | solution.py:428
  56.0 0.6 collective-permute-done.5.rest_0_
  56.6 0.4 collective-permute-done.6.rest_1_
  57.0 0.8 %collective-permute-done.7.rest_2_ = bf16[128,128]{1,0:T(8,128)(2,1)S(1)} collective-permute-done((bf16[128,128]{1,0:T(8,128)(2,1)S(1)}, bf16[128,128]{1,0:T(8,128)(2,1)S(1)}, u32[]{:S(2)}, u32[]{:S(2)}) %collective-permute-start.7) | collective-permute-done | bytes 32800 | tf_op jit(solution)/shard_map/ppermute | solution.py:428
  57.8 2.6 %all-to-all-done.1.parts_ref = bf16[8,128,128]{2,1,0:T(8,128)(2,1)S(1)} async-done(((bf16[8,128,128]{2,1,0:T(8,128)(2,1)}), bf16[8,128,128]{2,1,0:T(8,128)(2,1)S(1)}, u32[]{:S(2)}, u32[]{:S(2)}) %all-to-all-start.1) | async-done | bytes 262176 | tf_op jit(solution)/shard_map/all_to_all | solution.py:411
  60.4 0.7 %final.1 = bf16[128,128]{1,0:T(8,128)(2,1)} custom-call(bf16[8,128,128]{2,1,0:T(8,128)(2,1)S(1)} %all-to-all-done.1.parts_ref, f32[128,128]{1,0:T(8,128)S(1)} %get-tuple-element.27.own_ref, bf16[128,128]{1,0:T(8,128)(2,1)S(1)} %collective-permute-done.5.rest_0_, bf16[128,128]{1,0:T(8,128)(2,1)S(1)} %collective-permute-done.6.rest_1_, ...), custom_call_target="tpu_custom_call" | custom-call | tf_op jit(solution)/shard_map/final/pallas_call | solution.py:441
  (18 shorter events, 0.2 us)
Async XLA Ops:
  0.0 5.8 %copy-start.1 = (bf16[8,512,2,128]{3,2,1,0:T(2,128)(2,1)S(1)}, bf16[8,512,2,128]{3,2,1,0:T(2,128)(2,1)}, u32[]{:S(2)}) copy-start(bf16[8,512,2,128]{3,2,1,0:T(2,128)(2,1)} %param.12) | copy-start | bytes 6291460
  0.0 5.8 %copy-start.3 = (bf16[8,2,128]{2,1,0:T(2,128)(2,1)S(1)}, bf16[8,2,128]{2,1,0:T(2,128)(2,1)}, u32[]{:S(2)}) copy-start(bf16[8,2,128]{2,1,0:T(2,128)(2,1)} %key_ref.1) | copy-start | bytes 12292
  0.0 5.8 %copy-start.4 = (bf16[8,2,128]{2,1,0:T(2,128)(2,1)S(1)}, bf16[8,2,128]{2,1,0:T(2,128)(2,1)}, u32[]{:S(2)}) copy-start(bf16[8,2,128]{2,1,0:T(2,128)(2,1)} %value_ref.1) | copy-start | bytes 12292
  2.5 25.9 %collective-permute-start = (bf16[128,2048]{1,0:T(8,128)(2,1)S(1)}, bf16[128,2048]{1,0:T(8,128)(2,1)S(1)}, u32[]{:S(2)}, u32[]{:S(2)}) collective-permute-start(bf16[128,2048]{1,0:T(8,128)(2,1)S(1)} %get-tuple-element.22), channel_id=1, source_target_pairs={{0,1},{1,2},{2,3},{3,0},{4,5},{5,6},{6,7},{7,4},{8,9},{9,10},{10,1... | collective-permute-start | bytes 1572872 | tf_op jit(solution)/shard_map/ppermute | solution.py:336
  4.0 24.3 %collective-permute-start.1 = (bf16[128,2048]{1,0:T(8,128)(2,1)S(1)}, bf16[128,2048]{1,0:T(8,128)(2,1)S(1)}, u32[]{:S(2)}, u32[]{:S(2)}) collective-permute-start(bf16[128,2048]{1,0:T(8,128)(2,1)S(1)} %get-tuple-element.23), channel_id=1, source_target_pairs={{0,3},{1,0},{2,1},{3,2},{4,7},{5,4},{6,5},{7,6},{8,11},{9,8},{10,9... | collective-permute-start | bytes 1572872 | tf_op jit(solution)/shard_map/ppermute | solution.py:337
  5.8 22.6 %copy-start = (bf16[32,8,64,64]{3,2,1,0:T(8,128)(2,1)S(1)}, bf16[32,8,64,64]{3,2,1,0:T(8,128)(2,1)}, u32[]{:S(2)}) copy-start(bf16[32,8,64,64]{3,2,1,0:T(8,128)(2,1)} %down_ref.1) | copy-start | bytes 6291460
  6.8 21.5 %copy-start.5 = (s32[128]{0:T(128)S(1)}, s32[128]{0:T(128)}, u32[]{:S(2)}) copy-start(s32[128]{0:T(128)} %param.21) | copy-start | bytes 1540
  28.1 2.6 %collective-permute-start.3 = (bf16[8,128,128]{2,1,0:T(8,128)(2,1)S(1)}, bf16[8,128,128]{2,1,0:T(8,128)(2,1)S(1)}, u32[]{:S(2)}, u32[]{:S(2)}) collective-permute-start(bf16[8,128,128]{2,1,0:T(8,128)(2,1)S(1)} %get-tuple-element.21.order_ref), channel_id=1, source_target_pairs={{0,4},{4,0},{8,12},{12,8},{16,20},{20,16},{24,28},{28,24},{32,36},... | collective-permute-start | bytes 786440 | tf_op jit(solution)/shard_map/ppermute | solution.py:370
  30.3 19.6 %copy-start.2 = (bf16[32,64,512]{2,1,0:T(8,128)(2,1)S(1)}, bf16[32,64,512]{2,1,0:T(8,128)(2,1)}, u32[]{:S(2)}) copy-start(bf16[32,64,512]{2,1,0:T(8,128)(2,1)} %up_ref.1) | copy-start | bytes 6291460
  30.3 2.8 %collective-permute-start.2 = (bf16[1088,128]{1,0:T(8,128)(2,1)S(1)}, bf16[1088,128]{1,0:T(8,128)(2,1)S(1)}, u32[]{:S(2)}, u32[]{:S(2)}) collective-permute-start(bf16[1088,128]{1,0:T(8,128)(2,1)S(1)} %get-tuple-element.25), channel_id=1, source_target_pairs={{0,4},{4,0},{8,12},{12,8},{16,20},{20,16},{24,28},{28,24},{32,36},... | collective-permute-start | bytes 835592 | tf_op jit(solution)/shard_map/ppermute | solution.py:391
  30.8 9.9 %collective-permute-start.4 = (bf16[8,128,128]{2,1,0:T(8,128)(2,1)S(1)}, bf16[8,128,128]{2,1,0:T(8,128)(2,1)S(1)}, u32[]{:S(2)}, u32[]{:S(2)}) collective-permute-start(bf16[8,128,128]{2,1,0:T(8,128)(2,1)S(1)} %pair_across.1), channel_id=1, source_target_pairs={{0,2},{1,3},{2,0},{3,1},{4,6},{5,7},{6,4},{7,5},{8,10},{9,11},{10,... | collective-permute-start | bytes 786440 | tf_op jit(solution)/shard_map/ppermute | solution.py:415
  33.8 12.6 %all-to-all-start.2 = ((bf16[8,64,128]{2,1,0:T(8,128)(2,1)}), bf16[8,64,128]{2,1,0:T(8,128)(2,1)S(1)}, u32[]{:S(2)}, u32[]{:S(2)}) async-start(bf16[8,64,128]{2,1,0:T(8,128)(2,1)} %pair.1), calls=%async_computation.2 | async-start | bytes 262144 | tf_op jit(solution)/shard_map/all_to_all | solution.py:411
  46.4 14.0 %all-to-all-start.1 = ((bf16[8,128,128]{2,1,0:T(8,128)(2,1)}), bf16[8,128,128]{2,1,0:T(8,128)(2,1)S(1)}, u32[]{:S(2)}, u32[]{:S(2)}) async-start(bf16[8,128,128]{2,1,0:T(8,128)(2,1)} %add.1), calls=%async_computation.1 | async-start | bytes 524288 | tf_op jit(solution)/shard_map/all_to_all | solution.py:411
  51.4 5.2 %collective-permute-start.5 = (bf16[128,128]{1,0:T(8,128)(2,1)S(1)}, bf16[128,128]{1,0:T(8,128)(2,1)S(1)}, u32[]{:S(2)}, u32[]{:S(2)}) collective-permute-start(bf16[128,128]{1,0:T(8,128)(2,1)S(1)} %get-tuple-element.28), channel_id=1, source_target_pairs={{0,1},{1,2},{2,3},{3,0},{4,5},{5,6},{6,7},{7,4},{8,9},{9,10},{10,1... | collective-permute-start | bytes 98312 | tf_op jit(solution)/shard_map/ppermute | solution.py:428
  51.5 5.5 %collective-permute-start.6 = (bf16[128,128]{1,0:T(8,128)(2,1)S(1)}, bf16[128,128]{1,0:T(8,128)(2,1)S(1)}, u32[]{:S(2)}, u32[]{:S(2)}) collective-permute-start(bf16[128,128]{1,0:T(8,128)(2,1)S(1)} %get-tuple-element.29), channel_id=1, source_target_pairs={{0,2},{1,3},{2,0},{3,1},{4,6},{5,7},{6,4},{7,5},{8,10},{9,11},{10,... | collective-permute-start | bytes 98312 | tf_op jit(solution)/shard_map/ppermute | solution.py:428
  53.8 4.1 %collective-permute-start.7 = (bf16[128,128]{1,0:T(8,128)(2,1)S(1)}, bf16[128,128]{1,0:T(8,128)(2,1)S(1)}, u32[]{:S(2)}, u32[]{:S(2)}) collective-permute-start(bf16[128,128]{1,0:T(8,128)(2,1)S(1)} %get-tuple-element.30), channel_id=1, source_target_pairs={{0,3},{1,0},{2,1},{3,2},{4,7},{5,4},{6,5},{7,6},{8,11},{9,8},{10,9... | collective-permute-start | bytes 98312 | tf_op jit(solution)/shard_map/ppermute | solution.py:428

commit v14 on v12

--- a/solution.py
+++ b/solution.py
@@ -6,6 +6,7 @@
 from jax.sharding import PartitionSpec as P
 
 ADAPTER_SCALE = 2.0
+STEPS = (2, 1, 3)
 BF16 = jnp.bfloat16
 F32 = jnp.float32
 
@@ -264,7 +265,7 @@
 
     own_ref[...] = columns(owner)
     for i, send_ref in enumerate(send_refs):
-        send_ref[...] = columns(lax.rem(owner + i + 1, owners)).astype(BF16)
+        send_ref[...] = columns(lax.rem(owner + STEPS[i], owners)).astype(BF16)
 
 
 def final_kernel(parts_ref, own_ref, *rest):
@@ -425,7 +426,7 @@
         compiler_params=LIMIT,
     )(group, store, row_ids, near(codes), near(adapter_up_weight))
     updates = [
-        lax.ppermute(update, "owner", [(o, (o + i + 1) % owners) for o in range(owners)])
+        lax.ppermute(update, "owner", [(o, (o + STEPS[i]) % owners) for o in range(owners)])
         for i, update in enumerate(updates)
     ]
     parts = over_z(

time: 61.3 us -> 61.3 us (level)
  starting transfers between devices: 17.3 us -> 18 us
    ppermute x3, starting transfers between devices: 4.43 us -> 5.05 us  [shards(): lax.ppermute(update, 'owner', [(o, (o + STEPS[i]) % owners) for o in rang...]
  transfers between devices with their start and end apart: 10 -> 10, of which waited for: 6 -> 5; matrix products, arithmetic and copies ran while one was open for 0% -> 0% of each run, Pallas kernels for 10% -> 10%
where the time goes in v14:
time: 61.3 us; the launch traced here: 60.8 us
  blocking collectives  21 us (34%)
  starting transfers between devices  18 us (29%)
  waiting for transfers between devices  12.6 us (21%)
  Pallas kernels  9.09 us (15%)
    all_to_all x1, blocking collectives, shards(): lax.all_to_all(outgoing, ('owner', 'tensor'), split_axis=0, concat_axis=0...  21 us
    all_to_all x2, waiting for transfers between devices, over_z(): lax.all_to_all(pieces, 'tensor', split_axis=0, concat_axis=0, tiled=True,...  7.01 us
    all_to_all x2, starting transfers between devices, over_z(): lax.all_to_all(pieces, 'tensor', split_axis=0, concat_axis=0, tiled=True,...  6.78 us
    ppermute x3, starting transfers between devices, shards(): lax.ppermute(update, 'owner', [(o, (o + STEPS[i]) % owners) for o in rang...  5.05 us
    ppermute x1, waiting for transfers between devices, shards(): lax.ppermute(across, 'owner', [(o, (o + 2) % owners) for o in range(owner...  3.7 us
    pallas_call x1, Pallas kernels, shards(): pl.pallas_call(slab_kernel, name='slabs', out_shape=(pltpu.VMEM((feats, c...  2.44 us
    ppermute x1, starting transfers between devices, shards(): lax.ppermute(across, 'owner', [(o, (o + 2) % owners) for o in range(owner...  2.13 us
    ppermute x3, waiting for transfers between devices, shards(): lax.ppermute(update, 'owner', [(o, (o + STEPS[i]) % owners) for o in rang...  1.89 us
  transfers between devices with their start and end apart: 10, of which 5 were waited for; matrix products, arithmetic and copies ran while one was open for 0% of the time, Pallas kernels for 10%

profile of v14, /device:TPU:24, one launch (start us, length us, event | category | flops | bytes accessed | tf_op | source)
XLA Modules:
  0.0 60.8 jit_solution(766918494266782376)
XLA Ops:
  0.0 2.4 %slabs.1 = (bf16[128,8192]{1,0:T(8,128)(2,1)S(1)}, bf16[8,2048]{1,0:T(8,128)(2,1)S(1)}, bf16[8,1024,128]{2,1,0:T(8,128)(2,1)S(1)}, bf16[128,2048]{1,0:T(8,128)(2,1)S(1)}, bf16[128,2048]{1,0:T(8,128)(2,1)S(1)}) custom-call(bf16[128,8192]{1,0:T(8,128)(2,1)} %bitcast.13, bf16[8,2048]{1,0:T(8,128)(2,1)} %queries_hbm_ref.1, bf16[8,1024,128]{2,1,0:T(8,128)(2,1)} %bitcast.14), custom_call_target="tpu_custom_call" | custom-call | tf_op jit(solution)/shard_map/slabs/pallas_call | solution.py:315
  2.5 1.6 %collective-permute-start = (bf16[128,2048]{1,0:T(8,128)(2,1)S(1)}, bf16[128,2048]{1,0:T(8,128)(2,1)S(1)}, u32[]{:S(2)}, u32[]{:S(2)}) collective-permute-start(bf16[128,2048]{1,0:T(8,128)(2,1)S(1)} %get-tuple-element.24), channel_id=1, source_target_pairs={{0,1},{1,2},{2,3},{3,0},{4,5},{5,6},{6,7},{7,4},{8,9},{9,10},{10,1... | collective-permute-start | bytes 1572872 | tf_op jit(solution)/shard_map/ppermute | solution.py:337
  4.0 1.7 %collective-permute-start.1 = (bf16[128,2048]{1,0:T(8,128)(2,1)S(1)}, bf16[128,2048]{1,0:T(8,128)(2,1)S(1)}, u32[]{:S(2)}, u32[]{:S(2)}) collective-permute-start(bf16[128,2048]{1,0:T(8,128)(2,1)S(1)} %get-tuple-element.25), channel_id=1, source_target_pairs={{0,3},{1,0},{2,1},{3,2},{4,7},{5,4},{6,5},{7,6},{8,11},{9,8},{10,9... | collective-permute-start | bytes 1572872 | tf_op jit(solution)/shard_map/ppermute | solution.py:338
  5.8 1.0 %attend.1 = bf16[4,16,8,128]{3,2,1,0:T(8,128)(2,1)S(1)} custom-call(bf16[8,2048]{1,0:T(8,128)(2,1)S(1)} %get-tuple-element.20.queries_ref, bf16[8,1024,128]{2,1,0:T(8,128)(2,1)S(1)} %bitcast.7, bf16[8,1024,128]{2,1,0:T(8,128)(2,1)S(1)} %get-tuple-element.21.values_ref, bf16[8,2,128]{2,1,0:T(2,128)(2,1)S(1)} %copy-done.3, bf16[8,2,128]{2,1,0:T(2,128)(2,1)S(1)} %copy-done.4), custom_call_target="tpu_custom_call" | custom-call | tf_op jit(solution)/shard_map/attend/pallas_call | solution.py:340
  6.8 21.0 %all_to_all.15 = bf16[64,8,128]{2,1,0:T(8,128)(2,1)S(1)} all-to-all(bf16[64,8,128]{2,1,0:T(8,128)(2,1)S(1)} %bitcast.10), channel_id=1, replica_groups=mesh['dp'=4,'tensor'=16,'owner'=4] {'owner','tensor'}, dimensions={0} | all-to-all | bytes 262144 | tf_op jit(solution)/shard_map/all_to_all | solution.py:355
  27.8 0.3 across.1
  28.1 0.2 collective-permute-start.3
  28.4 1.7 %project.1 = (f32[1088,128]{1,0:T(8,128)S(1)}, bf16[1088,128]{1,0:T(8,128)(2,1)S(1)}) custom-call(s32[1,16]{1,0:T(1,128)} %group_ref.3, s32[1,128]{1,0:T(1,128)} %bitcast.15, s32[1,128]{1,0:T(1,128)S(1)} %bitcast.11, bf16[8,128,128]{2,1,0:T(8,128)(2,1)S(1)} %get-tuple-element.23.order_ref, bf16[4,128,128]{2,1,0:T(8,128)(2,1)S(1)} %bitcast.9, ...), custom_call_target="tpu_custom_call" | custom-call | tf_op jit(solution)/shard_map/project/pallas_call | solution.py:373
  30.1 0.5 collective-permute-start.2
  30.7 2.1 %collective-permute-start.4 = (bf16[8,128,128]{2,1,0:T(8,128)(2,1)S(1)}, bf16[8,128,128]{2,1,0:T(8,128)(2,1)S(1)}, u32[]{:S(2)}, u32[]{:S(2)}) collective-permute-start(bf16[8,128,128]{2,1,0:T(8,128)(2,1)S(1)} %pair_across.1), channel_id=1, source_target_pairs={{0,2},{1,3},{2,0},{3,1},{4,6},{5,7},{6,4},{7,5},{8,10},{9,11},{10,... | collective-permute-start | bytes 786440 | tf_op jit(solution)/shard_map/ppermute | solution.py:416
  32.8 0.7 %pair.1 = (f32[8,128,128]{2,1,0:T(8,128)S(1)}, bf16[8,64,128]{2,1,0:T(8,128)(2,1)}) custom-call(f32[1088,128]{1,0:T(8,128)S(1)} %get-tuple-element.26.keep_ref, bf16[1088,128]{1,0:T(8,128)(2,1)S(1)} %collective-permute-done.2.got_ref), custom_call_target="tpu_custom_call" | custom-call | tf_op jit(solution)/shard_map/pair/pallas_call | solution.py:401
  33.5 3.4 %all-to-all-start.2 = ((bf16[8,64,128]{2,1,0:T(8,128)(2,1)}), bf16[8,64,128]{2,1,0:T(8,128)(2,1)S(1)}, u32[]{:S(2)}, u32[]{:S(2)}) async-start(bf16[8,64,128]{2,1,0:T(8,128)(2,1)} %get-tuple-element.30), calls=%async_computation.2 | async-start | bytes 262144 | tf_op jit(solution)/shard_map/all_to_all | solution.py:412
  36.9 3.7 %collective-permute-done.4.two_ref = bf16[8,128,128]{2,1,0:T(8,128)(2,1)S(1)} collective-permute-done((bf16[8,128,128]{2,1,0:T(8,128)(2,1)S(1)}, bf16[8,128,128]{2,1,0:T(8,128)(2,1)S(1)}, u32[]{:S(2)}, u32[]{:S(2)}) %collective-permute-start.4) | collective-permute-done | bytes 262176 | tf_op jit(solution)/shard_map/ppermute | solution.py:416
  40.6 0.7 %add.1 = bf16[8,128,128]{2,1,0:T(8,128)(2,1)} custom-call(f32[8,128,128]{2,1,0:T(8,128)S(1)} %get-tuple-element.28.one_ref, bf16[8,128,128]{2,1,0:T(8,128)(2,1)S(1)} %collective-permute-done.4.two_ref), custom_call_target="tpu_custom_call" | custom-call | tf_op jit(solution)/shard_map/add/pallas_call | solution.py:433
  41.3 4.8 %all-to-all-done.2.codes_ref = bf16[8,64,128]{2,1,0:T(8,128)(2,1)S(1)} async-done(((bf16[8,64,128]{2,1,0:T(8,128)(2,1)}), bf16[8,64,128]{2,1,0:T(8,128)(2,1)S(1)}, u32[]{:S(2)}, u32[]{:S(2)}) %all-to-all-start.2) | async-done | bytes 131104 | tf_op jit(solution)/shard_map/all_to_all | solution.py:412
  46.1 3.4 %all-to-all-start.1 = ((bf16[8,128,128]{2,1,0:T(8,128)(2,1)}), bf16[8,128,128]{2,1,0:T(8,128)(2,1)S(1)}, u32[]{:S(2)}, u32[]{:S(2)}) async-start(bf16[8,128,128]{2,1,0:T(8,128)(2,1)} %add.1), calls=%async_computation.1 | async-start | bytes 524288 | tf_op jit(solution)/shard_map/all_to_all | solution.py:412
  49.5 1.4 %update.1 = (f32[128,128]{1,0:T(8,128)S(1)}, bf16[128,128]{1,0:T(8,128)(2,1)S(1)}, bf16[128,128]{1,0:T(8,128)(2,1)S(1)}, bf16[128,128]{1,0:T(8,128)(2,1)S(1)}) custom-call(s32[1,16]{1,0:T(1,128)} %group_ref.3, s32[1,128]{1,0:T(1,128)} %bitcast.16, s32[1,128]{1,0:T(1,128)S(1)} %bitcast.12, bf16[8,64,128]{2,1,0:T(8,128)(2,1)S(1)} %all-to-all-done.2.codes_ref, ...), custom_call_target="tpu_custom_call" | custom-call | tf_op jit(solution)/shard_map/update/pallas_call | solution.py:419
  51.0 1.8 %collective-permute-start.5 = (bf16[128,128]{1,0:T(8,128)(2,1)S(1)}, bf16[128,128]{1,0:T(8,128)(2,1)S(1)}, u32[]{:S(2)}, u32[]{:S(2)}) collective-permute-start(bf16[128,128]{1,0:T(8,128)(2,1)S(1)} %get-tuple-element.32), channel_id=1, source_target_pairs={{0,2},{1,3},{2,0},{3,1},{4,6},{5,7},{6,4},{7,5},{8,10},{9,11},{10,... | collective-permute-start | bytes 98312 | tf_op jit(solution)/shard_map/ppermute | solution.py:429
  52.8 0.9 %collective-permute-start.6 = (bf16[128,128]{1,0:T(8,128)(2,1)S(1)}, bf16[128,128]{1,0:T(8,128)(2,1)S(1)}, u32[]{:S(2)}, u32[]{:S(2)}) collective-permute-start(bf16[128,128]{1,0:T(8,128)(2,1)S(1)} %get-tuple-element.33), channel_id=1, source_target_pairs={{0,1},{1,2},{2,3},{3,0},{4,5},{5,6},{6,7},{7,4},{8,9},{9,10},{10,1... | collective-permute-start | bytes 98312 | tf_op jit(solution)/shard_map/ppermute | solution.py:429
  53.7 2.3 %collective-permute-start.7 = (bf16[128,128]{1,0:T(8,128)(2,1)S(1)}, bf16[128,128]{1,0:T(8,128)(2,1)S(1)}, u32[]{:S(2)}, u32[]{:S(2)}) collective-permute-start(bf16[128,128]{1,0:T(8,128)(2,1)S(1)} %get-tuple-element.34), channel_id=1, source_target_pairs={{0,3},{1,0},{2,1},{3,2},{4,7},{5,4},{6,5},{7,6},{8,11},{9,8},{10,9... | collective-permute-start | bytes 98312 | tf_op jit(solution)/shard_map/ppermute | solution.py:429
  56.0 0.4 collective-permute-done.5.rest_0_
  56.5 1.4 %collective-permute-done.6.rest_1_ = bf16[128,128]{1,0:T(8,128)(2,1)S(1)} collective-permute-done((bf16[128,128]{1,0:T(8,128)(2,1)S(1)}, bf16[128,128]{1,0:T(8,128)(2,1)S(1)}, u32[]{:S(2)}, u32[]{:S(2)}) %collective-permute-start.6) | collective-permute-done | bytes 32800 | tf_op jit(solution)/shard_map/ppermute | solution.py:429
  57.9 2.2 %all-to-all-done.1.parts_ref = bf16[8,128,128]{2,1,0:T(8,128)(2,1)S(1)} async-done(((bf16[8,128,128]{2,1,0:T(8,128)(2,1)}), bf16[8,128,128]{2,1,0:T(8,128)(2,1)S(1)}, u32[]{:S(2)}, u32[]{:S(2)}) %all-to-all-start.1) | async-done | bytes 262176 | tf_op jit(solution)/shard_map/all_to_all | solution.py:412
  60.1 0.7 %final.1 = bf16[128,128]{1,0:T(8,128)(2,1)} custom-call(bf16[8,128,128]{2,1,0:T(8,128)(2,1)S(1)} %all-to-all-done.1.parts_ref, f32[128,128]{1,0:T(8,128)S(1)} %get-tuple-element.31.own_ref, bf16[128,128]{1,0:T(8,128)(2,1)S(1)} %collective-permute-done.5.rest_0_, bf16[128,128]{1,0:T(8,128)(2,1)S(1)} %collective-permute-done.6.rest_1_, ...), custom_call_target="tpu_custom_call" | custom-call | tf_op jit(solution)/shard_map/final/pallas_call | solution.py:442
  (18 shorter events, 0.1 us)
Async XLA Ops:
  0.0 5.8 %copy-start.1 = (bf16[8,512,2,128]{3,2,1,0:T(2,128)(2,1)S(1)}, bf16[8,512,2,128]{3,2,1,0:T(2,128)(2,1)}, u32[]{:S(2)}) copy-start(bf16[8,512,2,128]{3,2,1,0:T(2,128)(2,1)} %param.12) | copy-start | bytes 6291460
  0.0 5.8 %copy-start.3 = (bf16[8,2,128]{2,1,0:T(2,128)(2,1)S(1)}, bf16[8,2,128]{2,1,0:T(2,128)(2,1)}, u32[]{:S(2)}) copy-start(bf16[8,2,128]{2,1,0:T(2,128)(2,1)} %key_ref.1) | copy-start | bytes 12292
  0.0 5.8 %copy-start.4 = (bf16[8,2,128]{2,1,0:T(2,128)(2,1)S(1)}, bf16[8,2,128]{2,1,0:T(2,128)(2,1)}, u32[]{:S(2)}) copy-start(bf16[8,2,128]{2,1,0:T(2,128)(2,1)} %value_ref.1) | copy-start | bytes 12292
  2.5 25.9 %collective-permute-start = (bf16[128,2048]{1,0:T(8,128)(2,1)S(1)}, bf16[128,2048]{1,0:T(8,128)(2,1)S(1)}, u32[]{:S(2)}, u32[]{:S(2)}) collective-permute-start(bf16[128,2048]{1,0:T(8,128)(2,1)S(1)} %get-tuple-element.24), channel_id=1, source_target_pairs={{0,1},{1,2},{2,3},{3,0},{4,5},{5,6},{6,7},{7,4},{8,9},{9,10},{10,1... | collective-permute-start | bytes 1572872 | tf_op jit(solution)/shard_map/ppermute | solution.py:337
  4.0 24.3 %collective-permute-start.1 = (bf16[128,2048]{1,0:T(8,128)(2,1)S(1)}, bf16[128,2048]{1,0:T(8,128)(2,1)S(1)}, u32[]{:S(2)}, u32[]{:S(2)}) collective-permute-start(bf16[128,2048]{1,0:T(8,128)(2,1)S(1)} %get-tuple-element.25), channel_id=1, source_target_pairs={{0,3},{1,0},{2,1},{3,2},{4,7},{5,4},{6,5},{7,6},{8,11},{9,8},{10,9... | collective-permute-start | bytes 1572872 | tf_op jit(solution)/shard_map/ppermute | solution.py:338
  5.8 22.6 %copy-start = (bf16[32,8,64,64]{3,2,1,0:T(8,128)(2,1)S(1)}, bf16[32,8,64,64]{3,2,1,0:T(8,128)(2,1)}, u32[]{:S(2)}) copy-start(bf16[32,8,64,64]{3,2,1,0:T(8,128)(2,1)} %down_ref.1) | copy-start | bytes 6291460
  6.8 21.5 %copy-start.5 = (s32[128]{0:T(128)S(1)}, s32[128]{0:T(128)}, u32[]{:S(2)}) copy-start(s32[128]{0:T(128)} %param.21) | copy-start | bytes 1540
  28.1 2.5 %collective-permute-start.3 = (bf16[8,128,128]{2,1,0:T(8,128)(2,1)S(1)}, bf16[8,128,128]{2,1,0:T(8,128)(2,1)S(1)}, u32[]{:S(2)}, u32[]{:S(2)}) collective-permute-start(bf16[8,128,128]{2,1,0:T(8,128)(2,1)S(1)} %get-tuple-element.23.order_ref), channel_id=1, source_target_pairs={{0,4},{4,0},{8,12},{12,8},{16,20},{20,16},{24,28},{28,24},{32,36},... | collective-permute-start | bytes 786440 | tf_op jit(solution)/shard_map/ppermute | solution.py:371
  30.1 19.4 %copy-start.2 = (bf16[32,64,512]{2,1,0:T(8,128)(2,1)S(1)}, bf16[32,64,512]{2,1,0:T(8,128)(2,1)}, u32[]{:S(2)}) copy-start(bf16[32,64,512]{2,1,0:T(8,128)(2,1)} %up_ref.1) | copy-start | bytes 6291460
  30.1 2.7 %collective-permute-start.2 = (bf16[1088,128]{1,0:T(8,128)(2,1)S(1)}, bf16[1088,128]{1,0:T(8,128)(2,1)S(1)}, u32[]{:S(2)}, u32[]{:S(2)}) collective-permute-start(bf16[1088,128]{1,0:T(8,128)(2,1)S(1)} %get-tuple-element.27), channel_id=1, source_target_pairs={{0,4},{4,0},{8,12},{12,8},{16,20},{20,16},{24,28},{28,24},{32,36},... | collective-permute-start | bytes 835592 | tf_op jit(solution)/shard_map/ppermute | solution.py:392
  30.7 9.9 %collective-permute-start.4 = (bf16[8,128,128]{2,1,0:T(8,128)(2,1)S(1)}, bf16[8,128,128]{2,1,0:T(8,128)(2,1)S(1)}, u32[]{:S(2)}, u32[]{:S(2)}) collective-permute-start(bf16[8,128,128]{2,1,0:T(8,128)(2,1)S(1)} %pair_across.1), channel_id=1, source_target_pairs={{0,2},{1,3},{2,0},{3,1},{4,6},{5,7},{6,4},{7,5},{8,10},{9,11},{10,... | collective-permute-start | bytes 786440 | tf_op jit(solution)/shard_map/ppermute | solution.py:416
  33.5 12.6 %all-to-all-start.2 = ((bf16[8,64,128]{2,1,0:T(8,128)(2,1)}), bf16[8,64,128]{2,1,0:T(8,128)(2,1)S(1)}, u32[]{:S(2)}, u32[]{:S(2)}) async-start(bf16[8,64,128]{2,1,0:T(8,128)(2,1)} %get-tuple-element.30), calls=%async_computation.2 | async-start | bytes 262144 | tf_op jit(solution)/shard_map/all_to_all | solution.py:412
  46.1 14.0 %all-to-all-start.1 = ((bf16[8,128,128]{2,1,0:T(8,128)(2,1)}), bf16[8,128,128]{2,1,0:T(8,128)(2,1)S(1)}, u32[]{:S(2)}, u32[]{:S(2)}) async-start(bf16[8,128,128]{2,1,0:T(8,128)(2,1)} %add.1), calls=%async_computation.1 | async-start | bytes 524288 | tf_op jit(solution)/shard_map/all_to_all | solution.py:412
  51.0 5.5 %collective-permute-start.5 = (bf16[128,128]{1,0:T(8,128)(2,1)S(1)}, bf16[128,128]{1,0:T(8,128)(2,1)S(1)}, u32[]{:S(2)}, u32[]{:S(2)}) collective-permute-start(bf16[128,128]{1,0:T(8,128)(2,1)S(1)} %get-tuple-element.32), channel_id=1, source_target_pairs={{0,2},{1,3},{2,0},{3,1},{4,6},{5,7},{6,4},{7,5},{8,10},{9,11},{10,... | collective-permute-start | bytes 98312 | tf_op jit(solution)/shard_map/ppermute | solution.py:429
  52.8 5.1 %collective-permute-start.6 = (bf16[128,128]{1,0:T(8,128)(2,1)S(1)}, bf16[128,128]{1,0:T(8,128)(2,1)S(1)}, u32[]{:S(2)}, u32[]{:S(2)}) collective-permute-start(bf16[128,128]{1,0:T(8,128)(2,1)S(1)} %get-tuple-element.33), channel_id=1, source_target_pairs={{0,1},{1,2},{2,3},{3,0},{4,5},{5,6},{6,7},{7,4},{8,9},{9,10},{10,1... | collective-permute-start | bytes 98312 | tf_op jit(solution)/shard_map/ppermute | solution.py:429
  53.7 4.2 %collective-permute-start.7 = (bf16[128,128]{1,0:T(8,128)(2,1)S(1)}, bf16[128,128]{1,0:T(8,128)(2,1)S(1)}, u32[]{:S(2)}, u32[]{:S(2)}) collective-permute-start(bf16[128,128]{1,0:T(8,128)(2,1)S(1)} %get-tuple-element.34), channel_id=1, source_target_pairs={{0,3},{1,0},{2,1},{3,2},{4,7},{5,4},{6,5},{7,6},{8,11},{9,8},{10,9... | collective-permute-start | bytes 98312 | tf_op jit(solution)/shard_map/ppermute | solution.py:429
